TPU v7x, 512 devices: a whole 4x4x16 slice. The times are simulated.
512 devices in a mesh: frame: 32 (over z_lo, y), chan: 16 (over x, z_hi, core).
Axes of the slice: x: 4, y: 4, z: 16 (z_hi: 2, z_lo: 8; z = z_hi * 8 + z_lo), core: 2. Of those that a mesh axis runs over, the one named last changes fastest.
Arguments:
- inputs: bfloat16 [1536, 12288], P('chan', 'frame'), may hold values from -6 to 6
- norm_gain: float32 [1536], replicated, may hold values from 0.5 to 2
- norm_bias: float32 [1536], replicated, may hold values from -3 to 3
- value_weight: bfloat16 [1536, 1536], P('chan'), may hold values from -0.15625 to 0.15625
- gate_weight: bfloat16 [1536, 1536], P('chan'), may hold values from -0.15625 to 0.15625
- conv_kernel: float32 [31, 1536], P(None, 'chan'), may hold values from -1 to 1
- project_weight: bfloat16 [1536, 1536], P('chan'), may hold values from -0.15625 to 0.15625
- frame_mask: int32 [12288], P('frame'), may hold values 0 or 1
- upstream: bfloat16 [1536, 12288], P('chan', 'frame'), may hold values from -6 to 6
Outputs:
- inputs_grad: bfloat16 [1536, 12288], P('chan', 'frame')
- value_grad: float32 [1536, 1536], P('chan', 'frame')
- gate_grad: float32 [1536, 1536], P('chan', 'frame')
- project_grad: float32 [1536, 1536], P('chan', 'frame')
- kernel_grad: float32 [31, 1536], P(None, 'chan')
- gain_grad: float32 [1536], P('chan')
- bias_grad: float32 [1536], P('chan')
All inputs are finite; a program needn't handle non-finite values. No bound on the sum of `frame_mask` on one device may be relied on, other than what follows from the above.
Results may differ from a plain program's by a relative error of at most 0.025.
Values may be sent and summed in bfloat16 or wider, within the bound.
No kernel may reach another device: no remote copies, remote signals or barrier semaphores. Data moves between devices by JAX's collectives and lax.ppermute only.
A program may use at most 64 MiB of HBM per device.

v0:
```python
import jax
import jax.numpy as jnp
from jax import lax
from jax.sharding import PartitionSpec as P

eps = 1e-05


def padded_2(cells, sides, width):
    for axis, dim in sides:
        count = lax.axis_size(axis)
        ends = count - 1
        head = lax.slice_in_dim(cells, 0, width, axis=dim)
        tail = lax.slice_in_dim(cells, cells.shape[dim] - width, cells.shape[dim], axis=dim)
        cells = jnp.concatenate(
            [
                lax.ppermute(tail, axis, [(i, (i + 1) % count) for i in range(ends)]),
                cells,
                lax.ppermute(head, axis, [((i + 1) % count, i) for i in range(ends)]),
            ],
            axis=dim,
        )
    return cells


def on_device(
    inputs,
    norm_gain,
    norm_bias,
    value_weight,
    gate_weight,
    conv_kernel,
    project_weight,
    frame_mask,
    upstream,
):
    chan_width = inputs.shape[0]
    frame_rows = inputs.shape[1]
    model_width = value_weight.shape[1]
    taps = conv_kernel.shape[0]
    reach = taps // 2
    chan_index = lax.axis_index("chan")
    offset = chan_index * chan_width
    full_inputs = lax.all_gather(inputs, "chan", axis=0, tiled=True)
    x_float = full_inputs.astype(jnp.float32)
    row_mean = jnp.mean(x_float, axis=0, keepdims=True)
    row_var = jnp.mean(x_float * x_float, axis=0, keepdims=True) - row_mean * row_mean
    inv_std = lax.rsqrt(row_var + eps)
    centred = (x_float - row_mean) * inv_std
    normed = (centred * norm_gain[:, None] + norm_bias[:, None]).astype(jnp.bfloat16)
    centred_local = lax.dynamic_slice_in_dim(centred, offset, chan_width, 0)
    gain_local = lax.dynamic_slice_in_dim(norm_gain, offset, chan_width, 0)[:, None]
    value_proj = jnp.dot(value_weight, normed, preferred_element_type=jnp.float32)
    gate_proj = jnp.dot(gate_weight, normed, preferred_element_type=jnp.float32)
    gate_sig = jax.nn.sigmoid(gate_proj)
    keep = frame_mask.astype(jnp.float32)[None, :]
    glu_out = (value_proj * gate_sig * keep).astype(jnp.bfloat16)
    padded = padded_2(glu_out, (("frame", 1),), reach)
    conv_out = jnp.zeros((chan_width, frame_rows), jnp.float32)
    for k in range(taps):
        conv_out = conv_out + conv_kernel[k][:, None] * padded[:, k : k + frame_rows].astype(
            jnp.float32
        )
    conv_sig = jax.nn.sigmoid(conv_out)
    activated = (conv_out * conv_sig).astype(jnp.bfloat16)
    full_grads = lax.all_gather(upstream, "chan", axis=0, tiled=True)
    act_grad = jnp.dot(project_weight, full_grads, preferred_element_type=jnp.float32).astype(
        jnp.bfloat16
    )
    project_part = lax.dot_general(
        activated, full_grads, (((1,), (1,)), ((), ())), preferred_element_type=jnp.float32
    )
    conv_grad = (
        act_grad.astype(jnp.float32) * (conv_sig + conv_out * conv_sig * (1.0 - conv_sig))
    ).astype(jnp.bfloat16)
    back_pad = padded_2(conv_grad, (("frame", 1),), reach)
    grad_float = conv_grad.astype(jnp.float32)
    glu_grad = jnp.zeros((chan_width, frame_rows), jnp.float32)
    kernel_rows = []
    for k in range(taps):
        glu_grad = glu_grad + conv_kernel[k][:, None] * back_pad[
            :, 2 * reach - k : 2 * reach - k + frame_rows
        ].astype(jnp.float32)
        kernel_rows.append(
            jnp.sum(grad_float * padded[:, k : k + frame_rows].astype(jnp.float32), axis=1)
        )
    kernel_part = jnp.stack(kernel_rows)
    glu_grad = glu_grad * keep
    value_back = (glu_grad * gate_sig).astype(jnp.bfloat16)
    gate_back = (glu_grad * value_proj * gate_sig * (1.0 - gate_sig)).astype(jnp.bfloat16)
    value_part = lax.dot_general(
        value_back, normed, (((1,), (1,)), ((), ())), preferred_element_type=jnp.float32
    )
    gate_part = lax.dot_general(
        gate_back, normed, (((1,), (1,)), ((), ())), preferred_element_type=jnp.float32
    )
    result = lax.dot_general(
        value_weight, value_back, (((0,), (0,)), ((), ())), preferred_element_type=jnp.float32
    )
    normed_grad = lax.psum_scatter(
        (
            result
            + lax.dot_general(
                gate_weight, gate_back, (((0,), (0,)), ((), ())), preferred_element_type=jnp.float32
            )
        ).astype(jnp.bfloat16),
        "chan",
        scatter_dimension=0,
        tiled=True,
    ).astype(jnp.float32)
    scaled_here = normed_grad * gain_local
    first_sum, second_sum = lax.psum(
        (
            jnp.sum(scaled_here, axis=0, keepdims=True),
            jnp.sum(scaled_here * centred_local, axis=0, keepdims=True),
        ),
        "chan",
    )
    first_sum = first_sum / model_width
    second_sum = second_sum / model_width
    scaled = normed_grad * gain_local
    inputs_grad = (
        upstream.astype(jnp.float32) + inv_std * (scaled - first_sum - centred_local * second_sum)
    ).astype(jnp.bfloat16)
    gain_part = jnp.sum(normed_grad * centred_local, axis=1)
    bias_part = jnp.sum(normed_grad, axis=1)
    value_grad, gate_grad, project_grad = (
        lax.psum_scatter(
            value_part.astype(jnp.bfloat16), "frame", scatter_dimension=1, tiled=True
        ).astype(jnp.float32),
        lax.psum_scatter(
            gate_part.astype(jnp.bfloat16), "frame", scatter_dimension=1, tiled=True
        ).astype(jnp.float32),
        lax.psum_scatter(
            project_part.astype(jnp.bfloat16), "frame", scatter_dimension=1, tiled=True
        ).astype(jnp.float32),
    )
    kernel_grad, gain_grad, bias_grad = lax.psum((kernel_part, gain_part, bias_part), "frame")
    return (inputs_grad, value_grad, gate_grad, project_grad, kernel_grad, gain_grad, bias_grad)


def solution(mesh):
    return jax.shard_map(
        on_device,
        mesh=mesh,
        in_specs=(
            P("chan", "frame"),
            P(),
            P(),
            P("chan", None),
            P("chan", None),
            P(None, "chan"),
            P("chan", None),
            P("frame"),
            P("chan", "frame"),
        ),
        out_specs=(
            P("chan", "frame"),
            P("chan", "frame"),
            P("chan", "frame"),
            P("chan", "frame"),
            P(None, "chan"),
            P("chan"),
            P("chan"),
        ),
        check_vma=False,
    )
```

profile of v0, /device:TPU:0, one launch (start us, length us, event | category | flops | bytes accessed | tf_op | source)
XLA Modules:
  0.0 1285.1 jit_solution(611325446421571735)
XLA Ops:
  7.2 0.7 all-gather.3.cloned.1.call-update
  8.0 0.7 all-gather.5.cloned.1.call-update
  8.7 0.7 convert_element_type.286
  9.4 1.0 slice_bitcast_fusion.30
  10.4 79.8 %all-gather.3.cloned.1.call-done = bf16[1536,384]{1,0:T(8,128)(2,1)} async-done(((bf16[96,384]{1,0:T(8,128)(2,1)}), bf16[1536,384]{1,0:T(8,128)(2,1)}) %all-gather.3.cloned.1.call-update) | async-done | bytes 1179664 | tf_op jit(solution)/shard_map/all_gather | solution.py:44
  90.2 1.7 convert_reduce_fusion
  92.0 1.9 fusion.3
  94.7 1.3 collective-permute-start.1
  96.0 4.5 collective-permute-start
  100.6 1.0 slice_bitcast_fusion.29
  102.1 1.6 fusion.43
  103.7 60.3 %all-gather.5.cloned.1.call-done = bf16[1536,384]{1,0:T(8,128)(2,1)} async-done(((bf16[96,384]{1,0:T(8,128)(2,1)}), bf16[1536,384]{1,0:T(8,128)(2,1)}) %all-gather.5.cloned.1.call-update) | async-done | bytes 1179664 | tf_op jit(solution)/shard_map/all_gather | solution.py:66
  164.0 2.0 fusion.79
  166.1 1.3 collective-permute-start.2
  167.4 4.5 collective-permute-start.3
  172.0 1.2 convolution_convert_fusion
  173.5 1.6 multiply_convert_fusion
  175.1 1.2 convolution_convert_fusion.2
  176.4 1.2 convolution_convert_fusion.1
  178.7 1.4 copy.20
  181.2 0.6 fusion.96
  181.8 224.1 %reduce-scatter.11.cloned.1.call-done = bf16[96,48]{0,1:T(8,128)(2,1)} async-done(((bf16[96,1536]{0,1:T(8,128)(2,1)}), bf16[96,48]{0,1:T(8,128)(2,1)}) %reduce-scatter.11.cloned.1.call-update) | async-done | bytes 9232 | tf_op jit(solution)/shard_map/reduce_scatter | solution.py:134
  405.9 1.3 convert_element_type.363
  407.2 233.2 %reduce-scatter.7.cloned.1.call-done = bf16[96,48]{0,1:T(8,128)(2,1)} async-done(((bf16[96,1536]{0,1:T(8,128)(2,1)}), bf16[96,48]{0,1:T(8,128)(2,1)}) %reduce-scatter.7.cloned.1.call-update) | async-done | bytes 9232 | tf_op jit(solution)/shard_map/reduce_scatter | solution.py:128
  640.4 1.3 convert_element_type.358
  641.8 233.0 %reduce-scatter.9.cloned.1.call-done = bf16[96,48]{0,1:T(8,128)(2,1)} async-done(((bf16[96,1536]{0,1:T(8,128)(2,1)}), bf16[96,48]{0,1:T(8,128)(2,1)}) %reduce-scatter.9.cloned.1.call-update) | async-done | bytes 9232 | tf_op jit(solution)/shard_map/reduce_scatter | solution.py:131
  874.8 1.3 convert_element_type.360
  876.1 105.3 %reduce-scatter.13.cloned.1.call-done = bf16[96,384]{1,0:T(8,128)(2,1)} async-done(((bf16[1536,384]{1,0:T(8,128)(2,1)}), bf16[96,384]{1,0:T(8,128)(2,1)}) %reduce-scatter.13.cloned.1.call-update) | async-done | bytes 73744 | tf_op jit(solution)/shard_map/reduce_scatter | solution.py:100
  981.4 1.1 fusion.49
  982.6 62.0 %all-reduce.1 = (f32[1,384]{1,0:T(1,128)S(1)}, f32[1,384]{1,0:T(1,128)S(1)}) all-reduce(f32[1,384]{1,0:T(1,128)S(1)} %broadcast_in_dim.5, f32[1,384]{1,0:T(1,128)S(1)} %broadcast_in_dim.4), channel_id=1, replica_groups=mesh['frame'=32,'chan'=16] {'chan'}, use_global_device_ids=true, to_apply=%region_6.0 | all-reduce | flops 768 | bytes 6144 | tf_op jit(solution)/shard_map/psum | solution.py:112
  1044.6 232.0 %all-reduce = (f32[31,96]{1,0:T(8,128)}, f32[96]{0:T(128)}, f32[96]{0:T(128)}) all-reduce(f32[31,96]{1,0:T(8,128)S(1)} %stack.127, f32[96]{0:T(128)S(1)} %get-tuple-element.14, f32[96]{0:T(128)S(1)} %get-tuple-element.50), channel_id=1, replica_groups=mesh['frame'=32,'chan'=16] {'frame'}, use_global_device_ids=true, to_apply=%region_41.0 | all-reduce | flops 3168 | bytes 25344 | tf_op jit(solution)/shard_map/psum | solution.py:138
  1276.6 1.7 fusion.47
  (45 shorter events, 4.2 us)
Async XLA Ops:
  7.2 87.1 %copy-start = (bf16[96,1536]{1,0:T(8,128)(2,1)S(1)}, bf16[96,1536]{1,0:T(8,128)(2,1)}, u32[]{:S(2)}) copy-start(bf16[96,1536]{1,0:T(8,128)(2,1)} %param.12) | copy-start | bytes 884740
  7.2 84.8 %copy-start.6 = (f32[1536]{0:T(1024)S(1)}, f32[1536]{0:T(1024)}, u32[]{:S(2)}) copy-start(f32[1536]{0:T(1024)} %param.10) | copy-start | bytes 18436
  7.2 84.8 %copy-start.5 = (f32[1536]{0:T(1024)S(1)}, f32[1536]{0:T(1024)}, u32[]{:S(2)}) copy-start(f32[1536]{0:T(1024)} %param.11) | copy-start | bytes 18436
  7.2 83.0 %all-gather.3.cloned.1.call-start = ((), (), s32[]{:S(2)}) async-start(), calls=%async_computation.4 | async-start | bytes 1253376 | tf_op jit(solution)/shard_map/all_gather | solution.py:44
  7.9 156.1 %all-gather.5.cloned.1.call-start = ((), (), s32[]{:S(2)}) async-start(), calls=%async_computation.5 | async-start | bytes 1253376 | tf_op jit(solution)/shard_map/all_gather | solution.py:66
  8.7 397.2 %reduce-scatter.11.cloned.1.call-start = ((), (), s32[]{:S(2)}) async-start(), calls=%async_computation.8 | async-start | bytes 405504 | tf_op jit(solution)/shard_map/reduce_scatter | solution.py:134
  90.2 1.8 copy-start.1
  92.0 1.9 copy-start.4
  94.3 69.8 %copy-start.7 = (bf16[96,1536]{1,0:T(8,128)(2,1)S(1)}, bf16[96,1536]{1,0:T(8,128)(2,1)}, u32[]{:S(2)}) copy-start(bf16[96,1536]{1,0:T(8,128)(2,1)} %param.15) | copy-start | bytes 884740
  94.7 6.8 collective-permute-start.1
  96.0 6.1 collective-permute-start
  164.0 7.9 copy-start.2
  166.1 7.2 collective-permute-start.2
  167.4 6.1 collective-permute-start.3
  173.2 467.2 %reduce-scatter.7.cloned.1.call-start = ((), (), s32[]{:S(2)}) async-start(), calls=%async_computation.6 | async-start | bytes 405504 | tf_op jit(solution)/shard_map/reduce_scatter | solution.py:128
  176.3 698.5 %reduce-scatter.9.cloned.1.call-start = ((), (), s32[]{:S(2)}) async-start(), calls=%async_computation.7 | async-start | bytes 405504 | tf_op jit(solution)/shard_map/reduce_scatter | solution.py:131
  177.6 803.8 %reduce-scatter.13.cloned.1.call-start = ((), (), s32[]{:S(2)}) async-start(), calls=%async_computation.9 | async-start | bytes 1253376 | tf_op jit(solution)/shard_map/reduce_scatter | solution.py:100
  180.1 1096.5 %copy-start.3 = (bf16[96,384]{1,0:T(8,128)(2,1)S(1)}, bf16[96,384]{1,0:T(8,128)(2,1)}, u32[]{:S(2)}) copy-start(bf16[96,384]{1,0:T(8,128)(2,1)} %param.17) | copy-start | bytes 221188
Sparse Core Ops, SparseCore 0:
  11.3 78.8 all-gather.2
  93.5 70.5 all-gather.4
  173.3 232.5 reduce-scatter.10
  408.8 231.6 reduce-scatter.6
  643.1 231.6 reduce-scatter.8
  880.1 101.3 reduce-scatter.12
where the time goes:
time: 1290 us
  waiting for transfers between devices  938 us (73%)
  blocking collectives  294 us (23%)
  other arithmetic  16 us (1%)
  between operations  14.3 us (1%)
    reduce_scatter x1, waiting for transfers between devices, on_device(): lax.psum_scatter(value_part.astype(jnp.bfloat16), 'frame', scatter_dimens...  233 us
    reduce_scatter x1, waiting for transfers between devices, on_device(): lax.psum_scatter(gate_part.astype(jnp.bfloat16), 'frame', scatter_dimensi...  233 us
    psum x1, blocking collectives, on_device(): lax.psum((kernel_part, gain_part, bias_part), 'frame')  232 us
    reduce_scatter x1, waiting for transfers between devices, on_device(): lax.psum_scatter(project_part.astype(jnp.bfloat16), 'frame', scatter_dime...  224 us
    reduce_scatter x1, waiting for transfers between devices, on_device(): lax.psum_scatter((result + lax.dot_general(gate_weight, gate_back, (((0,)...  105 us
    all_gather x1, waiting for transfers between devices, on_device(): full_inputs = lax.all_gather(inputs, 'chan', axis=0, tiled=True)  79.8 us
    psum x1, blocking collectives, on_device(): lax.psum((jnp.sum(scaled_here, axis=0, keepdims=True), jnp.sum(scaled_her...  62 us
    all_gather x1, waiting for transfers between devices, on_device(): full_grads = lax.all_gather(upstream, 'chan', axis=0, tiled=True)  60.3 us
  transfers between devices with their start and end apart: 10, of which 8 were waited for; matrix products, arithmetic and copies ran while one was open for 2% of the time, Pallas kernels for 0%

commit v1 on v0

v1 whole, which is shorter than its diff:
```python
import jax
import jax.numpy as jnp
from jax import lax
from jax.sharding import Mesh, PartitionSpec as P

eps = 1e-05
CHAN = ("x", "zh", "core")
FRAME = ("zl", "y")
SWAP = [(0, 1), (1, 0)]
f32 = jnp.float32
bf16 = jnp.bfloat16


def swap(value, axis):
    return lax.ppermute(value, axis, SWAP)


def ordered(own, other, index, axis):
    return jnp.where(
        index == 0, jnp.stack([own, other], axis), jnp.stack([other, own], axis)
    )


def halo(cells, width):
    count = 32
    head = cells[:, :width]
    tail = cells[:, cells.shape[1] - width :]
    left = lax.ppermute(tail, FRAME, [(i, i + 1) for i in range(count - 1)])
    right = lax.ppermute(head, FRAME, [(i + 1, i) for i in range(count - 1)])
    return jnp.concatenate([left, cells, right], axis=1)


def split_bf16(value):
    high = value.astype(bf16)
    return high, (value - high.astype(f32)).astype(bf16)


def on_device(
    inputs,
    norm_gain,
    norm_bias,
    value_weight,
    gate_weight,
    conv_kernel,
    project_weight,
    frame_mask,
    upstream,
):
    width, rows = inputs.shape
    model = value_weight.shape[1]
    taps = conv_kernel.shape[0]
    reach = taps // 2
    zh = lax.axis_index("zh")
    core = lax.axis_index("core")
    offset = lax.axis_index(CHAN) * width

    in_other = swap(inputs, "zh")
    in_pair = ordered(inputs, in_other, zh, 0)
    up_other = swap(lax.optimization_barrier((upstream, in_other))[0], "zh")
    in_x = lax.all_gather(in_pair, "x", axis=0, tiled=False)
    in_core = swap(in_x, "core")
    full_inputs = ordered(in_x, in_core, core, 2).reshape(model, rows)

    up_pair = ordered(upstream, up_other, zh, 0)
    up_pair = lax.optimization_barrier((up_pair, in_x))[0]
    up_x = lax.all_to_all(
        jnp.broadcast_to(up_pair[None], (4, 2, width, rows)), "x", 0, 0, tiled=True
    )
    up_core = swap(up_x, "core")
    full_grads = ordered(up_x, up_core, core, 2).reshape(model, rows)

    x_float = full_inputs.astype(f32)
    row_mean = jnp.mean(x_float, axis=0, keepdims=True)
    row_var = jnp.mean(x_float * x_float, axis=0, keepdims=True) - row_mean * row_mean
    inv_std = lax.rsqrt(row_var + eps)
    centred = (x_float - row_mean) * inv_std
    normed = (centred * norm_gain[:, None] + norm_bias[:, None]).astype(bf16)
    centred_local = (inputs.astype(f32) - row_mean) * inv_std
    gain_local = lax.dynamic_slice_in_dim(norm_gain, offset, width, 0)[:, None]

    value_proj = jnp.dot(value_weight, normed, preferred_element_type=f32)
    gate_proj = jnp.dot(gate_weight, normed, preferred_element_type=f32)
    gate_sig = jax.nn.sigmoid(gate_proj)
    keep = frame_mask.astype(f32)[None, :]
    glu_out = (value_proj * gate_sig * keep).astype(bf16)
    padded = halo(glu_out, reach)
    conv_out = jnp.zeros((width, rows), f32)
    for k in range(taps):
        conv_out = conv_out + conv_kernel[k][:, None] * padded[:, k : k + rows].astype(f32)
    conv_sig = jax.nn.sigmoid(conv_out)
    activated = (conv_out * conv_sig).astype(bf16)

    act_grad = jnp.dot(project_weight, full_grads, preferred_element_type=f32).astype(bf16)
    conv_grad = (
        act_grad.astype(f32) * (conv_sig + conv_out * conv_sig * (1.0 - conv_sig))
    ).astype(bf16)
    back_pad = halo(conv_grad, reach)
    grad_float = conv_grad.astype(f32)
    glu_grad = jnp.zeros((width, rows), f32)
    kernel_rows = []
    for k in range(taps):
        glu_grad = glu_grad + conv_kernel[k][:, None] * back_pad[
            :, 2 * reach - k : 2 * reach - k + rows
        ].astype(f32)
        kernel_rows.append(
            jnp.sum(grad_float * padded[:, k : k + rows].astype(f32), axis=1)
        )
    kernel_part = jnp.stack(kernel_rows)
    glu_grad = glu_grad * keep
    value_back = (glu_grad * gate_sig).astype(bf16)
    gate_back = (glu_grad * value_proj * gate_sig * (1.0 - gate_sig)).astype(bf16)

    across = (((0,), (0,)), ((), ()))
    partial = (
        lax.dot_general(value_weight, value_back, across, preferred_element_type=f32)
        + lax.dot_general(gate_weight, gate_back, across, preferred_element_type=f32)
    ).astype(bf16)
    scaled = partial.astype(f32) * norm_gain[:, None]
    sums = jnp.stack([jnp.sum(scaled, axis=0), jnp.sum(scaled * centred, axis=0)])
    sums_high, sums_low = split_bf16(sums)
    blocks = partial.reshape(4, 2, 2, width, rows)
    far = jnp.where(zh == 0, blocks[:, 1], blocks[:, 0]).reshape(8, width, rows)
    near = jnp.where(zh == 0, blocks[:, 0], blocks[:, 1]).reshape(8, width, rows)
    extra = jnp.concatenate([sums_high, sums_low, jnp.zeros((12, rows), bf16)])
    far = jnp.concatenate([far, jnp.broadcast_to(extra[None], (8, 16, rows))], axis=1)
    far = lax.all_to_all(far, ("x", "core"), 0, 0, tiled=True)
    far = jnp.sum(far.astype(f32), axis=0)
    far_sums = far[width : width + 2] + far[width + 2 : width + 4]
    sent_high, sent_low = split_bf16(far_sums)
    far = jnp.concatenate(
        [far[:width].astype(bf16), sent_high, sent_low, jnp.zeros((12, rows), bf16)]
    )
    came = swap(far, "zh").astype(f32)
    near = lax.optimization_barrier((near, far))[0]
    near = lax.all_to_all(near, ("x", "core"), 0, 0, tiled=True)
    normed_grad = jnp.sum(near.astype(f32), axis=0) + came[:width]
    sums = (far_sums + came[width : width + 2] + came[width + 2 : width + 4]) / model

    inputs_grad = (
        upstream.astype(f32)
        + inv_std * (normed_grad * gain_local - sums[0:1] - centred_local * sums[1:2])
    ).astype(bf16)
    tail = jnp.stack([jnp.sum(normed_grad * centred_local, axis=1), jnp.sum(normed_grad, axis=1)])
    tail = lax.all_to_all(
        jnp.broadcast_to(tail[None], (32, 2, width)), FRAME, 0, 0, tiled=True
    )
    tail = jnp.sum(tail, axis=0)

    over = (((1,), (1,)), ((), ()))
    zero = jnp.zeros((width, rows), bf16)
    grads = lax.dot_general(
        normed,
        jnp.concatenate([value_back, gate_back, zero, zero]),
        over,
        preferred_element_type=f32,
    ) + lax.dot_general(
        full_grads,
        jnp.concatenate([zero, zero, activated, zero]),
        over,
        preferred_element_type=f32,
    )
    piece = model // 32
    grads = grads.reshape(8, 4, piece, 4 * width).transpose(1, 0, 2, 3).astype(bf16)
    tap_high, tap_low = split_bf16(
        jnp.pad(kernel_part, ((0, piece - taps), (3 * width, 0)))
    )
    grads = jnp.concatenate(
        [
            grads[:, 0:1] + tap_high[None, None],
            grads[:, 1:2] + tap_low[None, None],
            grads[:, 2:],
        ],
        axis=1,
    )
    grads = lax.all_to_all(grads, "y", 0, 0, tiled=True)
    grads = jnp.sum(grads.astype(f32), axis=0)
    own_taps = (grads[0] + grads[1])[:, 3 * width :]
    grads = jnp.concatenate(
        [
            grads[:, :, : 3 * width].astype(bf16),
            jnp.broadcast_to(own_taps.astype(bf16)[None], (8, piece, width)),
        ],
        axis=2,
    )
    grads = lax.all_to_all(grads, "zl", 0, 0, tiled=True)
    grads = jnp.sum(grads.astype(f32), axis=0)
    value_grad = grads[:, :width].T
    gate_grad = grads[:, width : 2 * width].T
    project_grad = grads[:, 2 * width : 3 * width].T
    kernel_grad = grads[:taps, 3 * width :]
    return (inputs_grad, value_grad, gate_grad, project_grad, kernel_grad, tail[0], tail[1])


def solution(mesh):
    split = Mesh(mesh.devices.reshape(8, 4, 4, 2, 2), FRAME + CHAN)
    return jax.shard_map(
        on_device,
        mesh=split,
        in_specs=(
            P(CHAN, FRAME),
            P(),
            P(),
            P(CHAN, None),
            P(CHAN, None),
            P(None, CHAN),
            P(CHAN, None),
            P(FRAME),
            P(CHAN, FRAME),
        ),
        out_specs=(
            P(CHAN, FRAME),
            P(CHAN, FRAME),
            P(CHAN, FRAME),
            P(CHAN, FRAME),
            P(None, CHAN),
            P(CHAN),
            P(CHAN),
        ),
        check_vma=False,
    )
```

time: 1290 us -> 216 us (0.17)
  the two profiles are of different devices: /device:TPU:0 before, /device:TPU:32 now
where the time goes in v1:
time: 216 us; the launch traced here: 215 us
  waiting for transfers between devices  82.1 us (38%)
  starting transfers between devices  76.7 us (36%)
  other arithmetic  19.4 us (9%)
  blocking collectives  14 us (6%)
  local copies, waits for them, and re-layouts  13.7 us (6%)
  matrix products  7.13 us (3%)
    ppermute x5, starting transfers between devices, swap(): return lax.ppermute(value, axis, SWAP)  32.9 us
    ppermute x5, waiting for transfers between devices, swap(): return lax.ppermute(value, axis, SWAP)  22.8 us
    all_to_all x1, waiting for transfers between devices, on_device(): grads = lax.all_to_all(grads, 'zl', 0, 0, tiled=True)  15.7 us
    all_gather x1, blocking collectives, on_device(): in_x = lax.all_gather(in_pair, 'x', axis=0, tiled=False)  14 us
    ppermute x2, starting transfers between devices, halo(): right = lax.ppermute(head, FRAME, [(i + 1, i) for i in range(count - 1)])  11.6 us
    all_to_all x1, waiting for transfers between devices, on_device(): near = lax.all_to_all(near, ('x', 'core'), 0, 0, tiled=True)  10.6 us
    all_to_all x1, waiting for transfers between devices, on_device(): lax.all_to_all(jnp.broadcast_to(tail[None], (32, 2, width)), FRAME, 0, 0,...  10.5 us
    all_to_all x1, waiting for transfers between devices, on_device(): lax.all_to_all(jnp.broadcast_to(up_pair[None], (4, 2, width, rows)), 'x',...  9.82 us
  transfers between devices with their start and end apart: 15, of which 8 were waited for; matrix products, arithmetic and copies ran while one was open for 9% of the time, Pallas kernels for 0%

profile of v1, /device:TPU:32, one launch (start us, length us, event | category | flops | bytes accessed | tf_op | source)
XLA Modules:
  0.0 215.1 jit_solution(15165233306021615727)
XLA Ops:
  0.6 15.0 %collective-permute-start = (bf16[96,384]{1,0:T(8,128)(2,1)}, bf16[96,384]{1,0:T(8,128)(2,1)S(1)}, u32[]{:S(2)}, u32[]{:S(2)}) collective-permute-start(bf16[96,384]{1,0:T(8,128)(2,1)} %param.9), channel_id=1, source_target_pairs={{0,2},{2,0},{1,3},{3,1},{4,6},{6,4},{5,7},{7,5},{8,10},{10,8},{9,1... | collective-permute-start | bytes 221192 | tf_op jit(solution)/shard_map/ppermute | solution.py:15
  15.6 4.3 %collective-permute-done = bf16[96,384]{1,0:T(8,128)(2,1)S(1)} collective-permute-done((bf16[96,384]{1,0:T(8,128)(2,1)}, bf16[96,384]{1,0:T(8,128)(2,1)S(1)}, u32[]{:S(2)}, u32[]{:S(2)}) %collective-permute-start) | collective-permute-done | bytes 73760 | tf_op jit(solution)/shard_map/ppermute | solution.py:15
  19.9 11.9 %collective-permute-start.2 = (bf16[96,384]{1,0:T(8,128)(2,1)}, bf16[96,384]{1,0:T(8,128)(2,1)S(1)}, u32[]{:S(2)}, u32[]{:S(2)}) collective-permute-start(bf16[96,384]{1,0:T(8,128)(2,1)} %param.17), channel_id=1, source_target_pairs={{0,2},{2,0},{1,3},{3,1},{4,6},{6,4},{5,7},{7,5},{8,10},{10,8},{9,1... | collective-permute-start | bytes 221192 | tf_op jit(solution)/shard_map/ppermute | solution.py:15
  32.8 14.0 %all_gather.4 = bf16[4,2,96,384]{3,2,1,0:T(8,128)(2,1)S(1)} all-gather(bf16[1,2,96,384]{3,2,1,0:T(8,128)(2,1)S(1)} %maximum_select_fusion.2), channel_id=1, replica_groups=mesh['zl'=8,'y'=4,'x'=4,'zh'=2,'core'=2] {'x'}, dimensions={0}, use_global_device_ids=true | all-gather | bytes 737280 | tf_op jit(solution)/shard_map/all_gather | solution.py:60
  46.8 2.0 collective-permute-start.1
  50.7 3.5 %all-to-all-start = ((bf16[4,2,96,384]{3,2,1,0:T(8,128)(2,1)}), bf16[4,2,96,384]{3,2,1,0:T(8,128)(2,1)S(1)}, u32[]{:S(2)}, u32[]{:S(2)}) async-start(bf16[4,2,96,384]{3,2,1,0:T(8,128)(2,1)} %broadcast_in_dim.10), calls=%async_computation | async-start | bytes 1179648 | tf_op jit(solution)/shard_map/all_to_all | solution.py:66
  55.5 9.8 %all-to-all-done = bf16[4,2,96,384]{3,2,1,0:T(8,128)(2,1)S(1)} async-done(((bf16[4,2,96,384]{3,2,1,0:T(8,128)(2,1)}), bf16[4,2,96,384]{3,2,1,0:T(8,128)(2,1)S(1)}, u32[]{:S(2)}, u32[]{:S(2)}) %all-to-all-start) | async-done | bytes 589856 | tf_op jit(solution)/shard_map/all_to_all | solution.py:66
  65.3 1.9 collective-permute-start.3
  67.8 1.6 fusion.4
  69.4 2.1 copy.26
  73.9 3.5 %collective-permute-start.4 = (bf16[96,15]{1,0:T(8,128)(2,1)S(1)}, bf16[96,15]{1,0:T(8,128)(2,1)S(1)}, u32[]{:S(2)}, u32[]{:S(2)}) collective-permute-start(bf16[96,15]{1,0:T(8,128)(2,1)S(1)} %get-tuple-element.68), channel_id=1, source_target_pairs={{0,16},{16,32},{32,48},{48,64},{64,80},{80,96},{96,112},{112,128},... | collective-permute-start | bytes 8648 | tf_op jit(solution)/shard_map/ppermute | solution.py:28
  77.4 5.6 %collective-permute-start.5 = (bf16[96,15]{1,0:T(8,128)(2,1)S(1)}, bf16[96,15]{1,0:T(8,128)(2,1)S(1)}, u32[]{:S(2)}, u32[]{:S(2)}) collective-permute-start(bf16[96,15]{1,0:T(8,128)(2,1)S(1)} %get-tuple-element.69), channel_id=1, source_target_pairs={{16,0},{32,16},{48,32},{64,48},{80,64},{96,80},{112,96},{128,112},... | collective-permute-start | bytes 8648 | tf_op jit(solution)/shard_map/ppermute | solution.py:29
  84.9 2.3 %fusion.103 = (bf16[96,384]{1,0:T(8,128)(2,1)}, f32[96,384]{1,0:T(8,128)S(1)}) fusion(bf16[96,15]{1,0:T(8,128)(2,1)S(1)} %collective-permute-done.5, bf16[96,384]{1,0:T(8,128)(2,1)S(1)} %get-tuple-element.105, f32[96]{0:T(128)S(1)} %get-tuple-element.99, f32[96]{0:T(128)S(1)} %get-tuple-element.100, f32[96]{0:T(128)S(1)} %copy-done.17, ...), kind=kLoop, calls=%fused_computation.314 | loop fusion | flops 6893568 | bytes 312576 | tf_op jit(solution)/shard_map/convert_element_type | solution.py:91
  92.3 6.1 %collective-permute-start.6 = (bf16[96,15]{1,0:T(8,128)(2,1)S(1)}, bf16[96,15]{1,0:T(8,128)(2,1)S(1)}, u32[]{:S(2)}, u32[]{:S(2)}) collective-permute-start(bf16[96,15]{1,0:T(8,128)(2,1)S(1)} %get-tuple-element.66), channel_id=1, source_target_pairs={{16,0},{32,16},{48,32},{64,48},{80,64},{96,80},{112,96},{128,112},... | collective-permute-start | bytes 8648 | tf_op jit(solution)/shard_map/ppermute | solution.py:29
  98.3 1.9 collective-permute-start.7
  100.9 5.2 %collective-permute-done.7 = bf16[96,15]{1,0:T(8,128)(2,1)S(1)} collective-permute-done((bf16[96,15]{1,0:T(8,128)(2,1)S(1)}, bf16[96,15]{1,0:T(8,128)(2,1)S(1)}, u32[]{:S(2)}, u32[]{:S(2)}) %collective-permute-start.7) | collective-permute-done | bytes 2912 | tf_op jit(solution)/shard_map/ppermute | solution.py:28
  106.5 1.7 multiply_convert_fusion
  109.2 1.9 fusion.3
  112.1 2.4 %copy.27 = bf16[1536,384]{1,0:T(8,128)(2,1)} copy(bf16[1536,384]{0,1:T(8,128)(2,1)} %get-tuple-element.107) | data formatting | bytes 2359296 | tf_op jit(solution)/shard_map/convert_element_type | solution.py:117
  114.4 2.2 %broadcast_select_fusion.1 = (bf16[4,1,2,96,384]{4,3,2,1,0:T(8,128)(2,1)}, bf16[4,1,2,96,384]{4,3,2,1,0:T(8,128)(2,1)S(1)}) fusion(pred[]{:T(512)S(6)} %eq.5, bf16[4,2,2,96,384]{4,3,2,1,0:T(8,128)(2,1)} %bitcast.151), kind=kLoop, calls=%fused_computation.66 | loop fusion | flops 589824 | bytes 2359297 | tf_op jit(solution)/shard_map/jit(_where)/select_n | solution.py:123
  117.6 3.7 %all-to-all-start.1 = ((bf16[8,112,384]{2,1,0:T(8,128)(2,1)}), bf16[8,112,384]{2,1,0:T(8,128)(2,1)S(1)}, u32[]{:S(2)}, u32[]{:S(2)}) async-start(bf16[8,112,384]{2,1,0:T(8,128)(2,1)} %pad_maximum_fusion.1), calls=%async_computation.1 | async-start | bytes 1376256 | tf_op jit(solution)/shard_map/all_to_all | solution.py:126
  121.3 2.2 %fusion = bf16[1536,384]{1,0:T(8,128)(2,1)S(1)} fusion(f32[1536,384]{1,0:T(8,128)S(1)} %fusion.13, bf16[1536,384]{1,0:T(8,128)(2,1)} %bitcast.155, bf16[96,384]{1,0:T(8,128)(2,1)} %get-tuple-element.52, bf16[192,384]{1,0:T(8,128)(2,1)S(1)} %broadcast.76, bf16[384]{0:T(512)(128)(2,1)S(1)} %copy-done.77), kind=kOutput, calls=%fused_computation.2 | convolution fusion | flops 455049216 | bytes 4940544 | tf_op jit(solution)/shard_map/dot_general | solution.py:156
  125.6 7.5 %all-to-all-done.1 = bf16[8,112,384]{2,1,0:T(8,128)(2,1)S(1)} async-done(((bf16[8,112,384]{2,1,0:T(8,128)(2,1)}), bf16[8,112,384]{2,1,0:T(8,128)(2,1)S(1)}, u32[]{:S(2)}, u32[]{:S(2)}) %all-to-all-start.1) | async-done | bytes 688160 | tf_op jit(solution)/shard_map/all_to_all | solution.py:126
  133.2 3.5 %all-to-all-start.3 = ((bf16[4,8,48,384]{3,2,1,0:T(8,128)(2,1)}), bf16[4,8,48,384]{3,2,1,0:T(8,128)(2,1)S(1)}, u32[]{:S(2)}, u32[]{:S(2)}) async-start(bf16[4,8,48,384]{3,2,1,0:T(8,128)(2,1)} %pad_maximum_fusion), calls=%async_computation.3 | async-start | bytes 2359296 | tf_op jit(solution)/shard_map/all_to_all | solution.py:175
  136.8 2.1 collective-permute-start.8
  139.0 18.4 %collective-permute-done.8 = bf16[112,384]{1,0:T(8,128)(2,1)S(1)} collective-permute-done((bf16[112,384]{1,0:T(8,128)(2,1)S(1)}, bf16[112,384]{1,0:T(8,128)(2,1)S(1)}, u32[]{:S(2)}, u32[]{:S(2)}) %collective-permute-start.8) | collective-permute-done | bytes 86048 | tf_op jit(solution)/shard_map/ppermute | solution.py:15
  157.5 3.5 %all-to-all-start.2 = ((bf16[8,96,384]{2,1,0:T(8,128)(2,1)}), bf16[8,96,384]{2,1,0:T(8,128)(2,1)S(1)}, u32[]{:S(2)}, u32[]{:S(2)}) async-start(bf16[8,96,384]{2,1,0:T(8,128)(2,1)} %bitcast.46), calls=%async_computation.2 | async-start | bytes 1179648 | tf_op jit(solution)/shard_map/all_to_all | solution.py:135
  161.4 10.6 %all-to-all-done.2 = bf16[8,96,384]{2,1,0:T(8,128)(2,1)S(1)} async-done(((bf16[8,96,384]{2,1,0:T(8,128)(2,1)}), bf16[8,96,384]{2,1,0:T(8,128)(2,1)S(1)}, u32[]{:S(2)}, u32[]{:S(2)}) %all-to-all-start.2) | async-done | bytes 589856 | tf_op jit(solution)/shard_map/all_to_all | solution.py:135
  173.6 7.6 %all-to-all-start.5 = ((f32[32,2,96]{2,1,0:T(2,128)}), f32[32,2,96]{2,1,0:T(2,128)S(1)}, u32[]{:S(2)}, u32[]{:S(2)}) async-start(f32[32,2,96]{2,1,0:T(2,128)} %broadcast_in_dim.14), calls=%async_computation.5 | async-start | bytes 65536 | tf_op jit(solution)/shard_map/all_to_all | solution.py:144
  182.0 10.5 %all-to-all-done.5 = f32[32,2,96]{2,1,0:T(2,128)S(1)} async-done(((f32[32,2,96]{2,1,0:T(2,128)}), f32[32,2,96]{2,1,0:T(2,128)S(1)}, u32[]{:S(2)}, u32[]{:S(2)}) %all-to-all-start.5) | async-done | bytes 24608 | tf_op jit(solution)/shard_map/all_to_all | solution.py:144
  192.5 4.9 %all-to-all-start.4 = ((bf16[8,48,384]{2,1,0:T(8,128)(2,1)}), bf16[8,48,384]{2,1,0:T(8,128)(2,1)S(1)}, u32[]{:S(2)}, u32[]{:S(2)}) async-start(bf16[8,48,384]{2,1,0:T(8,128)(2,1)} %pad_maximum_fusion.2), calls=%async_computation.4 | async-start | bytes 589824 | tf_op jit(solution)/shard_map/all_to_all | solution.py:185
  198.0 15.7 %all-to-all-done.4 = bf16[8,48,384]{2,1,0:T(8,128)(2,1)S(1)} async-done(((bf16[8,48,384]{2,1,0:T(8,128)(2,1)}), bf16[8,48,384]{2,1,0:T(8,128)(2,1)S(1)}, u32[]{:S(2)}, u32[]{:S(2)}) %all-to-all-start.4) | async-done | bytes 294944 | tf_op jit(solution)/shard_map/all_to_all | solution.py:185
  (229 shorter events, 23.9 us)
Async XLA Ops:
  0.6 72.3 %copy-start = (bf16[96,1536]{1,0:T(8,128)(2,1)S(1)}, bf16[96,1536]{1,0:T(8,128)(2,1)}, u32[]{:S(2)}) copy-start(bf16[96,1536]{1,0:T(8,128)(2,1)} %param.12) | copy-start | bytes 884740
  0.6 19.3 %collective-permute-start = (bf16[96,384]{1,0:T(8,128)(2,1)}, bf16[96,384]{1,0:T(8,128)(2,1)S(1)}, u32[]{:S(2)}, u32[]{:S(2)}) collective-permute-start(bf16[96,384]{1,0:T(8,128)(2,1)} %param.9), channel_id=1, source_target_pairs={{0,2},{2,0},{1,3},{3,1},{4,6},{6,4},{5,7},{7,5},{8,10},{10,8},{9,1... | collective-permute-start | bytes 221192 | tf_op jit(solution)/shard_map/ppermute | solution.py:15
  19.9 28.9 %collective-permute-start.2 = (bf16[96,384]{1,0:T(8,128)(2,1)}, bf16[96,384]{1,0:T(8,128)(2,1)S(1)}, u32[]{:S(2)}, u32[]{:S(2)}) collective-permute-start(bf16[96,384]{1,0:T(8,128)(2,1)} %param.17), channel_id=1, source_target_pairs={{0,2},{2,0},{1,3},{3,1},{4,6},{6,4},{5,7},{7,5},{8,10},{10,8},{9,1... | collective-permute-start | bytes 221192 | tf_op jit(solution)/shard_map/ppermute | solution.py:15
  46.8 20.4 %collective-permute-start.1 = (bf16[4,2,96,384]{3,2,1,0:T(8,128)(2,1)S(1)}, bf16[4,2,96,384]{3,2,1,0:T(8,128)(2,1)S(1)}, u32[]{:S(2)}, u32[]{:S(2)}) collective-permute-start(bf16[4,2,96,384]{3,2,1,0:T(8,128)(2,1)S(1)} %all_gather.4), channel_id=1, source_target_pairs={{0,1},{1,0},{2,3},{3,2},{4,5},{5,4},{6,7},{7,6},{8,9},{9,8},{10,11... | collective-permute-start | bytes 1769480 | tf_op jit(solution)/shard_map/ppermute | solution.py:15
  50.7 14.6 %all-to-all-start = ((bf16[4,2,96,384]{3,2,1,0:T(8,128)(2,1)}), bf16[4,2,96,384]{3,2,1,0:T(8,128)(2,1)S(1)}, u32[]{:S(2)}, u32[]{:S(2)}) async-start(bf16[4,2,96,384]{3,2,1,0:T(8,128)(2,1)} %broadcast_in_dim.10), calls=%async_computation | async-start | bytes 1179648 | tf_op jit(solution)/shard_map/all_to_all | solution.py:66
  65.3 21.9 %collective-permute-start.3 = (bf16[4,2,96,384]{3,2,1,0:T(8,128)(2,1)S(1)}, bf16[4,2,96,384]{3,2,1,0:T(8,128)(2,1)}, u32[]{:S(2)}, u32[]{:S(2)}) collective-permute-start(bf16[4,2,96,384]{3,2,1,0:T(8,128)(2,1)S(1)} %all-to-all-done), channel_id=1, source_target_pairs={{0,1},{1,0},{2,3},{3,2},{4,5},{5,4},{6,7},{7,6},{8,9},{9,8},{10,11... | collective-permute-start | bytes 1769480 | tf_op jit(solution)/shard_map/ppermute | solution.py:15
  73.9 10.8 %collective-permute-start.4 = (bf16[96,15]{1,0:T(8,128)(2,1)S(1)}, bf16[96,15]{1,0:T(8,128)(2,1)S(1)}, u32[]{:S(2)}, u32[]{:S(2)}) collective-permute-start(bf16[96,15]{1,0:T(8,128)(2,1)S(1)} %get-tuple-element.68), channel_id=1, source_target_pairs={{0,16},{16,32},{32,48},{48,64},{64,80},{80,96},{96,112},{112,128},... | collective-permute-start | bytes 8648 | tf_op jit(solution)/shard_map/ppermute | solution.py:28
  77.4 7.3 %collective-permute-start.5 = (bf16[96,15]{1,0:T(8,128)(2,1)S(1)}, bf16[96,15]{1,0:T(8,128)(2,1)S(1)}, u32[]{:S(2)}, u32[]{:S(2)}) collective-permute-start(bf16[96,15]{1,0:T(8,128)(2,1)S(1)} %get-tuple-element.69), channel_id=1, source_target_pairs={{16,0},{32,16},{48,32},{64,48},{80,64},{96,80},{112,96},{128,112},... | collective-permute-start | bytes 8648 | tf_op jit(solution)/shard_map/ppermute | solution.py:29
  88.8 17.4 %copy-start.12 = (f32[384]{0:T(512)S(1)}, f32[384]{0:T(512)}, u32[]{:S(2)}) copy-start(f32[384]{0:T(512)} %convert_element_type.341) | copy-start | bytes 4612
  88.8 17.4 %copy-start.16 = (f32[96]{0:T(128)S(1)}, f32[96]{0:T(128)}, u32[]{:S(2)}) copy-start(f32[96]{0:T(128)} %get-tuple-element.70) | copy-start | bytes 1156
  88.8 17.3 %copy-start.18 = (f32[96]{0:T(128)S(1)}, f32[96]{0:T(128)}, u32[]{:S(2)}) copy-start(f32[96]{0:T(128)} %get-tuple-element.71) | copy-start | bytes 1156
  88.8 17.3 %copy-start.20 = (f32[96]{0:T(128)S(1)}, f32[96]{0:T(128)}, u32[]{:S(2)}) copy-start(f32[96]{0:T(128)} %get-tuple-element.72) | copy-start | bytes 1156
  88.8 17.3 %copy-start.22 = (f32[96]{0:T(128)S(1)}, f32[96]{0:T(128)}, u32[]{:S(2)}) copy-start(f32[96]{0:T(128)} %get-tuple-element.73) | copy-start | bytes 1156
  88.9 17.3 %copy-start.24 = (f32[96]{0:T(128)S(1)}, f32[96]{0:T(128)}, u32[]{:S(2)}) copy-start(f32[96]{0:T(128)} %get-tuple-element.74) | copy-start | bytes 1156
  88.9 17.3 %copy-start.26 = (f32[96]{0:T(128)S(1)}, f32[96]{0:T(128)}, u32[]{:S(2)}) copy-start(f32[96]{0:T(128)} %get-tuple-element.75) | copy-start | bytes 1156
  88.9 17.3 %copy-start.28 = (f32[96]{0:T(128)S(1)}, f32[96]{0:T(128)}, u32[]{:S(2)}) copy-start(f32[96]{0:T(128)} %get-tuple-element.76) | copy-start | bytes 1156
  88.9 17.3 %copy-start.30 = (f32[96]{0:T(128)S(1)}, f32[96]{0:T(128)}, u32[]{:S(2)}) copy-start(f32[96]{0:T(128)} %get-tuple-element.77) | copy-start | bytes 1156
  88.9 17.3 %copy-start.32 = (f32[96]{0:T(128)S(1)}, f32[96]{0:T(128)}, u32[]{:S(2)}) copy-start(f32[96]{0:T(128)} %get-tuple-element.78) | copy-start | bytes 1156
  88.9 17.3 %copy-start.34 = (f32[96]{0:T(128)S(1)}, f32[96]{0:T(128)}, u32[]{:S(2)}) copy-start(f32[96]{0:T(128)} %get-tuple-element.79) | copy-start | bytes 1156
  88.9 17.3 %copy-start.36 = (f32[96]{0:T(128)S(1)}, f32[96]{0:T(128)}, u32[]{:S(2)}) copy-start(f32[96]{0:T(128)} %get-tuple-element.80) | copy-start | bytes 1156
  88.9 17.3 %copy-start.38 = (f32[96]{0:T(128)S(1)}, f32[96]{0:T(128)}, u32[]{:S(2)}) copy-start(f32[96]{0:T(128)} %get-tuple-element.81) | copy-start | bytes 1156
  88.9 17.3 %copy-start.40 = (f32[96]{0:T(128)S(1)}, f32[96]{0:T(128)}, u32[]{:S(2)}) copy-start(f32[96]{0:T(128)} %get-tuple-element.82) | copy-start | bytes 1156
  88.9 17.3 %copy-start.42 = (f32[96]{0:T(128)S(1)}, f32[96]{0:T(128)}, u32[]{:S(2)}) copy-start(f32[96]{0:T(128)} %get-tuple-element.83) | copy-start | bytes 1156
  89.0 17.3 %copy-start.44 = (f32[96]{0:T(128)S(1)}, f32[96]{0:T(128)}, u32[]{:S(2)}) copy-start(f32[96]{0:T(128)} %get-tuple-element.84) | copy-start | bytes 1156
  92.3 8.7 %collective-permute-start.6 = (bf16[96,15]{1,0:T(8,128)(2,1)S(1)}, bf16[96,15]{1,0:T(8,128)(2,1)S(1)}, u32[]{:S(2)}, u32[]{:S(2)}) collective-permute-start(bf16[96,15]{1,0:T(8,128)(2,1)S(1)} %get-tuple-element.66), channel_id=1, source_target_pairs={{16,0},{32,16},{48,32},{64,48},{80,64},{96,80},{112,96},{128,112},... | collective-permute-start | bytes 8648 | tf_op jit(solution)/shard_map/ppermute | solution.py:29
  98.3 7.8 %collective-permute-start.7 = (bf16[96,15]{1,0:T(8,128)(2,1)S(1)}, bf16[96,15]{1,0:T(8,128)(2,1)S(1)}, u32[]{:S(2)}, u32[]{:S(2)}) collective-permute-start(bf16[96,15]{1,0:T(8,128)(2,1)S(1)} %get-tuple-element.67), channel_id=1, source_target_pairs={{0,16},{16,32},{32,48},{48,64},{64,80},{80,96},{96,112},{112,128},... | collective-permute-start | bytes 8648 | tf_op jit(solution)/shard_map/ppermute | solution.py:28
  117.6 15.6 %all-to-all-start.1 = ((bf16[8,112,384]{2,1,0:T(8,128)(2,1)}), bf16[8,112,384]{2,1,0:T(8,128)(2,1)S(1)}, u32[]{:S(2)}, u32[]{:S(2)}) async-start(bf16[8,112,384]{2,1,0:T(8,128)(2,1)} %pad_maximum_fusion.1), calls=%async_computation.1 | async-start | bytes 1376256 | tf_op jit(solution)/shard_map/all_to_all | solution.py:126
  133.2 24.3 %all-to-all-start.3 = ((bf16[4,8,48,384]{3,2,1,0:T(8,128)(2,1)}), bf16[4,8,48,384]{3,2,1,0:T(8,128)(2,1)S(1)}, u32[]{:S(2)}, u32[]{:S(2)}) async-start(bf16[4,8,48,384]{3,2,1,0:T(8,128)(2,1)} %pad_maximum_fusion), calls=%async_computation.3 | async-start | bytes 2359296 | tf_op jit(solution)/shard_map/all_to_all | solution.py:175
  136.8 20.6 %collective-permute-start.8 = (bf16[112,384]{1,0:T(8,128)(2,1)S(1)}, bf16[112,384]{1,0:T(8,128)(2,1)S(1)}, u32[]{:S(2)}, u32[]{:S(2)}) collective-permute-start(bf16[112,384]{1,0:T(8,128)(2,1)S(1)} %pad_maximum_fusion.3), channel_id=1, source_target_pairs={{0,2},{2,0},{1,3},{3,1},{4,6},{6,4},{5,7},{7,5},{8,10},{10,8},{9,1... | collective-permute-start | bytes 258056 | tf_op jit(solution)/shard_map/ppermute | solution.py:15
  157.5 14.5 %all-to-all-start.2 = ((bf16[8,96,384]{2,1,0:T(8,128)(2,1)}), bf16[8,96,384]{2,1,0:T(8,128)(2,1)S(1)}, u32[]{:S(2)}, u32[]{:S(2)}) async-start(bf16[8,96,384]{2,1,0:T(8,128)(2,1)} %bitcast.46), calls=%async_computation.2 | async-start | bytes 1179648 | tf_op jit(solution)/shard_map/all_to_all | solution.py:135
  173.6 18.9 %all-to-all-start.5 = ((f32[32,2,96]{2,1,0:T(2,128)}), f32[32,2,96]{2,1,0:T(2,128)S(1)}, u32[]{:S(2)}, u32[]{:S(2)}) async-start(f32[32,2,96]{2,1,0:T(2,128)} %broadcast_in_dim.14), calls=%async_computation.5 | async-start | bytes 65536 | tf_op jit(solution)/shard_map/all_to_all | solution.py:144
  192.5 21.2 %all-to-all-start.4 = ((bf16[8,48,384]{2,1,0:T(8,128)(2,1)}), bf16[8,48,384]{2,1,0:T(8,128)(2,1)S(1)}, u32[]{:S(2)}, u32[]{:S(2)}) async-start(bf16[8,48,384]{2,1,0:T(8,128)(2,1)} %pad_maximum_fusion.2), calls=%async_computation.4 | async-start | bytes 589824 | tf_op jit(solution)/shard_map/all_to_all | solution.py:185
  (63 other events, 592.9 us)

commit v2 on v1

--- a/solution.py
+++ b/solution.py
@@ -18,6 +18,12 @@
 def ordered(own, other, index, axis):
     return jnp.where(
         index == 0, jnp.stack([own, other], axis), jnp.stack([other, own], axis)
+    )
+
+
+def over_x(pair):
+    return lax.all_to_all(
+        jnp.broadcast_to(pair[None], (4,) + pair.shape), "x", 0, 0, tiled=True
     )
 
 
@@ -56,18 +62,13 @@
 
     in_other = swap(inputs, "zh")
     in_pair = ordered(inputs, in_other, zh, 0)
-    up_other = swap(lax.optimization_barrier((upstream, in_other))[0], "zh")
-    in_x = lax.all_gather(in_pair, "x", axis=0, tiled=False)
+    upstream_late, in_pair = lax.optimization_barrier((upstream, in_pair))
+    in_x = over_x(in_pair)
+    up_other = swap(upstream_late, "zh")
     in_core = swap(in_x, "core")
     full_inputs = ordered(in_x, in_core, core, 2).reshape(model, rows)
-
     up_pair = ordered(upstream, up_other, zh, 0)
-    up_pair = lax.optimization_barrier((up_pair, in_x))[0]
-    up_x = lax.all_to_all(
-        jnp.broadcast_to(up_pair[None], (4, 2, width, rows)), "x", 0, 0, tiled=True
-    )
-    up_core = swap(up_x, "core")
-    full_grads = ordered(up_x, up_core, core, 2).reshape(model, rows)
+    up_x = over_x(up_pair)
 
     x_float = full_inputs.astype(f32)
     row_mean = jnp.mean(x_float, axis=0, keepdims=True)
@@ -83,7 +84,10 @@
     gate_sig = jax.nn.sigmoid(gate_proj)
     keep = frame_mask.astype(f32)[None, :]
     glu_out = (value_proj * gate_sig * keep).astype(bf16)
+    up_x, glu_out = lax.optimization_barrier((up_x, glu_out))
     padded = halo(glu_out, reach)
+    up_core = swap(up_x, "core")
+    full_grads = ordered(up_x, up_core, core, 2).reshape(model, rows)
     conv_out = jnp.zeros((width, rows), f32)
     for k in range(taps):
         conv_out = conv_out + conv_kernel[k][:, None] * padded[:, k : k + rows].astype(f32)
@@ -110,20 +114,59 @@
     value_back = (glu_grad * gate_sig).astype(bf16)
     gate_back = (glu_grad * value_proj * gate_sig * (1.0 - gate_sig)).astype(bf16)
 
+    both = jnp.concatenate([value_back, gate_back])
+    weights = jnp.concatenate([value_weight, gate_weight])
+    by_gain = jnp.sum(weights.astype(f32) * norm_gain[None, :], axis=1, keepdims=True)
+    by_bias = jnp.sum(weights.astype(f32) * norm_bias[None, :], axis=1, keepdims=True)
+    proj = jnp.concatenate([value_proj, gate_proj])
+    sums = jnp.stack(
+        [
+            jnp.sum(both.astype(f32) * by_gain, axis=0),
+            jnp.sum(both.astype(f32) * (proj - by_bias), axis=0),
+        ]
+    )
+    sums_high, sums_low = split_bf16(sums)
+    blocks = weights.reshape(2 * width, 4, 2, 2, width)
+    far_w = jnp.where(zh == 0, blocks[:, :, 1], blocks[:, :, 0]).reshape(2 * width, -1)
+    near_w = jnp.where(zh == 0, blocks[:, :, 0], blocks[:, :, 1]).reshape(2 * width, -1)
     across = (((0,), (0,)), ((), ()))
-    partial = (
-        lax.dot_general(value_weight, value_back, across, preferred_element_type=f32)
-        + lax.dot_general(gate_weight, gate_back, across, preferred_element_type=f32)
-    ).astype(bf16)
-    scaled = partial.astype(f32) * norm_gain[:, None]
-    sums = jnp.stack([jnp.sum(scaled, axis=0), jnp.sum(scaled * centred, axis=0)])
-    sums_high, sums_low = split_bf16(sums)
-    blocks = partial.reshape(4, 2, 2, width, rows)
-    far = jnp.where(zh == 0, blocks[:, 1], blocks[:, 0]).reshape(8, width, rows)
-    near = jnp.where(zh == 0, blocks[:, 0], blocks[:, 1]).reshape(8, width, rows)
+    far = lax.dot_general(far_w, both, across, preferred_element_type=f32).astype(bf16)
+    near = lax.dot_general(near_w, both, across, preferred_element_type=f32).astype(bf16)
     extra = jnp.concatenate([sums_high, sums_low, jnp.zeros((12, rows), bf16)])
-    far = jnp.concatenate([far, jnp.broadcast_to(extra[None], (8, 16, rows))], axis=1)
+    far = jnp.concatenate(
+        [far.reshape(8, width, rows), jnp.broadcast_to(extra[None], (8, 16, rows))], axis=1
+    )
+    far, both = lax.optimization_barrier((far, both))
     far = lax.all_to_all(far, ("x", "core"), 0, 0, tiled=True)
+    over = (((1,), (1,)), ((), ()))
+    zero = jnp.zeros((width, rows), bf16)
+    grads = lax.dot_general(
+        normed,
+        jnp.concatenate([both, zero, zero]),
+        over,
+        preferred_element_type=f32,
+    ) + lax.dot_general(
+        full_grads,
+        jnp.concatenate([zero, zero, activated, zero]),
+        over,
+        preferred_element_type=f32,
+    )
+    piece = model // 32
+    grads = grads.reshape(8, 4, piece, 4 * width)
+    taps_part = jnp.pad(kernel_part, ((0, piece - taps), (3 * width, 0)))
+    y = lax.axis_index("y")
+    zl = lax.axis_index("zl")
+
+    def rows_for(step):
+        index = (y + step) % 4
+        return lax.dynamic_slice_in_dim(grads, index, 1, 1)[:, 0]
+
+    total = rows_for(0) + taps_part
+    for step in (1, 3, 2):
+        sent = (rows_for(step) + taps_part).astype(bf16)
+        total = total + lax.ppermute(sent, "y", [(i, (i + step) % 4) for i in range(4)]).astype(f32)
+    near, far, total = lax.optimization_barrier((near, far, total))
+    near = lax.all_to_all(near, ("x", "core"), 0, 0, tiled=True)
     far = jnp.sum(far.astype(f32), axis=0)
     far_sums = far[width : width + 2] + far[width + 2 : width + 4]
     sent_high, sent_low = split_bf16(far_sums)
@@ -131,8 +174,7 @@
         [far[:width].astype(bf16), sent_high, sent_low, jnp.zeros((12, rows), bf16)]
     )
     came = swap(far, "zh").astype(f32)
-    near = lax.optimization_barrier((near, far))[0]
-    near = lax.all_to_all(near, ("x", "core"), 0, 0, tiled=True)
+    near = near.reshape(8, width, rows)
     normed_grad = jnp.sum(near.astype(f32), axis=0) + came[:width]
     sums = (far_sums + came[width : width + 2] + came[width + 2 : width + 4]) / model
 
@@ -146,44 +188,12 @@
     )
     tail = jnp.sum(tail, axis=0)
 
-    over = (((1,), (1,)), ((), ()))
-    zero = jnp.zeros((width, rows), bf16)
-    grads = lax.dot_general(
-        normed,
-        jnp.concatenate([value_back, gate_back, zero, zero]),
-        over,
-        preferred_element_type=f32,
-    ) + lax.dot_general(
-        full_grads,
-        jnp.concatenate([zero, zero, activated, zero]),
-        over,
-        preferred_element_type=f32,
-    )
-    piece = model // 32
-    grads = grads.reshape(8, 4, piece, 4 * width).transpose(1, 0, 2, 3).astype(bf16)
-    tap_high, tap_low = split_bf16(
-        jnp.pad(kernel_part, ((0, piece - taps), (3 * width, 0)))
-    )
-    grads = jnp.concatenate(
-        [
-            grads[:, 0:1] + tap_high[None, None],
-            grads[:, 1:2] + tap_low[None, None],
-            grads[:, 2:],
-        ],
-        axis=1,
-    )
-    grads = lax.all_to_all(grads, "y", 0, 0, tiled=True)
-    grads = jnp.sum(grads.astype(f32), axis=0)
-    own_taps = (grads[0] + grads[1])[:, 3 * width :]
-    grads = jnp.concatenate(
-        [
-            grads[:, :, : 3 * width].astype(bf16),
-            jnp.broadcast_to(own_taps.astype(bf16)[None], (8, piece, width)),
-        ],
-        axis=2,
-    )
-    grads = lax.all_to_all(grads, "zl", 0, 0, tiled=True)
-    grads = jnp.sum(grads.astype(f32), axis=0)
+    for size in (4, 2, 1):
+        side = (zl // size) % 2
+        kept = lax.dynamic_slice_in_dim(total, side * size, size, 0)
+        sent = lax.dynamic_slice_in_dim(total, (1 - side) * size, size, 0).astype(bf16)
+        total = kept + lax.ppermute(sent, "zl", [(i, i ^ size) for i in range(8)]).astype(f32)
+    grads = total[0]
     value_grad = grads[:, :width].T
     gate_grad = grads[:, width : 2 * width].T
     project_grad = grads[:, 2 * width : 3 * width].T

time: 216 us -> 209 us (0.968)
  the two profiles are of different devices: /device:TPU:32 before, /device:TPU:1 now
where the time goes in v2:
time: 209 us; the launch traced here: 205 us
  starting transfers between devices  124 us (59%)
  waiting for transfers between devices  36.4 us (17%)
  other arithmetic  18.2 us (9%)
  local copies, waits for them, and re-layouts  15.4 us (7%)
  matrix products  9.29 us (4%)
    ppermute x5, starting transfers between devices, swap(): return lax.ppermute(value, axis, SWAP)  51 us
    ppermute x3, starting transfers between devices, on_device(): lax.ppermute(sent, 'zl', [(i, i ^ size) for i in range(8)]).astype(f32)  25.4 us
    ppermute x3, starting transfers between devices, on_device(): lax.ppermute(sent, 'y', [(i, (i + step) % 4) for i in range(4)]).astype(f32)  13.2 us
    all_to_all x2, waiting for transfers between devices, over_x(): lax.all_to_all(jnp.broadcast_to(pair[None], (4,) + pair.shape), 'x', 0, 0...  13.1 us
    all_to_all x1, waiting for transfers between devices, on_device(): lax.all_to_all(jnp.broadcast_to(tail[None], (32, 2, width)), FRAME, 0, 0,...  10.2 us
    ppermute x2, starting transfers between devices, halo(): left = lax.ppermute(tail, FRAME, [(i, i + 1) for i in range(count - 1)])  8.26 us
    all_to_all x2, starting transfers between devices, over_x(): lax.all_to_all(jnp.broadcast_to(pair[None], (4,) + pair.shape), 'x', 0, 0...  7.49 us
    ppermute x3, waiting for transfers between devices, on_device(): lax.ppermute(sent, 'zl', [(i, i ^ size) for i in range(8)]).astype(f32)  5.66 us
  transfers between devices with their start and end apart: 20, of which 9 were waited for; matrix products, arithmetic and copies ran while one was open for 14% of the time, Pallas kernels for 0%

profile of v2, /device:TPU:1, one launch (start us, length us, event | category | flops | bytes accessed | tf_op | source)
XLA Modules:
  0.0 205.1 jit_solution(10129499139544430860)
XLA Ops:
  0.6 16.4 %collective-permute-start = (bf16[96,384]{1,0:T(8,128)(2,1)}, bf16[96,384]{1,0:T(8,128)(2,1)S(1)}, u32[]{:S(2)}, u32[]{:S(2)}) collective-permute-start(bf16[96,384]{1,0:T(8,128)(2,1)} %param.9), channel_id=1, source_target_pairs={{0,2},{2,0},{1,3},{3,1},{4,6},{6,4},{5,7},{7,5},{8,10},{10,8},{9,1... | collective-permute-start | bytes 221192 | tf_op jit(solution)/shard_map/ppermute | solution.py:15
  21.1 4.0 %all-to-all-start = ((bf16[4,2,96,384]{3,2,1,0:T(8,128)(2,1)}), bf16[4,2,96,384]{3,2,1,0:T(8,128)(2,1)S(1)}, u32[]{:S(2)}, u32[]{:S(2)}) async-start(bf16[4,2,96,384]{3,2,1,0:T(8,128)(2,1)} %broadcast_in_dim.10), calls=%async_computation | async-start | bytes 1179648 | tf_op jit(solution)/shard_map/all_to_all | solution.py:25
  25.8 6.6 %all-to-all-done = bf16[4,2,96,384]{3,2,1,0:T(8,128)(2,1)S(1)} async-done(((bf16[4,2,96,384]{3,2,1,0:T(8,128)(2,1)}), bf16[4,2,96,384]{3,2,1,0:T(8,128)(2,1)S(1)}, u32[]{:S(2)}, u32[]{:S(2)}) %all-to-all-start) | async-done | bytes 589856 | tf_op jit(solution)/shard_map/all_to_all | solution.py:25
  32.4 7.3 %collective-permute-start.1 = (bf16[4,2,96,384]{3,2,1,0:T(8,128)(2,1)S(1)}, bf16[4,2,96,384]{3,2,1,0:T(8,128)(2,1)S(1)}, u32[]{:S(2)}, u32[]{:S(2)}) collective-permute-start(bf16[4,2,96,384]{3,2,1,0:T(8,128)(2,1)S(1)} %all-to-all-done), channel_id=1, source_target_pairs={{0,1},{1,0},{2,3},{3,2},{4,5},{5,4},{6,7},{7,6},{8,9},{9,8},{10,11... | collective-permute-start | bytes 1769480 | tf_op jit(solution)/shard_map/ppermute | solution.py:15
  42.3 12.7 %collective-permute-start.2 = (bf16[96,384]{1,0:T(8,128)(2,1)}, bf16[96,384]{1,0:T(8,128)(2,1)S(1)}, u32[]{:S(2)}, u32[]{:S(2)}) collective-permute-start(bf16[96,384]{1,0:T(8,128)(2,1)} %param.17), channel_id=1, source_target_pairs={{0,2},{2,0},{1,3},{3,1},{4,6},{6,4},{5,7},{7,5},{8,10},{10,8},{9,1... | collective-permute-start | bytes 221192 | tf_op jit(solution)/shard_map/ppermute | solution.py:15
  61.3 3.5 %all-to-all-start.1 = ((bf16[4,2,96,384]{3,2,1,0:T(8,128)(2,1)}), bf16[4,2,96,384]{3,2,1,0:T(8,128)(2,1)S(1)}, u32[]{:S(2)}, u32[]{:S(2)}) async-start(bf16[4,2,96,384]{3,2,1,0:T(8,128)(2,1)} %broadcast_in_dim.11), calls=%async_computation.1 | async-start | bytes 1179648 | tf_op jit(solution)/shard_map/all_to_all | solution.py:25
  68.3 6.5 %all-to-all-done.1 = bf16[4,2,96,384]{3,2,1,0:T(8,128)(2,1)S(1)} async-done(((bf16[4,2,96,384]{3,2,1,0:T(8,128)(2,1)}), bf16[4,2,96,384]{3,2,1,0:T(8,128)(2,1)S(1)}, u32[]{:S(2)}, u32[]{:S(2)}) %all-to-all-start.1) | async-done | bytes 589856 | tf_op jit(solution)/shard_map/all_to_all | solution.py:25
  74.8 3.0 %collective-permute-start.3 = (bf16[4,2,96,384]{3,2,1,0:T(8,128)(2,1)S(1)}, bf16[4,2,96,384]{3,2,1,0:T(8,128)(2,1)S(1)}, u32[]{:S(2)}, u32[]{:S(2)}) collective-permute-start(bf16[4,2,96,384]{3,2,1,0:T(8,128)(2,1)S(1)} %all-to-all-done.1), channel_id=1, source_target_pairs={{0,1},{1,0},{2,3},{3,2},{4,5},{5,4},{6,7},{7,6},{8,9},{9,8},{10,11... | collective-permute-start | bytes 1769480 | tf_op jit(solution)/shard_map/ppermute | solution.py:15
  79.2 4.0 %collective-permute-start.4 = (bf16[96,15]{1,0:T(8,128)(2,1)S(1)}, bf16[96,15]{1,0:T(8,128)(2,1)S(1)}, u32[]{:S(2)}, u32[]{:S(2)}) collective-permute-start(bf16[96,15]{1,0:T(8,128)(2,1)S(1)} %get-tuple-element.83), channel_id=1, source_target_pairs={{0,16},{16,32},{32,48},{48,64},{64,80},{80,96},{96,112},{112,128},... | collective-permute-start | bytes 8648 | tf_op jit(solution)/shard_map/ppermute | solution.py:34
  84.4 2.1 %fusion.105 = (bf16[96,384]{1,0:T(8,128)(2,1)}, f32[96,384]{1,0:T(8,128)S(1)}) fusion(bf16[96,399]{1,0:T(8,128)(2,1)S(1)} %constant_dynamic-update-slice_fusion.2, f32[96]{0:T(128)S(1)} %copy-done.45, f32[96]{0:T(128)S(1)} %copy-done.46, f32[96]{0:T(128)S(1)} %copy-done.17, f32[96]{0:T(128)S(1)} %copy-done.18, f32[96]{0:T(128)S(1)} %copy-done.19, ...), kind=kLoop, calls=%fused_computation.293 | loop fusion | flops 5234688 | bytes 1415616 | tf_op jit(solution)/shard_map/convert_element_type | solution.py:95
  90.0 4.3 %collective-permute-start.7 = (bf16[96,15]{1,0:T(8,128)(2,1)S(1)}, bf16[96,15]{1,0:T(8,128)(2,1)S(1)}, u32[]{:S(2)}, u32[]{:S(2)}) collective-permute-start(bf16[96,15]{1,0:T(8,128)(2,1)S(1)} %get-tuple-element.82), channel_id=1, source_target_pairs={{0,16},{16,32},{32,48},{48,64},{64,80},{80,96},{96,112},{112,128},... | collective-permute-start | bytes 8648 | tf_op jit(solution)/shard_map/ppermute | solution.py:34
  95.6 1.6 multiply_convert_fusion.1
  98.9 2.3 %fusion.22 = f32[1536,384]{1,0:T(8,128)} fusion(bf16[1536,384]{1,0:T(8,128)(2,1)S(1)} %fusion.3, bf16[192,384]{1,0:T(8,128)(2,1)S(1)} %pad_maximum_fusion.1), kind=kOutput, calls=%fused_computation.122 | convolution fusion | flops 452984832 | bytes 3686400 | tf_op jit(solution)/shard_map/dot_general | solution.py:143
  101.2 5.5 %all-to-all-start.2 = ((bf16[8,112,384]{2,1,0:T(8,128)(2,1)}), bf16[8,112,384]{2,1,0:T(8,128)(2,1)S(1)}, u32[]{:S(2)}, u32[]{:S(2)}) async-start(bf16[8,112,384]{2,1,0:T(8,128)(2,1)} %pad_maximum_fusion), calls=%async_computation.2 | async-start | bytes 1376256 | tf_op jit(solution)/shard_map/all_to_all | solution.py:140
  106.7 3.1 %convolution_add_fusion = f32[1536,384]{1,0:T(8,128)S(1)} fusion(f32[1536,384]{1,0:T(8,128)} %fusion.22, bf16[1536,384]{1,0:T(8,128)(2,1)} %bitcast.174, bf16[96,384]{1,0:T(8,128)(2,1)} %get-tuple-element.68, bf16[384]{0:T(512)(128)(2,1)S(1)} %copy-done.50, bf16[384]{0:T(512)(128)(2,1)S(1)} %copy-done.49), kind=kOutput, calls=%fused_computation | convolution fusion | flops 454459392 | bytes 5973504 | tf_op jit(solution)/shard_map/dot_general | solution.py:148
  110.8 6.0 %collective-permute-start.10 = (bf16[8,48,384]{2,1,0:T(8,128)(2,1)}, bf16[8,48,384]{2,1,0:T(8,128)(2,1)}, u32[]{:S(2)}, u32[]{:S(2)}) collective-permute-start(bf16[8,48,384]{2,1,0:T(8,128)(2,1)} %get-tuple-element.73), channel_id=1, source_target_pairs={{0,32},{16,48},{32,0},{48,16},{1,33},{17,49},{33,1},{49,17},{2,34}... | collective-permute-start | bytes 884744 | tf_op jit(solution)/shard_map/ppermute | solution.py:167
  116.8 5.4 %collective-permute-start.8 = (bf16[8,48,384]{2,1,0:T(8,128)(2,1)}, bf16[8,48,384]{2,1,0:T(8,128)(2,1)}, u32[]{:S(2)}, u32[]{:S(2)}) collective-permute-start(bf16[8,48,384]{2,1,0:T(8,128)(2,1)} %get-tuple-element.72), channel_id=1, source_target_pairs={{0,16},{16,32},{32,48},{48,0},{1,17},{17,33},{33,49},{49,1},{2,18}... | collective-permute-start | bytes 884744 | tf_op jit(solution)/shard_map/ppermute | solution.py:167
  122.1 1.9 collective-permute-start.9
  124.1 2.1 %select_n.134 = bf16[192,768]{1,0:T(8,128)(2,1)} reshape(bf16[192,4,1,2,96]{4,3,2,1,0:T(2,128)(2,1)} %get-tuple-element.76) | data formatting | bytes 589824 | tf_op jit(solution)/shard_map/jit(_where)/select_n | solution.py:131
  126.2 2.2 %convolution_convert_fusion.1 = bf16[768,384]{1,0:T(8,128)(2,1)} fusion(bf16[192,768]{1,0:T(8,128)(2,1)} %select_n.134, bf16[96,384]{1,0:T(8,128)(2,1)S(1)} %multiply_convert_fusion, bf16[96,384]{1,0:T(8,128)(2,1)S(1)} %get-tuple-element.70), kind=kOutput, calls=%fused_computation.11 | convolution fusion | flops 113836032 | bytes 1032192 | tf_op jit(solution)/shard_map/dot_general | solution.py:134
  128.4 2.5 %collective-permute-done.8 = bf16[8,48,384]{2,1,0:T(8,128)(2,1)} collective-permute-done((bf16[8,48,384]{2,1,0:T(8,128)(2,1)}, bf16[8,48,384]{2,1,0:T(8,128)(2,1)}, u32[]{:S(2)}, u32[]{:S(2)}) %collective-permute-start.8) | collective-permute-done | bytes 294944 | tf_op jit(solution)/shard_map/ppermute | solution.py:167
  130.9 2.8 %collective-permute-done.9 = bf16[8,48,384]{2,1,0:T(8,128)(2,1)} collective-permute-done((bf16[8,48,384]{2,1,0:T(8,128)(2,1)}, bf16[8,48,384]{2,1,0:T(8,128)(2,1)}, u32[]{:S(2)}, u32[]{:S(2)}) %collective-permute-start.9) | collective-permute-done | bytes 294944 | tf_op jit(solution)/shard_map/ppermute | solution.py:167
  133.7 2.1 %fusion.16 = f32[8,48,384]{2,1,0:T(8,128)} fusion(bf16[8,48,384]{2,1,0:T(8,128)(2,1)} %collective-permute-done.10, bf16[8,48,384]{2,1,0:T(8,128)(2,1)} %collective-permute-done.9, bf16[8,48,384]{2,1,0:T(8,128)(2,1)} %collective-permute-done.8, f32[8,4,48,384]{3,2,1,0:T(8,128)S(1)} %bitcast.170, s32[]{:T(128)S(6)} %select_n.141, f32[48,384]{1,0:T(8,128)} %pad.5), kind=kLoop, calls=%fused_computation.69 | loop fusion | flops 1032192 | bytes 2138116 | tf_op jit(solution)/shard_map/add | solution.py:167
  137.0 14.1 %collective-permute-start.12 = (bf16[4,48,384]{2,1,0:T(8,128)(2,1)S(1)}, bf16[4,48,384]{2,1,0:T(8,128)(2,1)S(1)}, u32[]{:S(2)}, u32[]{:S(2)}) collective-permute-start(bf16[4,48,384]{2,1,0:T(8,128)(2,1)S(1)} %dynamic-slice_convert_fusion), channel_id=1, source_target_pairs={{0,256},{64,320},{128,384},{192,448},{256,0},{320,64},{384,128},{4... | collective-permute-start | bytes 442376 | tf_op jit(solution)/shard_map/ppermute | solution.py:195
  151.1 11.7 %collective-permute-start.11 = (bf16[112,384]{1,0:T(8,128)(2,1)S(1)}, bf16[112,384]{1,0:T(8,128)(2,1)S(1)}, u32[]{:S(2)}, u32[]{:S(2)}) collective-permute-start(bf16[112,384]{1,0:T(8,128)(2,1)S(1)} %pad_maximum_fusion.2), channel_id=1, source_target_pairs={{0,2},{2,0},{1,3},{3,1},{4,6},{6,4},{5,7},{7,5},{8,10},{10,8},{9,1... | collective-permute-start | bytes 258056 | tf_op jit(solution)/shard_map/ppermute | solution.py:15
  162.9 5.5 %all-to-all-start.3 = ((bf16[8,96,384]{2,1,0:T(8,128)(2,1)}), bf16[8,96,384]{2,1,0:T(8,128)(2,1)S(1)}, u32[]{:S(2)}, u32[]{:S(2)}) async-start(bf16[8,96,384]{2,1,0:T(8,128)(2,1)} %bitcast.81), calls=%async_computation.3 | async-start | bytes 1179648 | tf_op jit(solution)/shard_map/all_to_all | solution.py:169
  168.5 1.9 collective-permute-start.13
  170.4 4.3 %collective-permute-done.13 = bf16[2,48,384]{2,1,0:T(8,128)(2,1)S(1)} collective-permute-done((bf16[2,48,384]{2,1,0:T(8,128)(2,1)S(1)}, bf16[2,48,384]{2,1,0:T(8,128)(2,1)S(1)}, u32[]{:S(2)}, u32[]{:S(2)}) %collective-permute-start.13) | collective-permute-done | bytes 73760 | tf_op jit(solution)/shard_map/ppermute | solution.py:195
  174.8 9.5 %collective-permute-start.14 = (bf16[1,48,384]{2,1,0:T(8,128)(2,1)S(1)}, bf16[1,48,384]{2,1,0:T(8,128)(2,1)S(1)}, u32[]{:S(2)}, u32[]{:S(2)}) collective-permute-start(bf16[1,48,384]{2,1,0:T(8,128)(2,1)S(1)} %dynamic-slice_convert_fusion.2), channel_id=1, source_target_pairs={{0,64},{64,0},{128,192},{192,128},{256,320},{320,256},{384,448},{4... | collective-permute-start | bytes 110600 | tf_op jit(solution)/shard_map/ppermute | solution.py:195
  185.8 1.7 multiply_reduce_fusion.1
  188.1 4.8 %all-to-all-start.4 = ((f32[32,2,96]{2,1,0:T(2,128)}), f32[32,2,96]{2,1,0:T(2,128)S(1)}, u32[]{:S(2)}, u32[]{:S(2)}) async-start(f32[32,2,96]{2,1,0:T(2,128)} %broadcast_in_dim.14), calls=%async_computation.4 | async-start | bytes 65536 | tf_op jit(solution)/shard_map/all_to_all | solution.py:186
  194.4 10.2 %all-to-all-done.4 = f32[32,2,96]{2,1,0:T(2,128)S(1)} async-done(((f32[32,2,96]{2,1,0:T(2,128)}), f32[32,2,96]{2,1,0:T(2,128)S(1)}, u32[]{:S(2)}, u32[]{:S(2)}) %all-to-all-start.4) | async-done | bytes 24608 | tf_op jit(solution)/shard_map/all_to_all | solution.py:186
  (185 shorter events, 32.0 us)
Async XLA Ops:
  0.6 86.0 %copy-start = (bf16[96,1536]{1,0:T(8,128)(2,1)S(1)}, bf16[96,1536]{1,0:T(8,128)(2,1)}, u32[]{:S(2)}) copy-start(bf16[96,1536]{1,0:T(8,128)(2,1)} %param.15) | copy-start | bytes 884740
  0.6 18.6 %collective-permute-start = (bf16[96,384]{1,0:T(8,128)(2,1)}, bf16[96,384]{1,0:T(8,128)(2,1)S(1)}, u32[]{:S(2)}, u32[]{:S(2)}) collective-permute-start(bf16[96,384]{1,0:T(8,128)(2,1)} %param.9), channel_id=1, source_target_pairs={{0,2},{2,0},{1,3},{3,1},{4,6},{6,4},{5,7},{7,5},{8,10},{10,8},{9,1... | collective-permute-start | bytes 221192 | tf_op jit(solution)/shard_map/ppermute | solution.py:15
  21.1 11.3 %all-to-all-start = ((bf16[4,2,96,384]{3,2,1,0:T(8,128)(2,1)}), bf16[4,2,96,384]{3,2,1,0:T(8,128)(2,1)S(1)}, u32[]{:S(2)}, u32[]{:S(2)}) async-start(bf16[4,2,96,384]{3,2,1,0:T(8,128)(2,1)} %broadcast_in_dim.10), calls=%async_computation | async-start | bytes 1179648 | tf_op jit(solution)/shard_map/all_to_all | solution.py:25
  32.4 32.4 %collective-permute-start.1 = (bf16[4,2,96,384]{3,2,1,0:T(8,128)(2,1)S(1)}, bf16[4,2,96,384]{3,2,1,0:T(8,128)(2,1)S(1)}, u32[]{:S(2)}, u32[]{:S(2)}) collective-permute-start(bf16[4,2,96,384]{3,2,1,0:T(8,128)(2,1)S(1)} %all-to-all-done), channel_id=1, source_target_pairs={{0,1},{1,0},{2,3},{3,2},{4,5},{5,4},{6,7},{7,6},{8,9},{9,8},{10,11... | collective-permute-start | bytes 1769480 | tf_op jit(solution)/shard_map/ppermute | solution.py:15
  42.3 17.2 %collective-permute-start.2 = (bf16[96,384]{1,0:T(8,128)(2,1)}, bf16[96,384]{1,0:T(8,128)(2,1)S(1)}, u32[]{:S(2)}, u32[]{:S(2)}) collective-permute-start(bf16[96,384]{1,0:T(8,128)(2,1)} %param.17), channel_id=1, source_target_pairs={{0,2},{2,0},{1,3},{3,1},{4,6},{6,4},{5,7},{7,5},{8,10},{10,8},{9,1... | collective-permute-start | bytes 221192 | tf_op jit(solution)/shard_map/ppermute | solution.py:15
  61.3 13.5 %all-to-all-start.1 = ((bf16[4,2,96,384]{3,2,1,0:T(8,128)(2,1)}), bf16[4,2,96,384]{3,2,1,0:T(8,128)(2,1)S(1)}, u32[]{:S(2)}, u32[]{:S(2)}) async-start(bf16[4,2,96,384]{3,2,1,0:T(8,128)(2,1)} %broadcast_in_dim.11), calls=%async_computation.1 | async-start | bytes 1179648 | tf_op jit(solution)/shard_map/all_to_all | solution.py:25
  67.6 16.5 %copy-start.16 = (f32[96]{0:T(128)S(1)}, f32[96]{0:T(128)}, u32[]{:S(2)}) copy-start(f32[96]{0:T(128)} %get-tuple-element.85) | copy-start | bytes 1156
  67.6 16.5 %copy-start.17 = (f32[96]{0:T(128)S(1)}, f32[96]{0:T(128)}, u32[]{:S(2)}) copy-start(f32[96]{0:T(128)} %get-tuple-element.86) | copy-start | bytes 1156
  67.6 16.5 %copy-start.18 = (f32[96]{0:T(128)S(1)}, f32[96]{0:T(128)}, u32[]{:S(2)}) copy-start(f32[96]{0:T(128)} %get-tuple-element.87) | copy-start | bytes 1156
  67.6 16.5 %copy-start.19 = (f32[96]{0:T(128)S(1)}, f32[96]{0:T(128)}, u32[]{:S(2)}) copy-start(f32[96]{0:T(128)} %get-tuple-element.88) | copy-start | bytes 1156
  67.6 16.5 %copy-start.20 = (f32[96]{0:T(128)S(1)}, f32[96]{0:T(128)}, u32[]{:S(2)}) copy-start(f32[96]{0:T(128)} %get-tuple-element.89) | copy-start | bytes 1156
  67.6 16.5 %copy-start.21 = (f32[96]{0:T(128)S(1)}, f32[96]{0:T(128)}, u32[]{:S(2)}) copy-start(f32[96]{0:T(128)} %get-tuple-element.90) | copy-start | bytes 1156
  67.6 16.5 %copy-start.22 = (f32[96]{0:T(128)S(1)}, f32[96]{0:T(128)}, u32[]{:S(2)}) copy-start(f32[96]{0:T(128)} %get-tuple-element.91) | copy-start | bytes 1156
  74.8 11.7 %collective-permute-start.3 = (bf16[4,2,96,384]{3,2,1,0:T(8,128)(2,1)S(1)}, bf16[4,2,96,384]{3,2,1,0:T(8,128)(2,1)S(1)}, u32[]{:S(2)}, u32[]{:S(2)}) collective-permute-start(bf16[4,2,96,384]{3,2,1,0:T(8,128)(2,1)S(1)} %all-to-all-done.1), channel_id=1, source_target_pairs={{0,1},{1,0},{2,3},{3,2},{4,5},{5,4},{6,7},{7,6},{8,9},{9,8},{10,11... | collective-permute-start | bytes 1769480 | tf_op jit(solution)/shard_map/ppermute | solution.py:15
  77.9 5.3 %collective-permute-start.5 = (bf16[96,15]{1,0:T(8,128)(2,1)S(1)}, bf16[96,15]{1,0:T(8,128)(2,1)S(1)}, u32[]{:S(2)}, u32[]{:S(2)}) collective-permute-start(bf16[96,15]{1,0:T(8,128)(2,1)S(1)} %get-tuple-element.84), channel_id=1, source_target_pairs={{16,0},{32,16},{48,32},{64,48},{80,64},{96,80},{112,96},{128,112},... | collective-permute-start | bytes 8648 | tf_op jit(solution)/shard_map/ppermute | solution.py:35
  79.2 4.9 %collective-permute-start.4 = (bf16[96,15]{1,0:T(8,128)(2,1)S(1)}, bf16[96,15]{1,0:T(8,128)(2,1)S(1)}, u32[]{:S(2)}, u32[]{:S(2)}) collective-permute-start(bf16[96,15]{1,0:T(8,128)(2,1)S(1)} %get-tuple-element.83), channel_id=1, source_target_pairs={{0,16},{16,32},{32,48},{48,64},{64,80},{80,96},{96,112},{112,128},... | collective-permute-start | bytes 8648 | tf_op jit(solution)/shard_map/ppermute | solution.py:34
  88.6 7.1 %collective-permute-start.6 = (bf16[96,15]{1,0:T(8,128)(2,1)S(1)}, bf16[96,15]{1,0:T(8,128)(2,1)S(1)}, u32[]{:S(2)}, u32[]{:S(2)}) collective-permute-start(bf16[96,15]{1,0:T(8,128)(2,1)S(1)} %get-tuple-element.81), channel_id=1, source_target_pairs={{16,0},{32,16},{48,32},{64,48},{80,64},{96,80},{112,96},{128,112},... | collective-permute-start | bytes 8648 | tf_op jit(solution)/shard_map/ppermute | solution.py:35
  90.0 5.6 %collective-permute-start.7 = (bf16[96,15]{1,0:T(8,128)(2,1)S(1)}, bf16[96,15]{1,0:T(8,128)(2,1)S(1)}, u32[]{:S(2)}, u32[]{:S(2)}) collective-permute-start(bf16[96,15]{1,0:T(8,128)(2,1)S(1)} %get-tuple-element.82), channel_id=1, source_target_pairs={{0,16},{16,32},{32,48},{48,64},{64,80},{80,96},{96,112},{112,128},... | collective-permute-start | bytes 8648 | tf_op jit(solution)/shard_map/ppermute | solution.py:34
  101.2 34.5 %all-to-all-start.2 = ((bf16[8,112,384]{2,1,0:T(8,128)(2,1)}), bf16[8,112,384]{2,1,0:T(8,128)(2,1)S(1)}, u32[]{:S(2)}, u32[]{:S(2)}) async-start(bf16[8,112,384]{2,1,0:T(8,128)(2,1)} %pad_maximum_fusion), calls=%async_computation.2 | async-start | bytes 1376256 | tf_op jit(solution)/shard_map/all_to_all | solution.py:140
  110.8 17.5 %collective-permute-start.10 = (bf16[8,48,384]{2,1,0:T(8,128)(2,1)}, bf16[8,48,384]{2,1,0:T(8,128)(2,1)}, u32[]{:S(2)}, u32[]{:S(2)}) collective-permute-start(bf16[8,48,384]{2,1,0:T(8,128)(2,1)} %get-tuple-element.73), channel_id=1, source_target_pairs={{0,32},{16,48},{32,0},{48,16},{1,33},{17,49},{33,1},{49,17},{2,34}... | collective-permute-start | bytes 884744 | tf_op jit(solution)/shard_map/ppermute | solution.py:167
  116.8 14.1 %collective-permute-start.8 = (bf16[8,48,384]{2,1,0:T(8,128)(2,1)}, bf16[8,48,384]{2,1,0:T(8,128)(2,1)}, u32[]{:S(2)}, u32[]{:S(2)}) collective-permute-start(bf16[8,48,384]{2,1,0:T(8,128)(2,1)} %get-tuple-element.72), channel_id=1, source_target_pairs={{0,16},{16,32},{32,48},{48,0},{1,17},{17,33},{33,49},{49,1},{2,18}... | collective-permute-start | bytes 884744 | tf_op jit(solution)/shard_map/ppermute | solution.py:167
  122.1 11.5 %collective-permute-start.9 = (bf16[8,48,384]{2,1,0:T(8,128)(2,1)}, bf16[8,48,384]{2,1,0:T(8,128)(2,1)}, u32[]{:S(2)}, u32[]{:S(2)}) collective-permute-start(bf16[8,48,384]{2,1,0:T(8,128)(2,1)} %get-tuple-element.74), channel_id=1, source_target_pairs={{0,48},{16,0},{32,16},{48,32},{1,49},{17,1},{33,17},{49,33},{2,50}... | collective-permute-start | bytes 884744 | tf_op jit(solution)/shard_map/ppermute | solution.py:167
  135.9 32.5 %copy-start.2 = (f32[8,48,384]{2,1,0:T(8,128)S(1)}, f32[8,48,384]{2,1,0:T(8,128)}, u32[]{:S(2)}) copy-start(f32[8,48,384]{2,1,0:T(8,128)} %fusion.16) | copy-start | bytes 1769476
  137.0 31.4 %collective-permute-start.12 = (bf16[4,48,384]{2,1,0:T(8,128)(2,1)S(1)}, bf16[4,48,384]{2,1,0:T(8,128)(2,1)S(1)}, u32[]{:S(2)}, u32[]{:S(2)}) collective-permute-start(bf16[4,48,384]{2,1,0:T(8,128)(2,1)S(1)} %dynamic-slice_convert_fusion), channel_id=1, source_target_pairs={{0,256},{64,320},{128,384},{192,448},{256,0},{320,64},{384,128},{4... | collective-permute-start | bytes 442376 | tf_op jit(solution)/shard_map/ppermute | solution.py:195
  151.1 17.3 %collective-permute-start.11 = (bf16[112,384]{1,0:T(8,128)(2,1)S(1)}, bf16[112,384]{1,0:T(8,128)(2,1)S(1)}, u32[]{:S(2)}, u32[]{:S(2)}) collective-permute-start(bf16[112,384]{1,0:T(8,128)(2,1)S(1)} %pad_maximum_fusion.2), channel_id=1, source_target_pairs={{0,2},{2,0},{1,3},{3,1},{4,6},{6,4},{5,7},{7,5},{8,10},{10,8},{9,1... | collective-permute-start | bytes 258056 | tf_op jit(solution)/shard_map/ppermute | solution.py:15
  162.9 22.8 %all-to-all-start.3 = ((bf16[8,96,384]{2,1,0:T(8,128)(2,1)}), bf16[8,96,384]{2,1,0:T(8,128)(2,1)S(1)}, u32[]{:S(2)}, u32[]{:S(2)}) async-start(bf16[8,96,384]{2,1,0:T(8,128)(2,1)} %bitcast.81), calls=%async_computation.3 | async-start | bytes 1179648 | tf_op jit(solution)/shard_map/all_to_all | solution.py:169
  168.4 17.4 %copy-start.7 = (bf16[96,384]{1,0:T(8,128)(2,1)S(1)}, bf16[96,384]{1,0:T(8,128)(2,1)}, u32[]{:S(2)}) copy-start(bf16[96,384]{1,0:T(8,128)(2,1)} %param.9) | copy-start | bytes 221188
  168.4 17.4 %copy-start.11 = (f32[384]{0:T(512)S(1)}, f32[384]{0:T(512)}, u32[]{:S(2)}) copy-start(f32[384]{0:T(512)} %copy-done.10) | copy-start | bytes 4612
  168.4 17.4 %copy-start.13 = (f32[384]{0:T(512)S(1)}, f32[384]{0:T(512)}, u32[]{:S(2)}) copy-start(f32[384]{0:T(512)} %copy-done.12) | copy-start | bytes 4612
  168.5 6.3 %collective-permute-start.13 = (bf16[2,48,384]{2,1,0:T(8,128)(2,1)S(1)}, bf16[2,48,384]{2,1,0:T(8,128)(2,1)S(1)}, u32[]{:S(2)}, u32[]{:S(2)}) collective-permute-start(bf16[2,48,384]{2,1,0:T(8,128)(2,1)S(1)} %dynamic-slice_convert_fusion.1), channel_id=1, source_target_pairs={{0,128},{64,192},{128,0},{192,64},{256,384},{320,448},{384,256},{4... | collective-permute-start | bytes 221192 | tf_op jit(solution)/shard_map/ppermute | solution.py:195
  174.8 10.8 %collective-permute-start.14 = (bf16[1,48,384]{2,1,0:T(8,128)(2,1)S(1)}, bf16[1,48,384]{2,1,0:T(8,128)(2,1)S(1)}, u32[]{:S(2)}, u32[]{:S(2)}) collective-permute-start(bf16[1,48,384]{2,1,0:T(8,128)(2,1)S(1)} %dynamic-slice_convert_fusion.2), channel_id=1, source_target_pairs={{0,64},{64,0},{128,192},{192,128},{256,320},{320,256},{384,448},{4... | collective-permute-start | bytes 110600 | tf_op jit(solution)/shard_map/ppermute | solution.py:195
  188.1 16.4 %all-to-all-start.4 = ((f32[32,2,96]{2,1,0:T(2,128)}), f32[32,2,96]{2,1,0:T(2,128)S(1)}, u32[]{:S(2)}, u32[]{:S(2)}) async-start(f32[32,2,96]{2,1,0:T(2,128)} %broadcast_in_dim.14), calls=%async_computation.4 | async-start | bytes 65536 | tf_op jit(solution)/shard_map/all_to_all | solution.py:186
  (39 other events, 486.0 us)

commit v3 on v2

v3 whole, which is shorter than its diff:
```python
import jax
import jax.numpy as jnp
from jax import lax
from jax.experimental import pallas as pl
from jax.experimental.pallas import tpu as pltpu
from jax.sharding import Mesh, PartitionSpec as P

eps = 1e-05
CHAN = ("x", "zh", "core")
FRAME = ("zl", "y")
SWAP = [(0, 1), (1, 0)]
f32 = jnp.float32
bf16 = jnp.bfloat16
VMEM = pl.BlockSpec(memory_space=pltpu.VMEM)
SMEM = pl.BlockSpec(memory_space=pltpu.SMEM)
OVER = (((1,), (1,)), ((), ()))


def swap(value, axis):
    return lax.ppermute(value, axis, SWAP)


def over_x(pair):
    return lax.all_to_all(
        jnp.broadcast_to(pair[None], (4,) + pair.shape), "x", 0, 0, tiled=True
    )


def split_bf16(value):
    high = value.astype(bf16)
    return high, (value - high.astype(f32)).astype(bf16)


def shape(dims, dtype):
    return jax.ShapeDtypeStruct(dims, dtype)


def call(kernel, outs, scratch=(), specs=None):
    return pl.pallas_call(
        kernel,
        out_shape=outs,
        in_specs=specs,
        out_specs=tuple(VMEM for _ in outs),
        scratch_shapes=list(scratch),
        compiler_params=pltpu.CompilerParams(vmem_limit_bytes=48 << 20),
    )


def blocks_of(where_ref, own_ref, other_ref):
    zh, core = where_ref[0], where_ref[1]
    for x in range(4):
        for far in range(2):
            side = zh if far == 0 else 1 - zh
            yield x * 4 + side * 2 + core, own_ref.at[x, far]
            yield x * 4 + side * 2 + 1 - core, other_ref.at[x, far]


def forward(
    where_ref, own_ref, other_ref, gain_ref, bias_ref, weight_ref, taps_ref, mask_ref,
    normed_ref, stats_ref, proj_ref, glu_ref, conv_ref,
):
    model = weight_ref.shape[1]
    width = own_ref.shape[2]
    lanes = own_ref.shape[3]
    total = jnp.zeros((8, lanes), f32)
    square = jnp.zeros((8, lanes), f32)
    for _, block in blocks_of(where_ref, own_ref, other_ref):
        x = block[...].astype(f32).reshape(width // 8, 8, lanes)
        total = total + jnp.sum(x, axis=0)
        square = square + jnp.sum(x * x, axis=0)
    row_mean = jnp.sum(total, axis=0, keepdims=True) / model
    row_var = jnp.sum(square, axis=0, keepdims=True) / model - row_mean * row_mean
    inv_std = lax.rsqrt(row_var + eps)
    stats_ref[...] = jnp.concatenate(
        [row_mean, inv_std, jnp.zeros((6, lanes), f32)], axis=0
    )
    for place, block in blocks_of(where_ref, own_ref, other_ref):
        centred = (block[...].astype(f32) - row_mean) * inv_std
        normed_ref[place] = (centred * gain_ref[place] + bias_ref[place]).astype(bf16)
    proj = jnp.dot(
        weight_ref[...], normed_ref[...].reshape(model, lanes), preferred_element_type=f32
    )
    proj_ref[...] = proj
    glu = (proj[:width] * jax.nn.sigmoid(proj[width:]) * mask_ref[...]).astype(bf16)
    glu_ref[...] = glu
    glu = glu.astype(f32)
    taps = taps_ref.shape[0]
    conv = jnp.zeros((width, lanes), f32)
    for k in range(taps):
        conv = conv + taps_ref[k] * pltpu.roll(glu, (taps // 2 - k) % lanes, 1)
    conv_ref[...] = conv


def backward(
    where_ref, own_ref, other_ref, edge_own_ref, edge_other_ref, project_ref, flipped_ref,
    by_gain_ref, by_bias_ref, taps_ref, mask_ref, proj_ref, glu_ref, conv_ref,
    far_ref, near_ref, full_ref, both_ref, act_ref, kernel_ref,
    wide_ref, partial_ref,
):
    model = project_ref.shape[1]
    width, lanes = conv_ref.shape
    rows = own_ref.shape[3]
    taps = taps_ref.shape[0]
    reach = taps // 2
    for (place, block), (_, edge) in zip(
        blocks_of(where_ref, own_ref, other_ref),
        blocks_of(where_ref, edge_own_ref, edge_other_ref),
    ):
        full_ref[place] = block[...]
        wide_ref[place, :, :rows] = block[...]
        wide_ref[place, :, rows:] = pltpu.roll(edge[:, rows:].astype(f32), 64, 1).astype(bf16)
    act_grad = jnp.dot(
        project_ref[...], wide_ref[...].reshape(model, lanes), preferred_element_type=f32
    ).astype(bf16)
    conv = conv_ref[...]
    sig = jax.nn.sigmoid(conv)
    act_ref[...] = (conv * sig)[:, :rows].astype(bf16)
    grad = (act_grad.astype(f32) * (sig + conv * sig * (1.0 - sig))).astype(bf16).astype(f32)
    glu = glu_ref[...].astype(f32)
    inner = grad[:, :rows]
    glu_grad = jnp.zeros((width, rows), f32)
    lane = lax.broadcasted_iota(jnp.int32, (width, 128), 1)
    kernel = jnp.zeros((width, 128), f32)
    for k in range(taps):
        glu_grad = glu_grad + taps_ref[k] * pltpu.roll(grad, (k - reach) % lanes, 1)[:, :rows]
        seen = jnp.sum(
            inner * pltpu.roll(glu, (reach - k) % lanes, 1)[:, :rows], axis=1, keepdims=True
        )
        kernel = jnp.where(lane == k, seen, kernel)
    kernel_ref[...] = kernel
    glu_grad = glu_grad * mask_ref[:, :rows]
    proj = proj_ref[:, :rows]
    value = proj[:width]
    gate = jax.nn.sigmoid(proj[width:])
    both_ref[:width] = (glu_grad * gate).astype(bf16)
    both_ref[width:] = (glu_grad * value * gate * (1.0 - gate)).astype(bf16)
    both = both_ref[...]
    partial = jnp.dot(flipped_ref[...], both, preferred_element_type=f32).astype(bf16)
    partial_ref[...] = partial.reshape(partial_ref.shape)
    both = both.astype(f32)
    first = jnp.sum(both * by_gain_ref[...], axis=0, keepdims=True)
    second = jnp.sum(both * (proj - by_bias_ref[...]), axis=0, keepdims=True)
    first_high = first.astype(bf16).astype(f32)
    second_high = second.astype(bf16).astype(f32)
    row = lax.broadcasted_iota(jnp.int32, (16, rows), 0)
    extra = jnp.where(row == 0, first_high, 0.0)
    extra = jnp.where(row == 1, second_high, extra)
    extra = jnp.where(row == 2, first - first_high, extra)
    extra = jnp.where(row == 3, second - second_high, extra).astype(bf16)
    zh = where_ref[0]
    for x in range(4):
        for core in range(2):
            far_ref[x * 2 + core, :width] = partial_ref[x, 1 - zh, core]
            far_ref[x * 2 + core, width:] = extra
            near_ref[x * 2 + core] = partial_ref[x, zh, core]


def weights_of(normed_ref, full_ref, both_ref, act_ref, kernel_ref, grads_ref):
    rows = full_ref.shape[2]
    width = act_ref.shape[0]
    model = normed_ref.shape[0] * width
    zero = jnp.zeros((width, rows), bf16)
    grads = lax.dot_general(
        normed_ref[:, :, :rows].reshape(model, rows),
        jnp.concatenate([zero, both_ref[...], zero], axis=0),
        OVER,
        preferred_element_type=f32,
    ) + lax.dot_general(
        full_ref[...].reshape(model, rows),
        jnp.concatenate([zero, zero, zero, act_ref[...]], axis=0),
        OVER,
        preferred_element_type=f32,
    )
    grads_ref[...] = grads.astype(bf16).reshape(grads_ref.shape)
    piece = grads_ref.shape[2]
    kernel = jnp.transpose(kernel_ref[...])[:piece].astype(bf16)
    for zl in range(8):
        for y in range(4):
            grads_ref[zl, y, :, :width] = kernel


def on_device(
    inputs,
    norm_gain,
    norm_bias,
    value_weight,
    gate_weight,
    conv_kernel,
    project_weight,
    frame_mask,
    upstream,
):
    width, rows = inputs.shape
    model = value_weight.shape[1]
    taps = conv_kernel.shape[0]
    reach = taps // 2
    lanes = rows + 128
    piece = model // 32
    zh = lax.axis_index("zh")
    core = lax.axis_index("core")
    y = lax.axis_index("y")
    zl = lax.axis_index("zl")
    offset = lax.axis_index(CHAN) * width
    where = jnp.stack([zh, core]).astype(jnp.int32)

    def empty(height, count):
        return jnp.zeros((height, count), bf16)

    mask = frame_mask.astype(bf16)[None, :]
    up_reach, in_reach = reach, 2 * reach
    gap = 64 - in_reach
    to_right = jnp.concatenate(
        [
            jnp.concatenate(
                [
                    empty(width, 64 - up_reach),
                    upstream[:, rows - up_reach :],
                    empty(width, gap),
                    inputs[:, rows - in_reach :],
                ],
                axis=1,
            ),
            jnp.broadcast_to(
                jnp.concatenate([empty(1, 128 - in_reach), mask[:, rows - in_reach :]], axis=1),
                (16, 128),
            ),
        ]
    )
    to_left = jnp.concatenate(
        [
            jnp.concatenate(
                [
                    inputs[:, :in_reach],
                    empty(width, gap),
                    upstream[:, :up_reach],
                    empty(width, 64 - up_reach),
                ],
                axis=1,
            ),
            jnp.broadcast_to(
                jnp.concatenate([mask[:, :in_reach], empty(1, 128 - in_reach)], axis=1), (16, 128)
            ),
        ]
    )
    edge = lax.ppermute(to_right, FRAME, [(i, i + 1) for i in range(31)]) + lax.ppermute(
        to_left, FRAME, [(i + 1, i) for i in range(31)]
    )
    keep = jnp.concatenate([mask, edge[width : width + 1]], axis=1).astype(f32)

    held = jnp.concatenate([inputs, edge[:width], upstream], axis=1)
    came = swap(held, "zh")
    pair = jnp.stack([held, came])
    in_own = over_x(pair[:, :, :lanes])
    up_pair, in_own = lax.optimization_barrier((pair[:, :, lanes:], in_own))
    in_other = swap(in_own, "core")
    up_own = over_x(up_pair)

    weights = jnp.concatenate([value_weight, gate_weight])
    by_gain = jnp.sum(weights.astype(f32) * norm_gain[None, :], axis=1, keepdims=True)
    by_bias = jnp.sum(weights.astype(f32) * norm_bias[None, :], axis=1, keepdims=True)
    columns = conv_kernel.reshape(taps, width, 1)
    normed, stats, proj, glu, conv = call(
        forward,
        (
            shape((16, width, lanes), bf16),
            shape((8, lanes), f32),
            shape((2 * width, lanes), f32),
            shape((width, lanes), bf16),
            shape((width, lanes), f32),
        ),
        specs=[SMEM] + [VMEM] * 7,
    )(
        where, in_own, in_other, norm_gain.reshape(16, width, 1), norm_bias.reshape(16, width, 1),
        weights, columns, keep,
    )
    up_own, conv = lax.optimization_barrier((up_own, conv))
    up_other = swap(up_own, "core")
    far, near, full_grads, both, activated, kernel_part = call(
        backward,
        (
            shape((8, width + 16, rows), bf16),
            shape((8, width, rows), bf16),
            shape((16, width, rows), bf16),
            shape((2 * width, rows), bf16),
            shape((width, rows), bf16),
            shape((width, 128), f32),
        ),
        scratch=(
            pltpu.VMEM((16, width, lanes), bf16),
            pltpu.VMEM((4, 2, 2, width, rows), bf16),
        ),
        specs=[SMEM] + [VMEM] * 13,
    )(
        where, up_own, up_other, in_own, in_other, project_weight, weights.T,
        by_gain, by_bias, columns, keep, proj, glu, conv,
    )

    far, both = lax.optimization_barrier((far, both))
    far = lax.all_to_all(far, ("x", "core"), 0, 0, tiled=True)
    (grads,) = call(
        weights_of, (shape((8, 4, piece, 4 * width), bf16),), specs=[VMEM] * 5
    )(normed, full_grads, both, activated, kernel_part)

    def rows_for(step):
        return lax.dynamic_slice_in_dim(grads, (y + step) % 4, 1, 1)[:, 0]

    parts = [
        lax.ppermute(rows_for(step), "y", [(i, (i + step) % 4) for i in range(4)])
        for step in (1, 3, 2)
    ]
    near, far = lax.optimization_barrier((near, far))
    near = lax.all_to_all(near, ("x", "core"), 0, 0, tiled=True)
    far = jnp.sum(far.astype(f32), axis=0)
    far_sums = far[width : width + 2] + far[width + 2 : width + 4]
    sent_high, sent_low = split_bf16(far_sums)
    far = jnp.concatenate(
        [far[:width].astype(bf16), sent_high, sent_low, jnp.zeros((12, rows), bf16)]
    )
    came = swap(far, "zh").astype(f32)

    total = rows_for(0).astype(f32)
    for part in parts:
        total = total + part.astype(f32)

    def halve(total, size):
        side = (zl // size) % 2
        kept = lax.dynamic_slice_in_dim(total, side * size, size, 0)
        sent = lax.dynamic_slice_in_dim(total, (1 - side) * size, size, 0).astype(bf16)
        return kept + lax.ppermute(sent, "zl", [(i, i ^ size) for i in range(8)]).astype(f32)

    total = halve(total, 4)

    normed_grad = jnp.sum(near.astype(f32), axis=0) + came[:width]
    sums = (far_sums + came[width : width + 2] + came[width + 2 : width + 4]) / model
    gain_local = lax.dynamic_slice_in_dim(norm_gain, offset, width, 0)[:, None]
    inv_std = stats[1:2, :rows]
    centred = (inputs.astype(f32) - stats[0:1, :rows]) * inv_std
    tail = jnp.stack([jnp.sum(normed_grad * centred, axis=1), jnp.sum(normed_grad, axis=1)])
    tail, total = lax.optimization_barrier((tail, total))
    tail = lax.all_to_all(
        jnp.broadcast_to(tail[None], (32, 2, width)), FRAME, 0, 0, tiled=True
    )
    tail = jnp.sum(tail, axis=0)
    inputs_grad = (
        upstream.astype(f32)
        + inv_std * (normed_grad * gain_local - sums[0:1] - centred * sums[1:2])
    ).astype(bf16)

    grads = halve(halve(total, 2), 1)[0]
    kernel_grad = grads[:taps, :width]
    value_grad = grads[:, width : 2 * width].T
    gate_grad = grads[:, 2 * width : 3 * width].T
    project_grad = grads[:, 3 * width :].T
    return (inputs_grad, value_grad, gate_grad, project_grad, kernel_grad, tail[0], tail[1])


def solution(mesh):
    split = Mesh(mesh.devices.reshape(8, 4, 4, 2, 2), FRAME + CHAN)
    return jax.shard_map(
        on_device,
        mesh=split,
        in_specs=(
            P(CHAN, FRAME),
            P(),
            P(),
            P(CHAN, None),
            P(CHAN, None),
            P(None, CHAN),
            P(CHAN, None),
            P(FRAME),
            P(CHAN, FRAME),
        ),
        out_specs=(
            P(CHAN, FRAME),
            P(CHAN, FRAME),
            P(CHAN, FRAME),
            P(CHAN, FRAME),
            P(None, CHAN),
            P(CHAN),
            P(CHAN),
        ),
        check_vma=False,
    )
```

time: 209 us -> 188 us (0.90)
  starting transfers between devices: 124 us -> 108 us
  Pallas kernels: 0 us -> 14.8 us
  other arithmetic: 18.2 us -> 8.37 us
  matrix products: 9.29 us -> 0 us
  local copies, waits for them, and re-layouts: 15.4 us -> 21.1 us
  waiting for transfers between devices: 36.4 us -> 31.5 us
    ppermute x10 -> x8, starting transfers between devices: 49.6 us -> 32.8 us  [the longest x3 17.7 us: halve(): lax.ppermute(sent, 'zl', [(i, i ^ size) for i in range(8)]).astype(f32)]
    pallas_call x0 -> x3, Pallas kernels: none -> 14.8 us  [the longest x1 8.89 us: on_device(): call(backward, (shape((8, width + 16, rows), bf16), shape((8, width, rows...]
    dot_general x7 -> x0, matrix products: 9.29 us -> none  [the longest x1 3.07 us: on_device(): lax.dot_general(full_grads, jnp.concatenate([zero, zero, activated, zero]...]
    ppermute x5 -> x4, starting transfers between devices: 51 us -> 42.9 us  [swap(): return lax.ppermute(value, axis, SWAP)]
    all_to_all x1, starting transfers between devices: 4.84 us -> 11.9 us  [on_device(): lax.all_to_all(jnp.broadcast_to(tail[None], (32, 2, width)), FRAME, 0, 0,...]
    unnamed x104 -> x44, local copies, waits for them, and re-layouts: 2.75 us -> 9.66 us
    ppermute x5 -> x4, waiting for transfers between devices: 1.17 us -> 8.07 us  [swap(): return lax.ppermute(value, axis, SWAP)]
    convert_element_type x8 -> x2, other arithmetic: 6.64 us -> 0.69 us  [the longest x1 0.69 us: on_device(): mask = frame_mask.astype(bf16)[None, :]]
  transfers between devices with their start and end apart: 20 -> 17, of which waited for: 9 -> 6; matrix products, arithmetic and copies ran while one was open for 14% -> 7% of each run, Pallas kernels for 0% -> 2%
where the time goes in v3:
time: 188 us; the launch traced here: 185 us
  starting transfers between devices  108 us (57%)
  waiting for transfers between devices  31.5 us (17%)
  local copies, waits for them, and re-layouts  21.1 us (11%)
  Pallas kernels  14.8 us (8%)
  other arithmetic  8.37 us (4%)
    ppermute x4, starting transfers between devices, swap(): return lax.ppermute(value, axis, SWAP)  42.9 us
    ppermute x3, starting transfers between devices, halve(): lax.ppermute(sent, 'zl', [(i, i ^ size) for i in range(8)]).astype(f32)  17.7 us
    all_to_all x1, starting transfers between devices, on_device(): lax.all_to_all(jnp.broadcast_to(tail[None], (32, 2, width)), FRAME, 0, 0,...  11.9 us
    ppermute x3, starting transfers between devices, on_device(): lax.ppermute(rows_for(step), 'y', [(i, (i + step) % 4) for i in range(4)])  9.75 us
    unnamed x44, local copies, waits for them, and re-layouts  9.66 us
    pallas_call x1, Pallas kernels, on_device(): call(backward, (shape((8, width + 16, rows), bf16), shape((8, width, rows...  8.89 us
    all_to_all x1, waiting for transfers between devices, on_device(): lax.all_to_all(jnp.broadcast_to(tail[None], (32, 2, width)), FRAME, 0, 0,...  8.33 us
    all_to_all x2, waiting for transfers between devices, over_x(): lax.all_to_all(jnp.broadcast_to(pair[None], (4,) + pair.shape), 'x', 0, 0...  8.32 us
  transfers between devices with their start and end apart: 17, of which 6 were waited for; matrix products, arithmetic and copies ran while one was open for 7% of the time, Pallas kernels for 2%

profile of v3, /device:TPU:1, one launch (start us, length us, event | category | flops | bytes accessed | tf_op | source)
XLA Modules:
  0.0 184.9 jit_solution(3999103057109970735)
XLA Ops:
  4.0 4.0 %collective-permute-start = (bf16[112,128]{1,0:T(8,128)(2,1)S(1)}, bf16[112,128]{1,0:T(8,128)(2,1)S(1)}, u32[]{:S(2)}, u32[]{:S(2)}) collective-permute-start(bf16[112,128]{1,0:T(8,128)(2,1)S(1)} %get-tuple-element.75), channel_id=1, source_target_pairs={{0,16},{16,32},{32,48},{48,64},{64,80},{80,96},{96,112},{112,128},... | collective-permute-start | bytes 86024 | tf_op jit(solution)/shard_map/ppermute | solution.py:245
  8.0 1.3 collective-permute-start.1
  9.3 3.3 %collective-permute-done.1 = bf16[112,128]{1,0:T(8,128)(2,1)S(1)} collective-permute-done((bf16[112,128]{1,0:T(8,128)(2,1)S(1)}, bf16[112,128]{1,0:T(8,128)(2,1)S(1)}, u32[]{:S(2)}, u32[]{:S(2)}) %collective-permute-start.1) | collective-permute-done | bytes 28704 | tf_op jit(solution)/shard_map/ppermute | solution.py:245
  13.6 15.4 %collective-permute-start.2 = (bf16[96,896]{1,0:T(8,128)(2,1)S(1)}, bf16[96,896]{1,0:T(8,128)(2,1)S(1)}, u32[]{:S(2)}, u32[]{:S(2)}) collective-permute-start(bf16[96,896]{1,0:T(8,128)(2,1)S(1)} %get-tuple-element.66), channel_id=1, source_target_pairs={{0,2},{2,0},{1,3},{3,1},{4,6},{6,4},{5,7},{7,5},{8,10},{10,8},{9,1... | collective-permute-start | bytes 516104 | tf_op jit(solution)/shard_map/ppermute | solution.py:20
  29.0 3.1 %collective-permute-done.2 = bf16[96,896]{1,0:T(8,128)(2,1)S(1)} collective-permute-done((bf16[96,896]{1,0:T(8,128)(2,1)S(1)}, bf16[96,896]{1,0:T(8,128)(2,1)S(1)}, u32[]{:S(2)}, u32[]{:S(2)}) %collective-permute-start.2) | collective-permute-done | bytes 172064 | tf_op jit(solution)/shard_map/ppermute | solution.py:20
  33.1 4.1 %all-to-all-start = ((bf16[4,2,96,512]{3,2,1,0:T(8,128)(2,1)}), bf16[4,2,96,512]{3,2,1,0:T(8,128)(2,1)S(1)}, u32[]{:S(2)}, u32[]{:S(2)}) async-start(bf16[4,2,96,512]{3,2,1,0:T(8,128)(2,1)} %broadcast_in_dim.52), calls=%async_computation | async-start | bytes 1572864 | tf_op jit(solution)/shard_map/all_to_all | solution.py:24
  37.3 8.3 %all-to-all-done.own_ref.edge_own_ref = bf16[4,2,96,512]{3,2,1,0:T(8,128)(2,1)S(1)} async-done(((bf16[4,2,96,512]{3,2,1,0:T(8,128)(2,1)}), bf16[4,2,96,512]{3,2,1,0:T(8,128)(2,1)S(1)}, u32[]{:S(2)}, u32[]{:S(2)}) %all-to-all-start) | async-done | bytes 786464 | tf_op jit(solution)/shard_map/all_to_all | solution.py:24
  45.6 15.6 %collective-permute-start.3 = (bf16[4,2,96,512]{3,2,1,0:T(8,128)(2,1)S(1)}, bf16[4,2,96,512]{3,2,1,0:T(8,128)(2,1)S(1)}, u32[]{:S(2)}, u32[]{:S(2)}) collective-permute-start(bf16[4,2,96,512]{3,2,1,0:T(8,128)(2,1)S(1)} %all-to-all-done.own_ref.edge_own_ref), channel_id=1, source_target_pairs={{0,1},{1,0},{2,3},{3,2},{4,5},{5,4},{6,7},{7,6},{8,9},{9,8},{10,11... | collective-permute-start | bytes 2359304 | tf_op jit(solution)/shard_map/ppermute | solution.py:20
  61.2 1.5 reshape.68.gain_ref
  62.8 1.5 reshape.69.bias_ref
  65.7 4.1 %all-to-all-start.1 = ((bf16[4,2,96,384]{3,2,1,0:T(8,128)(2,1)}), bf16[4,2,96,384]{3,2,1,0:T(8,128)(2,1)}, u32[]{:S(2)}, u32[]{:S(2)}) async-start(bf16[4,2,96,384]{3,2,1,0:T(8,128)(2,1)} %broadcast_in_dim.53), calls=%async_computation.1 | async-start | bytes 1179648 | tf_op jit(solution)/shard_map/all_to_all | solution.py:24
  69.9 1.3 fusion.9
  72.9 1.6 copy-done.1
  76.7 4.5 %shard_map.144 = (bf16[16,96,512]{2,1,0:T(8,128)(2,1)}, f32[8,512]{1,0:T(8,128)S(1)}, f32[192,512]{1,0:T(8,128)S(1)}, bf16[96,512]{1,0:T(8,128)(2,1)S(1)}, f32[96,512]{1,0:T(8,128)S(1)}) custom-call(s32[2]{0:T(128)S(1)} %pad_add_fusion.where_ref, bf16[4,2,96,512]{3,2,1,0:T(8,128)(2,1)S(1)} %all-to-all-done.own_ref.edge_own_ref, ...), custom_call_target="tpu_custom_call" | custom-call | tf_op jit(solution)/shard_map/pallas_call | solution.py:262
  82.5 2.1 %collective-permute-start.4 = (bf16[4,2,96,384]{3,2,1,0:T(8,128)(2,1)}, bf16[4,2,96,384]{3,2,1,0:T(8,128)(2,1)S(1)}, u32[]{:S(2)}, u32[]{:S(2)}) collective-permute-start(bf16[4,2,96,384]{3,2,1,0:T(8,128)(2,1)} %all-to-all-done.1.own_ref), channel_id=1, source_target_pairs={{0,1},{1,0},{2,3},{3,2},{4,5},{5,4},{6,7},{7,6},{8,9},{9,8},{10,11... | collective-permute-start | bytes 1769480 | tf_op jit(solution)/shard_map/ppermute | solution.py:20
  84.6 2.2 %fusion.1 = (f32[192]{0:T(256)S(1)}, f32[192]{0:T(256)S(1)}) fusion(f32[1536]{0:T(1024)S(1)} %copy-done.17, bf16[96,1536]{0,1:T(8,128)(2,1)} %copy-done.11, bf16[96,1536]{0,1:T(8,128)(2,1)} %copy-done.12, f32[1536]{0:T(1024)S(1)} %copy-done.19), kind=kLoop, calls=%fused_computation.3 | loop fusion | flops 2358912 | bytes 603648 | tf_op jit(solution)/shard_map/reduce_sum | solution.py:260
  89.9 8.9 %shard_map.145 = (bf16[8,112,384]{2,1,0:T(8,128)(2,1)}, bf16[8,96,384]{2,1,0:T(8,128)(2,1)}, bf16[16,96,384]{2,1,0:T(8,128)(2,1)}, bf16[192,384]{1,0:T(8,128)(2,...) custom-call(s32[2]{0:T(128)S(1)} %pad_add_fusion.where_ref, bf16[4,2,96,384]{3,2,1,0:T(8,128)(2,1)} %all-to-all-done.1.own_ref, ...), custom_call_target="tpu_custom_call" | custom-call | tf_op jit(solution)/shard_map/pallas_call | solution.py:278
  98.8 1.3 copy-done.5
  100.1 1.5 shard_map.146
  101.7 3.3 %collective-permute-start.8 = (bf16[8,48,384]{2,1,0:T(8,128)(2,1)S(1)}, bf16[8,48,384]{2,1,0:T(8,128)(2,1)S(1)}, u32[]{:S(2)}, u32[]{:S(2)}) collective-permute-start(bf16[8,48,384]{2,1,0:T(8,128)(2,1)S(1)} %get-tuple-element.60), channel_id=1, source_target_pairs={{0,32},{16,48},{32,0},{48,16},{1,33},{17,49},{33,1},{49,17},{2,34}... | collective-permute-start | bytes 884744 | tf_op jit(solution)/shard_map/ppermute | solution.py:308
  105.0 3.9 %collective-permute-start.7 = (bf16[8,48,384]{2,1,0:T(8,128)(2,1)S(1)}, bf16[8,48,384]{2,1,0:T(8,128)(2,1)S(1)}, u32[]{:S(2)}, u32[]{:S(2)}) collective-permute-start(bf16[8,48,384]{2,1,0:T(8,128)(2,1)S(1)} %get-tuple-element.61), channel_id=1, source_target_pairs={{0,48},{16,0},{32,16},{48,32},{1,49},{17,1},{33,17},{49,33},{2,50}... | collective-permute-start | bytes 884744 | tf_op jit(solution)/shard_map/ppermute | solution.py:308
  108.9 2.5 %collective-permute-start.6 = (bf16[8,48,384]{2,1,0:T(8,128)(2,1)S(1)}, bf16[8,48,384]{2,1,0:T(8,128)(2,1)}, u32[]{:S(2)}, u32[]{:S(2)}) collective-permute-start(bf16[8,48,384]{2,1,0:T(8,128)(2,1)S(1)} %get-tuple-element.59), channel_id=1, source_target_pairs={{0,16},{16,32},{32,48},{48,0},{1,17},{17,33},{33,49},{49,1},{2,18}... | collective-permute-start | bytes 884744 | tf_op jit(solution)/shard_map/ppermute | solution.py:308
  111.4 5.5 %all-to-all-start.2 = ((bf16[8,112,384]{2,1,0:T(8,128)(2,1)}), bf16[8,112,384]{2,1,0:T(8,128)(2,1)S(1)}, u32[]{:S(2)}, u32[]{:S(2)}) async-start(bf16[8,112,384]{2,1,0:T(8,128)(2,1)} %get-tuple-element.39), calls=%async_computation.2 | async-start | bytes 1376256 | tf_op jit(solution)/shard_map/all_to_all | solution.py:299
  117.2 3.5 %collective-permute-done.7 = bf16[8,48,384]{2,1,0:T(8,128)(2,1)S(1)} collective-permute-done((bf16[8,48,384]{2,1,0:T(8,128)(2,1)S(1)}, bf16[8,48,384]{2,1,0:T(8,128)(2,1)S(1)}, u32[]{:S(2)}, u32[]{:S(2)}) %collective-permute-start.7) | collective-permute-done | bytes 294944 | tf_op jit(solution)/shard_map/ppermute | solution.py:308
  121.8 8.2 %collective-permute-start.9 = (bf16[4,48,384]{2,1,0:T(8,128)(2,1)S(1)}, bf16[4,48,384]{2,1,0:T(8,128)(2,1)S(1)}, u32[]{:S(2)}, u32[]{:S(2)}) collective-permute-start(bf16[4,48,384]{2,1,0:T(8,128)(2,1)S(1)} %dynamic-slice_convert_fusion), channel_id=1, source_target_pairs={{0,256},{64,320},{128,384},{192,448},{256,0},{320,64},{384,128},{4... | collective-permute-start | bytes 442376 | tf_op jit(solution)/shard_map/ppermute | solution.py:329
  130.1 6.4 %all-to-all-start.3 = ((bf16[8,96,384]{2,1,0:T(8,128)(2,1)}), bf16[8,96,384]{2,1,0:T(8,128)(2,1)S(1)}, u32[]{:S(2)}, u32[]{:S(2)}) async-start(bf16[8,96,384]{2,1,0:T(8,128)(2,1)} %get-tuple-element.40), calls=%async_computation.3 | async-start | bytes 1179648 | tf_op jit(solution)/shard_map/all_to_all | solution.py:312
  136.6 9.7 %collective-permute-start.5 = (bf16[112,384]{1,0:T(8,128)(2,1)S(1)}, bf16[112,384]{1,0:T(8,128)(2,1)S(1)}, u32[]{:S(2)}, u32[]{:S(2)}) collective-permute-start(bf16[112,384]{1,0:T(8,128)(2,1)S(1)} %maximum_maximum_fusion), channel_id=1, source_target_pairs={{0,2},{2,0},{1,3},{3,1},{4,6},{6,4},{5,7},{7,5},{8,10},{10,8},{9,1... | collective-permute-start | bytes 258056 | tf_op jit(solution)/shard_map/ppermute | solution.py:20
  146.4 5.0 %collective-permute-done.5 = bf16[112,384]{1,0:T(8,128)(2,1)S(1)} collective-permute-done((bf16[112,384]{1,0:T(8,128)(2,1)S(1)}, bf16[112,384]{1,0:T(8,128)(2,1)S(1)}, u32[]{:S(2)}, u32[]{:S(2)}) %collective-permute-start.5) | collective-permute-done | bytes 86048 | tf_op jit(solution)/shard_map/ppermute | solution.py:20
  152.5 6.4 %collective-permute-start.10 = (bf16[2,48,384]{2,1,0:T(8,128)(2,1)S(1)}, bf16[2,48,384]{2,1,0:T(8,128)(2,1)S(1)}, u32[]{:S(2)}, u32[]{:S(2)}) collective-permute-start(bf16[2,48,384]{2,1,0:T(8,128)(2,1)S(1)} %dynamic-slice_convert_fusion.1), channel_id=1, source_target_pairs={{0,128},{64,192},{128,0},{192,64},{256,384},{320,448},{384,256},{4... | collective-permute-start | bytes 221192 | tf_op jit(solution)/shard_map/ppermute | solution.py:329
  159.5 11.9 %all-to-all-start.4 = ((f32[32,2,96]{2,1,0:T(2,128)}), f32[32,2,96]{2,1,0:T(2,128)S(1)}, u32[]{:S(2)}, u32[]{:S(2)}) async-start(f32[32,2,96]{2,1,0:T(2,128)} %broadcast_in_dim.57), calls=%async_computation.4 | async-start | bytes 65536 | tf_op jit(solution)/shard_map/all_to_all | solution.py:340
  171.5 3.1 %collective-permute-start.11 = (bf16[1,48,384]{2,1,0:T(8,128)(2,1)S(1)}, bf16[1,48,384]{2,1,0:T(8,128)(2,1)S(1)}, u32[]{:S(2)}, u32[]{:S(2)}) collective-permute-start(bf16[1,48,384]{2,1,0:T(8,128)(2,1)S(1)} %dynamic-slice_convert_fusion.2), channel_id=1, source_target_pairs={{0,64},{64,0},{128,192},{192,128},{256,320},{320,256},{384,448},{4... | collective-permute-start | bytes 110600 | tf_op jit(solution)/shard_map/ppermute | solution.py:329
  174.6 8.3 %all-to-all-done.4 = f32[32,2,96]{2,1,0:T(2,128)S(1)} async-done(((f32[32,2,96]{2,1,0:T(2,128)}), f32[32,2,96]{2,1,0:T(2,128)S(1)}, u32[]{:S(2)}, u32[]{:S(2)}) %all-to-all-start.4) | async-done | bytes 24608 | tf_op jit(solution)/shard_map/all_to_all | solution.py:340
  (106 shorter events, 20.2 us)
Async XLA Ops:
  4.0 5.3 %collective-permute-start = (bf16[112,128]{1,0:T(8,128)(2,1)S(1)}, bf16[112,128]{1,0:T(8,128)(2,1)S(1)}, u32[]{:S(2)}, u32[]{:S(2)}) collective-permute-start(bf16[112,128]{1,0:T(8,128)(2,1)S(1)} %get-tuple-element.75), channel_id=1, source_target_pairs={{0,16},{16,32},{32,48},{48,64},{64,80},{80,96},{96,112},{112,128},... | collective-permute-start | bytes 86024 | tf_op jit(solution)/shard_map/ppermute | solution.py:245
  8.0 4.6 %collective-permute-start.1 = (bf16[112,128]{1,0:T(8,128)(2,1)S(1)}, bf16[112,128]{1,0:T(8,128)(2,1)S(1)}, u32[]{:S(2)}, u32[]{:S(2)}) collective-permute-start(bf16[112,128]{1,0:T(8,128)(2,1)S(1)} %get-tuple-element.74), channel_id=1, source_target_pairs={{16,0},{32,16},{48,32},{64,48},{80,64},{96,80},{112,96},{128,112},... | collective-permute-start | bytes 86024 | tf_op jit(solution)/shard_map/ppermute | solution.py:245
  13.6 18.5 %collective-permute-start.2 = (bf16[96,896]{1,0:T(8,128)(2,1)S(1)}, bf16[96,896]{1,0:T(8,128)(2,1)S(1)}, u32[]{:S(2)}, u32[]{:S(2)}) collective-permute-start(bf16[96,896]{1,0:T(8,128)(2,1)S(1)} %get-tuple-element.66), channel_id=1, source_target_pairs={{0,2},{2,0},{1,3},{3,1},{4,6},{6,4},{5,7},{7,5},{8,10},{10,8},{9,1... | collective-permute-start | bytes 516104 | tf_op jit(solution)/shard_map/ppermute | solution.py:20
  32.1 29.1 %copy-start.18 = (f32[1536]{0:T(1024)S(1)}, f32[1536]{0:T(1024)}, u32[]{:S(2)}) copy-start(f32[1536]{0:T(1024)} %param.10) | copy-start | bytes 18436
  33.1 29.7 %copy-start.17 = (f32[1536]{0:T(1024)S(1)}, f32[1536]{0:T(1024)}, u32[]{:S(2)}) copy-start(f32[1536]{0:T(1024)} %param.11) | copy-start | bytes 18436
  33.1 31.2 %copy-start.15 = (bf16[96,1536]{1,0:T(8,128)(2,1)S(1)}, bf16[96,1536]{1,0:T(8,128)(2,1)}, u32[]{:S(2)}) copy-start(bf16[96,1536]{1,0:T(8,128)(2,1)} %param.13) | copy-start | bytes 884740
  33.1 12.5 %all-to-all-start = ((bf16[4,2,96,512]{3,2,1,0:T(8,128)(2,1)}), bf16[4,2,96,512]{3,2,1,0:T(8,128)(2,1)S(1)}, u32[]{:S(2)}, u32[]{:S(2)}) async-start(bf16[4,2,96,512]{3,2,1,0:T(8,128)(2,1)} %broadcast_in_dim.52), calls=%async_computation | async-start | bytes 1572864 | tf_op jit(solution)/shard_map/all_to_all | solution.py:24
  37.2 27.2 %copy-start.16 = (bf16[96,1536]{1,0:T(8,128)(2,1)S(1)}, bf16[96,1536]{1,0:T(8,128)(2,1)}, u32[]{:S(2)}) copy-start(bf16[96,1536]{1,0:T(8,128)(2,1)} %param.12) | copy-start | bytes 884740
  45.6 27.3 %collective-permute-start.3 = (bf16[4,2,96,512]{3,2,1,0:T(8,128)(2,1)S(1)}, bf16[4,2,96,512]{3,2,1,0:T(8,128)(2,1)S(1)}, u32[]{:S(2)}, u32[]{:S(2)}) collective-permute-start(bf16[4,2,96,512]{3,2,1,0:T(8,128)(2,1)S(1)} %all-to-all-done.own_ref.edge_own_ref), channel_id=1, source_target_pairs={{0,1},{1,0},{2,3},{3,2},{4,5},{5,4},{6,7},{7,6},{8,9},{9,8},{10,11... | collective-permute-start | bytes 2359304 | tf_op jit(solution)/shard_map/ppermute | solution.py:20
  64.5 6.6 %copy-start.11 = (bf16[96,1536]{0,1:T(8,128)(2,1)}, bf16[96,1536]{0,1:T(8,128)(2,1)S(1)}, u32[]{:S(2)}) copy-start(bf16[96,1536]{0,1:T(8,128)(2,1)S(1)} %copy.38) | copy-start | bytes 884740
  64.7 6.4 %copy-start.12 = (bf16[96,1536]{0,1:T(8,128)(2,1)}, bf16[96,1536]{0,1:T(8,128)(2,1)S(1)}, u32[]{:S(2)}) copy-start(bf16[96,1536]{0,1:T(8,128)(2,1)S(1)} %copy.37) | copy-start | bytes 884740
  65.7 16.8 %all-to-all-start.1 = ((bf16[4,2,96,384]{3,2,1,0:T(8,128)(2,1)}), bf16[4,2,96,384]{3,2,1,0:T(8,128)(2,1)}, u32[]{:S(2)}, u32[]{:S(2)}) async-start(bf16[4,2,96,384]{3,2,1,0:T(8,128)(2,1)} %broadcast_in_dim.53), calls=%async_computation.1 | async-start | bytes 1179648 | tf_op jit(solution)/shard_map/all_to_all | solution.py:24
  69.8 2.4 %copy-start.20 = (f32[31,96]{1,0:T(8,128)S(1)}, f32[31,96]{1,0:T(8,128)}, u32[]{:S(2)}) copy-start(f32[31,96]{1,0:T(8,128)} %param.14) | copy-start | bytes 35716
  72.8 8.4 %copy-start = (f32[31,96,1]{2,1,0:T(8,128)}, f32[31,96,1]{2,1,0:T(8,128)S(1)}, u32[]{:S(2)}) copy-start(f32[31,96,1]{2,1,0:T(8,128)S(1)} %copy.42.taps_ref) | copy-start | bytes 35716
  72.9 1.6 copy-start.1
  74.5 1.1 copy-start.2
  76.7 7.9 %copy-start.19 = (f32[1536]{0:T(1024)S(1)}, f32[1536]{0:T(1024)}, u32[]{:S(2)}) copy-start(f32[1536]{0:T(1024)} %param.10) | copy-start | bytes 18436
  82.5 4.6 %collective-permute-start.4 = (bf16[4,2,96,384]{3,2,1,0:T(8,128)(2,1)}, bf16[4,2,96,384]{3,2,1,0:T(8,128)(2,1)S(1)}, u32[]{:S(2)}, u32[]{:S(2)}) collective-permute-start(bf16[4,2,96,384]{3,2,1,0:T(8,128)(2,1)} %all-to-all-done.1.own_ref), channel_id=1, source_target_pairs={{0,1},{1,0},{2,3},{3,2},{4,5},{5,4},{6,7},{7,6},{8,9},{9,8},{10,11... | collective-permute-start | bytes 1769480 | tf_op jit(solution)/shard_map/ppermute | solution.py:20
  89.9 8.9 %copy-start.4 = (bf16[16,96,512]{2,1,0:T(8,128)(2,1)S(1)}, bf16[16,96,512]{2,1,0:T(8,128)(2,1)}, u32[]{:S(2)}) copy-start(bf16[16,96,512]{2,1,0:T(8,128)(2,1)} %get-tuple-element.42.normed_ref) | copy-start | bytes 4718596
  98.8 1.3 copy-start.5
  101.7 15.5 %collective-permute-start.8 = (bf16[8,48,384]{2,1,0:T(8,128)(2,1)S(1)}, bf16[8,48,384]{2,1,0:T(8,128)(2,1)S(1)}, u32[]{:S(2)}, u32[]{:S(2)}) collective-permute-start(bf16[8,48,384]{2,1,0:T(8,128)(2,1)S(1)} %get-tuple-element.60), channel_id=1, source_target_pairs={{0,32},{16,48},{32,0},{48,16},{1,33},{17,49},{33,1},{49,17},{2,34}... | collective-permute-start | bytes 884744 | tf_op jit(solution)/shard_map/ppermute | solution.py:308
  105.0 15.6 %collective-permute-start.7 = (bf16[8,48,384]{2,1,0:T(8,128)(2,1)S(1)}, bf16[8,48,384]{2,1,0:T(8,128)(2,1)S(1)}, u32[]{:S(2)}, u32[]{:S(2)}) collective-permute-start(bf16[8,48,384]{2,1,0:T(8,128)(2,1)S(1)} %get-tuple-element.61), channel_id=1, source_target_pairs={{0,48},{16,0},{32,16},{48,32},{1,49},{17,1},{33,17},{49,33},{2,50}... | collective-permute-start | bytes 884744 | tf_op jit(solution)/shard_map/ppermute | solution.py:308
  108.9 11.7 %collective-permute-start.6 = (bf16[8,48,384]{2,1,0:T(8,128)(2,1)S(1)}, bf16[8,48,384]{2,1,0:T(8,128)(2,1)}, u32[]{:S(2)}, u32[]{:S(2)}) collective-permute-start(bf16[8,48,384]{2,1,0:T(8,128)(2,1)S(1)} %get-tuple-element.59), channel_id=1, source_target_pairs={{0,16},{16,32},{32,48},{48,0},{1,17},{17,33},{33,49},{49,1},{2,18}... | collective-permute-start | bytes 884744 | tf_op jit(solution)/shard_map/ppermute | solution.py:308
  111.4 18.5 %all-to-all-start.2 = ((bf16[8,112,384]{2,1,0:T(8,128)(2,1)}), bf16[8,112,384]{2,1,0:T(8,128)(2,1)S(1)}, u32[]{:S(2)}, u32[]{:S(2)}) async-start(bf16[8,112,384]{2,1,0:T(8,128)(2,1)} %get-tuple-element.39), calls=%async_computation.2 | async-start | bytes 1376256 | tf_op jit(solution)/shard_map/all_to_all | solution.py:299
  121.8 24.6 %collective-permute-start.9 = (bf16[4,48,384]{2,1,0:T(8,128)(2,1)S(1)}, bf16[4,48,384]{2,1,0:T(8,128)(2,1)S(1)}, u32[]{:S(2)}, u32[]{:S(2)}) collective-permute-start(bf16[4,48,384]{2,1,0:T(8,128)(2,1)S(1)} %dynamic-slice_convert_fusion), channel_id=1, source_target_pairs={{0,256},{64,320},{128,384},{192,448},{256,0},{320,64},{384,128},{4... | collective-permute-start | bytes 442376 | tf_op jit(solution)/shard_map/ppermute | solution.py:329
  130.1 21.4 %copy-start.13 = (bf16[96,384]{1,0:T(8,128)(2,1)S(1)}, bf16[96,384]{1,0:T(8,128)(2,1)}, u32[]{:S(2)}) copy-start(bf16[96,384]{1,0:T(8,128)(2,1)} %param.9) | copy-start | bytes 221188
  130.1 21.4 %copy-start.14 = (bf16[96,384]{1,0:T(8,128)(2,1)S(1)}, bf16[96,384]{1,0:T(8,128)(2,1)}, u32[]{:S(2)}) copy-start(bf16[96,384]{1,0:T(8,128)(2,1)} %param.17) | copy-start | bytes 221188
  130.1 21.3 %all-to-all-start.3 = ((bf16[8,96,384]{2,1,0:T(8,128)(2,1)}), bf16[8,96,384]{2,1,0:T(8,128)(2,1)S(1)}, u32[]{:S(2)}, u32[]{:S(2)}) async-start(bf16[8,96,384]{2,1,0:T(8,128)(2,1)} %get-tuple-element.40), calls=%async_computation.3 | async-start | bytes 1179648 | tf_op jit(solution)/shard_map/all_to_all | solution.py:312
  136.6 14.8 %collective-permute-start.5 = (bf16[112,384]{1,0:T(8,128)(2,1)S(1)}, bf16[112,384]{1,0:T(8,128)(2,1)S(1)}, u32[]{:S(2)}, u32[]{:S(2)}) collective-permute-start(bf16[112,384]{1,0:T(8,128)(2,1)S(1)} %maximum_maximum_fusion), channel_id=1, source_target_pairs={{0,2},{2,0},{1,3},{3,1},{4,6},{6,4},{5,7},{7,5},{8,10},{10,8},{9,1... | collective-permute-start | bytes 258056 | tf_op jit(solution)/shard_map/ppermute | solution.py:20
  152.5 19.0 %collective-permute-start.10 = (bf16[2,48,384]{2,1,0:T(8,128)(2,1)S(1)}, bf16[2,48,384]{2,1,0:T(8,128)(2,1)S(1)}, u32[]{:S(2)}, u32[]{:S(2)}) collective-permute-start(bf16[2,48,384]{2,1,0:T(8,128)(2,1)S(1)} %dynamic-slice_convert_fusion.1), channel_id=1, source_target_pairs={{0,128},{64,192},{128,0},{192,64},{256,384},{320,448},{384,256},{4... | collective-permute-start | bytes 221192 | tf_op jit(solution)/shard_map/ppermute | solution.py:329
  159.5 23.4 %all-to-all-start.4 = ((f32[32,2,96]{2,1,0:T(2,128)}), f32[32,2,96]{2,1,0:T(2,128)S(1)}, u32[]{:S(2)}, u32[]{:S(2)}) async-start(f32[32,2,96]{2,1,0:T(2,128)} %broadcast_in_dim.57), calls=%async_computation.4 | async-start | bytes 65536 | tf_op jit(solution)/shard_map/all_to_all | solution.py:340
  171.5 12.0 %collective-permute-start.11 = (bf16[1,48,384]{2,1,0:T(8,128)(2,1)S(1)}, bf16[1,48,384]{2,1,0:T(8,128)(2,1)S(1)}, u32[]{:S(2)}, u32[]{:S(2)}) collective-permute-start(bf16[1,48,384]{2,1,0:T(8,128)(2,1)S(1)} %dynamic-slice_convert_fusion.2), channel_id=1, source_target_pairs={{0,64},{64,0},{128,192},{192,128},{256,320},{320,256},{384,448},{4... | collective-permute-start | bytes 110600 | tf_op jit(solution)/shard_map/ppermute | solution.py:329
  (6 other events, 5.2 us)

commit v4 on v3

v4 whole, which is shorter than its diff:
```python
import jax
import jax.numpy as jnp
from jax import lax
from jax.experimental import pallas as pl
from jax.experimental.pallas import tpu as pltpu
from jax.sharding import Mesh, PartitionSpec as P

eps = 1e-05
CHAN = ("x", "zh", "core")
FRAME = ("zl", "y")
SWAP = [(0, 1), (1, 0)]
f32 = jnp.float32
bf16 = jnp.bfloat16
VMEM = pl.BlockSpec(memory_space=pltpu.VMEM)
SMEM = pl.BlockSpec(memory_space=pltpu.SMEM)
OVER = (((1,), (1,)), ((), ()))


def swap(value, axis):
    return lax.ppermute(value, axis, SWAP)


def over_x(pair):
    return lax.all_to_all(
        jnp.broadcast_to(pair[None], (4,) + pair.shape), "x", 0, 0, tiled=True
    )


def split_bf16(value):
    high = value.astype(bf16)
    return high, (value - high.astype(f32)).astype(bf16)


def shape(dims, dtype):
    return jax.ShapeDtypeStruct(dims, dtype)


def call(kernel, outs, scratch=(), specs=None):
    return pl.pallas_call(
        kernel,
        out_shape=outs,
        in_specs=specs,
        out_specs=tuple(VMEM for _ in outs),
        scratch_shapes=list(scratch),
        compiler_params=pltpu.CompilerParams(vmem_limit_bytes=48 << 20),
    )


def blocks_of(where_ref, own_ref, other_ref):
    zh, core = where_ref[0], where_ref[1]
    for x in range(4):
        for far in range(2):
            side = zh if far == 0 else 1 - zh
            yield x * 4 + side * 2 + core, own_ref.at[x, far]
            yield x * 4 + side * 2 + 1 - core, other_ref.at[x, far]


def edges(inputs_ref, upstream_ref, mask_ref, right_ref, left_ref):
    width, rows = inputs_ref.shape
    lane = lax.broadcasted_iota(jnp.int32, (width, 128), 1)
    low = lax.broadcasted_iota(jnp.int32, (16, 128), 1)

    def pack(start, own, moved, ref):
        ends = inputs_ref[:, start : start + 128].astype(f32)
        up = pltpu.roll(upstream_ref[:, start : start + 128].astype(f32), 64, 1)
        ref[:width] = jnp.where(
            own(lane), ends, jnp.where(moved(lane), up, 0.0)
        ).astype(bf16)
        mask = jnp.broadcast_to(mask_ref[:, start : start + 128].astype(f32), (16, 128))
        ref[width:] = jnp.where(own(low), mask, 0.0).astype(bf16)

    pack(rows - 128, lambda i: i >= 98, lambda i: (i >= 49) & (i < 64), right_ref)
    pack(0, lambda i: i < 30, lambda i: (i >= 64) & (i < 79), left_ref)


def middle(
    where_ref, own_ref, other_ref, gain_ref, bias_ref, weight_ref, project_ref, flipped_ref,
    by_gain_ref, by_bias_ref, taps_ref, mask_ref,
    far_ref, near_ref, normed_ref, full_ref, stats_ref, both_ref, act_ref, kernel_ref,
    proj_ref, partial_ref, grad_ref, moved_ref,
):
    model = weight_ref.shape[1]
    width = own_ref.shape[2]
    lanes = normed_ref.shape[2]
    rows = near_ref.shape[2]
    taps = taps_ref.shape[0]
    reach = taps // 2
    total = jnp.zeros((8, lanes), f32)
    square = jnp.zeros((8, lanes), f32)
    for place, block in blocks_of(where_ref, own_ref, other_ref):
        x = block[:, :lanes].astype(f32).reshape(width // 8, 8, lanes)
        total = total + jnp.sum(x, axis=0)
        square = square + jnp.sum(x * x, axis=0)
        full_ref[place, :, :rows] = block[:, lanes:]
        full_ref[place, :, rows:] = pltpu.roll(
            block[:, rows:lanes].astype(f32), 64, 1
        ).astype(bf16)
    row_mean = jnp.sum(total, axis=0, keepdims=True) / model
    row_var = jnp.sum(square, axis=0, keepdims=True) / model - row_mean * row_mean
    inv_std = lax.rsqrt(row_var + eps)
    stats_ref[...] = jnp.concatenate(
        [row_mean, inv_std, jnp.zeros((6, lanes), f32)], axis=0
    )
    for place, block in blocks_of(where_ref, own_ref, other_ref):
        centred = (block[:, :lanes].astype(f32) - row_mean) * inv_std
        normed_ref[place] = (centred * gain_ref[place] + bias_ref[place]).astype(bf16)
    grad_ref[...] = jnp.dot(
        project_ref[...], full_ref[...].reshape(model, lanes), preferred_element_type=f32
    )
    proj_ref[...] = jnp.dot(
        weight_ref[...], normed_ref[...].reshape(model, lanes), preferred_element_type=f32
    )
    group = 16
    lane = lax.broadcasted_iota(jnp.int32, (group, 128), 1)

    def channels(step, carry):
        first = pl.multiple_of(step * group, group)
        mine = pl.ds(first, group)
        after = pl.ds(pl.multiple_of(width + first, group), group)
        value = proj_ref[mine, :]
        gate = jax.nn.sigmoid(proj_ref[after, :])
        keep = mask_ref[...]
        glu = (value * gate * keep).astype(bf16).astype(f32)
        conv = jnp.zeros((group, lanes), f32)
        for k in range(taps):
            moved = pltpu.roll(glu, (reach - k) % lanes, 1)
            moved_ref[k] = moved[:, :rows]
            conv = conv + taps_ref[k, mine, :] * moved
        sig = jax.nn.sigmoid(conv)
        act_ref[mine, :] = (conv * sig)[:, :rows].astype(bf16)
        act_grad = grad_ref[mine, :].astype(bf16).astype(f32)
        grad = (act_grad * (sig + conv * sig * (1.0 - sig))).astype(bf16).astype(f32)
        inner = grad[:, :rows]
        glu_grad = jnp.zeros((group, rows), f32)
        kernel = jnp.zeros((group, 128), f32)
        for k in range(taps):
            back = pltpu.roll(grad, (k - reach) % lanes, 1)[:, :rows]
            glu_grad = glu_grad + taps_ref[k, mine, :] * back
            seen = jnp.sum(inner * moved_ref[k], axis=1, keepdims=True)
            kernel = jnp.where(lane == k, seen, kernel)
        kernel_ref[mine, :] = kernel
        glu_grad = glu_grad * keep[:, :rows]
        gate = gate[:, :rows]
        both_ref[mine, :] = (glu_grad * gate).astype(bf16)
        both_ref[after, :] = (glu_grad * value[:, :rows] * gate * (1.0 - gate)).astype(bf16)
        return carry

    lax.fori_loop(0, width // group, channels, 0)
    both = both_ref[...]
    partial = jnp.dot(flipped_ref[...], both, preferred_element_type=f32).astype(bf16)
    partial_ref[...] = partial.reshape(partial_ref.shape)
    both = both.astype(f32)
    first = jnp.sum(both * by_gain_ref[...], axis=0, keepdims=True)
    second = jnp.sum(both * (proj_ref[:, :rows] - by_bias_ref[...]), axis=0, keepdims=True)
    first_high = first.astype(bf16).astype(f32)
    second_high = second.astype(bf16).astype(f32)
    row = lax.broadcasted_iota(jnp.int32, (16, rows), 0)
    extra = jnp.where(row == 0, first_high, 0.0)
    extra = jnp.where(row == 1, second_high, extra)
    extra = jnp.where(row == 2, first - first_high, extra)
    extra = jnp.where(row == 3, second - second_high, extra).astype(bf16)
    zh = where_ref[0]
    for x in range(4):
        for core in range(2):
            far_ref[x * 2 + core, :width] = partial_ref[x, 1 - zh, core]
            far_ref[x * 2 + core, width:] = extra
            near_ref[x * 2 + core] = partial_ref[x, zh, core]


def weights_of(normed_ref, full_ref, both_ref, act_ref, kernel_ref, grads_ref):
    width, rows = act_ref.shape
    model = normed_ref.shape[0] * width
    zero = jnp.zeros((width, rows), bf16)
    grads = lax.dot_general(
        normed_ref[:, :, :rows].reshape(model, rows),
        jnp.concatenate([zero, both_ref[...], zero], axis=0),
        OVER,
        preferred_element_type=f32,
    ) + lax.dot_general(
        full_ref[:, :, :rows].reshape(model, rows),
        jnp.concatenate([zero, zero, zero, act_ref[...]], axis=0),
        OVER,
        preferred_element_type=f32,
    )
    grads_ref[...] = grads.astype(bf16).reshape(grads_ref.shape)
    piece = grads_ref.shape[2]
    kernel = jnp.transpose(kernel_ref[...])[:piece].astype(bf16)
    for zl in range(8):
        for y in range(4):
            grads_ref[zl, y, :, :width] = kernel


def on_device(
    inputs,
    norm_gain,
    norm_bias,
    value_weight,
    gate_weight,
    conv_kernel,
    project_weight,
    frame_mask,
    upstream,
):
    width, rows = inputs.shape
    model = value_weight.shape[1]
    taps = conv_kernel.shape[0]
    lanes = rows + 128
    piece = model // 32
    zh = lax.axis_index("zh")
    core = lax.axis_index("core")
    y = lax.axis_index("y")
    zl = lax.axis_index("zl")
    offset = lax.axis_index(CHAN) * width
    where = jnp.stack([zh, core]).astype(jnp.int32)

    to_right, to_left = call(
        edges,
        (shape((width + 16, 128), bf16), shape((width + 16, 128), bf16)),
        specs=[VMEM] * 3,
    )(inputs, upstream, frame_mask.reshape(1, rows))
    edge = lax.ppermute(to_right, FRAME, [(i, i + 1) for i in range(31)]) + lax.ppermute(
        to_left, FRAME, [(i + 1, i) for i in range(31)]
    )

    weights = jnp.concatenate([value_weight, gate_weight])
    by_gain = jnp.sum(weights.astype(f32) * norm_gain[None, :], axis=1, keepdims=True)
    by_bias = jnp.sum(weights.astype(f32) * norm_bias[None, :], axis=1, keepdims=True)
    gain_local = lax.dynamic_slice_in_dim(norm_gain, offset, width, 0)[:, None]
    early = (
        weights, weights.T, by_gain, by_bias, conv_kernel.reshape(taps, width, 1),
        norm_gain.reshape(16, width, 1), norm_bias.reshape(16, width, 1), gain_local, where,
    )

    held = jnp.concatenate([inputs, edge[:width], upstream], axis=1)
    keep = jnp.concatenate([frame_mask.astype(f32)[None, :], edge[width : width + 1].astype(f32)], axis=1)
    came = swap(held, "zh")
    came, keep, early = lax.optimization_barrier((came, keep, early))
    weights, flipped, by_gain, by_bias, columns, gain, bias, gain_local, where = early
    own = over_x(jnp.stack([held, came]))
    other = swap(own, "core")
    far, near, normed, full_grads, stats, both, activated, kernel_part = call(
        middle,
        (
            shape((8, width + 16, rows), bf16),
            shape((8, width, rows), bf16),
            shape((16, width, lanes), bf16),
            shape((16, width, lanes), bf16),
            shape((8, lanes), f32),
            shape((2 * width, rows), bf16),
            shape((width, rows), bf16),
            shape((width, 128), f32),
        ),
        scratch=(
            pltpu.VMEM((2 * width, lanes), f32),
            pltpu.VMEM((4, 2, 2, width, rows), bf16),
            pltpu.VMEM((width, lanes), f32),
            pltpu.VMEM((taps, 16, rows), f32),
        ),
        specs=[SMEM] + [VMEM] * 11,
    )(
        where, own, other, gain, bias, weights, project_weight, flipped,
        by_gain, by_bias, columns, keep,
    )

    far, both = lax.optimization_barrier((far, both))
    far = lax.all_to_all(far, ("x", "core"), 0, 0, tiled=True)
    (grads,) = call(
        weights_of, (shape((8, 4, piece, 4 * width), bf16),), specs=[VMEM] * 5
    )(normed, full_grads, both, activated, kernel_part)

    def rows_for(step):
        return lax.dynamic_slice_in_dim(grads, (y + step) % 4, 1, 1)[:, 0]

    parts = [
        lax.ppermute(rows_for(step), "y", [(i, (i + step) % 4) for i in range(4)])
        for step in (1, 3, 2)
    ]
    near, far = lax.optimization_barrier((near, far))
    near = lax.all_to_all(near, ("x", "core"), 0, 0, tiled=True)
    far = jnp.sum(far.astype(f32), axis=0)
    far_sums = far[width : width + 2] + far[width + 2 : width + 4]
    sent_high, sent_low = split_bf16(far_sums)
    far = jnp.concatenate(
        [far[:width].astype(bf16), sent_high, sent_low, jnp.zeros((12, rows), bf16)]
    )
    came = swap(far, "zh").astype(f32)

    total, far_copy = lax.optimization_barrier((rows_for(0), far))
    total = total.astype(f32)
    for part in parts:
        total = total + part.astype(f32)

    def halve(total, size):
        side = (zl // size) % 2
        kept = lax.dynamic_slice_in_dim(total, side * size, size, 0)
        sent = lax.dynamic_slice_in_dim(total, (1 - side) * size, size, 0).astype(bf16)
        return kept + lax.ppermute(sent, "zl", [(i, i ^ size) for i in range(8)]).astype(f32)

    total = halve(total, 4)

    normed_grad = jnp.sum(near.astype(f32), axis=0) + came[:width]
    kept = far_copy[width : width + 4].astype(f32)
    sums = (kept[:2] + kept[2:] + came[width : width + 2] + came[width + 2 : width + 4]) / model
    inv_std = stats[1:2, :rows]
    centred = (inputs.astype(f32) - stats[0:1, :rows]) * inv_std
    tail = jnp.stack([jnp.sum(normed_grad * centred, axis=1), jnp.sum(normed_grad, axis=1)])
    tail, total = lax.optimization_barrier((tail, total))
    tail = lax.all_to_all(
        jnp.broadcast_to(tail[None], (32, 2, width)), FRAME, 0, 0, tiled=True
    )
    tail = jnp.sum(tail, axis=0)
    inputs_grad = (
        upstream.astype(f32)
        + inv_std * (normed_grad * gain_local - sums[0:1] - centred * sums[1:2])
    ).astype(bf16)

    grads = halve(halve(total, 2), 1)[0]
    kernel_grad = grads[:taps, :width]
    value_grad = grads[:, width : 2 * width].T
    gate_grad = grads[:, 2 * width : 3 * width].T
    project_grad = grads[:, 3 * width :].T
    return (inputs_grad, value_grad, gate_grad, project_grad, kernel_grad, tail[0], tail[1])


def solution(mesh):
    split = Mesh(mesh.devices.reshape(8, 4, 4, 2, 2), FRAME + CHAN)
    return jax.shard_map(
        on_device,
        mesh=split,
        in_specs=(
            P(CHAN, FRAME),
            P(),
            P(),
            P(CHAN, None),
            P(CHAN, None),
            P(None, CHAN),
            P(CHAN, None),
            P(FRAME),
            P(CHAN, FRAME),
        ),
        out_specs=(
            P(CHAN, FRAME),
            P(CHAN, FRAME),
            P(CHAN, FRAME),
            P(CHAN, FRAME),
            P(None, CHAN),
            P(CHAN),
            P(CHAN),
        ),
        check_vma=False,
    )
```

time: 188 us -> 169 us (0.90)
  starting transfers between devices: 108 us -> 92.2 us
  blocking collectives: 0 us -> 15.5 us
  waiting for transfers between devices: 31.5 us -> 22.7 us
  local copies, waits for them, and re-layouts: 21.1 us -> 16.4 us
  other arithmetic: 8.37 us -> 3.94 us
    all_to_all x0 -> x1, blocking collectives: none -> 15.5 us  [over_x(): lax.all_to_all(jnp.broadcast_to(pair[None], (4,) + pair.shape), 'x', 0, 0...]
    ppermute x3, waiting for transfers between devices: 0.01 us -> 10.8 us  [halve(): lax.ppermute(sent, 'zl', [(i, i ^ size) for i in range(8)]).astype(f32)]
    all_to_all x2 -> x0, waiting for transfers between devices: 8.32 us -> none  [over_x(): lax.all_to_all(jnp.broadcast_to(pair[None], (4,) + pair.shape), 'x', 0, 0...]
    all_to_all x2 -> x0, starting transfers between devices: 8.29 us -> none  [over_x(): lax.all_to_all(jnp.broadcast_to(pair[None], (4,) + pair.shape), 'x', 0, 0...]
    ppermute x4 -> x3, waiting for transfers between devices: 8.07 us -> 3.64 us  [swap(): return lax.ppermute(value, axis, SWAP)]
    all_to_all x1, starting transfers between devices: 11.9 us -> 7.89 us  [on_device(): lax.all_to_all(jnp.broadcast_to(tail[None], (32, 2, width)), FRAME, 0, 0,...]
    optimization_barrier x0 -> x6, local copies, waits for them, and re-layouts: none -> 3.91 us  [on_device(): came, keep, early = lax.optimization_barrier((came, keep, early))]
    ppermute x3, waiting for transfers between devices: 3.49 us -> 0.01 us  [on_device(): lax.ppermute(rows_for(step), 'y', [(i, (i + step) % 4) for i in range(4)])]
  transfers between devices with their start and end apart: 17 -> 14, of which waited for: 6 -> 3; matrix products, arithmetic and copies ran while one was open for 7% -> 7% of each run, Pallas kernels for 2% -> 1%
where the time goes in v4:
time: 169 us; the launch traced here: 168 us
  starting transfers between devices  92.2 us (55%)
  waiting for transfers between devices  22.7 us (13%)
  local copies, waits for them, and re-layouts  16.4 us (10%)
  Pallas kernels  15.7 us (9%)
  blocking collectives  15.5 us (9%)
  other arithmetic  3.94 us (2%)
    ppermute x3, starting transfers between devices, swap(): return lax.ppermute(value, axis, SWAP)  43.6 us
    ppermute x3, starting transfers between devices, halve(): lax.ppermute(sent, 'zl', [(i, i ^ size) for i in range(8)]).astype(f32)  17.6 us
    all_to_all x1, blocking collectives, over_x(): lax.all_to_all(jnp.broadcast_to(pair[None], (4,) + pair.shape), 'x', 0, 0...  15.5 us
    pallas_call x1, Pallas kernels, on_device(): call(middle, (shape((8, width + 16, rows), bf16), shape((8, width, rows),...  14.1 us
    ppermute x3, waiting for transfers between devices, halve(): lax.ppermute(sent, 'zl', [(i, i ^ size) for i in range(8)]).astype(f32)  10.8 us
    ppermute x3, starting transfers between devices, on_device(): lax.ppermute(rows_for(step), 'y', [(i, (i + step) % 4) for i in range(4)])  8.41 us
    all_to_all x1, waiting for transfers between devices, on_device(): lax.all_to_all(jnp.broadcast_to(tail[None], (32, 2, width)), FRAME, 0, 0,...  8.33 us
    unnamed x30, local copies, waits for them, and re-layouts  8.01 us
  transfers between devices with their start and end apart: 14, of which 3 were waited for; matrix products, arithmetic and copies ran while one was open for 7% of the time, Pallas kernels for 1%

profile of v4, /device:TPU:1, one launch (start us, length us, event | category | flops | bytes accessed | tf_op | source)
XLA Modules:
  0.0 167.7 jit_solution(11875729302692835205)
XLA Ops:
  1.3 0.9 copy-done.3
  2.2 0.9 copy-done.5
  3.2 4.0 %collective-permute-start = (bf16[112,128]{1,0:T(8,128)(2,1)S(1)}, bf16[112,128]{1,0:T(8,128)(2,1)S(1)}, u32[]{:S(2)}, u32[]{:S(2)}) collective-permute-start(bf16[112,128]{1,0:T(8,128)(2,1)S(1)} %get-tuple-element.36), channel_id=1, source_target_pairs={{0,16},{16,32},{32,48},{48,64},{64,80},{80,96},{96,112},{112,128},... | collective-permute-start | bytes 86024 | tf_op jit(solution)/shard_map/ppermute | solution.py:221
  7.2 1.3 collective-permute-start.1
  8.5 1.2 copy.35
  9.7 1.2 copy.36
  11.7 1.3 fusion.6
  13.0 1.1 fusion.1
  14.4 15.4 %collective-permute-start.2 = (bf16[96,896]{1,0:T(8,128)(2,1)S(1)}, bf16[96,896]{1,0:T(8,128)(2,1)S(1)}, u32[]{:S(2)}, u32[]{:S(2)}) collective-permute-start(bf16[96,896]{1,0:T(8,128)(2,1)S(1)} %get-tuple-element.83), channel_id=1, source_target_pairs={{0,2},{2,0},{1,3},{3,1},{4,6},{6,4},{5,7},{7,5},{8,10},{10,8},{9,1... | collective-permute-start | bytes 516104 | tf_op jit(solution)/shard_map/ppermute | solution.py:20
  29.9 3.6 %collective-permute-done.2 = bf16[96,896]{1,0:T(8,128)(2,1)S(1)} collective-permute-done((bf16[96,896]{1,0:T(8,128)(2,1)S(1)}, bf16[96,896]{1,0:T(8,128)(2,1)S(1)}, u32[]{:S(2)}, u32[]{:S(2)}) %collective-permute-start.2) | collective-permute-done | bytes 172064 | tf_op jit(solution)/shard_map/ppermute | solution.py:20
  33.7 15.5 %all_to_all.20.own_ref = bf16[4,2,96,896]{3,2,1,0:T(8,128)(2,1)} all-to-all(bf16[4,2,96,896]{3,2,1,0:T(8,128)(2,1)S(1)} %broadcast_in_dim.33), channel_id=1, replica_groups=mesh['zl'=8,'y'=4,'x'=4,'zh'=2,'core'=2] {'x'}, dimensions={0} | all-to-all | bytes 2752512 | tf_op jit(solution)/shard_map/all_to_all | solution.py:24
  49.2 15.2 %collective-permute-start.3 = (bf16[4,2,96,896]{3,2,1,0:T(8,128)(2,1)}, bf16[4,2,96,896]{3,2,1,0:T(8,128)(2,1)}, u32[]{:S(2)}, u32[]{:S(2)}) collective-permute-start(bf16[4,2,96,896]{3,2,1,0:T(8,128)(2,1)} %all_to_all.20.own_ref), channel_id=1, source_target_pairs={{0,1},{1,0},{2,3},{3,2},{4,5},{5,4},{6,7},{7,6},{8,9},{9,8},{10,11... | collective-permute-start | bytes 4128776 | tf_op jit(solution)/shard_map/ppermute | solution.py:20
  64.5 1.7 copy.42.taps_ref
  66.8 1.4 copy.39.weight_ref
  68.4 1.0 copy-done.7
  69.4 14.1 %shard_map.145 = (bf16[8,112,384]{2,1,0:T(8,128)(2,1)S(1)}, bf16[8,96,384]{2,1,0:T(8,128)(2,1)}, bf16[16,96,512]{2,1,0:T(8,128)(2,1)}, bf16[16,96,512]{2,1,0:T(8...) custom-call(s32[2]{0:T(128)S(1)} %pad_add_fusion.where_ref, ...), custom_call_target="tpu_custom_call" | custom-call | tf_op jit(solution)/shard_map/pallas_call | solution.py:241
  83.5 0.8 copy-done.2
  85.0 3.6 %all-to-all-start.1 = ((bf16[8,112,384]{2,1,0:T(8,128)(2,1)}), bf16[8,112,384]{2,1,0:T(8,128)(2,1)S(1)}, u32[]{:S(2)}, u32[]{:S(2)}) async-start(bf16[8,112,384]{2,1,0:T(8,128)(2,1)} %copy-done.2), calls=%async_computation.1 | async-start | bytes 1376256 | tf_op jit(solution)/shard_map/all_to_all | solution.py:266
  88.8 1.4 copy-done.1
  90.2 1.5 shard_map.146
  91.8 1.9 %collective-permute-start.5 = (bf16[8,48,384]{2,1,0:T(8,128)(2,1)S(1)}, bf16[8,48,384]{2,1,0:T(8,128)(2,1)S(1)}, u32[]{:S(2)}, u32[]{:S(2)}) collective-permute-start(bf16[8,48,384]{2,1,0:T(8,128)(2,1)S(1)} %get-tuple-element.75), channel_id=1, source_target_pairs={{0,16},{16,32},{32,48},{48,0},{1,17},{17,33},{33,49},{49,1},{2,18}... | collective-permute-start | bytes 884744 | tf_op jit(solution)/shard_map/ppermute | solution.py:275
  93.8 4.6 %collective-permute-start.6 = (bf16[8,48,384]{2,1,0:T(8,128)(2,1)S(1)}, bf16[8,48,384]{2,1,0:T(8,128)(2,1)S(1)}, u32[]{:S(2)}, u32[]{:S(2)}) collective-permute-start(bf16[8,48,384]{2,1,0:T(8,128)(2,1)S(1)} %get-tuple-element.77), channel_id=1, source_target_pairs={{0,48},{16,0},{32,16},{48,32},{1,49},{17,1},{33,17},{49,33},{2,50}... | collective-permute-start | bytes 884744 | tf_op jit(solution)/shard_map/ppermute | solution.py:275
  98.3 1.9 %collective-permute-start.7 = (bf16[8,48,384]{2,1,0:T(8,128)(2,1)S(1)}, bf16[8,48,384]{2,1,0:T(8,128)(2,1)S(1)}, u32[]{:S(2)}, u32[]{:S(2)}) collective-permute-start(bf16[8,48,384]{2,1,0:T(8,128)(2,1)S(1)} %get-tuple-element.76), channel_id=1, source_target_pairs={{0,32},{16,48},{32,0},{48,16},{1,33},{17,49},{33,1},{49,17},{2,34}... | collective-permute-start | bytes 884744 | tf_op jit(solution)/shard_map/ppermute | solution.py:275
  100.5 12.9 %collective-permute-start.4 = (bf16[112,384]{1,0:T(8,128)(2,1)S(1)}, bf16[112,384]{1,0:T(8,128)(2,1)S(1)}, u32[]{:S(2)}, u32[]{:S(2)}) collective-permute-start(bf16[112,384]{1,0:T(8,128)(2,1)S(1)} %maximum_maximum_fusion), channel_id=1, source_target_pairs={{0,2},{2,0},{1,3},{3,1},{4,6},{6,4},{5,7},{7,5},{8,10},{10,8},{9,1... | collective-permute-start | bytes 258056 | tf_op jit(solution)/shard_map/ppermute | solution.py:20
  113.6 10.3 %collective-permute-start.8 = (bf16[4,48,384]{2,1,0:T(8,128)(2,1)S(1)}, bf16[4,48,384]{2,1,0:T(8,128)(2,1)S(1)}, u32[]{:S(2)}, u32[]{:S(2)}) collective-permute-start(bf16[4,48,384]{2,1,0:T(8,128)(2,1)S(1)} %dynamic-slice_convert_fusion), channel_id=1, source_target_pairs={{0,256},{64,320},{128,384},{192,448},{256,0},{320,64},{384,128},{4... | collective-permute-start | bytes 442376 | tf_op jit(solution)/shard_map/ppermute | solution.py:297
  124.0 5.8 %all-to-all-start.2 = ((bf16[8,96,384]{2,1,0:T(8,128)(2,1)}), bf16[8,96,384]{2,1,0:T(8,128)(2,1)S(1)}, u32[]{:S(2)}, u32[]{:S(2)}) async-start(bf16[8,96,384]{2,1,0:T(8,128)(2,1)} %get-tuple-element.53), calls=%async_computation.2 | async-start | bytes 1179648 | tf_op jit(solution)/shard_map/all_to_all | solution.py:279
  129.8 10.7 %collective-permute-done.8 = bf16[4,48,384]{2,1,0:T(8,128)(2,1)S(1)} collective-permute-done((bf16[4,48,384]{2,1,0:T(8,128)(2,1)S(1)}, bf16[4,48,384]{2,1,0:T(8,128)(2,1)S(1)}, u32[]{:S(2)}, u32[]{:S(2)}) %collective-permute-start.8) | collective-permute-done | bytes 147488 | tf_op jit(solution)/shard_map/ppermute | solution.py:297
  140.7 0.8 multiply_reduce_fusion
  141.6 4.1 %collective-permute-start.9 = (bf16[2,48,384]{2,1,0:T(8,128)(2,1)S(1)}, bf16[2,48,384]{2,1,0:T(8,128)(2,1)S(1)}, u32[]{:S(2)}, u32[]{:S(2)}) collective-permute-start(bf16[2,48,384]{2,1,0:T(8,128)(2,1)S(1)} %dynamic-slice_convert_fusion.1), channel_id=1, source_target_pairs={{0,128},{64,192},{128,0},{192,64},{256,384},{320,448},{384,256},{4... | collective-permute-start | bytes 221192 | tf_op jit(solution)/shard_map/ppermute | solution.py:297
  146.4 7.9 %all-to-all-start.3 = ((f32[32,2,96]{2,1,0:T(2,128)}), f32[32,2,96]{2,1,0:T(2,128)S(1)}, u32[]{:S(2)}, u32[]{:S(2)}) async-start(f32[32,2,96]{2,1,0:T(2,128)} %broadcast_in_dim.35), calls=%async_computation.3 | async-start | bytes 65536 | tf_op jit(solution)/shard_map/all_to_all | solution.py:308
  154.3 3.1 %collective-permute-start.10 = (bf16[1,48,384]{2,1,0:T(8,128)(2,1)S(1)}, bf16[1,48,384]{2,1,0:T(8,128)(2,1)S(1)}, u32[]{:S(2)}, u32[]{:S(2)}) collective-permute-start(bf16[1,48,384]{2,1,0:T(8,128)(2,1)S(1)} %dynamic-slice_convert_fusion.2), channel_id=1, source_target_pairs={{0,64},{64,0},{128,192},{192,128},{256,320},{320,256},{384,448},{4... | collective-permute-start | bytes 110600 | tf_op jit(solution)/shard_map/ppermute | solution.py:297
  157.5 8.3 %all-to-all-done.3 = f32[32,2,96]{2,1,0:T(2,128)S(1)} async-done(((f32[32,2,96]{2,1,0:T(2,128)}), f32[32,2,96]{2,1,0:T(2,128)S(1)}, u32[]{:S(2)}, u32[]{:S(2)}) %all-to-all-start.3) | async-done | bytes 24608 | tf_op jit(solution)/shard_map/all_to_all | solution.py:308
  (79 shorter events, 6.9 us)
Async XLA Ops:
  1.3 0.9 copy-start.3
  2.2 0.9 copy-start.5
  3.2 11.2 %collective-permute-start = (bf16[112,128]{1,0:T(8,128)(2,1)S(1)}, bf16[112,128]{1,0:T(8,128)(2,1)S(1)}, u32[]{:S(2)}, u32[]{:S(2)}) collective-permute-start(bf16[112,128]{1,0:T(8,128)(2,1)S(1)} %get-tuple-element.36), channel_id=1, source_target_pairs={{0,16},{16,32},{32,48},{48,64},{64,80},{80,96},{96,112},{112,128},... | collective-permute-start | bytes 86024 | tf_op jit(solution)/shard_map/ppermute | solution.py:221
  7.2 7.1 %collective-permute-start.1 = (bf16[112,128]{1,0:T(8,128)(2,1)S(1)}, bf16[112,128]{1,0:T(8,128)(2,1)S(1)}, u32[]{:S(2)}, u32[]{:S(2)}) collective-permute-start(bf16[112,128]{1,0:T(8,128)(2,1)S(1)} %get-tuple-element.37), channel_id=1, source_target_pairs={{16,0},{32,16},{48,32},{64,48},{80,64},{96,80},{112,96},{128,112},... | collective-permute-start | bytes 86024 | tf_op jit(solution)/shard_map/ppermute | solution.py:221
  9.7 3.3 %copy-start.10 = (f32[1536]{0:T(1024)S(1)}, f32[1536]{0:T(1024)}, u32[]{:S(2)}) copy-start(f32[1536]{0:T(1024)} %param.10) | copy-start | bytes 18436
  9.7 3.3 %copy-start.11 = (f32[1536]{0:T(1024)S(1)}, f32[1536]{0:T(1024)}, u32[]{:S(2)}) copy-start(f32[1536]{0:T(1024)} %param.11) | copy-start | bytes 18436
  11.7 2.5 %copy-start.13 = (s32[384]{0:T(512)S(1)}, s32[384]{0:T(512)}, u32[]{:S(2)}) copy-start(s32[384]{0:T(512)} %param.16) | copy-start | bytes 4612
  11.7 2.7 %copy-start.4 = (bf16[96,384]{1,0:T(8,128)(2,1)S(1)}, bf16[96,384]{1,0:T(8,128)(2,1)}, u32[]{:S(2)}) copy-start(bf16[96,384]{1,0:T(8,128)(2,1)} %inputs_ref.1) | copy-start | bytes 221188
  11.7 2.7 %copy-start.6 = (bf16[96,384]{1,0:T(8,128)(2,1)S(1)}, bf16[96,384]{1,0:T(8,128)(2,1)}, u32[]{:S(2)}) copy-start(bf16[96,384]{1,0:T(8,128)(2,1)} %upstream_ref.1) | copy-start | bytes 221188
  14.4 19.1 %collective-permute-start.2 = (bf16[96,896]{1,0:T(8,128)(2,1)S(1)}, bf16[96,896]{1,0:T(8,128)(2,1)S(1)}, u32[]{:S(2)}, u32[]{:S(2)}) collective-permute-start(bf16[96,896]{1,0:T(8,128)(2,1)S(1)} %get-tuple-element.83), channel_id=1, source_target_pairs={{0,2},{2,0},{1,3},{3,1},{4,6},{6,4},{5,7},{7,5},{8,10},{10,8},{9,1... | collective-permute-start | bytes 516104 | tf_op jit(solution)/shard_map/ppermute | solution.py:20
  33.7 30.8 %copy-start.12 = (f32[31,96]{1,0:T(8,128)S(1)}, f32[31,96]{1,0:T(8,128)}, u32[]{:S(2)}) copy-start(f32[31,96]{1,0:T(8,128)} %param.14) | copy-start | bytes 35716
  49.2 19.2 %collective-permute-start.3 = (bf16[4,2,96,896]{3,2,1,0:T(8,128)(2,1)}, bf16[4,2,96,896]{3,2,1,0:T(8,128)(2,1)}, u32[]{:S(2)}, u32[]{:S(2)}) collective-permute-start(bf16[4,2,96,896]{3,2,1,0:T(8,128)(2,1)} %all_to_all.20.own_ref), channel_id=1, source_target_pairs={{0,1},{1,0},{2,3},{3,2},{4,5},{5,4},{6,7},{7,6},{8,9},{9,8},{10,11... | collective-permute-start | bytes 4128776 | tf_op jit(solution)/shard_map/ppermute | solution.py:20
  68.4 1.0 copy-start.7
  83.5 0.8 copy-start.2
  84.3 0.6 copy-start.8
  85.0 3.8 %copy-start = (bf16[16,96,512]{2,1,0:T(8,128)(2,1)S(1)}, bf16[16,96,512]{2,1,0:T(8,128)(2,1)}, u32[]{:S(2)}) copy-start(bf16[16,96,512]{2,1,0:T(8,128)(2,1)} %get-tuple-element.56.normed_ref) | copy-start | bytes 4718596
  85.0 3.8 %copy-start.9 = (f32[96,128]{1,0:T(8,128)S(1)}, f32[96,128]{1,0:T(8,128)}, u32[]{:S(2)}) copy-start(f32[96,128]{1,0:T(8,128)} %copy-done.8) | copy-start | bytes 147460
  85.0 15.3 %all-to-all-start.1 = ((bf16[8,112,384]{2,1,0:T(8,128)(2,1)}), bf16[8,112,384]{2,1,0:T(8,128)(2,1)S(1)}, u32[]{:S(2)}, u32[]{:S(2)}) async-start(bf16[8,112,384]{2,1,0:T(8,128)(2,1)} %copy-done.2), calls=%async_computation.1 | async-start | bytes 1376256 | tf_op jit(solution)/shard_map/all_to_all | solution.py:266
  88.8 1.4 copy-start.1
  91.8 21.6 %collective-permute-start.5 = (bf16[8,48,384]{2,1,0:T(8,128)(2,1)S(1)}, bf16[8,48,384]{2,1,0:T(8,128)(2,1)S(1)}, u32[]{:S(2)}, u32[]{:S(2)}) collective-permute-start(bf16[8,48,384]{2,1,0:T(8,128)(2,1)S(1)} %get-tuple-element.75), channel_id=1, source_target_pairs={{0,16},{16,32},{32,48},{48,0},{1,17},{17,33},{33,49},{49,1},{2,18}... | collective-permute-start | bytes 884744 | tf_op jit(solution)/shard_map/ppermute | solution.py:275
  93.8 19.7 %collective-permute-start.6 = (bf16[8,48,384]{2,1,0:T(8,128)(2,1)S(1)}, bf16[8,48,384]{2,1,0:T(8,128)(2,1)S(1)}, u32[]{:S(2)}, u32[]{:S(2)}) collective-permute-start(bf16[8,48,384]{2,1,0:T(8,128)(2,1)S(1)} %get-tuple-element.77), channel_id=1, source_target_pairs={{0,48},{16,0},{32,16},{48,32},{1,49},{17,1},{33,17},{49,33},{2,50}... | collective-permute-start | bytes 884744 | tf_op jit(solution)/shard_map/ppermute | solution.py:275
  98.3 15.1 %collective-permute-start.7 = (bf16[8,48,384]{2,1,0:T(8,128)(2,1)S(1)}, bf16[8,48,384]{2,1,0:T(8,128)(2,1)S(1)}, u32[]{:S(2)}, u32[]{:S(2)}) collective-permute-start(bf16[8,48,384]{2,1,0:T(8,128)(2,1)S(1)} %get-tuple-element.76), channel_id=1, source_target_pairs={{0,32},{16,48},{32,0},{48,16},{1,33},{17,49},{33,1},{49,17},{2,34}... | collective-permute-start | bytes 884744 | tf_op jit(solution)/shard_map/ppermute | solution.py:275
  100.5 29.2 %collective-permute-start.4 = (bf16[112,384]{1,0:T(8,128)(2,1)S(1)}, bf16[112,384]{1,0:T(8,128)(2,1)S(1)}, u32[]{:S(2)}, u32[]{:S(2)}) collective-permute-start(bf16[112,384]{1,0:T(8,128)(2,1)S(1)} %maximum_maximum_fusion), channel_id=1, source_target_pairs={{0,2},{2,0},{1,3},{3,1},{4,6},{6,4},{5,7},{7,5},{8,10},{10,8},{9,1... | collective-permute-start | bytes 258056 | tf_op jit(solution)/shard_map/ppermute | solution.py:20
  113.6 26.9 %collective-permute-start.8 = (bf16[4,48,384]{2,1,0:T(8,128)(2,1)S(1)}, bf16[4,48,384]{2,1,0:T(8,128)(2,1)S(1)}, u32[]{:S(2)}, u32[]{:S(2)}) collective-permute-start(bf16[4,48,384]{2,1,0:T(8,128)(2,1)S(1)} %dynamic-slice_convert_fusion), channel_id=1, source_target_pairs={{0,256},{64,320},{128,384},{192,448},{256,0},{320,64},{384,128},{4... | collective-permute-start | bytes 442376 | tf_op jit(solution)/shard_map/ppermute | solution.py:297
  124.0 16.6 %all-to-all-start.2 = ((bf16[8,96,384]{2,1,0:T(8,128)(2,1)}), bf16[8,96,384]{2,1,0:T(8,128)(2,1)S(1)}, u32[]{:S(2)}, u32[]{:S(2)}) async-start(bf16[8,96,384]{2,1,0:T(8,128)(2,1)} %get-tuple-element.53), calls=%async_computation.2 | async-start | bytes 1179648 | tf_op jit(solution)/shard_map/all_to_all | solution.py:279
  141.6 12.7 %collective-permute-start.9 = (bf16[2,48,384]{2,1,0:T(8,128)(2,1)S(1)}, bf16[2,48,384]{2,1,0:T(8,128)(2,1)S(1)}, u32[]{:S(2)}, u32[]{:S(2)}) collective-permute-start(bf16[2,48,384]{2,1,0:T(8,128)(2,1)S(1)} %dynamic-slice_convert_fusion.1), channel_id=1, source_target_pairs={{0,128},{64,192},{128,0},{192,64},{256,384},{320,448},{384,256},{4... | collective-permute-start | bytes 221192 | tf_op jit(solution)/shard_map/ppermute | solution.py:297
  146.4 19.4 %all-to-all-start.3 = ((f32[32,2,96]{2,1,0:T(2,128)}), f32[32,2,96]{2,1,0:T(2,128)S(1)}, u32[]{:S(2)}, u32[]{:S(2)}) async-start(f32[32,2,96]{2,1,0:T(2,128)} %broadcast_in_dim.35), calls=%async_computation.3 | async-start | bytes 65536 | tf_op jit(solution)/shard_map/all_to_all | solution.py:308
  154.3 12.0 %collective-permute-start.10 = (bf16[1,48,384]{2,1,0:T(8,128)(2,1)S(1)}, bf16[1,48,384]{2,1,0:T(8,128)(2,1)S(1)}, u32[]{:S(2)}, u32[]{:S(2)}) collective-permute-start(bf16[1,48,384]{2,1,0:T(8,128)(2,1)S(1)} %dynamic-slice_convert_fusion.2), channel_id=1, source_target_pairs={{0,64},{64,0},{128,192},{192,128},{256,320},{320,256},{384,448},{4... | collective-permute-start | bytes 110600 | tf_op jit(solution)/shard_map/ppermute | solution.py:297

commit v5 on v4

--- a/solution.py
+++ b/solution.py
@@ -42,7 +42,7 @@
         in_specs=specs,
         out_specs=tuple(VMEM for _ in outs),
         scratch_shapes=list(scratch),
-        compiler_params=pltpu.CompilerParams(vmem_limit_bytes=48 << 20),
+        compiler_params=pltpu.CompilerParams(vmem_limit_bytes=24 << 20),
     )
 
 
@@ -55,8 +55,10 @@
             yield x * 4 + side * 2 + 1 - core, other_ref.at[x, far]
 
 
-def edges(inputs_ref, upstream_ref, mask_ref, right_ref, left_ref):
+def edges(inputs_ref, upstream_ref, mask_ref, main_ref, right_ref, left_ref):
     width, rows = inputs_ref.shape
+    main_ref[:, :rows] = inputs_ref[...]
+    main_ref[:, rows:] = upstream_ref[...]
     lane = lax.broadcasted_iota(jnp.int32, (width, 128), 1)
     low = lax.broadcasted_iota(jnp.int32, (16, 128), 1)
 
@@ -76,14 +78,14 @@
 def middle(
     where_ref, own_ref, other_ref, gain_ref, bias_ref, weight_ref, project_ref, flipped_ref,
     by_gain_ref, by_bias_ref, taps_ref, mask_ref,
-    far_ref, near_ref, normed_ref, full_ref, stats_ref, both_ref, act_ref, kernel_ref,
+    mixed_ref, normed_ref, full_ref, stats_ref, both_ref, act_ref, kernel_ref,
     proj_ref, partial_ref, grad_ref, moved_ref,
 ):
     model = weight_ref.shape[1]
     width = own_ref.shape[2]
     lanes = normed_ref.shape[2]
-    rows = near_ref.shape[2]
-    taps = taps_ref.shape[0]
+    rows = mixed_ref.shape[2]
+    taps = taps_ref.shape[1]
     reach = taps // 2
     total = jnp.zeros((8, lanes), f32)
     square = jnp.zeros((8, lanes), f32)
@@ -101,9 +103,11 @@
     stats_ref[...] = jnp.concatenate(
         [row_mean, inv_std, jnp.zeros((6, lanes), f32)], axis=0
     )
-    for place, block in blocks_of(where_ref, own_ref, other_ref):
+    for i, (place, block) in enumerate(blocks_of(where_ref, own_ref, other_ref)):
         centred = (block[:, :lanes].astype(f32) - row_mean) * inv_std
-        normed_ref[place] = (centred * gain_ref[place] + bias_ref[place]).astype(bf16)
+        normed_ref[place] = (
+            centred * gain_ref[:, i : i + 1] + bias_ref[:, i : i + 1]
+        ).astype(bf16)
     grad_ref[...] = jnp.dot(
         project_ref[...], full_ref[...].reshape(model, lanes), preferred_element_type=f32
     )
@@ -125,7 +129,7 @@
         for k in range(taps):
             moved = pltpu.roll(glu, (reach - k) % lanes, 1)
             moved_ref[k] = moved[:, :rows]
-            conv = conv + taps_ref[k, mine, :] * moved
+            conv = conv + taps_ref[mine, k : k + 1] * moved
         sig = jax.nn.sigmoid(conv)
         act_ref[mine, :] = (conv * sig)[:, :rows].astype(bf16)
         act_grad = grad_ref[mine, :].astype(bf16).astype(f32)
@@ -135,7 +139,7 @@
         kernel = jnp.zeros((group, 128), f32)
         for k in range(taps):
             back = pltpu.roll(grad, (k - reach) % lanes, 1)[:, :rows]
-            glu_grad = glu_grad + taps_ref[k, mine, :] * back
+            glu_grad = glu_grad + taps_ref[mine, k : k + 1] * back
             seen = jnp.sum(inner * moved_ref[k], axis=1, keepdims=True)
             kernel = jnp.where(lane == k, seen, kernel)
         kernel_ref[mine, :] = kernel
@@ -162,9 +166,9 @@
     zh = where_ref[0]
     for x in range(4):
         for core in range(2):
-            far_ref[x * 2 + core, :width] = partial_ref[x, 1 - zh, core]
-            far_ref[x * 2 + core, width:] = extra
-            near_ref[x * 2 + core] = partial_ref[x, zh, core]
+            mixed_ref[x * 2 + core, :width] = partial_ref[x, 1 - zh, core]
+            mixed_ref[x * 2 + core, width : 2 * width] = partial_ref[x, zh, core]
+            mixed_ref[x * 2 + core, 2 * width :] = extra
 
 
 def weights_of(normed_ref, full_ref, both_ref, act_ref, kernel_ref, grads_ref):
@@ -213,36 +217,57 @@
     offset = lax.axis_index(CHAN) * width
     where = jnp.stack([zh, core]).astype(jnp.int32)
 
-    to_right, to_left = call(
+    main, to_right, to_left = call(
         edges,
-        (shape((width + 16, 128), bf16), shape((width + 16, 128), bf16)),
+        (
+            shape((width, 2 * rows), bf16),
+            shape((width + 16, 128), bf16),
+            shape((width + 16, 128), bf16),
+        ),
         specs=[VMEM] * 3,
     )(inputs, upstream, frame_mask.reshape(1, rows))
+    came = swap(main, "zh")
     edge = lax.ppermute(to_right, FRAME, [(i, i + 1) for i in range(31)]) + lax.ppermute(
         to_left, FRAME, [(i + 1, i) for i in range(31)]
     )
+    across = FRAME + ("zh",)
+    pairs = [(i, i + 1, z) for i in range(31) for z in range(2)]
+    edge_came = lax.ppermute(
+        to_right[:width], across, [(2 * i + z, 2 * j + 1 - z) for i, j, z in pairs]
+    ) + lax.ppermute(to_left[:width], across, [(2 * j + z, 2 * i + 1 - z) for i, j, z in pairs])
 
     weights = jnp.concatenate([value_weight, gate_weight])
     by_gain = jnp.sum(weights.astype(f32) * norm_gain[None, :], axis=1, keepdims=True)
     by_bias = jnp.sum(weights.astype(f32) * norm_bias[None, :], axis=1, keepdims=True)
     gain_local = lax.dynamic_slice_in_dim(norm_gain, offset, width, 0)[:, None]
+
+    def columns_of(parameter):
+        parameter = parameter.reshape(4, 2, 2, width)
+        parameter = jnp.where(zh == 0, parameter, parameter[:, ::-1])
+        parameter = jnp.where(core == 0, parameter, parameter[:, :, ::-1])
+        return parameter.reshape(16, width).T
+
     early = (
-        weights, weights.T, by_gain, by_bias, conv_kernel.reshape(taps, width, 1),
-        norm_gain.reshape(16, width, 1), norm_bias.reshape(16, width, 1), gain_local, where,
-    )
-
-    held = jnp.concatenate([inputs, edge[:width], upstream], axis=1)
+        weights, weights.T, by_gain, by_bias, conv_kernel.T,
+        columns_of(norm_gain), columns_of(norm_bias), gain_local, where,
+    )
+
     keep = jnp.concatenate([frame_mask.astype(f32)[None, :], edge[width : width + 1].astype(f32)], axis=1)
-    came = swap(held, "zh")
     came, keep, early = lax.optimization_barrier((came, keep, early))
     weights, flipped, by_gain, by_bias, columns, gain, bias, gain_local, where = early
-    own = over_x(jnp.stack([held, came]))
+    own = over_x(
+        jnp.stack(
+            [
+                jnp.concatenate([inputs, edge[:width], upstream], axis=1),
+                jnp.concatenate([came[:, :rows], edge_came, came[:, rows:]], axis=1),
+            ]
+        )
+    )
     other = swap(own, "core")
-    far, near, normed, full_grads, stats, both, activated, kernel_part = call(
+    mixed, normed, full_grads, stats, both, activated, kernel_part = call(
         middle,
         (
-            shape((8, width + 16, rows), bf16),
-            shape((8, width, rows), bf16),
+            shape((8, 2 * width + 16, rows), bf16),
             shape((16, width, lanes), bf16),
             shape((16, width, lanes), bf16),
             shape((8, lanes), f32),
@@ -262,8 +287,8 @@
         by_gain, by_bias, columns, keep,
     )
 
-    far, both = lax.optimization_barrier((far, both))
-    far = lax.all_to_all(far, ("x", "core"), 0, 0, tiled=True)
+    mixed, both = lax.optimization_barrier((mixed, both))
+    mixed = lax.all_to_all(mixed, ("x", "core"), 0, 0, tiled=True)
     (grads,) = call(
         weights_of, (shape((8, 4, piece, 4 * width), bf16),), specs=[VMEM] * 5
     )(normed, full_grads, both, activated, kernel_part)
@@ -275,13 +300,11 @@
         lax.ppermute(rows_for(step), "y", [(i, (i + step) % 4) for i in range(4)])
         for step in (1, 3, 2)
     ]
-    near, far = lax.optimization_barrier((near, far))
-    near = lax.all_to_all(near, ("x", "core"), 0, 0, tiled=True)
-    far = jnp.sum(far.astype(f32), axis=0)
-    far_sums = far[width : width + 2] + far[width + 2 : width + 4]
+    mixed = jnp.sum(mixed.astype(f32), axis=0)
+    far_sums = mixed[2 * width : 2 * width + 2] + mixed[2 * width + 2 : 2 * width + 4]
     sent_high, sent_low = split_bf16(far_sums)
     far = jnp.concatenate(
-        [far[:width].astype(bf16), sent_high, sent_low, jnp.zeros((12, rows), bf16)]
+        [mixed[:width].astype(bf16), sent_high, sent_low, jnp.zeros((12, rows), bf16)]
     )
     came = swap(far, "zh").astype(f32)
 
@@ -298,7 +321,7 @@
 
     total = halve(total, 4)
 
-    normed_grad = jnp.sum(near.astype(f32), axis=0) + came[:width]
+    normed_grad = mixed[width : 2 * width] + came[:width]
     kept = far_copy[width : width + 4].astype(f32)
     sums = (kept[:2] + kept[2:] + came[width : width + 2] + came[width + 2 : width + 4]) / model
     inv_std = stats[1:2, :rows]

time: 169 us -> 177 us (1.047)
  starting transfers between devices: 92.2 us -> 71.6 us
  waiting for transfers between devices: 22.7 us -> 42.1 us
  blocking collectives: 15.5 us -> 21.4 us
  local copies, waits for them, and re-layouts: 16.4 us -> 20 us
    ppermute x3, starting transfers between devices: 43.6 us -> 26.6 us  [swap(): return lax.ppermute(value, axis, SWAP)]
    ppermute x0 -> x2, waiting for transfers between devices: none -> 10.6 us  [the longest x1 8.43 us: on_device(): lax.ppermute(to_left[:width], across, [(2 * j + z, 2 * i + 1 - z) for i,...]
    ppermute x3, starting transfers between devices: 17.6 us -> 9.23 us  [halve(): lax.ppermute(sent, 'zl', [(i, i ^ size) for i in range(8)]).astype(f32)]
    all_to_all x1, blocking collectives: 15.5 us -> 21.4 us  [over_x(): lax.all_to_all(jnp.broadcast_to(pair[None], (4,) + pair.shape), 'x', 0, 0...]
    ppermute x3, waiting for transfers between devices: 10.8 us -> 16.4 us  [halve(): lax.ppermute(sent, 'zl', [(i, i ^ size) for i in range(8)]).astype(f32)]
    ppermute x0 -> x2, starting transfers between devices: none -> 5.01 us  [the longest x1 3.72 us: on_device(): lax.ppermute(to_right[:width], across, [(2 * i + z, 2 * j + 1 - z) for i,...]
    all_to_all x2 -> x1, starting transfers between devices: 9.42 us -> 4.65 us  [on_device(): mixed = lax.all_to_all(mixed, ('x', 'core'), 0, 0, tiled=True)]
    unnamed x30 -> x47, local copies, waits for them, and re-layouts: 8.01 us -> 11.6 us
  transfers between devices with their start and end apart: 14 -> 15, of which waited for: 3 -> 7; matrix products, arithmetic and copies ran while one was open for 7% -> 8% of each run, Pallas kernels for 1% -> 1%
where the time goes in v5:
time: 177 us; the launch traced here: 176 us
  starting transfers between devices  71.6 us (40%)
  waiting for transfers between devices  42.1 us (24%)
  blocking collectives  21.4 us (12%)
  local copies, waits for them, and re-layouts  20 us (11%)
  Pallas kernels  14.5 us (8%)
  other arithmetic  5.3 us (3%)
    ppermute x3, starting transfers between devices, swap(): return lax.ppermute(value, axis, SWAP)  26.6 us
    all_to_all x1, blocking collectives, over_x(): lax.all_to_all(jnp.broadcast_to(pair[None], (4,) + pair.shape), 'x', 0, 0...  21.4 us
    ppermute x3, waiting for transfers between devices, halve(): lax.ppermute(sent, 'zl', [(i, i ^ size) for i in range(8)]).astype(f32)  16.4 us
    pallas_call x1, Pallas kernels, on_device(): call(middle, (shape((8, 2 * width + 16, rows), bf16), shape((16, width, l...  13 us
    unnamed x47, local copies, waits for them, and re-layouts  11.6 us
    ppermute x3, starting transfers between devices, on_device(): lax.ppermute(rows_for(step), 'y', [(i, (i + step) % 4) for i in range(4)])  10.9 us
    all_to_all x1, starting transfers between devices, on_device(): lax.all_to_all(jnp.broadcast_to(tail[None], (32, 2, width)), FRAME, 0, 0,...  9.91 us
    ppermute x3, starting transfers between devices, halve(): lax.ppermute(sent, 'zl', [(i, i ^ size) for i in range(8)]).astype(f32)  9.23 us
  transfers between devices with their start and end apart: 15, of which 7 were waited for; matrix products, arithmetic and copies ran while one was open for 8% of the time, Pallas kernels for 1%

profile of v5, /device:TPU:1, one launch (start us, length us, event | category | flops | bytes accessed | tf_op | source)
XLA Modules:
  0.0 176.1 jit_solution(8339421171741154891)
XLA Ops:
  3.2 4.0 %collective-permute-start.1 = (bf16[112,128]{1,0:T(8,128)(2,1)S(1)}, bf16[112,128]{1,0:T(8,128)(2,1)S(1)}, u32[]{:S(2)}, u32[]{:S(2)}) collective-permute-start(bf16[112,128]{1,0:T(8,128)(2,1)S(1)} %get-tuple-element.35), channel_id=1, source_target_pairs={{0,16},{16,32},{32,48},{48,64},{64,80},{80,96},{96,112},{112,128},... | collective-permute-start | bytes 86024 | tf_op jit(solution)/shard_map/ppermute | solution.py:230
  7.2 1.3 collective-permute-start.2
  8.5 15.4 %collective-permute-start = (bf16[96,768]{1,0:T(8,128)(2,1)S(1)}, bf16[96,768]{1,0:T(8,128)(2,1)S(1)}, u32[]{:S(2)}, u32[]{:S(2)}) collective-permute-start(bf16[96,768]{1,0:T(8,128)(2,1)S(1)} %get-tuple-element.34), channel_id=1, source_target_pairs={{0,2},{2,0},{1,3},{3,1},{4,6},{6,4},{5,7},{7,5},{8,10},{10,8},{9,1... | collective-permute-start | bytes 442376 | tf_op jit(solution)/shard_map/ppermute | solution.py:20
  24.0 3.7 %collective-permute-start.3 = (bf16[96,128]{1,0:T(8,128)(2,1)S(1)}, bf16[96,128]{1,0:T(8,128)(2,1)S(1)}, u32[]{:S(2)}, u32[]{:S(2)}) collective-permute-start(bf16[96,128]{1,0:T(8,128)(2,1)S(1)} %slice.82), channel_id=1, source_target_pairs={{0,18},{2,16},{16,34},{18,32},{32,50},{34,48},{48,66},{50,64},{64,... | collective-permute-start | bytes 73736 | tf_op jit(solution)/shard_map/ppermute | solution.py:235
  27.7 1.3 collective-permute-start.4
  30.6 1.2 copy.36
  31.8 1.2 copy.37
  33.0 1.2 fusion.5
  36.5 2.2 %collective-permute-done.3 = bf16[96,128]{1,0:T(8,128)(2,1)S(1)} collective-permute-done((bf16[96,128]{1,0:T(8,128)(2,1)S(1)}, bf16[96,128]{1,0:T(8,128)(2,1)S(1)}, u32[]{:S(2)}, u32[]{:S(2)}) %collective-permute-start.3) | collective-permute-done | bytes 24608 | tf_op jit(solution)/shard_map/ppermute | solution.py:235
  38.7 8.4 %collective-permute-done.4 = bf16[96,128]{1,0:T(8,128)(2,1)S(1)} collective-permute-done((bf16[96,128]{1,0:T(8,128)(2,1)S(1)}, bf16[96,128]{1,0:T(8,128)(2,1)S(1)}, u32[]{:S(2)}, u32[]{:S(2)}) %collective-permute-start.4) | collective-permute-done | bytes 24608 | tf_op jit(solution)/shard_map/ppermute | solution.py:237
  47.5 21.4 %all_to_all.15.own_ref = bf16[4,2,96,896]{3,2,1,0:T(8,128)(2,1)S(1)} all-to-all(bf16[4,2,96,896]{3,2,1,0:T(8,128)(2,1)S(1)} %broadcast_in_dim.33), channel_id=1, replica_groups=mesh['zl'=8,'y'=4,'x'=4,'zh'=2,'core'=2] {'x'}, dimensions={0} | all-to-all | bytes 2752512 | tf_op jit(solution)/shard_map/all_to_all | solution.py:24
  68.9 4.1 %collective-permute-start.5 = (bf16[4,2,96,896]{3,2,1,0:T(8,128)(2,1)S(1)}, bf16[4,2,96,896]{3,2,1,0:T(8,128)(2,1)}, u32[]{:S(2)}, u32[]{:S(2)}) collective-permute-start(bf16[4,2,96,896]{3,2,1,0:T(8,128)(2,1)S(1)} %all_to_all.15.own_ref), channel_id=1, source_target_pairs={{0,1},{1,0},{2,3},{3,2},{4,5},{5,4},{6,7},{7,6},{8,9},{9,8},{10,11... | collective-permute-start | bytes 4128776 | tf_op jit(solution)/shard_map/ppermute | solution.py:20
  72.9 1.4 copy.41.weight_ref
  74.6 1.2 collective-permute-done.5.other_ref
  75.8 13.0 %shard_map.145 = (bf16[8,208,384]{2,1,0:T(8,128)(2,1)S(1)}, bf16[16,96,512]{2,1,0:T(8,128)(2,1)S(1)}, bf16[16,96,512]{2,1,0:T(8,128)(2,1)S(1)}, f32[8,512]{1,0:T...) custom-call(s32[2]{0:T(128)S(1)} %pad_add_fusion.where_ref, ...), custom_call_target="tpu_custom_call" | custom-call | tf_op jit(solution)/shard_map/pallas_call | solution.py:267
  89.9 1.2 copy-done.2
  94.6 4.6 %all-to-all-start.1 = ((bf16[8,208,384]{2,1,0:T(8,128)(2,1)}), bf16[8,208,384]{2,1,0:T(8,128)(2,1)}, u32[]{:S(2)}, u32[]{:S(2)}) async-start(bf16[8,208,384]{2,1,0:T(8,128)(2,1)} %copy-done.4), calls=%async_computation.1 | async-start | bytes 2555904 | tf_op jit(solution)/shard_map/all_to_all | solution.py:291
  99.4 1.4 copy-done.3
  100.8 1.5 shard_map.146
  102.4 3.8 %collective-permute-start.7 = (bf16[8,48,384]{2,1,0:T(8,128)(2,1)S(1)}, bf16[8,48,384]{2,1,0:T(8,128)(2,1)S(1)}, u32[]{:S(2)}, u32[]{:S(2)}) collective-permute-start(bf16[8,48,384]{2,1,0:T(8,128)(2,1)S(1)} %get-tuple-element.71), channel_id=1, source_target_pairs={{0,16},{16,32},{32,48},{48,0},{1,17},{17,33},{33,49},{49,1},{2,18}... | collective-permute-start | bytes 884744 | tf_op jit(solution)/shard_map/ppermute | solution.py:300
  106.2 4.1 %collective-permute-start.8 = (bf16[8,48,384]{2,1,0:T(8,128)(2,1)S(1)}, bf16[8,48,384]{2,1,0:T(8,128)(2,1)S(1)}, u32[]{:S(2)}, u32[]{:S(2)}) collective-permute-start(bf16[8,48,384]{2,1,0:T(8,128)(2,1)S(1)} %get-tuple-element.73), channel_id=1, source_target_pairs={{0,48},{16,0},{32,16},{48,32},{1,49},{17,1},{33,17},{49,33},{2,50}... | collective-permute-start | bytes 884744 | tf_op jit(solution)/shard_map/ppermute | solution.py:300
  110.3 3.1 %collective-permute-start.9 = (bf16[8,48,384]{2,1,0:T(8,128)(2,1)S(1)}, bf16[8,48,384]{2,1,0:T(8,128)(2,1)S(1)}, u32[]{:S(2)}, u32[]{:S(2)}) collective-permute-start(bf16[8,48,384]{2,1,0:T(8,128)(2,1)S(1)} %get-tuple-element.72), channel_id=1, source_target_pairs={{0,32},{16,48},{32,0},{48,16},{1,33},{17,49},{33,1},{49,17},{2,34}... | collective-permute-start | bytes 884744 | tf_op jit(solution)/shard_map/ppermute | solution.py:300
  114.2 2.8 %all-to-all-done.1 = bf16[8,208,384]{2,1,0:T(8,128)(2,1)} async-done(((bf16[8,208,384]{2,1,0:T(8,128)(2,1)}), bf16[8,208,384]{2,1,0:T(8,128)(2,1)}, u32[]{:S(2)}, u32[]{:S(2)}) %all-to-all-start.1) | async-done | bytes 1277984 | tf_op jit(solution)/shard_map/all_to_all | solution.py:291
  117.0 1.5 convert_reduce_fusion
  118.6 7.1 %collective-permute-start.6 = (bf16[112,384]{1,0:T(8,128)(2,1)S(1)}, bf16[112,384]{1,0:T(8,128)(2,1)S(1)}, u32[]{:S(2)}, u32[]{:S(2)}) collective-permute-start(bf16[112,384]{1,0:T(8,128)(2,1)S(1)} %maximum_maximum_fusion), channel_id=1, source_target_pairs={{0,2},{2,0},{1,3},{3,1},{4,6},{6,4},{5,7},{7,5},{8,10},{10,8},{9,1... | collective-permute-start | bytes 258056 | tf_op jit(solution)/shard_map/ppermute | solution.py:20
  125.9 4.2 %collective-permute-start.10 = (bf16[4,48,384]{2,1,0:T(8,128)(2,1)S(1)}, bf16[4,48,384]{2,1,0:T(8,128)(2,1)S(1)}, u32[]{:S(2)}, u32[]{:S(2)}) collective-permute-start(bf16[4,48,384]{2,1,0:T(8,128)(2,1)S(1)} %dynamic-slice_convert_fusion), channel_id=1, source_target_pairs={{0,256},{64,320},{128,384},{192,448},{256,0},{320,64},{384,128},{4... | collective-permute-start | bytes 442376 | tf_op jit(solution)/shard_map/ppermute | solution.py:320
  130.1 2.7 %collective-permute-done.6 = bf16[112,384]{1,0:T(8,128)(2,1)S(1)} collective-permute-done((bf16[112,384]{1,0:T(8,128)(2,1)S(1)}, bf16[112,384]{1,0:T(8,128)(2,1)S(1)}, u32[]{:S(2)}, u32[]{:S(2)}) %collective-permute-start.6) | collective-permute-done | bytes 86048 | tf_op jit(solution)/shard_map/ppermute | solution.py:20
  133.7 16.4 %collective-permute-done.10 = bf16[4,48,384]{2,1,0:T(8,128)(2,1)S(1)} collective-permute-done((bf16[4,48,384]{2,1,0:T(8,128)(2,1)S(1)}, bf16[4,48,384]{2,1,0:T(8,128)(2,1)S(1)}, u32[]{:S(2)}, u32[]{:S(2)}) %collective-permute-start.10) | collective-permute-done | bytes 147488 | tf_op jit(solution)/shard_map/ppermute | solution.py:320
  150.2 1.9 %collective-permute-start.11 = (bf16[2,48,384]{2,1,0:T(8,128)(2,1)S(1)}, bf16[2,48,384]{2,1,0:T(8,128)(2,1)S(1)}, u32[]{:S(2)}, u32[]{:S(2)}) collective-permute-start(bf16[2,48,384]{2,1,0:T(8,128)(2,1)S(1)} %dynamic-slice_convert_fusion.1), channel_id=1, source_target_pairs={{0,128},{64,192},{128,0},{192,64},{256,384},{320,448},{384,256},{4... | collective-permute-start | bytes 221192 | tf_op jit(solution)/shard_map/ppermute | solution.py:320
  152.8 9.9 %all-to-all-start.2 = ((f32[32,2,96]{2,1,0:T(2,128)}), f32[32,2,96]{2,1,0:T(2,128)S(1)}, u32[]{:S(2)}, u32[]{:S(2)}) async-start(f32[32,2,96]{2,1,0:T(2,128)} %broadcast_in_dim.35), calls=%async_computation.2 | async-start | bytes 65536 | tf_op jit(solution)/shard_map/all_to_all | solution.py:331
  162.7 3.1 %collective-permute-start.12 = (bf16[1,48,384]{2,1,0:T(8,128)(2,1)S(1)}, bf16[1,48,384]{2,1,0:T(8,128)(2,1)S(1)}, u32[]{:S(2)}, u32[]{:S(2)}) collective-permute-start(bf16[1,48,384]{2,1,0:T(8,128)(2,1)S(1)} %dynamic-slice_convert_fusion.2), channel_id=1, source_target_pairs={{0,64},{64,0},{128,192},{192,128},{256,320},{320,256},{384,448},{4... | collective-permute-start | bytes 110600 | tf_op jit(solution)/shard_map/ppermute | solution.py:320
  165.9 8.3 %all-to-all-done.2 = f32[32,2,96]{2,1,0:T(2,128)S(1)} async-done(((f32[32,2,96]{2,1,0:T(2,128)}), f32[32,2,96]{2,1,0:T(2,128)S(1)}, u32[]{:S(2)}, u32[]{:S(2)}) %all-to-all-start.2) | async-done | bytes 24608 | tf_op jit(solution)/shard_map/all_to_all | solution.py:331
  (106 shorter events, 16.3 us)
Async XLA Ops:
  1.3 0.9 copy-start.5
  3.2 44.0 %collective-permute-start.1 = (bf16[112,128]{1,0:T(8,128)(2,1)S(1)}, bf16[112,128]{1,0:T(8,128)(2,1)S(1)}, u32[]{:S(2)}, u32[]{:S(2)}) collective-permute-start(bf16[112,128]{1,0:T(8,128)(2,1)S(1)} %get-tuple-element.35), channel_id=1, source_target_pairs={{0,16},{16,32},{32,48},{48,64},{64,80},{80,96},{96,112},{112,128},... | collective-permute-start | bytes 86024 | tf_op jit(solution)/shard_map/ppermute | solution.py:230
  7.2 39.9 %collective-permute-start.2 = (bf16[112,128]{1,0:T(8,128)(2,1)S(1)}, bf16[112,128]{1,0:T(8,128)(2,1)S(1)}, u32[]{:S(2)}, u32[]{:S(2)}) collective-permute-start(bf16[112,128]{1,0:T(8,128)(2,1)S(1)} %get-tuple-element.36), channel_id=1, source_target_pairs={{16,0},{32,16},{48,32},{64,48},{80,64},{96,80},{112,96},{128,112},... | collective-permute-start | bytes 86024 | tf_op jit(solution)/shard_map/ppermute | solution.py:230
  8.5 38.8 %collective-permute-start = (bf16[96,768]{1,0:T(8,128)(2,1)S(1)}, bf16[96,768]{1,0:T(8,128)(2,1)S(1)}, u32[]{:S(2)}, u32[]{:S(2)}) collective-permute-start(bf16[96,768]{1,0:T(8,128)(2,1)S(1)} %get-tuple-element.34), channel_id=1, source_target_pairs={{0,2},{2,0},{1,3},{3,1},{4,6},{6,4},{5,7},{7,5},{8,10},{10,8},{9,1... | collective-permute-start | bytes 442376 | tf_op jit(solution)/shard_map/ppermute | solution.py:20
  24.0 14.7 %collective-permute-start.3 = (bf16[96,128]{1,0:T(8,128)(2,1)S(1)}, bf16[96,128]{1,0:T(8,128)(2,1)S(1)}, u32[]{:S(2)}, u32[]{:S(2)}) collective-permute-start(bf16[96,128]{1,0:T(8,128)(2,1)S(1)} %slice.82), channel_id=1, source_target_pairs={{0,18},{2,16},{16,34},{18,32},{32,50},{34,48},{48,66},{50,64},{64,... | collective-permute-start | bytes 73736 | tf_op jit(solution)/shard_map/ppermute | solution.py:235
  27.7 19.4 %collective-permute-start.4 = (bf16[96,128]{1,0:T(8,128)(2,1)S(1)}, bf16[96,128]{1,0:T(8,128)(2,1)S(1)}, u32[]{:S(2)}, u32[]{:S(2)}) collective-permute-start(bf16[96,128]{1,0:T(8,128)(2,1)S(1)} %slice.83), channel_id=1, source_target_pairs={{16,2},{18,0},{32,18},{34,16},{48,34},{50,32},{64,50},{66,48},{80,... | collective-permute-start | bytes 73736 | tf_op jit(solution)/shard_map/ppermute | solution.py:237
  31.8 2.5 %copy-start.17 = (f32[1536]{0:T(1024)S(1)}, f32[1536]{0:T(1024)}, u32[]{:S(2)}) copy-start(f32[1536]{0:T(1024)} %param.11) | copy-start | bytes 18436
  31.8 2.5 %copy-start.18 = (f32[1536]{0:T(1024)S(1)}, f32[1536]{0:T(1024)}, u32[]{:S(2)}) copy-start(f32[1536]{0:T(1024)} %param.10) | copy-start | bytes 18436
  33.0 3.2 %copy-start.20 = (s32[384]{0:T(512)S(1)}, s32[384]{0:T(512)}, u32[]{:S(2)}) copy-start(s32[384]{0:T(512)} %param.16) | copy-start | bytes 4612
  33.0 3.4 %copy-start.19 = (f32[31,96]{1,0:T(8,128)S(1)}, f32[31,96]{1,0:T(8,128)}, u32[]{:S(2)}) copy-start(f32[31,96]{1,0:T(8,128)} %param.14) | copy-start | bytes 35716
  33.0 14.2 %copy-start.6 = (bf16[96,384]{1,0:T(8,128)(2,1)S(1)}, bf16[96,384]{1,0:T(8,128)(2,1)}, u32[]{:S(2)}) copy-start(bf16[96,384]{1,0:T(8,128)(2,1)} %inputs_ref.1) | copy-start | bytes 221188
  33.0 14.2 %copy-start.8 = (bf16[96,384]{1,0:T(8,128)(2,1)S(1)}, bf16[96,384]{1,0:T(8,128)(2,1)}, u32[]{:S(2)}) copy-start(bf16[96,384]{1,0:T(8,128)(2,1)} %upstream_ref.1) | copy-start | bytes 221188
  47.5 28.3 %copy-start.9 = (bf16[96,1536]{1,0:T(8,128)(2,1)S(1)}, bf16[96,1536]{1,0:T(8,128)(2,1)}, u32[]{:S(2)}) copy-start(bf16[96,1536]{1,0:T(8,128)(2,1)} %project_ref.1) | copy-start | bytes 884740
  68.9 6.9 %collective-permute-start.5 = (bf16[4,2,96,896]{3,2,1,0:T(8,128)(2,1)S(1)}, bf16[4,2,96,896]{3,2,1,0:T(8,128)(2,1)}, u32[]{:S(2)}, u32[]{:S(2)}) collective-permute-start(bf16[4,2,96,896]{3,2,1,0:T(8,128)(2,1)S(1)} %all_to_all.15.own_ref), channel_id=1, source_target_pairs={{0,1},{1,0},{2,3},{3,2},{4,5},{5,4},{6,7},{7,6},{8,9},{9,8},{10,11... | collective-permute-start | bytes 4128776 | tf_op jit(solution)/shard_map/ppermute | solution.py:20
  88.8 1.1 copy-start
  89.9 1.2 copy-start.2
  91.1 1.0 copy-start.4
  94.6 4.7 %copy-start.1 = (bf16[16,96,512]{2,1,0:T(8,128)(2,1)S(1)}, bf16[16,96,512]{2,1,0:T(8,128)(2,1)}, u32[]{:S(2)}) copy-start(bf16[16,96,512]{2,1,0:T(8,128)(2,1)} %copy-done) | copy-start | bytes 4718596
  94.6 4.7 %copy-start.11 = (bf16[192,384]{1,0:T(8,128)(2,1)S(1)}, bf16[192,384]{1,0:T(8,128)(2,1)}, u32[]{:S(2)}) copy-start(bf16[192,384]{1,0:T(8,128)(2,1)} %copy-done.10) | copy-start | bytes 442372
  94.6 4.7 %copy-start.13 = (bf16[96,384]{1,0:T(8,128)(2,1)S(1)}, bf16[96,384]{1,0:T(8,128)(2,1)}, u32[]{:S(2)}) copy-start(bf16[96,384]{1,0:T(8,128)(2,1)} %copy-done.12) | copy-start | bytes 221188
  94.6 4.7 %copy-start.15 = (f32[96,128]{1,0:T(8,128)S(1)}, f32[96,128]{1,0:T(8,128)}, u32[]{:S(2)}) copy-start(f32[96,128]{1,0:T(8,128)} %copy-done.14) | copy-start | bytes 147460
  94.6 22.3 %all-to-all-start.1 = ((bf16[8,208,384]{2,1,0:T(8,128)(2,1)}), bf16[8,208,384]{2,1,0:T(8,128)(2,1)}, u32[]{:S(2)}, u32[]{:S(2)}) async-start(bf16[8,208,384]{2,1,0:T(8,128)(2,1)} %copy-done.4), calls=%async_computation.1 | async-start | bytes 2555904 | tf_op jit(solution)/shard_map/all_to_all | solution.py:291
  99.4 1.4 copy-start.3
  102.4 23.3 %collective-permute-start.7 = (bf16[8,48,384]{2,1,0:T(8,128)(2,1)S(1)}, bf16[8,48,384]{2,1,0:T(8,128)(2,1)S(1)}, u32[]{:S(2)}, u32[]{:S(2)}) collective-permute-start(bf16[8,48,384]{2,1,0:T(8,128)(2,1)S(1)} %get-tuple-element.71), channel_id=1, source_target_pairs={{0,16},{16,32},{32,48},{48,0},{1,17},{17,33},{33,49},{49,1},{2,18}... | collective-permute-start | bytes 884744 | tf_op jit(solution)/shard_map/ppermute | solution.py:300
  106.2 19.5 %collective-permute-start.8 = (bf16[8,48,384]{2,1,0:T(8,128)(2,1)S(1)}, bf16[8,48,384]{2,1,0:T(8,128)(2,1)S(1)}, u32[]{:S(2)}, u32[]{:S(2)}) collective-permute-start(bf16[8,48,384]{2,1,0:T(8,128)(2,1)S(1)} %get-tuple-element.73), channel_id=1, source_target_pairs={{0,48},{16,0},{32,16},{48,32},{1,49},{17,1},{33,17},{49,33},{2,50}... | collective-permute-start | bytes 884744 | tf_op jit(solution)/shard_map/ppermute | solution.py:300
  110.3 15.4 %collective-permute-start.9 = (bf16[8,48,384]{2,1,0:T(8,128)(2,1)S(1)}, bf16[8,48,384]{2,1,0:T(8,128)(2,1)S(1)}, u32[]{:S(2)}, u32[]{:S(2)}) collective-permute-start(bf16[8,48,384]{2,1,0:T(8,128)(2,1)S(1)} %get-tuple-element.72), channel_id=1, source_target_pairs={{0,32},{16,48},{32,0},{48,16},{1,33},{17,49},{33,1},{49,17},{2,34}... | collective-permute-start | bytes 884744 | tf_op jit(solution)/shard_map/ppermute | solution.py:300
  118.5 14.3 %copy-start.21 = (f32[96,1]{0,1:T(1,128)S(1)}, f32[96,1]{0,1:T(1,128)}, u32[]{:S(2)}) copy-start(f32[96,1]{0,1:T(1,128)} %dynamic-slice_bitcast_fusion.4) | copy-start | bytes 1156
  118.6 14.1 %collective-permute-start.6 = (bf16[112,384]{1,0:T(8,128)(2,1)S(1)}, bf16[112,384]{1,0:T(8,128)(2,1)S(1)}, u32[]{:S(2)}, u32[]{:S(2)}) collective-permute-start(bf16[112,384]{1,0:T(8,128)(2,1)S(1)} %maximum_maximum_fusion), channel_id=1, source_target_pairs={{0,2},{2,0},{1,3},{3,1},{4,6},{6,4},{5,7},{7,5},{8,10},{10,8},{9,1... | collective-permute-start | bytes 258056 | tf_op jit(solution)/shard_map/ppermute | solution.py:20
  125.9 24.2 %collective-permute-start.10 = (bf16[4,48,384]{2,1,0:T(8,128)(2,1)S(1)}, bf16[4,48,384]{2,1,0:T(8,128)(2,1)S(1)}, u32[]{:S(2)}, u32[]{:S(2)}) collective-permute-start(bf16[4,48,384]{2,1,0:T(8,128)(2,1)S(1)} %dynamic-slice_convert_fusion), channel_id=1, source_target_pairs={{0,256},{64,320},{128,384},{192,448},{256,0},{320,64},{384,128},{4... | collective-permute-start | bytes 442376 | tf_op jit(solution)/shard_map/ppermute | solution.py:320
  150.2 12.5 %collective-permute-start.11 = (bf16[2,48,384]{2,1,0:T(8,128)(2,1)S(1)}, bf16[2,48,384]{2,1,0:T(8,128)(2,1)S(1)}, u32[]{:S(2)}, u32[]{:S(2)}) collective-permute-start(bf16[2,48,384]{2,1,0:T(8,128)(2,1)S(1)} %dynamic-slice_convert_fusion.1), channel_id=1, source_target_pairs={{0,128},{64,192},{128,0},{192,64},{256,384},{320,448},{384,256},{4... | collective-permute-start | bytes 221192 | tf_op jit(solution)/shard_map/ppermute | solution.py:320
  152.8 21.5 %all-to-all-start.2 = ((f32[32,2,96]{2,1,0:T(2,128)}), f32[32,2,96]{2,1,0:T(2,128)S(1)}, u32[]{:S(2)}, u32[]{:S(2)}) async-start(f32[32,2,96]{2,1,0:T(2,128)} %broadcast_in_dim.35), calls=%async_computation.2 | async-start | bytes 65536 | tf_op jit(solution)/shard_map/all_to_all | solution.py:331
  162.7 12.0 %collective-permute-start.12 = (bf16[1,48,384]{2,1,0:T(8,128)(2,1)S(1)}, bf16[1,48,384]{2,1,0:T(8,128)(2,1)S(1)}, u32[]{:S(2)}, u32[]{:S(2)}) collective-permute-start(bf16[1,48,384]{2,1,0:T(8,128)(2,1)S(1)} %dynamic-slice_convert_fusion.2), channel_id=1, source_target_pairs={{0,64},{64,0},{128,192},{192,128},{256,320},{320,256},{384,448},{4... | collective-permute-start | bytes 110600 | tf_op jit(solution)/shard_map/ppermute | solution.py:320
  (5 other events, 3.4 us)

commit v6 on v5

--- a/solution.py
+++ b/solution.py
@@ -55,10 +55,8 @@
             yield x * 4 + side * 2 + 1 - core, other_ref.at[x, far]
 
 
-def edges(inputs_ref, upstream_ref, mask_ref, main_ref, right_ref, left_ref):
+def edges(inputs_ref, upstream_ref, mask_ref, right_ref, left_ref):
     width, rows = inputs_ref.shape
-    main_ref[:, :rows] = inputs_ref[...]
-    main_ref[:, rows:] = upstream_ref[...]
     lane = lax.broadcasted_iota(jnp.int32, (width, 128), 1)
     low = lax.broadcasted_iota(jnp.int32, (16, 128), 1)
 
@@ -78,15 +76,15 @@
 def middle(
     where_ref, own_ref, other_ref, gain_ref, bias_ref, weight_ref, project_ref, flipped_ref,
     by_gain_ref, by_bias_ref, taps_ref, mask_ref,
-    mixed_ref, normed_ref, full_ref, stats_ref, both_ref, act_ref, kernel_ref,
-    proj_ref, partial_ref, grad_ref, moved_ref,
+    mixed_out, grads_ref, stats_ref,
+    mixed_ref, normed_ref, full_ref, both_ref, act_ref, kernel_ref,
+    proj_ref, grad_ref, moved_ref, back_ref, sem,
 ):
     model = weight_ref.shape[1]
     width = own_ref.shape[2]
     lanes = normed_ref.shape[2]
     rows = mixed_ref.shape[2]
-    taps = taps_ref.shape[1]
-    reach = taps // 2
+    taps = taps_ref.shape[0]
     total = jnp.zeros((8, lanes), f32)
     square = jnp.zeros((8, lanes), f32)
     for place, block in blocks_of(where_ref, own_ref, other_ref):
@@ -116,6 +114,7 @@
     )
     group = 16
     lane = lax.broadcasted_iota(jnp.int32, (group, 128), 1)
+    inside = lax.broadcasted_iota(jnp.int32, (group, lanes), 1) < rows
 
     def channels(step, carry):
         first = pl.multiple_of(step * group, group)
@@ -125,23 +124,43 @@
         gate = jax.nn.sigmoid(proj_ref[after, :])
         keep = mask_ref[...]
         glu = (value * gate * keep).astype(bf16).astype(f32)
-        conv = jnp.zeros((group, lanes), f32)
-        for k in range(taps):
-            moved = pltpu.roll(glu, (reach - k) % lanes, 1)
-            moved_ref[k] = moved[:, :rows]
-            conv = conv + taps_ref[mine, k : k + 1] * moved
+
+        def shifted(x, by):
+            return pltpu.roll(x, by % lanes, 1) if by % lanes else x
+
+        def tap(k):
+            return jnp.concatenate([taps_ref[k, mine, :]] * (lanes // 128), axis=1)
+
+        def spread(fine, sign):
+            result = None
+            for a in range(4):
+                part = None
+                for b in range(8):
+                    if 8 * a + b < taps:
+                        term = tap(8 * a + b) * fine[b]
+                        part = term if part is None else part + term
+                part = shifted(part, sign * (8 * a - 8))
+                result = part if result is None else result + part
+            return result
+
+        for b in range(8):
+            moved_ref[b] = shifted(glu, 7 - b)
+        conv = spread(moved_ref, -1)
         sig = jax.nn.sigmoid(conv)
         act_ref[mine, :] = (conv * sig)[:, :rows].astype(bf16)
         act_grad = grad_ref[mine, :].astype(bf16).astype(f32)
         grad = (act_grad * (sig + conv * sig * (1.0 - sig))).astype(bf16).astype(f32)
-        inner = grad[:, :rows]
-        glu_grad = jnp.zeros((group, rows), f32)
+        for b in range(8):
+            back_ref[b] = shifted(grad, b - 7)
+        glu_grad = spread(back_ref, 1)[:, :rows]
+        inner = jnp.where(inside, grad, 0.0)
         kernel = jnp.zeros((group, 128), f32)
-        for k in range(taps):
-            back = pltpu.roll(grad, (k - reach) % lanes, 1)[:, :rows]
-            glu_grad = glu_grad + taps_ref[mine, k : k + 1] * back
-            seen = jnp.sum(inner * moved_ref[k], axis=1, keepdims=True)
-            kernel = jnp.where(lane == k, seen, kernel)
+        for a in range(4):
+            here = shifted(inner, 8 * a - 8)
+            for b in range(8):
+                if 8 * a + b < taps:
+                    seen = jnp.sum(here * moved_ref[b], axis=1, keepdims=True)
+                    kernel = jnp.where(lane == 8 * a + b, seen, kernel)
         kernel_ref[mine, :] = kernel
         glu_grad = glu_grad * keep[:, :rows]
         gate = gate[:, :rows]
@@ -152,7 +171,7 @@
     lax.fori_loop(0, width // group, channels, 0)
     both = both_ref[...]
     partial = jnp.dot(flipped_ref[...], both, preferred_element_type=f32).astype(bf16)
-    partial_ref[...] = partial.reshape(partial_ref.shape)
+    partial = partial.reshape(4, 2, 2, width, rows)
     both = both.astype(f32)
     first = jnp.sum(both * by_gain_ref[...], axis=0, keepdims=True)
     second = jnp.sum(both * (proj_ref[:, :rows] - by_bias_ref[...]), axis=0, keepdims=True)
@@ -166,14 +185,13 @@
     zh = where_ref[0]
     for x in range(4):
         for core in range(2):
-            mixed_ref[x * 2 + core, :width] = partial_ref[x, 1 - zh, core]
-            mixed_ref[x * 2 + core, width : 2 * width] = partial_ref[x, zh, core]
+            for side in range(2):
+                start = pl.multiple_of(jnp.where(side == zh, width, 0), width)
+                mixed_ref[x * 2 + core, pl.ds(start, width)] = partial[x, side, core]
             mixed_ref[x * 2 + core, 2 * width :] = extra
-
-
-def weights_of(normed_ref, full_ref, both_ref, act_ref, kernel_ref, grads_ref):
-    width, rows = act_ref.shape
-    model = normed_ref.shape[0] * width
+    copy = pltpu.make_async_copy(mixed_ref, mixed_out, sem)
+    copy.start()
+
     zero = jnp.zeros((width, rows), bf16)
     grads = lax.dot_general(
         normed_ref[:, :, :rows].reshape(model, rows),
@@ -187,11 +205,11 @@
         preferred_element_type=f32,
     )
     grads_ref[...] = grads.astype(bf16).reshape(grads_ref.shape)
-    piece = grads_ref.shape[2]
-    kernel = jnp.transpose(kernel_ref[...])[:piece].astype(bf16)
+    kernel = jnp.transpose(kernel_ref[...])[: grads_ref.shape[2]].astype(bf16)
     for zl in range(8):
         for y in range(4):
             grads_ref[zl, y, :, :width] = kernel
+    copy.wait()
 
 
 def on_device(
@@ -217,24 +235,14 @@
     offset = lax.axis_index(CHAN) * width
     where = jnp.stack([zh, core]).astype(jnp.int32)
 
-    main, to_right, to_left = call(
+    to_right, to_left = call(
         edges,
-        (
-            shape((width, 2 * rows), bf16),
-            shape((width + 16, 128), bf16),
-            shape((width + 16, 128), bf16),
-        ),
+        (shape((width + 16, 128), bf16), shape((width + 16, 128), bf16)),
         specs=[VMEM] * 3,
     )(inputs, upstream, frame_mask.reshape(1, rows))
-    came = swap(main, "zh")
     edge = lax.ppermute(to_right, FRAME, [(i, i + 1) for i in range(31)]) + lax.ppermute(
         to_left, FRAME, [(i + 1, i) for i in range(31)]
     )
-    across = FRAME + ("zh",)
-    pairs = [(i, i + 1, z) for i in range(31) for z in range(2)]
-    edge_came = lax.ppermute(
-        to_right[:width], across, [(2 * i + z, 2 * j + 1 - z) for i, j, z in pairs]
-    ) + lax.ppermute(to_left[:width], across, [(2 * j + z, 2 * i + 1 - z) for i, j, z in pairs])
 
     weights = jnp.concatenate([value_weight, gate_weight])
     by_gain = jnp.sum(weights.astype(f32) * norm_gain[None, :], axis=1, keepdims=True)
@@ -248,50 +256,47 @@
         return parameter.reshape(16, width).T
 
     early = (
-        weights, weights.T, by_gain, by_bias, conv_kernel.T,
+        weights, weights.T, by_gain, by_bias,
+        jnp.broadcast_to(conv_kernel[:, :, None], (taps, width, 128)),
         columns_of(norm_gain), columns_of(norm_bias), gain_local, where,
     )
 
+    held = jnp.concatenate([inputs, edge[:width], upstream], axis=1)
     keep = jnp.concatenate([frame_mask.astype(f32)[None, :], edge[width : width + 1].astype(f32)], axis=1)
+    came = swap(held, "zh")
     came, keep, early = lax.optimization_barrier((came, keep, early))
     weights, flipped, by_gain, by_bias, columns, gain, bias, gain_local, where = early
-    own = over_x(
-        jnp.stack(
-            [
-                jnp.concatenate([inputs, edge[:width], upstream], axis=1),
-                jnp.concatenate([came[:, :rows], edge_came, came[:, rows:]], axis=1),
-            ]
-        )
-    )
+    own = over_x(jnp.stack([held, came]))
     other = swap(own, "core")
-    mixed, normed, full_grads, stats, both, activated, kernel_part = call(
+    mixed, grads, stats = pl.pallas_call(
         middle,
-        (
+        out_shape=(
             shape((8, 2 * width + 16, rows), bf16),
-            shape((16, width, lanes), bf16),
-            shape((16, width, lanes), bf16),
+            shape((8, 4, piece, 4 * width), bf16),
             shape((8, lanes), f32),
-            shape((2 * width, rows), bf16),
-            shape((width, rows), bf16),
-            shape((width, 128), f32),
         ),
-        scratch=(
+        in_specs=[SMEM] + [VMEM] * 11,
+        out_specs=(pl.BlockSpec(memory_space=pltpu.HBM), VMEM, VMEM),
+        scratch_shapes=[
+            pltpu.VMEM((8, 2 * width + 16, rows), bf16),
+            pltpu.VMEM((16, width, lanes), bf16),
+            pltpu.VMEM((16, width, lanes), bf16),
+            pltpu.VMEM((2 * width, rows), bf16),
+            pltpu.VMEM((width, rows), bf16),
+            pltpu.VMEM((width, 128), f32),
             pltpu.VMEM((2 * width, lanes), f32),
-            pltpu.VMEM((4, 2, 2, width, rows), bf16),
             pltpu.VMEM((width, lanes), f32),
-            pltpu.VMEM((taps, 16, rows), f32),
-        ),
-        specs=[SMEM] + [VMEM] * 11,
+            pltpu.VMEM((8, 16, lanes), f32),
+            pltpu.VMEM((8, 16, lanes), f32),
+            pltpu.SemaphoreType.DMA,
+        ],
+        compiler_params=pltpu.CompilerParams(vmem_limit_bytes=30 << 20),
     )(
         where, own, other, gain, bias, weights, project_weight, flipped,
         by_gain, by_bias, columns, keep,
     )
 
-    mixed, both = lax.optimization_barrier((mixed, both))
     mixed = lax.all_to_all(mixed, ("x", "core"), 0, 0, tiled=True)
-    (grads,) = call(
-        weights_of, (shape((8, 4, piece, 4 * width), bf16),), specs=[VMEM] * 5
-    )(normed, full_grads, both, activated, kernel_part)
 
     def rows_for(step):
         return lax.dynamic_slice_in_dim(grads, (y + step) % 4, 1, 1)[:, 0]
@@ -315,11 +320,13 @@
 
     def halve(total, size):
         side = (zl // size) % 2
-        kept = lax.dynamic_slice_in_dim(total, side * size, size, 0)
-        sent = lax.dynamic_slice_in_dim(total, (1 - side) * size, size, 0).astype(bf16)
+        half = total.shape[0] // 2
+        total = total.reshape(half, 2, piece, 4 * width)
+        kept = lax.dynamic_slice_in_dim(total, side, 1, 1)[:, 0]
+        sent = lax.dynamic_slice_in_dim(total, 1 - side, 1, 1)[:, 0].astype(bf16)
         return kept + lax.ppermute(sent, "zl", [(i, i ^ size) for i in range(8)]).astype(f32)
 
-    total = halve(total, 4)
+    total = halve(total, 1)
 
     normed_grad = mixed[width : 2 * width] + came[:width]
     kept = far_copy[width : width + 4].astype(f32)
@@ -327,17 +334,18 @@
     inv_std = stats[1:2, :rows]
     centred = (inputs.astype(f32) - stats[0:1, :rows]) * inv_std
     tail = jnp.stack([jnp.sum(normed_grad * centred, axis=1), jnp.sum(normed_grad, axis=1)])
-    tail, total = lax.optimization_barrier((tail, total))
+    total, normed_grad = lax.optimization_barrier((total, normed_grad))
     tail = lax.all_to_all(
         jnp.broadcast_to(tail[None], (32, 2, width)), FRAME, 0, 0, tiled=True
     )
-    tail = jnp.sum(tail, axis=0)
     inputs_grad = (
         upstream.astype(f32)
         + inv_std * (normed_grad * gain_local - sums[0:1] - centred * sums[1:2])
     ).astype(bf16)
 
-    grads = halve(halve(total, 2), 1)[0]
+    grads = halve(halve(total, 2), 4)[0]
+    tail, grads = lax.optimization_barrier((tail, grads))
+    tail = jnp.sum(tail, axis=0)
     kernel_grad = grads[:taps, :width]
     value_grad = grads[:, width : 2 * width].T
     gate_grad = grads[:, 2 * width : 3 * width].T

time: 177 us -> 163 us (0.921)
  the two profiles are of different devices: /device:TPU:1 before, /device:TPU:8 now
where the time goes in v6:
time: 163 us; the launch traced here: 162 us
  starting transfers between devices  87.2 us (53%)
  local copies, waits for them, and re-layouts  23.1 us (14%)
  blocking collectives  21.2 us (13%)
  waiting for transfers between devices  14.7 us (9%)
  Pallas kernels  8.96 us (5%)
  other arithmetic  5.21 us (3%)
    ppermute x3, starting transfers between devices, swap(): return lax.ppermute(value, axis, SWAP)  26.6 us
    ppermute x3, starting transfers between devices, halve(): lax.ppermute(sent, 'zl', [(i, i ^ size) for i in range(8)]).astype(f32)  23.8 us
    all_to_all x1, blocking collectives, over_x(): lax.all_to_all(jnp.broadcast_to(pair[None], (4,) + pair.shape), 'x', 0, 0...  21.2 us
    ppermute x3, starting transfers between devices, on_device(): lax.ppermute(rows_for(step), 'y', [(i, (i + step) % 4) for i in range(4)])  13 us
    unnamed x42, local copies, waits for them, and re-layouts  11.6 us
    all_to_all x1, starting transfers between devices, on_device(): lax.all_to_all(jnp.broadcast_to(tail[None], (32, 2, width)), FRAME, 0, 0,...  11.1 us
    pallas_call x1, Pallas kernels, on_device(): pl.pallas_call(middle, out_shape=(shape((8, 2 * width + 16, rows), bf16),...  8.87 us
    ppermute x3, waiting for transfers between devices, halve(): lax.ppermute(sent, 'zl', [(i, i ^ size) for i in range(8)]).astype(f32)  7.04 us
  transfers between devices with their start and end apart: 13, of which 5 were waited for; matrix products, arithmetic and copies ran while one was open for 10% of the time, Pallas kernels for 0%

profile of v6, /device:TPU:8, one launch (start us, length us, event | category | flops | bytes accessed | tf_op | source)
XLA Modules:
  0.0 161.7 jit_solution(13180780203800276934)
XLA Ops:
  3.2 3.5 %collective-permute-start = (bf16[112,128]{1,0:T(8,128)(2,1)S(1)}, bf16[112,128]{1,0:T(8,128)(2,1)S(1)}, u32[]{:S(2)}, u32[]{:S(2)}) collective-permute-start(bf16[112,128]{1,0:T(8,128)(2,1)S(1)} %get-tuple-element.29), channel_id=1, source_target_pairs={{0,16},{16,32},{32,48},{48,64},{64,80},{80,96},{96,112},{112,128},... | collective-permute-start | bytes 86024 | tf_op jit(solution)/shard_map/ppermute | solution.py:243
  6.7 5.5 %collective-permute-start.1 = (bf16[112,128]{1,0:T(8,128)(2,1)S(1)}, bf16[112,128]{1,0:T(8,128)(2,1)S(1)}, u32[]{:S(2)}, u32[]{:S(2)}) collective-permute-start(bf16[112,128]{1,0:T(8,128)(2,1)S(1)} %get-tuple-element.30), channel_id=1, source_target_pairs={{16,0},{32,16},{48,32},{64,48},{80,64},{96,80},{112,96},{128,112},... | collective-permute-start | bytes 86024 | tf_op jit(solution)/shard_map/ppermute | solution.py:243
  13.8 1.2 copy.26
  15.0 1.2 copy.27
  16.2 1.5 fusion.7
  17.8 1.1 fusion.1
  20.6 12.5 %collective-permute-start.2 = (bf16[96,896]{1,0:T(8,128)(2,1)S(1)}, bf16[96,896]{1,0:T(8,128)(2,1)S(1)}, u32[]{:S(2)}, u32[]{:S(2)}) collective-permute-start(bf16[96,896]{1,0:T(8,128)(2,1)S(1)} %get-tuple-element.69), channel_id=1, source_target_pairs={{0,2},{2,0},{1,3},{3,1},{4,6},{6,4},{5,7},{7,5},{8,10},{10,8},{9,1... | collective-permute-start | bytes 516104 | tf_op jit(solution)/shard_map/ppermute | solution.py:20
  33.1 4.1 %collective-permute-done.2 = bf16[96,896]{1,0:T(8,128)(2,1)S(1)} collective-permute-done((bf16[96,896]{1,0:T(8,128)(2,1)S(1)}, bf16[96,896]{1,0:T(8,128)(2,1)S(1)}, u32[]{:S(2)}, u32[]{:S(2)}) %collective-permute-start.2) | collective-permute-done | bytes 172064 | tf_op jit(solution)/shard_map/ppermute | solution.py:20
  37.8 21.2 %all_to_all.15.own_ref = bf16[4,2,96,896]{3,2,1,0:T(8,128)(2,1)S(1)} all-to-all(bf16[4,2,96,896]{3,2,1,0:T(8,128)(2,1)S(1)} %broadcast_in_dim.40), channel_id=1, replica_groups=mesh['zl'=8,'y'=4,'x'=4,'zh'=2,'core'=2] {'x'}, dimensions={0} | all-to-all | bytes 2752512 | tf_op jit(solution)/shard_map/all_to_all | solution.py:24
  59.1 1.9 %collective-permute-start.3 = (bf16[4,2,96,896]{3,2,1,0:T(8,128)(2,1)S(1)}, bf16[4,2,96,896]{3,2,1,0:T(8,128)(2,1)}, u32[]{:S(2)}, u32[]{:S(2)}) collective-permute-start(bf16[4,2,96,896]{3,2,1,0:T(8,128)(2,1)S(1)} %all_to_all.15.own_ref), channel_id=1, source_target_pairs={{0,1},{1,0},{2,3},{3,2},{4,5},{5,4},{6,7},{7,6},{8,9},{9,8},{10,11... | collective-permute-start | bytes 4128776 | tf_op jit(solution)/shard_map/ppermute | solution.py:20
  61.0 1.4 copy.30.weight_ref
  64.2 1.1 copy-done
  65.3 0.9 copy-done.10
  66.2 0.9 copy-done.11
  67.1 1.0 copy-done.12
  68.9 8.9 %shard_map.145 = (bf16[8,208,384]{2,1,0:T(8,128)(2,1)S(1)}, bf16[8,4,48,384]{3,2,1,0:T(8,128)(2,1)S(1)}, f32[8,512]{1,0:T(8,128)S(1)}) custom-call(s32[2]{0:T(128)S(1)} %pad_add_fusion.where_ref, bf16[4,2,96,896]{3,2,1,0:T(8,128)(2,1)S(1)} %all_to_all.15.own_ref, bf16[4,2,96,896]{3,2,1,0:T(8,128)(2,1)} %collective-permute-done.3.other_ref, ...), custom_call_target="tpu_custom_call" | custom-call | tf_op jit(solution)/shard_map/pallas_call | solution.py:271
  77.8 1.1 copy-done.1
  78.8 1.0 copy-done.2
  80.4 3.7 %all-to-all-start.1 = ((bf16[8,208,384]{2,1,0:T(8,128)(2,1)}), bf16[8,208,384]{2,1,0:T(8,128)(2,1)S(1)}, u32[]{:S(2)}, u32[]{:S(2)}) async-start(bf16[8,208,384]{2,1,0:T(8,128)(2,1)} %copy-done.1), calls=%async_computation.1 | async-start | bytes 2555904 | tf_op jit(solution)/shard_map/all_to_all | solution.py:299
  84.4 1.0 dynamic-slice_bitcast_fusion.3
  85.4 3.5 %collective-permute-start.4 = (bf16[8,48,384]{2,1,0:T(8,128)(2,1)}, bf16[8,48,384]{2,1,0:T(8,128)(2,1)S(1)}, u32[]{:S(2)}, u32[]{:S(2)}) collective-permute-start(bf16[8,48,384]{2,1,0:T(8,128)(2,1)} %get-tuple-element.65), channel_id=1, source_target_pairs={{0,16},{16,32},{32,48},{48,0},{1,17},{17,33},{33,49},{49,1},{2,18}... | collective-permute-start | bytes 884744 | tf_op jit(solution)/shard_map/ppermute | solution.py:305
  88.8 5.6 %collective-permute-start.5 = (bf16[8,48,384]{2,1,0:T(8,128)(2,1)}, bf16[8,48,384]{2,1,0:T(8,128)(2,1)S(1)}, u32[]{:S(2)}, u32[]{:S(2)}) collective-permute-start(bf16[8,48,384]{2,1,0:T(8,128)(2,1)} %get-tuple-element.64), channel_id=1, source_target_pairs={{0,48},{16,0},{32,16},{48,32},{1,49},{17,1},{33,17},{49,33},{2,50}... | collective-permute-start | bytes 884744 | tf_op jit(solution)/shard_map/ppermute | solution.py:305
  94.4 4.0 %collective-permute-start.6 = (bf16[8,48,384]{2,1,0:T(8,128)(2,1)}, bf16[8,48,384]{2,1,0:T(8,128)(2,1)}, u32[]{:S(2)}, u32[]{:S(2)}) collective-permute-start(bf16[8,48,384]{2,1,0:T(8,128)(2,1)} %get-tuple-element.63), channel_id=1, source_target_pairs={{0,32},{16,48},{32,0},{48,16},{1,33},{17,49},{33,1},{49,17},{2,34}... | collective-permute-start | bytes 884744 | tf_op jit(solution)/shard_map/ppermute | solution.py:305
  99.2 3.3 %all-to-all-done.1 = bf16[8,208,384]{2,1,0:T(8,128)(2,1)S(1)} async-done(((bf16[8,208,384]{2,1,0:T(8,128)(2,1)}), bf16[8,208,384]{2,1,0:T(8,128)(2,1)S(1)}, u32[]{:S(2)}, u32[]{:S(2)}) %all-to-all-start.1) | async-done | bytes 1277984 | tf_op jit(solution)/shard_map/all_to_all | solution.py:299
  102.8 12.1 %collective-permute-start.8 = (bf16[112,384]{1,0:T(8,128)(2,1)S(1)}, bf16[112,384]{1,0:T(8,128)(2,1)S(1)}, u32[]{:S(2)}, u32[]{:S(2)}) collective-permute-start(bf16[112,384]{1,0:T(8,128)(2,1)S(1)} %maximum_maximum_fusion), channel_id=1, source_target_pairs={{0,2},{2,0},{1,3},{3,1},{4,6},{6,4},{5,7},{7,5},{8,10},{10,8},{9,1... | collective-permute-start | bytes 258056 | tf_op jit(solution)/shard_map/ppermute | solution.py:20
  115.0 1.1 convert_add_fusion
  116.1 13.3 %collective-permute-start.7 = (bf16[4,48,384]{2,1,0:T(8,128)(2,1)S(1)}, bf16[4,48,384]{2,1,0:T(8,128)(2,1)S(1)}, u32[]{:S(2)}, u32[]{:S(2)}) collective-permute-start(bf16[4,48,384]{2,1,0:T(8,128)(2,1)S(1)} %fusion.2), channel_id=1, source_target_pairs={{0,64},{64,0},{128,192},{192,128},{256,320},{320,256},{384,448},{4... | collective-permute-start | bytes 442376 | tf_op jit(solution)/shard_map/ppermute | solution.py:327
  130.2 11.1 %all-to-all-start.2 = ((f32[32,2,96]{2,1,0:T(2,128)}), f32[32,2,96]{2,1,0:T(2,128)S(1)}, u32[]{:S(2)}, u32[]{:S(2)}) async-start(f32[32,2,96]{2,1,0:T(2,128)} %broadcast_in_dim.42), calls=%async_computation.2 | async-start | bytes 65536 | tf_op jit(solution)/shard_map/all_to_all | solution.py:338
  141.4 4.3 %collective-permute-start.9 = (bf16[2,48,384]{2,1,0:T(8,128)(2,1)S(1)}, bf16[2,48,384]{2,1,0:T(8,128)(2,1)S(1)}, u32[]{:S(2)}, u32[]{:S(2)}) collective-permute-start(bf16[2,48,384]{2,1,0:T(8,128)(2,1)S(1)} %fusion.3), channel_id=1, source_target_pairs={{0,128},{64,192},{128,0},{192,64},{256,384},{320,448},{384,256},{4... | collective-permute-start | bytes 221192 | tf_op jit(solution)/shard_map/ppermute | solution.py:327
  145.8 3.9 %collective-permute-done.9 = bf16[2,48,384]{2,1,0:T(8,128)(2,1)S(1)} collective-permute-done((bf16[2,48,384]{2,1,0:T(8,128)(2,1)S(1)}, bf16[2,48,384]{2,1,0:T(8,128)(2,1)S(1)}, u32[]{:S(2)}, u32[]{:S(2)}) %collective-permute-start.9) | collective-permute-done | bytes 73760 | tf_op jit(solution)/shard_map/ppermute | solution.py:327
  149.7 6.2 %collective-permute-start.10 = (bf16[1,48,384]{2,1,0:T(8,128)(2,1)S(1)}, bf16[1,48,384]{2,1,0:T(8,128)(2,1)S(1)}, u32[]{:S(2)}, u32[]{:S(2)}) collective-permute-start(bf16[1,48,384]{2,1,0:T(8,128)(2,1)S(1)} %dynamic-slice_convert_fusion.2), channel_id=1, source_target_pairs={{0,256},{64,320},{128,384},{192,448},{256,0},{320,64},{384,128},{4... | collective-permute-start | bytes 110600 | tf_op jit(solution)/shard_map/ppermute | solution.py:327
  156.7 3.1 %collective-permute-done.10 = bf16[1,48,384]{2,1,0:T(8,128)(2,1)S(1)} collective-permute-done((bf16[1,48,384]{2,1,0:T(8,128)(2,1)S(1)}, bf16[1,48,384]{2,1,0:T(8,128)(2,1)S(1)}, u32[]{:S(2)}, u32[]{:S(2)}) %collective-permute-start.10) | collective-permute-done | bytes 36896 | tf_op jit(solution)/shard_map/ppermute | solution.py:327
  (93 shorter events, 14.3 us)
Async XLA Ops:
  1.3 0.9 copy-start.4
  2.2 0.9 copy-start.7
  3.2 17.3 %collective-permute-start = (bf16[112,128]{1,0:T(8,128)(2,1)S(1)}, bf16[112,128]{1,0:T(8,128)(2,1)S(1)}, u32[]{:S(2)}, u32[]{:S(2)}) collective-permute-start(bf16[112,128]{1,0:T(8,128)(2,1)S(1)} %get-tuple-element.29), channel_id=1, source_target_pairs={{0,16},{16,32},{32,48},{48,64},{64,80},{80,96},{96,112},{112,128},... | collective-permute-start | bytes 86024 | tf_op jit(solution)/shard_map/ppermute | solution.py:243
  6.7 13.8 %collective-permute-start.1 = (bf16[112,128]{1,0:T(8,128)(2,1)S(1)}, bf16[112,128]{1,0:T(8,128)(2,1)S(1)}, u32[]{:S(2)}, u32[]{:S(2)}) collective-permute-start(bf16[112,128]{1,0:T(8,128)(2,1)S(1)} %get-tuple-element.30), channel_id=1, source_target_pairs={{16,0},{32,16},{48,32},{64,48},{80,64},{96,80},{112,96},{128,112},... | collective-permute-start | bytes 86024 | tf_op jit(solution)/shard_map/ppermute | solution.py:243
  15.0 2.8 %copy-start.15 = (f32[1536]{0:T(1024)S(1)}, f32[1536]{0:T(1024)}, u32[]{:S(2)}) copy-start(f32[1536]{0:T(1024)} %param.11) | copy-start | bytes 18436
  15.0 2.8 %copy-start.16 = (f32[1536]{0:T(1024)S(1)}, f32[1536]{0:T(1024)}, u32[]{:S(2)}) copy-start(f32[1536]{0:T(1024)} %param.10) | copy-start | bytes 18436
  16.2 3.5 %copy-start.18 = (s32[384]{0:T(512)S(1)}, s32[384]{0:T(512)}, u32[]{:S(2)}) copy-start(s32[384]{0:T(512)} %param.16) | copy-start | bytes 4612
  16.2 4.3 %copy-start.5 = (bf16[96,384]{1,0:T(8,128)(2,1)S(1)}, bf16[96,384]{1,0:T(8,128)(2,1)}, u32[]{:S(2)}) copy-start(bf16[96,384]{1,0:T(8,128)(2,1)} %inputs_ref.1) | copy-start | bytes 221188
  16.2 4.3 %copy-start.8 = (bf16[96,384]{1,0:T(8,128)(2,1)S(1)}, bf16[96,384]{1,0:T(8,128)(2,1)}, u32[]{:S(2)}) copy-start(bf16[96,384]{1,0:T(8,128)(2,1)} %upstream_ref.1) | copy-start | bytes 221188
  16.2 21.0 %copy-start.17 = (f32[31,96]{1,0:T(8,128)S(1)}, f32[31,96]{1,0:T(8,128)}, u32[]{:S(2)}) copy-start(f32[31,96]{1,0:T(8,128)} %param.14) | copy-start | bytes 35716
  20.6 16.6 %collective-permute-start.2 = (bf16[96,896]{1,0:T(8,128)(2,1)S(1)}, bf16[96,896]{1,0:T(8,128)(2,1)S(1)}, u32[]{:S(2)}, u32[]{:S(2)}) collective-permute-start(bf16[96,896]{1,0:T(8,128)(2,1)S(1)} %get-tuple-element.69), channel_id=1, source_target_pairs={{0,2},{2,0},{1,3},{3,1},{4,6},{6,4},{5,7},{7,5},{8,10},{10,8},{9,1... | collective-permute-start | bytes 516104 | tf_op jit(solution)/shard_map/ppermute | solution.py:20
  59.1 5.1 %collective-permute-start.3 = (bf16[4,2,96,896]{3,2,1,0:T(8,128)(2,1)S(1)}, bf16[4,2,96,896]{3,2,1,0:T(8,128)(2,1)}, u32[]{:S(2)}, u32[]{:S(2)}) collective-permute-start(bf16[4,2,96,896]{3,2,1,0:T(8,128)(2,1)S(1)} %all_to_all.15.own_ref), channel_id=1, source_target_pairs={{0,1},{1,0},{2,3},{3,2},{4,5},{5,4},{6,7},{7,6},{8,9},{9,8},{10,11... | collective-permute-start | bytes 4128776 | tf_op jit(solution)/shard_map/ppermute | solution.py:20
  64.2 1.1 copy-start
  65.3 0.9 copy-start.10
  66.2 0.9 copy-start.11
  67.1 1.0 copy-start.12
  68.1 0.8 copy-start.13
  77.8 1.1 copy-start.1
  78.8 1.0 copy-start.2
  80.4 3.9 %copy-start.3 = (bf16[8,4,48,384]{3,2,1,0:T(8,128)(2,1)S(1)}, bf16[8,4,48,384]{3,2,1,0:T(8,128)(2,1)}, u32[]{:S(2)}) copy-start(bf16[8,4,48,384]{3,2,1,0:T(8,128)(2,1)} %copy-done.2) | copy-start | bytes 3538948
  80.4 22.0 %all-to-all-start.1 = ((bf16[8,208,384]{2,1,0:T(8,128)(2,1)}), bf16[8,208,384]{2,1,0:T(8,128)(2,1)S(1)}, u32[]{:S(2)}, u32[]{:S(2)}) async-start(bf16[8,208,384]{2,1,0:T(8,128)(2,1)} %copy-done.1), calls=%async_computation.1 | async-start | bytes 2555904 | tf_op jit(solution)/shard_map/all_to_all | solution.py:299
  85.4 29.6 %collective-permute-start.4 = (bf16[8,48,384]{2,1,0:T(8,128)(2,1)}, bf16[8,48,384]{2,1,0:T(8,128)(2,1)S(1)}, u32[]{:S(2)}, u32[]{:S(2)}) collective-permute-start(bf16[8,48,384]{2,1,0:T(8,128)(2,1)} %get-tuple-element.65), channel_id=1, source_target_pairs={{0,16},{16,32},{32,48},{48,0},{1,17},{17,33},{33,49},{49,1},{2,18}... | collective-permute-start | bytes 884744 | tf_op jit(solution)/shard_map/ppermute | solution.py:305
  88.8 26.1 %collective-permute-start.5 = (bf16[8,48,384]{2,1,0:T(8,128)(2,1)}, bf16[8,48,384]{2,1,0:T(8,128)(2,1)S(1)}, u32[]{:S(2)}, u32[]{:S(2)}) collective-permute-start(bf16[8,48,384]{2,1,0:T(8,128)(2,1)} %get-tuple-element.64), channel_id=1, source_target_pairs={{0,48},{16,0},{32,16},{48,32},{1,49},{17,1},{33,17},{49,33},{2,50}... | collective-permute-start | bytes 884744 | tf_op jit(solution)/shard_map/ppermute | solution.py:305
  94.4 20.6 %collective-permute-start.6 = (bf16[8,48,384]{2,1,0:T(8,128)(2,1)}, bf16[8,48,384]{2,1,0:T(8,128)(2,1)}, u32[]{:S(2)}, u32[]{:S(2)}) collective-permute-start(bf16[8,48,384]{2,1,0:T(8,128)(2,1)} %get-tuple-element.63), channel_id=1, source_target_pairs={{0,32},{16,48},{32,0},{48,16},{1,33},{17,49},{33,1},{49,17},{2,34}... | collective-permute-start | bytes 884744 | tf_op jit(solution)/shard_map/ppermute | solution.py:305
  102.7 26.8 %copy-start.6 = (bf16[96,384]{1,0:T(8,128)(2,1)S(1)}, bf16[96,384]{1,0:T(8,128)(2,1)}, u32[]{:S(2)}) copy-start(bf16[96,384]{1,0:T(8,128)(2,1)} %inputs_ref.1) | copy-start | bytes 221188
  102.8 26.6 %collective-permute-start.8 = (bf16[112,384]{1,0:T(8,128)(2,1)S(1)}, bf16[112,384]{1,0:T(8,128)(2,1)S(1)}, u32[]{:S(2)}, u32[]{:S(2)}) collective-permute-start(bf16[112,384]{1,0:T(8,128)(2,1)S(1)} %maximum_maximum_fusion), channel_id=1, source_target_pairs={{0,2},{2,0},{1,3},{3,1},{4,6},{6,4},{5,7},{7,5},{8,10},{10,8},{9,1... | collective-permute-start | bytes 258056 | tf_op jit(solution)/shard_map/ppermute | solution.py:20
  116.1 39.9 %copy-start.9 = (bf16[96,384]{1,0:T(8,128)(2,1)S(1)}, bf16[96,384]{1,0:T(8,128)(2,1)}, u32[]{:S(2)}) copy-start(bf16[96,384]{1,0:T(8,128)(2,1)} %upstream_ref.1) | copy-start | bytes 221188
  116.1 39.9 %copy-start.19 = (f32[96,1]{0,1:T(1,128)S(1)}, f32[96,1]{0,1:T(1,128)}, u32[]{:S(2)}) copy-start(f32[96,1]{0,1:T(1,128)} %dynamic-slice_bitcast_fusion.4) | copy-start | bytes 1156
  116.1 25.2 %collective-permute-start.7 = (bf16[4,48,384]{2,1,0:T(8,128)(2,1)S(1)}, bf16[4,48,384]{2,1,0:T(8,128)(2,1)S(1)}, u32[]{:S(2)}, u32[]{:S(2)}) collective-permute-start(bf16[4,48,384]{2,1,0:T(8,128)(2,1)S(1)} %fusion.2), channel_id=1, source_target_pairs={{0,64},{64,0},{128,192},{192,128},{256,320},{320,256},{384,448},{4... | collective-permute-start | bytes 442376 | tf_op jit(solution)/shard_map/ppermute | solution.py:327
  130.2 29.6 %all-to-all-start.2 = ((f32[32,2,96]{2,1,0:T(2,128)}), f32[32,2,96]{2,1,0:T(2,128)S(1)}, u32[]{:S(2)}, u32[]{:S(2)}) async-start(f32[32,2,96]{2,1,0:T(2,128)} %broadcast_in_dim.42), calls=%async_computation.2 | async-start | bytes 65536 | tf_op jit(solution)/shard_map/all_to_all | solution.py:338
  141.4 8.2 %collective-permute-start.9 = (bf16[2,48,384]{2,1,0:T(8,128)(2,1)S(1)}, bf16[2,48,384]{2,1,0:T(8,128)(2,1)S(1)}, u32[]{:S(2)}, u32[]{:S(2)}) collective-permute-start(bf16[2,48,384]{2,1,0:T(8,128)(2,1)S(1)} %fusion.3), channel_id=1, source_target_pairs={{0,128},{64,192},{128,0},{192,64},{256,384},{320,448},{384,256},{4... | collective-permute-start | bytes 221192 | tf_op jit(solution)/shard_map/ppermute | solution.py:327
  149.7 10.1 %collective-permute-start.10 = (bf16[1,48,384]{2,1,0:T(8,128)(2,1)S(1)}, bf16[1,48,384]{2,1,0:T(8,128)(2,1)S(1)}, u32[]{:S(2)}, u32[]{:S(2)}) collective-permute-start(bf16[1,48,384]{2,1,0:T(8,128)(2,1)S(1)} %dynamic-slice_convert_fusion.2), channel_id=1, source_target_pairs={{0,256},{64,320},{128,384},{192,448},{256,0},{320,64},{384,128},{4... | collective-permute-start | bytes 110600 | tf_op jit(solution)/shard_map/ppermute | solution.py:327
  (1 other events, 0.6 us)

commit v7 on v6

--- a/solution.py
+++ b/solution.py
@@ -74,20 +74,43 @@
 
 
 def middle(
-    where_ref, own_ref, other_ref, gain_ref, bias_ref, weight_ref, project_ref, flipped_ref,
-    by_gain_ref, by_bias_ref, taps_ref, mask_ref,
-    mixed_out, grads_ref, stats_ref,
-    mixed_ref, normed_ref, full_ref, both_ref, act_ref, kernel_ref,
-    proj_ref, grad_ref, moved_ref, back_ref, sem,
+    where_ref, own_hbm, other_hbm, small_hbm, weight_hbm, project_hbm, flipped_hbm, taps_hbm, mask_hbm,
+    mixed_out, part0_out, part1_out, part2_out, part3_out, stats_out,
+    own_ref, other_ref, small_ref, weight_ref, project_ref, flipped_ref, taps_ref, mask_ref,
+    mixed_ref, grads_ref, stats_ref, normed_ref, full_ref, both_ref, act_ref, kernel_ref,
+    proj_ref, grad_ref, moved_ref, back_ref, sems,
 ):
     model = weight_ref.shape[1]
     width = own_ref.shape[2]
     lanes = normed_ref.shape[2]
     rows = mixed_ref.shape[2]
     taps = taps_ref.shape[0]
+    count = 0
+
+    def copy(source, target):
+        nonlocal count
+        started = pltpu.make_async_copy(source, target, sems.at[count])
+        started.start()
+        count += 1
+        return started
+
+    blocks = [
+        copy(source.at[x], target.at[x])
+        for x in range(4)
+        for source, target in ((own_hbm, own_ref), (other_hbm, other_ref))
+    ]
+    small_copy = copy(small_hbm, small_ref)
+    mask_copy = copy(mask_hbm, mask_ref)
+    project_copy = copy(project_hbm, project_ref)
+    weight_copy = copy(weight_hbm, weight_ref)
+    taps_copy = copy(taps_hbm, taps_ref)
+    flipped_copy = copy(flipped_hbm, flipped_ref)
     total = jnp.zeros((8, lanes), f32)
     square = jnp.zeros((8, lanes), f32)
-    for place, block in blocks_of(where_ref, own_ref, other_ref):
+    for i, (place, block) in enumerate(blocks_of(where_ref, own_ref, other_ref)):
+        if i % 4 == 0:
+            blocks[i // 2].wait()
+            blocks[i // 2 + 1].wait()
         x = block[:, :lanes].astype(f32).reshape(width // 8, 8, lanes)
         total = total + jnp.sum(x, axis=0)
         square = square + jnp.sum(x * x, axis=0)
@@ -101,17 +124,23 @@
     stats_ref[...] = jnp.concatenate(
         [row_mean, inv_std, jnp.zeros((6, lanes), f32)], axis=0
     )
+    finished = [copy(stats_ref, stats_out)]
+    small_copy.wait()
     for i, (place, block) in enumerate(blocks_of(where_ref, own_ref, other_ref)):
         centred = (block[:, :lanes].astype(f32) - row_mean) * inv_std
         normed_ref[place] = (
-            centred * gain_ref[:, i : i + 1] + bias_ref[:, i : i + 1]
+            centred * small_ref[:width, i : i + 1] + small_ref[:width, 16 + i : 17 + i]
         ).astype(bf16)
+    project_copy.wait()
     grad_ref[...] = jnp.dot(
         project_ref[...], full_ref[...].reshape(model, lanes), preferred_element_type=f32
     )
+    weight_copy.wait()
     proj_ref[...] = jnp.dot(
         weight_ref[...], normed_ref[...].reshape(model, lanes), preferred_element_type=f32
     )
+    mask_copy.wait()
+    taps_copy.wait()
     group = 16
     lane = lax.broadcasted_iota(jnp.int32, (group, 128), 1)
     inside = lax.broadcasted_iota(jnp.int32, (group, lanes), 1) < rows
@@ -170,11 +199,12 @@
 
     lax.fori_loop(0, width // group, channels, 0)
     both = both_ref[...]
+    flipped_copy.wait()
     partial = jnp.dot(flipped_ref[...], both, preferred_element_type=f32).astype(bf16)
     partial = partial.reshape(4, 2, 2, width, rows)
     both = both.astype(f32)
-    first = jnp.sum(both * by_gain_ref[...], axis=0, keepdims=True)
-    second = jnp.sum(both * (proj_ref[:, :rows] - by_bias_ref[...]), axis=0, keepdims=True)
+    first = jnp.sum(both * small_ref[:, 32:33], axis=0, keepdims=True)
+    second = jnp.sum(both * (proj_ref[:, :rows] - small_ref[:, 33:34]), axis=0, keepdims=True)
     first_high = first.astype(bf16).astype(f32)
     second_high = second.astype(bf16).astype(f32)
     row = lax.broadcasted_iota(jnp.int32, (16, rows), 0)
@@ -189,8 +219,7 @@
                 start = pl.multiple_of(jnp.where(side == zh, width, 0), width)
                 mixed_ref[x * 2 + core, pl.ds(start, width)] = partial[x, side, core]
             mixed_ref[x * 2 + core, 2 * width :] = extra
-    copy = pltpu.make_async_copy(mixed_ref, mixed_out, sem)
-    copy.start()
+    finished.append(copy(mixed_ref, mixed_out))
 
     zero = jnp.zeros((width, rows), bf16)
     grads = lax.dot_general(
@@ -209,7 +238,10 @@
     for zl in range(8):
         for y in range(4):
             grads_ref[zl, y, :, :width] = kernel
-    copy.wait()
+    for step, out in zip((0, 1, 3, 2), (part0_out, part1_out, part2_out, part3_out)):
+        out[...] = grads_ref[:, lax.rem(where_ref[2] + step, 4)]
+    for started in finished:
+        started.wait()
 
 
 def on_device(
@@ -233,7 +265,7 @@
     y = lax.axis_index("y")
     zl = lax.axis_index("zl")
     offset = lax.axis_index(CHAN) * width
-    where = jnp.stack([zh, core]).astype(jnp.int32)
+    where = jnp.stack([zh, core, y]).astype(jnp.int32)
 
     to_right, to_left = call(
         edges,
@@ -255,30 +287,35 @@
         parameter = jnp.where(core == 0, parameter, parameter[:, :, ::-1])
         return parameter.reshape(16, width).T
 
-    early = (
-        weights, weights.T, by_gain, by_bias,
-        jnp.broadcast_to(conv_kernel[:, :, None], (taps, width, 128)),
-        columns_of(norm_gain), columns_of(norm_bias), gain_local, where,
-    )
+    small = jnp.concatenate([columns_of(norm_gain), columns_of(norm_bias)], axis=1)
+    small = jnp.concatenate([jnp.pad(small, ((0, width), (0, 0))), by_gain, by_bias], axis=1)
+    small = jnp.pad(small, ((0, 0), (0, 128 - small.shape[1])))
+    wide_taps = jnp.broadcast_to(conv_kernel[:, :, None], (taps, width, 128))
+    early = (weights, weights.T, small, wide_taps, gain_local, where)
 
     held = jnp.concatenate([inputs, edge[:width], upstream], axis=1)
     keep = jnp.concatenate([frame_mask.astype(f32)[None, :], edge[width : width + 1].astype(f32)], axis=1)
     came = swap(held, "zh")
     came, keep, early = lax.optimization_barrier((came, keep, early))
-    weights, flipped, by_gain, by_bias, columns, gain, bias, gain_local, where = early
+    weights, flipped, small, wide_taps, gain_local, where = early
     own = over_x(jnp.stack([held, came]))
     other = swap(own, "core")
-    mixed, grads, stats = pl.pallas_call(
+    piece_shape = (8, piece, 4 * width)
+    operands = (own, other, small, weights, project_weight, flipped, wide_taps, keep)
+    mixed, *pieces, stats = pl.pallas_call(
         middle,
         out_shape=(
-            shape((8, 2 * width + 16, rows), bf16),
-            shape((8, 4, piece, 4 * width), bf16),
-            shape((8, lanes), f32),
+            pltpu.HBM((8, 2 * width + 16, rows), bf16),
+            *(pltpu.VMEM(piece_shape, bf16) for _ in range(4)),
+            pltpu.HBM((8, lanes), f32),
         ),
-        in_specs=[SMEM] + [VMEM] * 11,
-        out_specs=(pl.BlockSpec(memory_space=pltpu.HBM), VMEM, VMEM),
-        scratch_shapes=[
+        in_specs=[SMEM] + [pl.BlockSpec(memory_space=pltpu.HBM)] * len(operands),
+        out_specs=tuple(pl.BlockSpec(memory_space=pltpu.HBM if i in (0, 5) else pltpu.VMEM) for i in range(6)),
+        scratch_shapes=[pltpu.VMEM(operand.shape, operand.dtype) for operand in operands]
+        + [
             pltpu.VMEM((8, 2 * width + 16, rows), bf16),
+            pltpu.VMEM((8, 4, piece, 4 * width), bf16),
+            pltpu.VMEM((8, lanes), f32),
             pltpu.VMEM((16, width, lanes), bf16),
             pltpu.VMEM((16, width, lanes), bf16),
             pltpu.VMEM((2 * width, rows), bf16),
@@ -288,22 +325,16 @@
             pltpu.VMEM((width, lanes), f32),
             pltpu.VMEM((8, 16, lanes), f32),
             pltpu.VMEM((8, 16, lanes), f32),
-            pltpu.SemaphoreType.DMA,
+            pltpu.SemaphoreType.DMA((20,)),
         ],
-        compiler_params=pltpu.CompilerParams(vmem_limit_bytes=30 << 20),
-    )(
-        where, own, other, gain, bias, weights, project_weight, flipped,
-        by_gain, by_bias, columns, keep,
-    )
+        compiler_params=pltpu.CompilerParams(vmem_limit_bytes=40 << 20),
+    )(where, *(pltpu.with_memory_space_constraint(operand, pltpu.HBM) for operand in operands))
 
     mixed = lax.all_to_all(mixed, ("x", "core"), 0, 0, tiled=True)
 
-    def rows_for(step):
-        return lax.dynamic_slice_in_dim(grads, (y + step) % 4, 1, 1)[:, 0]
-
     parts = [
-        lax.ppermute(rows_for(step), "y", [(i, (i + step) % 4) for i in range(4)])
-        for step in (1, 3, 2)
+        lax.ppermute(sent, "y", [(i, (i + step) % 4) for i in range(4)])
+        for step, sent in zip((1, 3, 2), pieces[1:])
     ]
     mixed = jnp.sum(mixed.astype(f32), axis=0)
     far_sums = mixed[2 * width : 2 * width + 2] + mixed[2 * width + 2 : 2 * width + 4]
@@ -313,20 +344,19 @@
     )
     came = swap(far, "zh").astype(f32)
 
-    total, far_copy = lax.optimization_barrier((rows_for(0), far))
+    total, far_copy = lax.optimization_barrier((pieces[0], far))
     total = total.astype(f32)
     for part in parts:
         total = total + part.astype(f32)
 
-    def halve(total, size):
-        side = (zl // size) % 2
-        half = total.shape[0] // 2
-        total = total.reshape(half, 2, piece, 4 * width)
-        kept = lax.dynamic_slice_in_dim(total, side, 1, 1)[:, 0]
-        sent = lax.dynamic_slice_in_dim(total, 1 - side, 1, 1)[:, 0].astype(bf16)
-        return kept + lax.ppermute(sent, "zl", [(i, i ^ size) for i in range(8)]).astype(f32)
-
-    total = halve(total, 1)
+    def block(index):
+        return lax.dynamic_slice_in_dim(total, index, 1, 0)[0]
+
+    side = zl % 2
+    total = total.reshape(4, 2, piece, 4 * width)
+    sent = lax.dynamic_slice_in_dim(total, 1 - side, 1, 1)[:, 0].astype(bf16)
+    total = lax.dynamic_slice_in_dim(total, side, 1, 1)[:, 0]
+    total = total + lax.ppermute(sent, "zl", [(i, i ^ 1) for i in range(8)]).astype(f32)
 
     normed_grad = mixed[width : 2 * width] + came[:width]
     kept = far_copy[width : width + 4].astype(f32)
@@ -334,7 +364,6 @@
     inv_std = stats[1:2, :rows]
     centred = (inputs.astype(f32) - stats[0:1, :rows]) * inv_std
     tail = jnp.stack([jnp.sum(normed_grad * centred, axis=1), jnp.sum(normed_grad, axis=1)])
-    total, normed_grad = lax.optimization_barrier((total, normed_grad))
     tail = lax.all_to_all(
         jnp.broadcast_to(tail[None], (32, 2, width)), FRAME, 0, 0, tiled=True
     )
@@ -343,7 +372,10 @@
         + inv_std * (normed_grad * gain_local - sums[0:1] - centred * sums[1:2])
     ).astype(bf16)
 
-    grads = halve(halve(total, 2), 4)[0]
+    grads = block(zl // 2)
+    for step in (3, 2, 1):
+        sent = block((zl // 2) ^ step).astype(bf16)
+        grads = grads + lax.ppermute(sent, "zl", [(i, i ^ (2 * step)) for i in range(8)]).astype(f32)
     tail, grads = lax.optimization_barrier((tail, grads))
     tail = jnp.sum(tail, axis=0)
     kernel_grad = grads[:taps, :width]

time: 163 us -> 165 us (1.012)
  the two profiles are of different devices: /device:TPU:8 before, /device:TPU:1 now
where the time goes in v7:
time: 165 us; the launch traced here: 164 us
  starting transfers between devices  87.5 us (53%)
  waiting for transfers between devices  30.9 us (19%)
  blocking collectives  15.4 us (9%)
  local copies, waits for them, and re-layouts  13.5 us (8%)
  Pallas kernels  10.7 us (6%)
  other arithmetic  4.55 us (3%)
    ppermute x3, starting transfers between devices, swap(): return lax.ppermute(value, axis, SWAP)  43.5 us
    all_to_all x1, blocking collectives, over_x(): lax.all_to_all(jnp.broadcast_to(pair[None], (4,) + pair.shape), 'x', 0, 0...  15.4 us
    ppermute x3, starting transfers between devices, on_device(): lax.ppermute(sent, 'zl', [(i, i ^ 2 * step) for i in range(8)]).astype(f32)  13.2 us
    all_to_all x1, waiting for transfers between devices, on_device(): lax.all_to_all(jnp.broadcast_to(tail[None], (32, 2, width)), FRAME, 0, 0,...  11.5 us
    pallas_call x1, Pallas kernels, on_device(): pl.pallas_call(middle, out_shape=(pltpu.HBM((8, 2 * width + 16, rows), bf...  10.6 us
    ppermute x1, starting transfers between devices, on_device(): lax.ppermute(sent, 'zl', [(i, i ^ 1) for i in range(8)]).astype(f32)  9.29 us
    ppermute x3, starting transfers between devices, on_device(): lax.ppermute(sent, 'y', [(i, (i + step) % 4) for i in range(4)])  8.4 us
    all_to_all x1, waiting for transfers between devices, on_device(): mixed = lax.all_to_all(mixed, ('x', 'core'), 0, 0, tiled=True)  8.27 us
  transfers between devices with their start and end apart: 14, of which 5 were waited for; matrix products, arithmetic and copies ran while one was open for 7% of the time, Pallas kernels for 0%

profile of v7, /device:TPU:1, one launch (start us, length us, event | category | flops | bytes accessed | tf_op | source)
XLA Modules:
  0.0 163.7 jit_solution(4752622952979310547)
XLA Ops:
  1.3 0.9 copy-done
  2.2 0.9 copy-done.2
  3.2 4.0 %collective-permute-start = (bf16[112,128]{1,0:T(8,128)(2,1)S(1)}, bf16[112,128]{1,0:T(8,128)(2,1)S(1)}, u32[]{:S(2)}, u32[]{:S(2)}) collective-permute-start(bf16[112,128]{1,0:T(8,128)(2,1)S(1)} %get-tuple-element.27), channel_id=1, source_target_pairs={{0,16},{16,32},{32,48},{48,64},{64,80},{80,96},{96,112},{112,128},... | collective-permute-start | bytes 86024 | tf_op jit(solution)/shard_map/ppermute | solution.py:275
  7.2 1.3 collective-permute-start.1
  8.5 0.8 reshape.42
  10.1 1.2 copy.28
  11.3 1.2 copy.29
  12.5 1.1 fusion
  13.7 1.3 fusion.12
  16.1 15.4 %collective-permute-start.2 = (bf16[96,896]{1,0:T(8,128)(2,1)S(1)}, bf16[96,896]{1,0:T(8,128)(2,1)S(1)}, u32[]{:S(2)}, u32[]{:S(2)}) collective-permute-start(bf16[96,896]{1,0:T(8,128)(2,1)S(1)} %get-tuple-element.64), channel_id=1, source_target_pairs={{0,2},{2,0},{1,3},{3,1},{4,6},{6,4},{5,7},{7,5},{8,10},{10,8},{9,1... | collective-permute-start | bytes 516104 | tf_op jit(solution)/shard_map/ppermute | solution.py:20
  32.1 3.1 %collective-permute-done.2 = bf16[96,896]{1,0:T(8,128)(2,1)S(1)} collective-permute-done((bf16[96,896]{1,0:T(8,128)(2,1)S(1)}, bf16[96,896]{1,0:T(8,128)(2,1)S(1)}, u32[]{:S(2)}, u32[]{:S(2)}) %collective-permute-start.2) | collective-permute-done | bytes 172064 | tf_op jit(solution)/shard_map/ppermute | solution.py:20
  35.2 1.6 broadcast_in_dim.38.taps_hbm
  36.9 15.4 %all_to_all.15.own_hbm = bf16[4,2,96,896]{3,2,1,0:T(8,128)(2,1)S(1)} all-to-all(bf16[4,2,96,896]{3,2,1,0:T(8,128)(2,1)S(1)} %broadcast_in_dim.40), channel_id=1, replica_groups=mesh['zl'=8,'y'=4,'x'=4,'zh'=2,'core'=2] {'x'}, dimensions={0} | all-to-all | bytes 2752512 | tf_op jit(solution)/shard_map/all_to_all | solution.py:24
  52.3 15.2 %collective-permute-start.3 = (bf16[4,2,96,896]{3,2,1,0:T(8,128)(2,1)S(1)}, bf16[4,2,96,896]{3,2,1,0:T(8,128)(2,1)}, u32[]{:S(2)}, u32[]{:S(2)}) collective-permute-start(bf16[4,2,96,896]{3,2,1,0:T(8,128)(2,1)S(1)} %all_to_all.15.own_hbm), channel_id=1, source_target_pairs={{0,1},{1,0},{2,3},{3,2},{4,5},{5,4},{6,7},{7,6},{8,9},{9,8},{10,11... | collective-permute-start | bytes 4128776 | tf_op jit(solution)/shard_map/ppermute | solution.py:20
  67.6 1.1 copy.31.weight_hbm
  68.7 1.8 %collective-permute-done.3.other_hbm = bf16[4,2,96,896]{3,2,1,0:T(8,128)(2,1)} collective-permute-done((bf16[4,2,96,896]{3,2,1,0:T(8,128)(2,1)S(1)}, bf16[4,2,96,896]{3,2,1,0:T(8,128)(2,1)}, u32[]{:S(2)}, u32[]{:S(2)}) %collective-permute-start.3) | collective-permute-done | bytes 1376288 | tf_op jit(solution)/shard_map/ppermute | solution.py:20
  70.4 10.6 %shard_map.145 = (bf16[8,208,384]{2,1,0:T(8,128)(2,1)}, bf16[8,48,384]{2,1,0:T(8,128)(2,1)S(1)}, bf16[8,48,384]{2,1,0:T(8,128)(2,1)S(1)}, bf16[8,48,384]{2,1,0:T...) custom-call(s32[3]{0:T(128)S(1)} %pad_add_fusion.where_ref, bf16[4,2,96,896]{3,2,1,0:T(8,128)(2,1)} %copy-done.4, ...), custom_call_target="tpu_custom_call" | custom-call | tf_op jit(solution)/shard_map/pallas_call | solution.py:305
  81.0 3.9 %all-to-all-start.1 = ((bf16[8,208,384]{2,1,0:T(8,128)(2,1)}), bf16[8,208,384]{2,1,0:T(8,128)(2,1)S(1)}, u32[]{:S(2)}, u32[]{:S(2)}) async-start(bf16[8,208,384]{2,1,0:T(8,128)(2,1)} %get-tuple-element.37), calls=%async_computation.1 | async-start | bytes 2555904 | tf_op jit(solution)/shard_map/all_to_all | solution.py:333
  85.0 1.9 %collective-permute-start.5 = (bf16[8,48,384]{2,1,0:T(8,128)(2,1)S(1)}, bf16[8,48,384]{2,1,0:T(8,128)(2,1)S(1)}, u32[]{:S(2)}, u32[]{:S(2)}) collective-permute-start(bf16[8,48,384]{2,1,0:T(8,128)(2,1)S(1)} %get-tuple-element.42), channel_id=1, source_target_pairs={{0,16},{16,32},{32,48},{48,0},{1,17},{17,33},{33,49},{49,1},{2,18}... | collective-permute-start | bytes 884744 | tf_op jit(solution)/shard_map/ppermute | solution.py:336
  86.9 4.6 %collective-permute-start.6 = (bf16[8,48,384]{2,1,0:T(8,128)(2,1)S(1)}, bf16[8,48,384]{2,1,0:T(8,128)(2,1)S(1)}, u32[]{:S(2)}, u32[]{:S(2)}) collective-permute-start(bf16[8,48,384]{2,1,0:T(8,128)(2,1)S(1)} %get-tuple-element.43), channel_id=1, source_target_pairs={{0,48},{16,0},{32,16},{48,32},{1,49},{17,1},{33,17},{49,33},{2,50}... | collective-permute-start | bytes 884744 | tf_op jit(solution)/shard_map/ppermute | solution.py:336
  91.5 1.9 %collective-permute-start.7 = (bf16[8,48,384]{2,1,0:T(8,128)(2,1)S(1)}, bf16[8,48,384]{2,1,0:T(8,128)(2,1)S(1)}, u32[]{:S(2)}, u32[]{:S(2)}) collective-permute-start(bf16[8,48,384]{2,1,0:T(8,128)(2,1)S(1)} %get-tuple-element.44), channel_id=1, source_target_pairs={{0,32},{16,48},{32,0},{48,16},{1,33},{17,49},{33,1},{49,17},{2,34}... | collective-permute-start | bytes 884744 | tf_op jit(solution)/shard_map/ppermute | solution.py:336
  93.4 0.8 slice_reduce_fusion.3
  94.2 8.3 %all-to-all-done.1 = bf16[8,208,384]{2,1,0:T(8,128)(2,1)S(1)} async-done(((bf16[8,208,384]{2,1,0:T(8,128)(2,1)}), bf16[8,208,384]{2,1,0:T(8,128)(2,1)S(1)}, u32[]{:S(2)}, u32[]{:S(2)}) %all-to-all-start.1) | async-done | bytes 1277984 | tf_op jit(solution)/shard_map/all_to_all | solution.py:333
  102.8 12.9 %collective-permute-start.4 = (bf16[112,384]{1,0:T(8,128)(2,1)S(1)}, bf16[112,384]{1,0:T(8,128)(2,1)S(1)}, u32[]{:S(2)}, u32[]{:S(2)}) collective-permute-start(bf16[112,384]{1,0:T(8,128)(2,1)S(1)} %maximum_maximum_fusion), channel_id=1, source_target_pairs={{0,2},{2,0},{1,3},{3,1},{4,6},{6,4},{5,7},{7,5},{8,10},{10,8},{9,1... | collective-permute-start | bytes 258056 | tf_op jit(solution)/shard_map/ppermute | solution.py:20
  115.9 9.3 %collective-permute-start.8 = (bf16[4,48,384]{2,1,0:T(8,128)(2,1)S(1)}, bf16[4,48,384]{2,1,0:T(8,128)(2,1)S(1)}, u32[]{:S(2)}, u32[]{:S(2)}) collective-permute-start(bf16[4,48,384]{2,1,0:T(8,128)(2,1)S(1)} %fusion.2), channel_id=1, source_target_pairs={{0,64},{64,0},{128,192},{192,128},{256,320},{320,256},{384,448},{4... | collective-permute-start | bytes 442376 | tf_op jit(solution)/shard_map/ppermute | solution.py:359
  125.3 0.8 multiply_reduce_fusion
  126.1 6.3 %collective-permute-done.8 = bf16[4,48,384]{2,1,0:T(8,128)(2,1)S(1)} collective-permute-done((bf16[4,48,384]{2,1,0:T(8,128)(2,1)S(1)}, bf16[4,48,384]{2,1,0:T(8,128)(2,1)S(1)}, u32[]{:S(2)}, u32[]{:S(2)}) %collective-permute-start.8) | collective-permute-done | bytes 147488 | tf_op jit(solution)/shard_map/ppermute | solution.py:359
  132.5 2.3 %collective-permute-start.10 = (bf16[48,384]{1,0:T(8,128)(2,1)S(1)}, bf16[48,384]{1,0:T(8,128)(2,1)S(1)}, u32[]{:S(2)}, u32[]{:S(2)}) collective-permute-start(bf16[48,384]{1,0:T(8,128)(2,1)S(1)} %get-tuple-element.62), channel_id=1, source_target_pairs={{0,256},{64,320},{128,384},{192,448},{256,0},{320,64},{384,128},{4... | collective-permute-start | bytes 110600 | tf_op jit(solution)/shard_map/ppermute | solution.py:378
  134.8 2.1 %collective-permute-start.11 = (bf16[48,384]{1,0:T(8,128)(2,1)S(1)}, bf16[48,384]{1,0:T(8,128)(2,1)S(1)}, u32[]{:S(2)}, u32[]{:S(2)}) collective-permute-start(bf16[48,384]{1,0:T(8,128)(2,1)S(1)} %get-tuple-element.61), channel_id=1, source_target_pairs={{0,128},{64,192},{128,0},{192,64},{256,384},{320,448},{384,256},{4... | collective-permute-start | bytes 110600 | tf_op jit(solution)/shard_map/ppermute | solution.py:378
  136.9 8.7 %collective-permute-start.9 = (bf16[48,384]{1,0:T(8,128)(2,1)S(1)}, bf16[48,384]{1,0:T(8,128)(2,1)S(1)}, u32[]{:S(2)}, u32[]{:S(2)}) collective-permute-start(bf16[48,384]{1,0:T(8,128)(2,1)S(1)} %get-tuple-element.60), channel_id=1, source_target_pairs={{0,384},{64,448},{128,256},{192,320},{256,128},{320,192},{384,0},{... | collective-permute-start | bytes 110600 | tf_op jit(solution)/shard_map/ppermute | solution.py:378
  146.3 3.9 %all-to-all-start.2 = ((f32[32,2,96]{2,1,0:T(2,128)}), f32[32,2,96]{2,1,0:T(2,128)S(1)}, u32[]{:S(2)}, u32[]{:S(2)}) async-start(f32[32,2,96]{2,1,0:T(2,128)} %broadcast_in_dim.42), calls=%async_computation.2 | async-start | bytes 65536 | tf_op jit(solution)/shard_map/all_to_all | solution.py:367
  150.3 11.5 %all-to-all-done.2 = f32[32,2,96]{2,1,0:T(2,128)S(1)} async-done(((f32[32,2,96]{2,1,0:T(2,128)}), f32[32,2,96]{2,1,0:T(2,128)S(1)}, u32[]{:S(2)}, u32[]{:S(2)}) %all-to-all-start.2) | async-done | bytes 24608 | tf_op jit(solution)/shard_map/all_to_all | solution.py:367
  (69 shorter events, 6.5 us)
Async XLA Ops:
  1.3 0.9 copy-start
  2.2 0.9 copy-start.2
  3.1 9.4 %copy-start.5 = (f32[1536]{0:T(1024)S(1)}, f32[1536]{0:T(1024)}, u32[]{:S(2)}) copy-start(f32[1536]{0:T(1024)} %param.11) | copy-start | bytes 18436
  3.1 9.4 %copy-start.6 = (f32[1536]{0:T(1024)S(1)}, f32[1536]{0:T(1024)}, u32[]{:S(2)}) copy-start(f32[1536]{0:T(1024)} %param.10) | copy-start | bytes 18436
  3.2 12.8 %collective-permute-start = (bf16[112,128]{1,0:T(8,128)(2,1)S(1)}, bf16[112,128]{1,0:T(8,128)(2,1)S(1)}, u32[]{:S(2)}, u32[]{:S(2)}) collective-permute-start(bf16[112,128]{1,0:T(8,128)(2,1)S(1)} %get-tuple-element.27), channel_id=1, source_target_pairs={{0,16},{16,32},{32,48},{48,64},{64,80},{80,96},{96,112},{112,128},... | collective-permute-start | bytes 86024 | tf_op jit(solution)/shard_map/ppermute | solution.py:275
  7.2 8.8 %collective-permute-start.1 = (bf16[112,128]{1,0:T(8,128)(2,1)S(1)}, bf16[112,128]{1,0:T(8,128)(2,1)S(1)}, u32[]{:S(2)}, u32[]{:S(2)}) collective-permute-start(bf16[112,128]{1,0:T(8,128)(2,1)S(1)} %get-tuple-element.28), channel_id=1, source_target_pairs={{16,0},{32,16},{48,32},{64,48},{80,64},{96,80},{112,96},{128,112},... | collective-permute-start | bytes 86024 | tf_op jit(solution)/shard_map/ppermute | solution.py:275
  13.6 1.6 copy-start.8
  13.6 2.4 %copy-start.1 = (bf16[96,384]{1,0:T(8,128)(2,1)S(1)}, bf16[96,384]{1,0:T(8,128)(2,1)}, u32[]{:S(2)}) copy-start(bf16[96,384]{1,0:T(8,128)(2,1)} %inputs_ref.1) | copy-start | bytes 221188
  13.6 2.4 %copy-start.3 = (bf16[96,384]{1,0:T(8,128)(2,1)S(1)}, bf16[96,384]{1,0:T(8,128)(2,1)}, u32[]{:S(2)}) copy-start(bf16[96,384]{1,0:T(8,128)(2,1)} %upstream_ref.1) | copy-start | bytes 221188
  13.6 21.5 %copy-start.7 = (f32[31,96]{1,0:T(8,128)S(1)}, f32[31,96]{1,0:T(8,128)}, u32[]{:S(2)}) copy-start(f32[31,96]{1,0:T(8,128)} %param.14) | copy-start | bytes 35716
  16.1 19.1 %collective-permute-start.2 = (bf16[96,896]{1,0:T(8,128)(2,1)S(1)}, bf16[96,896]{1,0:T(8,128)(2,1)S(1)}, u32[]{:S(2)}, u32[]{:S(2)}) collective-permute-start(bf16[96,896]{1,0:T(8,128)(2,1)S(1)} %get-tuple-element.64), channel_id=1, source_target_pairs={{0,2},{2,0},{1,3},{3,1},{4,6},{6,4},{5,7},{7,5},{8,10},{10,8},{9,1... | collective-permute-start | bytes 516104 | tf_op jit(solution)/shard_map/ppermute | solution.py:20
  52.3 18.1 %copy-start.4 = (bf16[4,2,96,896]{3,2,1,0:T(8,128)(2,1)}, bf16[4,2,96,896]{3,2,1,0:T(8,128)(2,1)S(1)}, u32[]{:S(2)}) copy-start(bf16[4,2,96,896]{3,2,1,0:T(8,128)(2,1)S(1)} %all_to_all.15.own_hbm) | copy-start | bytes 4128772
  52.3 18.1 %collective-permute-start.3 = (bf16[4,2,96,896]{3,2,1,0:T(8,128)(2,1)S(1)}, bf16[4,2,96,896]{3,2,1,0:T(8,128)(2,1)}, u32[]{:S(2)}, u32[]{:S(2)}) collective-permute-start(bf16[4,2,96,896]{3,2,1,0:T(8,128)(2,1)S(1)} %all_to_all.15.own_hbm), channel_id=1, source_target_pairs={{0,1},{1,0},{2,3},{3,2},{4,5},{5,4},{6,7},{7,6},{8,9},{9,8},{10,11... | collective-permute-start | bytes 4128776 | tf_op jit(solution)/shard_map/ppermute | solution.py:20
  81.0 21.4 %all-to-all-start.1 = ((bf16[8,208,384]{2,1,0:T(8,128)(2,1)}), bf16[8,208,384]{2,1,0:T(8,128)(2,1)S(1)}, u32[]{:S(2)}, u32[]{:S(2)}) async-start(bf16[8,208,384]{2,1,0:T(8,128)(2,1)} %get-tuple-element.37), calls=%async_computation.1 | async-start | bytes 2555904 | tf_op jit(solution)/shard_map/all_to_all | solution.py:333
  85.0 30.7 %collective-permute-start.5 = (bf16[8,48,384]{2,1,0:T(8,128)(2,1)S(1)}, bf16[8,48,384]{2,1,0:T(8,128)(2,1)S(1)}, u32[]{:S(2)}, u32[]{:S(2)}) collective-permute-start(bf16[8,48,384]{2,1,0:T(8,128)(2,1)S(1)} %get-tuple-element.42), channel_id=1, source_target_pairs={{0,16},{16,32},{32,48},{48,0},{1,17},{17,33},{33,49},{49,1},{2,18}... | collective-permute-start | bytes 884744 | tf_op jit(solution)/shard_map/ppermute | solution.py:336
  86.9 28.8 %collective-permute-start.6 = (bf16[8,48,384]{2,1,0:T(8,128)(2,1)S(1)}, bf16[8,48,384]{2,1,0:T(8,128)(2,1)S(1)}, u32[]{:S(2)}, u32[]{:S(2)}) collective-permute-start(bf16[8,48,384]{2,1,0:T(8,128)(2,1)S(1)} %get-tuple-element.43), channel_id=1, source_target_pairs={{0,48},{16,0},{32,16},{48,32},{1,49},{17,1},{33,17},{49,33},{2,50}... | collective-permute-start | bytes 884744 | tf_op jit(solution)/shard_map/ppermute | solution.py:336
  91.5 24.2 %collective-permute-start.7 = (bf16[8,48,384]{2,1,0:T(8,128)(2,1)S(1)}, bf16[8,48,384]{2,1,0:T(8,128)(2,1)S(1)}, u32[]{:S(2)}, u32[]{:S(2)}) collective-permute-start(bf16[8,48,384]{2,1,0:T(8,128)(2,1)S(1)} %get-tuple-element.44), channel_id=1, source_target_pairs={{0,32},{16,48},{32,0},{48,16},{1,33},{17,49},{33,1},{49,17},{2,34}... | collective-permute-start | bytes 884744 | tf_op jit(solution)/shard_map/ppermute | solution.py:336
  102.8 22.4 %collective-permute-start.4 = (bf16[112,384]{1,0:T(8,128)(2,1)S(1)}, bf16[112,384]{1,0:T(8,128)(2,1)S(1)}, u32[]{:S(2)}, u32[]{:S(2)}) collective-permute-start(bf16[112,384]{1,0:T(8,128)(2,1)S(1)} %maximum_maximum_fusion), channel_id=1, source_target_pairs={{0,2},{2,0},{1,3},{3,1},{4,6},{6,4},{5,7},{7,5},{8,10},{10,8},{9,1... | collective-permute-start | bytes 258056 | tf_op jit(solution)/shard_map/ppermute | solution.py:20
  115.9 16.5 %collective-permute-start.8 = (bf16[4,48,384]{2,1,0:T(8,128)(2,1)S(1)}, bf16[4,48,384]{2,1,0:T(8,128)(2,1)S(1)}, u32[]{:S(2)}, u32[]{:S(2)}) collective-permute-start(bf16[4,48,384]{2,1,0:T(8,128)(2,1)S(1)} %fusion.2), channel_id=1, source_target_pairs={{0,64},{64,0},{128,192},{192,128},{256,320},{320,256},{384,448},{4... | collective-permute-start | bytes 442376 | tf_op jit(solution)/shard_map/ppermute | solution.py:359
  132.5 17.8 %collective-permute-start.10 = (bf16[48,384]{1,0:T(8,128)(2,1)S(1)}, bf16[48,384]{1,0:T(8,128)(2,1)S(1)}, u32[]{:S(2)}, u32[]{:S(2)}) collective-permute-start(bf16[48,384]{1,0:T(8,128)(2,1)S(1)} %get-tuple-element.62), channel_id=1, source_target_pairs={{0,256},{64,320},{128,384},{192,448},{256,0},{320,64},{384,128},{4... | collective-permute-start | bytes 110600 | tf_op jit(solution)/shard_map/ppermute | solution.py:378
  134.8 15.5 %collective-permute-start.11 = (bf16[48,384]{1,0:T(8,128)(2,1)S(1)}, bf16[48,384]{1,0:T(8,128)(2,1)S(1)}, u32[]{:S(2)}, u32[]{:S(2)}) collective-permute-start(bf16[48,384]{1,0:T(8,128)(2,1)S(1)} %get-tuple-element.61), channel_id=1, source_target_pairs={{0,128},{64,192},{128,0},{192,64},{256,384},{320,448},{384,256},{4... | collective-permute-start | bytes 110600 | tf_op jit(solution)/shard_map/ppermute | solution.py:378
  136.9 13.3 %collective-permute-start.9 = (bf16[48,384]{1,0:T(8,128)(2,1)S(1)}, bf16[48,384]{1,0:T(8,128)(2,1)S(1)}, u32[]{:S(2)}, u32[]{:S(2)}) collective-permute-start(bf16[48,384]{1,0:T(8,128)(2,1)S(1)} %get-tuple-element.60), channel_id=1, source_target_pairs={{0,384},{64,448},{128,256},{192,320},{256,128},{320,192},{384,0},{... | collective-permute-start | bytes 110600 | tf_op jit(solution)/shard_map/ppermute | solution.py:378
  146.3 15.5 %all-to-all-start.2 = ((f32[32,2,96]{2,1,0:T(2,128)}), f32[32,2,96]{2,1,0:T(2,128)S(1)}, u32[]{:S(2)}, u32[]{:S(2)}) async-start(f32[32,2,96]{2,1,0:T(2,128)} %broadcast_in_dim.42), calls=%async_computation.2 | async-start | bytes 65536 | tf_op jit(solution)/shard_map/all_to_all | solution.py:367

commit v8 on v7

--- a/solution.py
+++ b/solution.py
@@ -74,10 +74,10 @@
 
 
 def middle(
-    where_ref, own_hbm, other_hbm, small_hbm, weight_hbm, project_hbm, flipped_hbm, taps_hbm, mask_hbm,
+    where_ref, own_hbm, other_hbm, small_hbm, weight_hbm, project_hbm, flipped_hbm, mask_hbm,
     mixed_out, part0_out, part1_out, part2_out, part3_out, stats_out,
-    own_ref, other_ref, small_ref, weight_ref, project_ref, flipped_ref, taps_ref, mask_ref,
-    mixed_ref, grads_ref, stats_ref, normed_ref, full_ref, both_ref, act_ref, kernel_ref,
+    own_ref, other_ref, small_ref, weight_ref, project_ref, flipped_ref, mask_ref,
+    taps_ref, mixed_ref, grads_ref, stats_ref, normed_ref, full_ref, both_ref, act_ref, kernel_ref,
     proj_ref, grad_ref, moved_ref, back_ref, sems,
 ):
     model = weight_ref.shape[1]
@@ -94,17 +94,19 @@
         count += 1
         return started
 
+    small_copy = copy(small_hbm, small_ref)
     blocks = [
         copy(source.at[x], target.at[x])
         for x in range(4)
         for source, target in ((own_hbm, own_ref), (other_hbm, other_ref))
     ]
-    small_copy = copy(small_hbm, small_ref)
     mask_copy = copy(mask_hbm, mask_ref)
     project_copy = copy(project_hbm, project_ref)
     weight_copy = copy(weight_hbm, weight_ref)
-    taps_copy = copy(taps_hbm, taps_ref)
     flipped_copy = copy(flipped_hbm, flipped_ref)
+    small_copy.wait()
+    for k in range(taps):
+        taps_ref[k] = jnp.broadcast_to(small_ref[:width, 34 + k : 35 + k], (width, 128))
     total = jnp.zeros((8, lanes), f32)
     square = jnp.zeros((8, lanes), f32)
     for i, (place, block) in enumerate(blocks_of(where_ref, own_ref, other_ref)):
@@ -125,7 +127,6 @@
         [row_mean, inv_std, jnp.zeros((6, lanes), f32)], axis=0
     )
     finished = [copy(stats_ref, stats_out)]
-    small_copy.wait()
     for i, (place, block) in enumerate(blocks_of(where_ref, own_ref, other_ref)):
         centred = (block[:, :lanes].astype(f32) - row_mean) * inv_std
         normed_ref[place] = (
@@ -140,7 +141,6 @@
         weight_ref[...], normed_ref[...].reshape(model, lanes), preferred_element_type=f32
     )
     mask_copy.wait()
-    taps_copy.wait()
     group = 16
     lane = lax.broadcasted_iota(jnp.int32, (group, 128), 1)
     inside = lax.broadcasted_iota(jnp.int32, (group, lanes), 1) < rows
@@ -288,20 +288,26 @@
         return parameter.reshape(16, width).T
 
     small = jnp.concatenate([columns_of(norm_gain), columns_of(norm_bias)], axis=1)
-    small = jnp.concatenate([jnp.pad(small, ((0, width), (0, 0))), by_gain, by_bias], axis=1)
-    small = jnp.pad(small, ((0, 0), (0, 128 - small.shape[1])))
-    wide_taps = jnp.broadcast_to(conv_kernel[:, :, None], (taps, width, 128))
-    early = (weights, weights.T, small, wide_taps, gain_local, where)
+    small = jnp.concatenate(
+        [
+            jnp.pad(small, ((0, width), (0, 0))),
+            by_gain,
+            by_bias,
+            jnp.pad(conv_kernel.T, ((0, width), (0, 128 - 34 - taps))),
+        ],
+        axis=1,
+    )
+    early = (weights, weights.T, small, gain_local, where)
 
     held = jnp.concatenate([inputs, edge[:width], upstream], axis=1)
     keep = jnp.concatenate([frame_mask.astype(f32)[None, :], edge[width : width + 1].astype(f32)], axis=1)
     came = swap(held, "zh")
     came, keep, early = lax.optimization_barrier((came, keep, early))
-    weights, flipped, small, wide_taps, gain_local, where = early
+    weights, flipped, small, gain_local, where = early
     own = over_x(jnp.stack([held, came]))
     other = swap(own, "core")
     piece_shape = (8, piece, 4 * width)
-    operands = (own, other, small, weights, project_weight, flipped, wide_taps, keep)
+    operands = (own, other, small, weights, project_weight, flipped, keep)
     mixed, *pieces, stats = pl.pallas_call(
         middle,
         out_shape=(
@@ -313,6 +319,7 @@
         out_specs=tuple(pl.BlockSpec(memory_space=pltpu.HBM if i in (0, 5) else pltpu.VMEM) for i in range(6)),
         scratch_shapes=[pltpu.VMEM(operand.shape, operand.dtype) for operand in operands]
         + [
+            pltpu.VMEM((taps, width, 128), f32),
             pltpu.VMEM((8, 2 * width + 16, rows), bf16),
             pltpu.VMEM((8, 4, piece, 4 * width), bf16),
             pltpu.VMEM((8, lanes), f32),
@@ -364,6 +371,7 @@
     inv_std = stats[1:2, :rows]
     centred = (inputs.astype(f32) - stats[0:1, :rows]) * inv_std
     tail = jnp.stack([jnp.sum(normed_grad * centred, axis=1), jnp.sum(normed_grad, axis=1)])
+    total, normed_grad = lax.optimization_barrier((total, normed_grad))
     tail = lax.all_to_all(
         jnp.broadcast_to(tail[None], (32, 2, width)), FRAME, 0, 0, tiled=True
     )

time: 165 us -> 161 us (0.976)
  the two profiles are of different devices: /device:TPU:1 before, /device:TPU:8 now
where the time goes in v8:
time: 161 us; the launch traced here: 160 us
  starting transfers between devices  91.7 us (57%)
  blocking collectives  21.2 us (13%)
  waiting for transfers between devices  18.4 us (11%)
  local copies, waits for them, and re-layouts  11.6 us (7%)
  Pallas kernels  10.7 us (7%)
  other arithmetic  5.35 us (3%)
    ppermute x3, starting transfers between devices, swap(): return lax.ppermute(value, axis, SWAP)  26.6 us
    all_to_all x1, blocking collectives, over_x(): lax.all_to_all(jnp.broadcast_to(pair[None], (4,) + pair.shape), 'x', 0, 0...  21.2 us
    ppermute x3, starting transfers between devices, on_device(): lax.ppermute(sent, 'zl', [(i, i ^ 2 * step) for i in range(8)]).astype(f32)  14 us
    ppermute x1, starting transfers between devices, on_device(): lax.ppermute(sent, 'zl', [(i, i ^ 1) for i in range(8)]).astype(f32)  13.3 us
    ppermute x3, starting transfers between devices, on_device(): lax.ppermute(sent, 'y', [(i, (i + step) % 4) for i in range(4)])  13 us
    all_to_all x1, starting transfers between devices, on_device(): lax.all_to_all(jnp.broadcast_to(tail[None], (32, 2, width)), FRAME, 0, 0,...  12.1 us
    pallas_call x1, Pallas kernels, on_device(): pl.pallas_call(middle, out_shape=(pltpu.HBM((8, 2 * width + 16, rows), bf...  10.6 us
    ppermute x3, waiting for transfers between devices, on_device(): lax.ppermute(sent, 'zl', [(i, i ^ 2 * step) for i in range(8)]).astype(f32)  8.39 us
  transfers between devices with their start and end apart: 14, of which 4 were waited for; matrix products, arithmetic and copies ran while one was open for 8% of the time, Pallas kernels for 0%

profile of v8, /device:TPU:8, one launch (start us, length us, event | category | flops | bytes accessed | tf_op | source)
XLA Modules:
  0.0 160.0 jit_solution(6748355531462439588)
XLA Ops:
  1.3 0.9 copy-done
  2.2 0.9 copy-done.2
  3.2 3.5 %collective-permute-start = (bf16[112,128]{1,0:T(8,128)(2,1)S(1)}, bf16[112,128]{1,0:T(8,128)(2,1)S(1)}, u32[]{:S(2)}, u32[]{:S(2)}) collective-permute-start(bf16[112,128]{1,0:T(8,128)(2,1)S(1)} %get-tuple-element.28), channel_id=1, source_target_pairs={{0,16},{16,32},{32,48},{48,64},{64,80},{80,96},{96,112},{112,128},... | collective-permute-start | bytes 86024 | tf_op jit(solution)/shard_map/ppermute | solution.py:275
  6.7 5.5 %collective-permute-start.1 = (bf16[112,128]{1,0:T(8,128)(2,1)S(1)}, bf16[112,128]{1,0:T(8,128)(2,1)S(1)}, u32[]{:S(2)}, u32[]{:S(2)}) collective-permute-start(bf16[112,128]{1,0:T(8,128)(2,1)S(1)} %get-tuple-element.29), channel_id=1, source_target_pairs={{16,0},{32,16},{48,32},{64,48},{80,64},{96,80},{112,96},{128,112},... | collective-permute-start | bytes 86024 | tf_op jit(solution)/shard_map/ppermute | solution.py:275
  12.2 0.8 reshape.41
  13.0 0.8 reshape.43
  13.8 1.2 copy.30
  15.0 1.2 copy.31
  16.2 1.1 fusion
  17.4 1.3 fusion.12
  19.3 0.8 select_maximum_fusion.small_hbm
  20.2 12.5 %collective-permute-start.2 = (bf16[96,896]{1,0:T(8,128)(2,1)S(1)}, bf16[96,896]{1,0:T(8,128)(2,1)S(1)}, u32[]{:S(2)}, u32[]{:S(2)}) collective-permute-start(bf16[96,896]{1,0:T(8,128)(2,1)S(1)} %get-tuple-element.66), channel_id=1, source_target_pairs={{0,2},{2,0},{1,3},{3,1},{4,6},{6,4},{5,7},{7,5},{8,10},{10,8},{9,1... | collective-permute-start | bytes 516104 | tf_op jit(solution)/shard_map/ppermute | solution.py:20
  33.4 3.5 %collective-permute-done.2 = bf16[96,896]{1,0:T(8,128)(2,1)S(1)} collective-permute-done((bf16[96,896]{1,0:T(8,128)(2,1)S(1)}, bf16[96,896]{1,0:T(8,128)(2,1)S(1)}, u32[]{:S(2)}, u32[]{:S(2)}) %collective-permute-start.2) | collective-permute-done | bytes 172064 | tf_op jit(solution)/shard_map/ppermute | solution.py:20
  37.0 21.2 %all_to_all.15.own_hbm = bf16[4,2,96,896]{3,2,1,0:T(8,128)(2,1)S(1)} all-to-all(bf16[4,2,96,896]{3,2,1,0:T(8,128)(2,1)S(1)} %broadcast_in_dim.33), channel_id=1, replica_groups=mesh['zl'=8,'y'=4,'x'=4,'zh'=2,'core'=2] {'x'}, dimensions={0} | all-to-all | bytes 2752512 | tf_op jit(solution)/shard_map/all_to_all | solution.py:24
  58.3 1.9 %collective-permute-start.3 = (bf16[4,2,96,896]{3,2,1,0:T(8,128)(2,1)S(1)}, bf16[4,2,96,896]{3,2,1,0:T(8,128)(2,1)}, u32[]{:S(2)}, u32[]{:S(2)}) collective-permute-start(bf16[4,2,96,896]{3,2,1,0:T(8,128)(2,1)S(1)} %all_to_all.15.own_hbm), channel_id=1, source_target_pairs={{0,1},{1,0},{2,3},{3,2},{4,5},{5,4},{6,7},{7,6},{8,9},{9,8},{10,11... | collective-permute-start | bytes 4128776 | tf_op jit(solution)/shard_map/ppermute | solution.py:20
  60.2 1.1 copy.36.weight_hbm
  61.3 2.1 %collective-permute-done.3.other_hbm = bf16[4,2,96,896]{3,2,1,0:T(8,128)(2,1)} collective-permute-done((bf16[4,2,96,896]{3,2,1,0:T(8,128)(2,1)S(1)}, bf16[4,2,96,896]{3,2,1,0:T(8,128)(2,1)}, u32[]{:S(2)}, u32[]{:S(2)}) %collective-permute-start.3) | collective-permute-done | bytes 1376288 | tf_op jit(solution)/shard_map/ppermute | solution.py:20
  63.4 10.6 %shard_map.145 = (bf16[8,208,384]{2,1,0:T(8,128)(2,1)}, bf16[8,48,384]{2,1,0:T(8,128)(2,1)S(1)}, bf16[8,48,384]{2,1,0:T(8,128)(2,1)S(1)}, bf16[8,48,384]{2,1,0:T...) custom-call(s32[3]{0:T(128)S(1)} %pad_add_fusion.where_ref, bf16[4,2,96,896]{3,2,1,0:T(8,128)(2,1)} %copy-done.4, ...), custom_call_target="tpu_custom_call" | custom-call | tf_op jit(solution)/shard_map/pallas_call | solution.py:311
  74.0 3.6 %all-to-all-start.1 = ((bf16[8,208,384]{2,1,0:T(8,128)(2,1)}), bf16[8,208,384]{2,1,0:T(8,128)(2,1)S(1)}, u32[]{:S(2)}, u32[]{:S(2)}) async-start(bf16[8,208,384]{2,1,0:T(8,128)(2,1)} %get-tuple-element.38), calls=%async_computation.1 | async-start | bytes 2555904 | tf_op jit(solution)/shard_map/all_to_all | solution.py:340
  77.7 3.5 %collective-permute-start.4 = (bf16[8,48,384]{2,1,0:T(8,128)(2,1)S(1)}, bf16[8,48,384]{2,1,0:T(8,128)(2,1)S(1)}, u32[]{:S(2)}, u32[]{:S(2)}) collective-permute-start(bf16[8,48,384]{2,1,0:T(8,128)(2,1)S(1)} %get-tuple-element.40), channel_id=1, source_target_pairs={{0,16},{16,32},{32,48},{48,0},{1,17},{17,33},{33,49},{49,1},{2,18}... | collective-permute-start | bytes 884744 | tf_op jit(solution)/shard_map/ppermute | solution.py:343
  81.2 5.6 %collective-permute-start.5 = (bf16[8,48,384]{2,1,0:T(8,128)(2,1)S(1)}, bf16[8,48,384]{2,1,0:T(8,128)(2,1)S(1)}, u32[]{:S(2)}, u32[]{:S(2)}) collective-permute-start(bf16[8,48,384]{2,1,0:T(8,128)(2,1)S(1)} %get-tuple-element.41), channel_id=1, source_target_pairs={{0,48},{16,0},{32,16},{48,32},{1,49},{17,1},{33,17},{49,33},{2,50}... | collective-permute-start | bytes 884744 | tf_op jit(solution)/shard_map/ppermute | solution.py:343
  86.8 4.0 %collective-permute-start.6 = (bf16[8,48,384]{2,1,0:T(8,128)(2,1)S(1)}, bf16[8,48,384]{2,1,0:T(8,128)(2,1)S(1)}, u32[]{:S(2)}, u32[]{:S(2)}) collective-permute-start(bf16[8,48,384]{2,1,0:T(8,128)(2,1)S(1)} %get-tuple-element.42), channel_id=1, source_target_pairs={{0,32},{16,48},{32,0},{48,16},{1,33},{17,49},{33,1},{49,17},{2,34}... | collective-permute-start | bytes 884744 | tf_op jit(solution)/shard_map/ppermute | solution.py:343
  90.8 0.8 slice_reduce_fusion.3
  91.6 4.4 %all-to-all-done.1 = bf16[8,208,384]{2,1,0:T(8,128)(2,1)S(1)} async-done(((bf16[8,208,384]{2,1,0:T(8,128)(2,1)}), bf16[8,208,384]{2,1,0:T(8,128)(2,1)S(1)}, u32[]{:S(2)}, u32[]{:S(2)}) %all-to-all-start.1) | async-done | bytes 1277984 | tf_op jit(solution)/shard_map/all_to_all | solution.py:340
  96.2 12.1 %collective-permute-start.8 = (bf16[112,384]{1,0:T(8,128)(2,1)S(1)}, bf16[112,384]{1,0:T(8,128)(2,1)S(1)}, u32[]{:S(2)}, u32[]{:S(2)}) collective-permute-start(bf16[112,384]{1,0:T(8,128)(2,1)S(1)} %maximum_maximum_fusion), channel_id=1, source_target_pairs={{0,2},{2,0},{1,3},{3,1},{4,6},{6,4},{5,7},{7,5},{8,10},{10,8},{9,1... | collective-permute-start | bytes 258056 | tf_op jit(solution)/shard_map/ppermute | solution.py:20
  108.6 13.3 %collective-permute-start.7 = (bf16[4,48,384]{2,1,0:T(8,128)(2,1)S(1)}, bf16[4,48,384]{2,1,0:T(8,128)(2,1)S(1)}, u32[]{:S(2)}, u32[]{:S(2)}) collective-permute-start(bf16[4,48,384]{2,1,0:T(8,128)(2,1)S(1)} %fusion.2), channel_id=1, source_target_pairs={{0,64},{64,0},{128,192},{192,128},{256,320},{320,256},{384,448},{4... | collective-permute-start | bytes 442376 | tf_op jit(solution)/shard_map/ppermute | solution.py:366
  122.7 12.1 %all-to-all-start.2 = ((f32[32,2,96]{2,1,0:T(2,128)}), f32[32,2,96]{2,1,0:T(2,128)S(1)}, u32[]{:S(2)}, u32[]{:S(2)}) async-start(f32[32,2,96]{2,1,0:T(2,128)} %broadcast_in_dim.35), calls=%async_computation.2 | async-start | bytes 65536 | tf_op jit(solution)/shard_map/all_to_all | solution.py:375
  134.9 7.3 %collective-permute-start.10 = (bf16[48,384]{1,0:T(8,128)(2,1)S(1)}, bf16[48,384]{1,0:T(8,128)(2,1)S(1)}, u32[]{:S(2)}, u32[]{:S(2)}) collective-permute-start(bf16[48,384]{1,0:T(8,128)(2,1)S(1)} %get-tuple-element.64), channel_id=1, source_target_pairs={{0,256},{64,320},{128,384},{192,448},{256,0},{320,64},{384,128},{4... | collective-permute-start | bytes 110600 | tf_op jit(solution)/shard_map/ppermute | solution.py:386
  142.2 4.3 %collective-permute-start.11 = (bf16[48,384]{1,0:T(8,128)(2,1)S(1)}, bf16[48,384]{1,0:T(8,128)(2,1)S(1)}, u32[]{:S(2)}, u32[]{:S(2)}) collective-permute-start(bf16[48,384]{1,0:T(8,128)(2,1)S(1)} %get-tuple-element.63), channel_id=1, source_target_pairs={{0,128},{64,192},{128,0},{192,64},{256,384},{320,448},{384,256},{4... | collective-permute-start | bytes 110600 | tf_op jit(solution)/shard_map/ppermute | solution.py:386
  146.6 2.4 %collective-permute-start.9 = (bf16[48,384]{1,0:T(8,128)(2,1)S(1)}, bf16[48,384]{1,0:T(8,128)(2,1)S(1)}, u32[]{:S(2)}, u32[]{:S(2)}) collective-permute-start(bf16[48,384]{1,0:T(8,128)(2,1)S(1)} %get-tuple-element.62), channel_id=1, source_target_pairs={{0,384},{64,448},{128,256},{192,320},{256,128},{320,192},{384,0},{... | collective-permute-start | bytes 110600 | tf_op jit(solution)/shard_map/ppermute | solution.py:386
  149.0 0.7 add_convert_fusion
  149.7 8.4 %collective-permute-done.9 = bf16[48,384]{1,0:T(8,128)(2,1)S(1)} collective-permute-done((bf16[48,384]{1,0:T(8,128)(2,1)S(1)}, bf16[48,384]{1,0:T(8,128)(2,1)S(1)}, u32[]{:S(2)}, u32[]{:S(2)}) %collective-permute-start.9) | collective-permute-done | bytes 36896 | tf_op jit(solution)/shard_map/ppermute | solution.py:386
  (71 shorter events, 5.6 us)
Async XLA Ops:
  1.3 0.9 copy-start
  2.2 0.9 copy-start.2
  3.1 13.1 %copy-start.5 = (f32[1536]{0:T(1024)S(1)}, f32[1536]{0:T(1024)}, u32[]{:S(2)}) copy-start(f32[1536]{0:T(1024)} %param.11) | copy-start | bytes 18436
  3.1 13.1 %copy-start.6 = (f32[1536]{0:T(1024)S(1)}, f32[1536]{0:T(1024)}, u32[]{:S(2)}) copy-start(f32[1536]{0:T(1024)} %param.10) | copy-start | bytes 18436
  3.2 17.0 %collective-permute-start = (bf16[112,128]{1,0:T(8,128)(2,1)S(1)}, bf16[112,128]{1,0:T(8,128)(2,1)S(1)}, u32[]{:S(2)}, u32[]{:S(2)}) collective-permute-start(bf16[112,128]{1,0:T(8,128)(2,1)S(1)} %get-tuple-element.28), channel_id=1, source_target_pairs={{0,16},{16,32},{32,48},{48,64},{64,80},{80,96},{96,112},{112,128},... | collective-permute-start | bytes 86024 | tf_op jit(solution)/shard_map/ppermute | solution.py:275
  6.7 13.5 %collective-permute-start.1 = (bf16[112,128]{1,0:T(8,128)(2,1)S(1)}, bf16[112,128]{1,0:T(8,128)(2,1)S(1)}, u32[]{:S(2)}, u32[]{:S(2)}) collective-permute-start(bf16[112,128]{1,0:T(8,128)(2,1)S(1)} %get-tuple-element.29), channel_id=1, source_target_pairs={{16,0},{32,16},{48,32},{64,48},{80,64},{96,80},{112,96},{128,112},... | collective-permute-start | bytes 86024 | tf_op jit(solution)/shard_map/ppermute | solution.py:275
  17.3 1.8 %copy-start.7 = (f32[31,96]{1,0:T(8,128)S(1)}, f32[31,96]{1,0:T(8,128)}, u32[]{:S(2)}) copy-start(f32[31,96]{1,0:T(8,128)} %param.14) | copy-start | bytes 35716
  17.3 2.8 %copy-start.8 = (s32[384]{0:T(512)S(1)}, s32[384]{0:T(512)}, u32[]{:S(2)}) copy-start(s32[384]{0:T(512)} %param.16) | copy-start | bytes 4612
  17.3 2.9 %copy-start.1 = (bf16[96,384]{1,0:T(8,128)(2,1)S(1)}, bf16[96,384]{1,0:T(8,128)(2,1)}, u32[]{:S(2)}) copy-start(bf16[96,384]{1,0:T(8,128)(2,1)} %inputs_ref.1) | copy-start | bytes 221188
  17.3 2.9 %copy-start.3 = (bf16[96,384]{1,0:T(8,128)(2,1)S(1)}, bf16[96,384]{1,0:T(8,128)(2,1)}, u32[]{:S(2)}) copy-start(bf16[96,384]{1,0:T(8,128)(2,1)} %upstream_ref.1) | copy-start | bytes 221188
  20.2 16.6 %collective-permute-start.2 = (bf16[96,896]{1,0:T(8,128)(2,1)S(1)}, bf16[96,896]{1,0:T(8,128)(2,1)S(1)}, u32[]{:S(2)}, u32[]{:S(2)}) collective-permute-start(bf16[96,896]{1,0:T(8,128)(2,1)S(1)} %get-tuple-element.66), channel_id=1, source_target_pairs={{0,2},{2,0},{1,3},{3,1},{4,6},{6,4},{5,7},{7,5},{8,10},{10,8},{9,1... | collective-permute-start | bytes 516104 | tf_op jit(solution)/shard_map/ppermute | solution.py:20
  58.3 5.1 %copy-start.4 = (bf16[4,2,96,896]{3,2,1,0:T(8,128)(2,1)}, bf16[4,2,96,896]{3,2,1,0:T(8,128)(2,1)S(1)}, u32[]{:S(2)}) copy-start(bf16[4,2,96,896]{3,2,1,0:T(8,128)(2,1)S(1)} %all_to_all.15.own_hbm) | copy-start | bytes 4128772
  58.3 5.1 %collective-permute-start.3 = (bf16[4,2,96,896]{3,2,1,0:T(8,128)(2,1)S(1)}, bf16[4,2,96,896]{3,2,1,0:T(8,128)(2,1)}, u32[]{:S(2)}, u32[]{:S(2)}) collective-permute-start(bf16[4,2,96,896]{3,2,1,0:T(8,128)(2,1)S(1)} %all_to_all.15.own_hbm), channel_id=1, source_target_pairs={{0,1},{1,0},{2,3},{3,2},{4,5},{5,4},{6,7},{7,6},{8,9},{9,8},{10,11... | collective-permute-start | bytes 4128776 | tf_op jit(solution)/shard_map/ppermute | solution.py:20
  74.0 21.9 %all-to-all-start.1 = ((bf16[8,208,384]{2,1,0:T(8,128)(2,1)}), bf16[8,208,384]{2,1,0:T(8,128)(2,1)S(1)}, u32[]{:S(2)}, u32[]{:S(2)}) async-start(bf16[8,208,384]{2,1,0:T(8,128)(2,1)} %get-tuple-element.38), calls=%async_computation.1 | async-start | bytes 2555904 | tf_op jit(solution)/shard_map/all_to_all | solution.py:340
  77.7 30.7 %collective-permute-start.4 = (bf16[8,48,384]{2,1,0:T(8,128)(2,1)S(1)}, bf16[8,48,384]{2,1,0:T(8,128)(2,1)S(1)}, u32[]{:S(2)}, u32[]{:S(2)}) collective-permute-start(bf16[8,48,384]{2,1,0:T(8,128)(2,1)S(1)} %get-tuple-element.40), channel_id=1, source_target_pairs={{0,16},{16,32},{32,48},{48,0},{1,17},{17,33},{33,49},{49,1},{2,18}... | collective-permute-start | bytes 884744 | tf_op jit(solution)/shard_map/ppermute | solution.py:343
  81.2 27.2 %collective-permute-start.5 = (bf16[8,48,384]{2,1,0:T(8,128)(2,1)S(1)}, bf16[8,48,384]{2,1,0:T(8,128)(2,1)S(1)}, u32[]{:S(2)}, u32[]{:S(2)}) collective-permute-start(bf16[8,48,384]{2,1,0:T(8,128)(2,1)S(1)} %get-tuple-element.41), channel_id=1, source_target_pairs={{0,48},{16,0},{32,16},{48,32},{1,49},{17,1},{33,17},{49,33},{2,50}... | collective-permute-start | bytes 884744 | tf_op jit(solution)/shard_map/ppermute | solution.py:343
  86.8 21.6 %collective-permute-start.6 = (bf16[8,48,384]{2,1,0:T(8,128)(2,1)S(1)}, bf16[8,48,384]{2,1,0:T(8,128)(2,1)S(1)}, u32[]{:S(2)}, u32[]{:S(2)}) collective-permute-start(bf16[8,48,384]{2,1,0:T(8,128)(2,1)S(1)} %get-tuple-element.42), channel_id=1, source_target_pairs={{0,32},{16,48},{32,0},{48,16},{1,33},{17,49},{33,1},{49,17},{2,34}... | collective-permute-start | bytes 884744 | tf_op jit(solution)/shard_map/ppermute | solution.py:343
  96.2 25.7 %collective-permute-start.8 = (bf16[112,384]{1,0:T(8,128)(2,1)S(1)}, bf16[112,384]{1,0:T(8,128)(2,1)S(1)}, u32[]{:S(2)}, u32[]{:S(2)}) collective-permute-start(bf16[112,384]{1,0:T(8,128)(2,1)S(1)} %maximum_maximum_fusion), channel_id=1, source_target_pairs={{0,2},{2,0},{1,3},{3,1},{4,6},{6,4},{5,7},{7,5},{8,10},{10,8},{9,1... | collective-permute-start | bytes 258056 | tf_op jit(solution)/shard_map/ppermute | solution.py:20
  108.6 26.3 %collective-permute-start.7 = (bf16[4,48,384]{2,1,0:T(8,128)(2,1)S(1)}, bf16[4,48,384]{2,1,0:T(8,128)(2,1)S(1)}, u32[]{:S(2)}, u32[]{:S(2)}) collective-permute-start(bf16[4,48,384]{2,1,0:T(8,128)(2,1)S(1)} %fusion.2), channel_id=1, source_target_pairs={{0,64},{64,0},{128,192},{192,128},{256,320},{320,256},{384,448},{4... | collective-permute-start | bytes 442376 | tf_op jit(solution)/shard_map/ppermute | solution.py:366
  122.7 35.5 %all-to-all-start.2 = ((f32[32,2,96]{2,1,0:T(2,128)}), f32[32,2,96]{2,1,0:T(2,128)S(1)}, u32[]{:S(2)}, u32[]{:S(2)}) async-start(f32[32,2,96]{2,1,0:T(2,128)} %broadcast_in_dim.35), calls=%async_computation.2 | async-start | bytes 65536 | tf_op jit(solution)/shard_map/all_to_all | solution.py:375
  134.9 14.8 %collective-permute-start.10 = (bf16[48,384]{1,0:T(8,128)(2,1)S(1)}, bf16[48,384]{1,0:T(8,128)(2,1)S(1)}, u32[]{:S(2)}, u32[]{:S(2)}) collective-permute-start(bf16[48,384]{1,0:T(8,128)(2,1)S(1)} %get-tuple-element.64), channel_id=1, source_target_pairs={{0,256},{64,320},{128,384},{192,448},{256,0},{320,64},{384,128},{4... | collective-permute-start | bytes 110600 | tf_op jit(solution)/shard_map/ppermute | solution.py:386
  142.2 7.5 %collective-permute-start.11 = (bf16[48,384]{1,0:T(8,128)(2,1)S(1)}, bf16[48,384]{1,0:T(8,128)(2,1)S(1)}, u32[]{:S(2)}, u32[]{:S(2)}) collective-permute-start(bf16[48,384]{1,0:T(8,128)(2,1)S(1)} %get-tuple-element.63), channel_id=1, source_target_pairs={{0,128},{64,192},{128,0},{192,64},{256,384},{320,448},{384,256},{4... | collective-permute-start | bytes 110600 | tf_op jit(solution)/shard_map/ppermute | solution.py:386
  146.6 11.6 %collective-permute-start.9 = (bf16[48,384]{1,0:T(8,128)(2,1)S(1)}, bf16[48,384]{1,0:T(8,128)(2,1)S(1)}, u32[]{:S(2)}, u32[]{:S(2)}) collective-permute-start(bf16[48,384]{1,0:T(8,128)(2,1)S(1)} %get-tuple-element.62), channel_id=1, source_target_pairs={{0,384},{64,448},{128,256},{192,320},{256,128},{320,192},{384,0},{... | collective-permute-start | bytes 110600 | tf_op jit(solution)/shard_map/ppermute | solution.py:386

commit v9 on v8

--- a/solution.py
+++ b/solution.py
@@ -26,6 +26,12 @@
     )
 
 
+def ordered(own, other, index, axis):
+    return jnp.where(
+        index == 0, jnp.stack([own, other], axis), jnp.stack([other, own], axis)
+    )
+
+
 def split_bf16(value):
     high = value.astype(bf16)
     return high, (value - high.astype(f32)).astype(bf16)
@@ -55,22 +61,33 @@
             yield x * 4 + side * 2 + 1 - core, other_ref.at[x, far]
 
 
-def edges(inputs_ref, upstream_ref, mask_ref, right_ref, left_ref):
-    width, rows = inputs_ref.shape
+def edges(inputs_hbm, upstream_hbm, mask_ref, right_ref, left_ref, ends_ref, sems):
+    width, rows = inputs_hbm.shape
+    starts = (rows - 128, 0)
+    copies = []
+    for i, start in enumerate(starts):
+        for j, source in enumerate((inputs_hbm, upstream_hbm)):
+            copies.append(
+                pltpu.make_async_copy(
+                    source.at[:, start : start + 128], ends_ref.at[i, j], sems.at[2 * i + j]
+                )
+            )
+            copies[-1].start()
+    for started in copies:
+        started.wait()
     lane = lax.broadcasted_iota(jnp.int32, (width, 128), 1)
     low = lax.broadcasted_iota(jnp.int32, (16, 128), 1)
 
-    def pack(start, own, moved, ref):
-        ends = inputs_ref[:, start : start + 128].astype(f32)
-        up = pltpu.roll(upstream_ref[:, start : start + 128].astype(f32), 64, 1)
+    def pack(i, own, moved, ref):
+        up = pltpu.roll(ends_ref[i, 1].astype(f32), 64, 1)
         ref[:width] = jnp.where(
-            own(lane), ends, jnp.where(moved(lane), up, 0.0)
+            own(lane), ends_ref[i, 0].astype(f32), jnp.where(moved(lane), up, 0.0)
         ).astype(bf16)
-        mask = jnp.broadcast_to(mask_ref[:, start : start + 128].astype(f32), (16, 128))
-        ref[width:] = jnp.where(own(low), mask, 0.0).astype(bf16)
-
-    pack(rows - 128, lambda i: i >= 98, lambda i: (i >= 49) & (i < 64), right_ref)
-    pack(0, lambda i: i < 30, lambda i: (i >= 64) & (i < 79), left_ref)
+        mask = mask_ref[:, starts[i] : starts[i] + 128].astype(f32)
+        ref[width:] = jnp.where(own(low), jnp.broadcast_to(mask, (16, 128)), 0.0).astype(bf16)
+
+    pack(0, lambda i: i >= 98, lambda i: (i >= 49) & (i < 64), right_ref)
+    pack(1, lambda i: i < 30, lambda i: (i >= 64) & (i < 79), left_ref)
 
 
 def middle(
@@ -270,8 +287,13 @@
     to_right, to_left = call(
         edges,
         (shape((width + 16, 128), bf16), shape((width + 16, 128), bf16)),
-        specs=[VMEM] * 3,
-    )(inputs, upstream, frame_mask.reshape(1, rows))
+        scratch=(pltpu.VMEM((2, 2, width, 128), bf16), pltpu.SemaphoreType.DMA((4,))),
+        specs=[pl.BlockSpec(memory_space=pltpu.HBM)] * 2 + [VMEM],
+    )(
+        pltpu.with_memory_space_constraint(inputs, pltpu.HBM),
+        pltpu.with_memory_space_constraint(upstream, pltpu.HBM),
+        frame_mask.reshape(1, rows),
+    )
     edge = lax.ppermute(to_right, FRAME, [(i, i + 1) for i in range(31)]) + lax.ppermute(
         to_left, FRAME, [(i + 1, i) for i in range(31)]
     )
@@ -304,6 +326,7 @@
     came = swap(held, "zh")
     came, keep, early = lax.optimization_barrier((came, keep, early))
     weights, flipped, small, gain_local, where = early
+    far_inputs = came[:, :rows]
     own = over_x(jnp.stack([held, came]))
     other = swap(own, "core")
     piece_shape = (8, piece, 4 * width)
@@ -344,12 +367,24 @@
         for step, sent in zip((1, 3, 2), pieces[1:])
     ]
     mixed = jnp.sum(mixed.astype(f32), axis=0)
+    near = mixed[width : 2 * width]
+    inv_std = stats[1:2, :rows]
+    centred = (inputs.astype(f32) - stats[0:1, :rows]) * inv_std
+    centred_far = (far_inputs.astype(f32) - stats[0:1, :rows]) * inv_std
+    near_tail = jnp.stack([jnp.sum(near * centred, axis=1), jnp.sum(near, axis=1)])
+    far_tail = jnp.stack([jnp.sum(mixed[:width] * centred_far, axis=1), jnp.sum(mixed[:width], axis=1)])
+    tail, near = lax.optimization_barrier((ordered(near_tail, far_tail, zh, 0), near))
     far_sums = mixed[2 * width : 2 * width + 2] + mixed[2 * width + 2 : 2 * width + 4]
     sent_high, sent_low = split_bf16(far_sums)
     far = jnp.concatenate(
         [mixed[:width].astype(bf16), sent_high, sent_low, jnp.zeros((12, rows), bf16)]
     )
     came = swap(far, "zh").astype(f32)
+
+    tail = lax.all_to_all(
+        jnp.broadcast_to(tail[None], (32, 2, 2, width)).reshape(64, 2, width),
+        FRAME + ("zh",), 0, 0, tiled=True,
+    )
 
     total, far_copy = lax.optimization_barrier((pieces[0], far))
     total = total.astype(f32)
@@ -365,16 +400,10 @@
     total = lax.dynamic_slice_in_dim(total, side, 1, 1)[:, 0]
     total = total + lax.ppermute(sent, "zl", [(i, i ^ 1) for i in range(8)]).astype(f32)
 
-    normed_grad = mixed[width : 2 * width] + came[:width]
+    normed_grad = near + came[:width]
     kept = far_copy[width : width + 4].astype(f32)
     sums = (kept[:2] + kept[2:] + came[width : width + 2] + came[width + 2 : width + 4]) / model
-    inv_std = stats[1:2, :rows]
-    centred = (inputs.astype(f32) - stats[0:1, :rows]) * inv_std
-    tail = jnp.stack([jnp.sum(normed_grad * centred, axis=1), jnp.sum(normed_grad, axis=1)])
     total, normed_grad = lax.optimization_barrier((total, normed_grad))
-    tail = lax.all_to_all(
-        jnp.broadcast_to(tail[None], (32, 2, width)), FRAME, 0, 0, tiled=True
-    )
     inputs_grad = (
         upstream.astype(f32)
         + inv_std * (normed_grad * gain_local - sums[0:1] - centred * sums[1:2])

time: 161 us -> 159 us (0.988)
  the two profiles are of different devices: /device:TPU:8 before, /device:TPU:1 now
where the time goes in v9:
time: 159 us; the launch traced here: 156 us
  starting transfers between devices  90.7 us (57%)
  waiting for transfers between devices  20.8 us (13%)
  blocking collectives  15.4 us (10%)
  Pallas kernels  11.5 us (7%)
  local copies, waits for them, and re-layouts  9.85 us (6%)
  other arithmetic  6.43 us (4%)
    ppermute x3, starting transfers between devices, swap(): return lax.ppermute(value, axis, SWAP)  43.5 us
    all_to_all x1, blocking collectives, over_x(): lax.all_to_all(jnp.broadcast_to(pair[None], (4,) + pair.shape), 'x', 0, 0...  15.4 us
    ppermute x3, starting transfers between devices, on_device(): lax.ppermute(sent, 'zl', [(i, i ^ 2 * step) for i in range(8)]).astype(f32)  13.2 us
    pallas_call x1, Pallas kernels, on_device(): pl.pallas_call(middle, out_shape=(pltpu.HBM((8, 2 * width + 16, rows), bf...  10.6 us
    ppermute x1, starting transfers between devices, on_device(): lax.ppermute(sent, 'zl', [(i, i ^ 1) for i in range(8)]).astype(f32)  9.29 us
    ppermute x3, starting transfers between devices, on_device(): lax.ppermute(sent, 'y', [(i, (i + step) % 4) for i in range(4)])  8.4 us
    all_to_all x1, waiting for transfers between devices, on_device(): mixed = lax.all_to_all(mixed, ('x', 'core'), 0, 0, tiled=True)  8.37 us
    ppermute x3, waiting for transfers between devices, on_device(): lax.ppermute(sent, 'zl', [(i, i ^ 2 * step) for i in range(8)]).astype(f32)  7.52 us
  transfers between devices with their start and end apart: 14, of which 4 were waited for; matrix products, arithmetic and copies ran while one was open for 9% of the time, Pallas kernels for 0%

profile of v9, /device:TPU:1, one launch (start us, length us, event | category | flops | bytes accessed | tf_op | source)
XLA Modules:
  0.0 155.8 jit_solution(12920218004284427071)
XLA Ops:
  1.3 0.9 shard_map.144
  2.3 4.0 %collective-permute-start = (bf16[112,128]{1,0:T(8,128)(2,1)S(1)}, bf16[112,128]{1,0:T(8,128)(2,1)S(1)}, u32[]{:S(2)}, u32[]{:S(2)}) collective-permute-start(bf16[112,128]{1,0:T(8,128)(2,1)S(1)} %get-tuple-element.30), channel_id=1, source_target_pairs={{0,16},{16,32},{32,48},{48,64},{64,80},{80,96},{96,112},{112,128},... | collective-permute-start | bytes 86024 | tf_op jit(solution)/shard_map/ppermute | solution.py:297
  6.3 1.3 collective-permute-start.1
  7.6 0.8 reshape.44
  8.4 0.8 reshape.46
  9.2 1.2 copy.30
  10.4 1.2 copy.31
  11.6 1.1 fusion
  12.7 1.3 fusion.12
  14.7 0.8 select_maximum_fusion.small_hbm
  15.6 15.4 %collective-permute-start.2 = (bf16[96,896]{1,0:T(8,128)(2,1)S(1)}, bf16[96,896]{1,0:T(8,128)(2,1)S(1)}, u32[]{:S(2)}, u32[]{:S(2)}) collective-permute-start(bf16[96,896]{1,0:T(8,128)(2,1)S(1)} %get-tuple-element.72), channel_id=1, source_target_pairs={{0,2},{2,0},{1,3},{3,1},{4,6},{6,4},{5,7},{7,5},{8,10},{10,8},{9,1... | collective-permute-start | bytes 516104 | tf_op jit(solution)/shard_map/ppermute | solution.py:20
  31.7 3.1 %collective-permute-done.2 = bf16[96,896]{1,0:T(8,128)(2,1)S(1)} collective-permute-done((bf16[96,896]{1,0:T(8,128)(2,1)S(1)}, bf16[96,896]{1,0:T(8,128)(2,1)S(1)}, u32[]{:S(2)}, u32[]{:S(2)}) %collective-permute-start.2) | collective-permute-done | bytes 172064 | tf_op jit(solution)/shard_map/ppermute | solution.py:20
  34.9 15.4 %all_to_all.15.own_hbm = bf16[4,2,96,896]{3,2,1,0:T(8,128)(2,1)S(1)} all-to-all(bf16[4,2,96,896]{3,2,1,0:T(8,128)(2,1)S(1)} %broadcast_in_dim.33), channel_id=1, replica_groups=mesh['zl'=8,'y'=4,'x'=4,'zh'=2,'core'=2] {'x'}, dimensions={0} | all-to-all | bytes 2752512 | tf_op jit(solution)/shard_map/all_to_all | solution.py:24
  50.3 15.2 %collective-permute-start.3 = (bf16[4,2,96,896]{3,2,1,0:T(8,128)(2,1)S(1)}, bf16[4,2,96,896]{3,2,1,0:T(8,128)(2,1)}, u32[]{:S(2)}, u32[]{:S(2)}) collective-permute-start(bf16[4,2,96,896]{3,2,1,0:T(8,128)(2,1)S(1)} %all_to_all.15.own_hbm), channel_id=1, source_target_pairs={{0,1},{1,0},{2,3},{3,2},{4,5},{5,4},{6,7},{7,6},{8,9},{9,8},{10,11... | collective-permute-start | bytes 4128776 | tf_op jit(solution)/shard_map/ppermute | solution.py:20
  65.6 1.1 copy.36.weight_hbm
  66.6 1.8 %collective-permute-done.3.other_hbm = bf16[4,2,96,896]{3,2,1,0:T(8,128)(2,1)} collective-permute-done((bf16[4,2,96,896]{3,2,1,0:T(8,128)(2,1)S(1)}, bf16[4,2,96,896]{3,2,1,0:T(8,128)(2,1)}, u32[]{:S(2)}, u32[]{:S(2)}) %collective-permute-start.3) | collective-permute-done | bytes 1376288 | tf_op jit(solution)/shard_map/ppermute | solution.py:20
  68.4 10.6 %shard_map.145 = (bf16[8,208,384]{2,1,0:T(8,128)(2,1)}, bf16[8,48,384]{2,1,0:T(8,128)(2,1)S(1)}, bf16[8,48,384]{2,1,0:T(8,128)(2,1)S(1)}, bf16[8,48,384]{2,1,0:T...) custom-call(s32[3]{0:T(128)S(1)} %pad_add_fusion.where_ref, bf16[4,2,96,896]{3,2,1,0:T(8,128)(2,1)} %copy-done, ...), custom_call_target="tpu_custom_call" | custom-call | tf_op jit(solution)/shard_map/pallas_call | solution.py:334
  79.0 3.9 %all-to-all-start.1 = ((bf16[8,208,384]{2,1,0:T(8,128)(2,1)}), bf16[8,208,384]{2,1,0:T(8,128)(2,1)S(1)}, u32[]{:S(2)}, u32[]{:S(2)}) async-start(bf16[8,208,384]{2,1,0:T(8,128)(2,1)} %get-tuple-element.40), calls=%async_computation.1 | async-start | bytes 2555904 | tf_op jit(solution)/shard_map/all_to_all | solution.py:363
  82.9 1.9 %collective-permute-start.4 = (bf16[8,48,384]{2,1,0:T(8,128)(2,1)S(1)}, bf16[8,48,384]{2,1,0:T(8,128)(2,1)S(1)}, u32[]{:S(2)}, u32[]{:S(2)}) collective-permute-start(bf16[8,48,384]{2,1,0:T(8,128)(2,1)S(1)} %get-tuple-element.42), channel_id=1, source_target_pairs={{0,16},{16,32},{32,48},{48,0},{1,17},{17,33},{33,49},{49,1},{2,18}... | collective-permute-start | bytes 884744 | tf_op jit(solution)/shard_map/ppermute | solution.py:366
  84.9 4.6 %collective-permute-start.5 = (bf16[8,48,384]{2,1,0:T(8,128)(2,1)S(1)}, bf16[8,48,384]{2,1,0:T(8,128)(2,1)S(1)}, u32[]{:S(2)}, u32[]{:S(2)}) collective-permute-start(bf16[8,48,384]{2,1,0:T(8,128)(2,1)S(1)} %get-tuple-element.43), channel_id=1, source_target_pairs={{0,48},{16,0},{32,16},{48,32},{1,49},{17,1},{33,17},{49,33},{2,50}... | collective-permute-start | bytes 884744 | tf_op jit(solution)/shard_map/ppermute | solution.py:366
  89.4 1.9 %collective-permute-start.6 = (bf16[8,48,384]{2,1,0:T(8,128)(2,1)S(1)}, bf16[8,48,384]{2,1,0:T(8,128)(2,1)}, u32[]{:S(2)}, u32[]{:S(2)}) collective-permute-start(bf16[8,48,384]{2,1,0:T(8,128)(2,1)S(1)} %get-tuple-element.44), channel_id=1, source_target_pairs={{0,32},{16,48},{32,0},{48,16},{1,33},{17,49},{33,1},{49,17},{2,34}... | collective-permute-start | bytes 884744 | tf_op jit(solution)/shard_map/ppermute | solution.py:366
  91.4 0.8 slice_reduce_fusion.4
  92.2 8.4 %all-to-all-done.1 = bf16[8,208,384]{2,1,0:T(8,128)(2,1)S(1)} async-done(((bf16[8,208,384]{2,1,0:T(8,128)(2,1)}), bf16[8,208,384]{2,1,0:T(8,128)(2,1)S(1)}, u32[]{:S(2)}, u32[]{:S(2)}) %all-to-all-start.1) | async-done | bytes 1277984 | tf_op jit(solution)/shard_map/all_to_all | solution.py:363
  101.1 12.9 %collective-permute-start.8 = (bf16[112,384]{1,0:T(8,128)(2,1)S(1)}, bf16[112,384]{1,0:T(8,128)(2,1)S(1)}, u32[]{:S(2)}, u32[]{:S(2)}) collective-permute-start(bf16[112,384]{1,0:T(8,128)(2,1)S(1)} %maximum_maximum_fusion), channel_id=1, source_target_pairs={{0,2},{2,0},{1,3},{3,1},{4,6},{6,4},{5,7},{7,5},{8,10},{10,8},{9,1... | collective-permute-start | bytes 258056 | tf_op jit(solution)/shard_map/ppermute | solution.py:20
  114.0 1.1 convert_add_fusion
  115.1 9.3 %collective-permute-start.7 = (bf16[4,48,384]{2,1,0:T(8,128)(2,1)S(1)}, bf16[4,48,384]{2,1,0:T(8,128)(2,1)S(1)}, u32[]{:S(2)}, u32[]{:S(2)}) collective-permute-start(bf16[4,48,384]{2,1,0:T(8,128)(2,1)S(1)} %fusion.2), channel_id=1, source_target_pairs={{0,64},{64,0},{128,192},{192,128},{256,320},{320,256},{384,448},{4... | collective-permute-start | bytes 442376 | tf_op jit(solution)/shard_map/ppermute | solution.py:401
  125.1 7.1 %all-to-all-start.2 = ((f32[64,2,96]{2,1,0:T(2,128)}), f32[64,2,96]{2,1,0:T(2,128)S(1)}, u32[]{:S(2)}, u32[]{:S(2)}) async-start(f32[64,2,96]{2,1,0:T(2,128)} %bitcast.24), calls=%async_computation.2 | async-start | bytes 131072 | tf_op jit(solution)/shard_map/all_to_all | solution.py:384
  132.4 6.9 %collective-permute-start.10 = (bf16[48,384]{1,0:T(8,128)(2,1)S(1)}, bf16[48,384]{1,0:T(8,128)(2,1)S(1)}, u32[]{:S(2)}, u32[]{:S(2)}) collective-permute-start(bf16[48,384]{1,0:T(8,128)(2,1)S(1)} %get-tuple-element.70), channel_id=1, source_target_pairs={{0,256},{64,320},{128,384},{192,448},{256,0},{320,64},{384,128},{4... | collective-permute-start | bytes 110600 | tf_op jit(solution)/shard_map/ppermute | solution.py:415
  139.3 4.1 %collective-permute-start.11 = (bf16[48,384]{1,0:T(8,128)(2,1)S(1)}, bf16[48,384]{1,0:T(8,128)(2,1)S(1)}, u32[]{:S(2)}, u32[]{:S(2)}) collective-permute-start(bf16[48,384]{1,0:T(8,128)(2,1)S(1)} %get-tuple-element.69), channel_id=1, source_target_pairs={{0,128},{64,192},{128,0},{192,64},{256,384},{320,448},{384,256},{4... | collective-permute-start | bytes 110600 | tf_op jit(solution)/shard_map/ppermute | solution.py:415
  143.4 2.2 %collective-permute-start.9 = (bf16[48,384]{1,0:T(8,128)(2,1)S(1)}, bf16[48,384]{1,0:T(8,128)(2,1)S(1)}, u32[]{:S(2)}, u32[]{:S(2)}) collective-permute-start(bf16[48,384]{1,0:T(8,128)(2,1)S(1)} %get-tuple-element.68), channel_id=1, source_target_pairs={{0,384},{64,448},{128,256},{192,320},{256,128},{320,192},{384,0},{... | collective-permute-start | bytes 110600 | tf_op jit(solution)/shard_map/ppermute | solution.py:415
  145.6 0.7 add_convert_fusion
  146.3 7.5 %collective-permute-done.9 = bf16[48,384]{1,0:T(8,128)(2,1)S(1)} collective-permute-done((bf16[48,384]{1,0:T(8,128)(2,1)S(1)}, bf16[48,384]{1,0:T(8,128)(2,1)S(1)}, u32[]{:S(2)}, u32[]{:S(2)}) %collective-permute-start.9) | collective-permute-done | bytes 36896 | tf_op jit(solution)/shard_map/ppermute | solution.py:415
  (70 shorter events, 5.5 us)
Async XLA Ops:
  0.6 10.9 %copy-start.4 = (f32[1536]{0:T(1024)S(1)}, f32[1536]{0:T(1024)}, u32[]{:S(2)}) copy-start(f32[1536]{0:T(1024)} %param.10) | copy-start | bytes 18436
  0.6 10.9 %copy-start.3 = (f32[1536]{0:T(1024)S(1)}, f32[1536]{0:T(1024)}, u32[]{:S(2)}) copy-start(f32[1536]{0:T(1024)} %param.11) | copy-start | bytes 18436
  2.3 13.3 %collective-permute-start = (bf16[112,128]{1,0:T(8,128)(2,1)S(1)}, bf16[112,128]{1,0:T(8,128)(2,1)S(1)}, u32[]{:S(2)}, u32[]{:S(2)}) collective-permute-start(bf16[112,128]{1,0:T(8,128)(2,1)S(1)} %get-tuple-element.30), channel_id=1, source_target_pairs={{0,16},{16,32},{32,48},{48,64},{64,80},{80,96},{96,112},{112,128},... | collective-permute-start | bytes 86024 | tf_op jit(solution)/shard_map/ppermute | solution.py:297
  6.3 9.2 %collective-permute-start.1 = (bf16[112,128]{1,0:T(8,128)(2,1)S(1)}, bf16[112,128]{1,0:T(8,128)(2,1)S(1)}, u32[]{:S(2)}, u32[]{:S(2)}) collective-permute-start(bf16[112,128]{1,0:T(8,128)(2,1)S(1)} %get-tuple-element.31), channel_id=1, source_target_pairs={{16,0},{32,16},{48,32},{64,48},{80,64},{96,80},{112,96},{128,112},... | collective-permute-start | bytes 86024 | tf_op jit(solution)/shard_map/ppermute | solution.py:297
  12.7 1.8 %copy-start.5 = (f32[31,96]{1,0:T(8,128)S(1)}, f32[31,96]{1,0:T(8,128)}, u32[]{:S(2)}) copy-start(f32[31,96]{1,0:T(8,128)} %param.14) | copy-start | bytes 35716
  12.7 2.8 %copy-start.6 = (s32[384]{0:T(512)S(1)}, s32[384]{0:T(512)}, u32[]{:S(2)}) copy-start(s32[384]{0:T(512)} %param.16) | copy-start | bytes 4612
  12.7 2.9 %copy-start.1 = (bf16[96,384]{1,0:T(8,128)(2,1)S(1)}, bf16[96,384]{1,0:T(8,128)(2,1)}, u32[]{:S(2)}) copy-start(bf16[96,384]{1,0:T(8,128)(2,1)} %inputs_hbm.1) | copy-start | bytes 221188
  12.7 2.9 %copy-start.2 = (bf16[96,384]{1,0:T(8,128)(2,1)S(1)}, bf16[96,384]{1,0:T(8,128)(2,1)}, u32[]{:S(2)}) copy-start(bf16[96,384]{1,0:T(8,128)(2,1)} %upstream_hbm.1) | copy-start | bytes 221188
  15.6 19.1 %collective-permute-start.2 = (bf16[96,896]{1,0:T(8,128)(2,1)S(1)}, bf16[96,896]{1,0:T(8,128)(2,1)S(1)}, u32[]{:S(2)}, u32[]{:S(2)}) collective-permute-start(bf16[96,896]{1,0:T(8,128)(2,1)S(1)} %get-tuple-element.72), channel_id=1, source_target_pairs={{0,2},{2,0},{1,3},{3,1},{4,6},{6,4},{5,7},{7,5},{8,10},{10,8},{9,1... | collective-permute-start | bytes 516104 | tf_op jit(solution)/shard_map/ppermute | solution.py:20
  50.3 18.1 %copy-start = (bf16[4,2,96,896]{3,2,1,0:T(8,128)(2,1)}, bf16[4,2,96,896]{3,2,1,0:T(8,128)(2,1)S(1)}, u32[]{:S(2)}) copy-start(bf16[4,2,96,896]{3,2,1,0:T(8,128)(2,1)S(1)} %all_to_all.15.own_hbm) | copy-start | bytes 4128772
  50.3 18.1 %collective-permute-start.3 = (bf16[4,2,96,896]{3,2,1,0:T(8,128)(2,1)S(1)}, bf16[4,2,96,896]{3,2,1,0:T(8,128)(2,1)}, u32[]{:S(2)}, u32[]{:S(2)}) collective-permute-start(bf16[4,2,96,896]{3,2,1,0:T(8,128)(2,1)S(1)} %all_to_all.15.own_hbm), channel_id=1, source_target_pairs={{0,1},{1,0},{2,3},{3,2},{4,5},{5,4},{6,7},{7,6},{8,9},{9,8},{10,11... | collective-permute-start | bytes 4128776 | tf_op jit(solution)/shard_map/ppermute | solution.py:20
  79.0 21.5 %all-to-all-start.1 = ((bf16[8,208,384]{2,1,0:T(8,128)(2,1)}), bf16[8,208,384]{2,1,0:T(8,128)(2,1)S(1)}, u32[]{:S(2)}, u32[]{:S(2)}) async-start(bf16[8,208,384]{2,1,0:T(8,128)(2,1)} %get-tuple-element.40), calls=%async_computation.1 | async-start | bytes 2555904 | tf_op jit(solution)/shard_map/all_to_all | solution.py:363
  82.9 31.0 %collective-permute-start.4 = (bf16[8,48,384]{2,1,0:T(8,128)(2,1)S(1)}, bf16[8,48,384]{2,1,0:T(8,128)(2,1)S(1)}, u32[]{:S(2)}, u32[]{:S(2)}) collective-permute-start(bf16[8,48,384]{2,1,0:T(8,128)(2,1)S(1)} %get-tuple-element.42), channel_id=1, source_target_pairs={{0,16},{16,32},{32,48},{48,0},{1,17},{17,33},{33,49},{49,1},{2,18}... | collective-permute-start | bytes 884744 | tf_op jit(solution)/shard_map/ppermute | solution.py:366
  84.9 29.1 %collective-permute-start.5 = (bf16[8,48,384]{2,1,0:T(8,128)(2,1)S(1)}, bf16[8,48,384]{2,1,0:T(8,128)(2,1)S(1)}, u32[]{:S(2)}, u32[]{:S(2)}) collective-permute-start(bf16[8,48,384]{2,1,0:T(8,128)(2,1)S(1)} %get-tuple-element.43), channel_id=1, source_target_pairs={{0,48},{16,0},{32,16},{48,32},{1,49},{17,1},{33,17},{49,33},{2,50}... | collective-permute-start | bytes 884744 | tf_op jit(solution)/shard_map/ppermute | solution.py:366
  89.4 24.5 %collective-permute-start.6 = (bf16[8,48,384]{2,1,0:T(8,128)(2,1)S(1)}, bf16[8,48,384]{2,1,0:T(8,128)(2,1)}, u32[]{:S(2)}, u32[]{:S(2)}) collective-permute-start(bf16[8,48,384]{2,1,0:T(8,128)(2,1)S(1)} %get-tuple-element.44), channel_id=1, source_target_pairs={{0,32},{16,48},{32,0},{48,16},{1,33},{17,49},{33,1},{49,17},{2,34}... | collective-permute-start | bytes 884744 | tf_op jit(solution)/shard_map/ppermute | solution.py:366
  101.1 31.1 %collective-permute-start.8 = (bf16[112,384]{1,0:T(8,128)(2,1)S(1)}, bf16[112,384]{1,0:T(8,128)(2,1)S(1)}, u32[]{:S(2)}, u32[]{:S(2)}) collective-permute-start(bf16[112,384]{1,0:T(8,128)(2,1)S(1)} %maximum_maximum_fusion), channel_id=1, source_target_pairs={{0,2},{2,0},{1,3},{3,1},{4,6},{6,4},{5,7},{7,5},{8,10},{10,8},{9,1... | collective-permute-start | bytes 258056 | tf_op jit(solution)/shard_map/ppermute | solution.py:20
  115.1 17.2 %collective-permute-start.7 = (bf16[4,48,384]{2,1,0:T(8,128)(2,1)S(1)}, bf16[4,48,384]{2,1,0:T(8,128)(2,1)S(1)}, u32[]{:S(2)}, u32[]{:S(2)}) collective-permute-start(bf16[4,48,384]{2,1,0:T(8,128)(2,1)S(1)} %fusion.2), channel_id=1, source_target_pairs={{0,64},{64,0},{128,192},{192,128},{256,320},{320,256},{384,448},{4... | collective-permute-start | bytes 442376 | tf_op jit(solution)/shard_map/ppermute | solution.py:401
  125.1 28.8 %all-to-all-start.2 = ((f32[64,2,96]{2,1,0:T(2,128)}), f32[64,2,96]{2,1,0:T(2,128)S(1)}, u32[]{:S(2)}, u32[]{:S(2)}) async-start(f32[64,2,96]{2,1,0:T(2,128)} %bitcast.24), calls=%async_computation.2 | async-start | bytes 131072 | tf_op jit(solution)/shard_map/all_to_all | solution.py:384
  132.4 13.9 %collective-permute-start.10 = (bf16[48,384]{1,0:T(8,128)(2,1)S(1)}, bf16[48,384]{1,0:T(8,128)(2,1)S(1)}, u32[]{:S(2)}, u32[]{:S(2)}) collective-permute-start(bf16[48,384]{1,0:T(8,128)(2,1)S(1)} %get-tuple-element.70), channel_id=1, source_target_pairs={{0,256},{64,320},{128,384},{192,448},{256,0},{320,64},{384,128},{4... | collective-permute-start | bytes 110600 | tf_op jit(solution)/shard_map/ppermute | solution.py:415
  139.3 7.0 %collective-permute-start.11 = (bf16[48,384]{1,0:T(8,128)(2,1)S(1)}, bf16[48,384]{1,0:T(8,128)(2,1)S(1)}, u32[]{:S(2)}, u32[]{:S(2)}) collective-permute-start(bf16[48,384]{1,0:T(8,128)(2,1)S(1)} %get-tuple-element.69), channel_id=1, source_target_pairs={{0,128},{64,192},{128,0},{192,64},{256,384},{320,448},{384,256},{4... | collective-permute-start | bytes 110600 | tf_op jit(solution)/shard_map/ppermute | solution.py:415
  143.4 10.4 %collective-permute-start.9 = (bf16[48,384]{1,0:T(8,128)(2,1)S(1)}, bf16[48,384]{1,0:T(8,128)(2,1)S(1)}, u32[]{:S(2)}, u32[]{:S(2)}) collective-permute-start(bf16[48,384]{1,0:T(8,128)(2,1)S(1)} %get-tuple-element.68), channel_id=1, source_target_pairs={{0,384},{64,448},{128,256},{192,320},{256,128},{320,192},{384,0},{... | collective-permute-start | bytes 110600 | tf_op jit(solution)/shard_map/ppermute | solution.py:415

commit v10 on v9

--- a/solution.py
+++ b/solution.py
@@ -366,6 +366,17 @@
         lax.ppermute(sent, "y", [(i, (i + step) % 4) for i in range(4)])
         for step, sent in zip((1, 3, 2), pieces[1:])
     ]
+    total = pieces[0].astype(f32)
+    for part in parts:
+        total = total + part.astype(f32)
+
+    side = zl % 2
+    total = total.reshape(4, 2, piece, 4 * width)
+    sent = lax.dynamic_slice_in_dim(total, 1 - side, 1, 1)[:, 0].astype(bf16)
+    total = lax.dynamic_slice_in_dim(total, side, 1, 1)[:, 0]
+    sent, mixed = lax.optimization_barrier((sent, mixed))
+    total = total + lax.ppermute(sent, "zl", [(i, i ^ 1) for i in range(8)]).astype(f32)
+
     mixed = jnp.sum(mixed.astype(f32), axis=0)
     near = mixed[width : 2 * width]
     inv_std = stats[1:2, :rows]
@@ -386,22 +397,8 @@
         FRAME + ("zh",), 0, 0, tiled=True,
     )
 
-    total, far_copy = lax.optimization_barrier((pieces[0], far))
-    total = total.astype(f32)
-    for part in parts:
-        total = total + part.astype(f32)
-
-    def block(index):
-        return lax.dynamic_slice_in_dim(total, index, 1, 0)[0]
-
-    side = zl % 2
-    total = total.reshape(4, 2, piece, 4 * width)
-    sent = lax.dynamic_slice_in_dim(total, 1 - side, 1, 1)[:, 0].astype(bf16)
-    total = lax.dynamic_slice_in_dim(total, side, 1, 1)[:, 0]
-    total = total + lax.ppermute(sent, "zl", [(i, i ^ 1) for i in range(8)]).astype(f32)
-
     normed_grad = near + came[:width]
-    kept = far_copy[width : width + 4].astype(f32)
+    kept = far[width : width + 4].astype(f32)
     sums = (kept[:2] + kept[2:] + came[width : width + 2] + came[width + 2 : width + 4]) / model
     total, normed_grad = lax.optimization_barrier((total, normed_grad))
     inputs_grad = (
@@ -409,10 +406,13 @@
         + inv_std * (normed_grad * gain_local - sums[0:1] - centred * sums[1:2])
     ).astype(bf16)
 
-    grads = block(zl // 2)
-    for step in (3, 2, 1):
-        sent = block((zl // 2) ^ step).astype(bf16)
-        grads = grads + lax.ppermute(sent, "zl", [(i, i ^ (2 * step)) for i in range(8)]).astype(f32)
+    for size in (2, 4):
+        side = (zl // size) % 2
+        total = total.reshape(4 // size, 2, piece, 4 * width)
+        sent = lax.dynamic_slice_in_dim(total, 1 - side, 1, 1)[:, 0].astype(bf16)
+        total = lax.dynamic_slice_in_dim(total, side, 1, 1)[:, 0]
+        total = total + lax.ppermute(sent, "zl", [(i, i ^ size) for i in range(8)]).astype(f32)
+    grads = total[0]
     tail, grads = lax.optimization_barrier((tail, grads))
     tail = jnp.sum(tail, axis=0)
     kernel_grad = grads[:taps, :width]

time: 159 us -> 158 us (level)
    ppermute x3, waiting for transfers between devices: 0.01 us -> 9.21 us  [on_device(): lax.ppermute(sent, 'y', [(i, (i + step) % 4) for i in range(4)])]
    all_to_all x1, waiting for transfers between devices: 8.37 us -> 0.01 us  [on_device(): mixed = lax.all_to_all(mixed, ('x', 'core'), 0, 0, tiled=True)]
    all_to_all x1, starting transfers between devices: 7.12 us -> 10 us  [on_device(): lax.all_to_all(jnp.broadcast_to(tail[None], (32, 2, 2, width)).reshape(64...]
    ppermute x3 -> x2, waiting for transfers between devices: 7.52 us -> 5.3 us  [on_device(): lax.ppermute(sent, 'zl', [(i, i ^ size) for i in range(8)]).astype(f32)]
    ppermute x3 -> x2, starting transfers between devices: 13.2 us -> 11.3 us  [on_device(): lax.ppermute(sent, 'zl', [(i, i ^ size) for i in range(8)]).astype(f32)]
  transfers between devices with their start and end apart: 14 -> 13, of which waited for: 4 -> 6; matrix products, arithmetic and copies ran while one was open for 9% -> 8% of each run, Pallas kernels for 0% -> 0%
where the time goes in v10:
time: 158 us; the launch traced here: 156 us
  starting transfers between devices  91.7 us (58%)
  waiting for transfers between devices  19.4 us (12%)
  blocking collectives  15.4 us (10%)
  Pallas kernels  11.5 us (7%)
  local copies, waits for them, and re-layouts  9.87 us (6%)
  other arithmetic  6.41 us (4%)
    ppermute x3, starting transfers between devices, swap(): return lax.ppermute(value, axis, SWAP)  43.6 us
    all_to_all x1, blocking collectives, over_x(): lax.all_to_all(jnp.broadcast_to(pair[None], (4,) + pair.shape), 'x', 0, 0...  15.4 us
    ppermute x2, starting transfers between devices, on_device(): lax.ppermute(sent, 'zl', [(i, i ^ size) for i in range(8)]).astype(f32)  11.3 us
    pallas_call x1, Pallas kernels, on_device(): pl.pallas_call(middle, out_shape=(pltpu.HBM((8, 2 * width + 16, rows), bf...  10.6 us
    all_to_all x1, starting transfers between devices, on_device(): lax.all_to_all(jnp.broadcast_to(tail[None], (32, 2, 2, width)).reshape(64...  10 us
    ppermute x1, starting transfers between devices, on_device(): lax.ppermute(sent, 'zl', [(i, i ^ 1) for i in range(8)]).astype(f32)  9.28 us
    ppermute x3, waiting for transfers between devices, on_device(): lax.ppermute(sent, 'y', [(i, (i + step) % 4) for i in range(4)])  9.21 us
    ppermute x3, starting transfers between devices, on_device(): lax.ppermute(sent, 'y', [(i, (i + step) % 4) for i in range(4)])  8.4 us
  transfers between devices with their start and end apart: 13, of which 6 were waited for; matrix products, arithmetic and copies ran while one was open for 8% of the time, Pallas kernels for 0%

profile of v10, /device:TPU:1, one launch (start us, length us, event | category | flops | bytes accessed | tf_op | source)
XLA Modules:
  0.0 155.5 jit_solution(16943377534704565110)
XLA Ops:
  1.3 0.9 shard_map.144
  2.3 4.0 %collective-permute-start = (bf16[112,128]{1,0:T(8,128)(2,1)S(1)}, bf16[112,128]{1,0:T(8,128)(2,1)S(1)}, u32[]{:S(2)}, u32[]{:S(2)}) collective-permute-start(bf16[112,128]{1,0:T(8,128)(2,1)S(1)} %get-tuple-element.30), channel_id=1, source_target_pairs={{0,16},{16,32},{32,48},{48,64},{64,80},{80,96},{96,112},{112,128},... | collective-permute-start | bytes 86024 | tf_op jit(solution)/shard_map/ppermute | solution.py:297
  6.3 1.3 collective-permute-start.1
  7.6 0.8 reshape.52
  8.4 0.8 reshape.54
  9.2 1.2 copy.29
  10.4 1.2 copy.30
  11.6 1.1 fusion
  12.7 1.3 fusion.8
  14.7 0.8 select_maximum_fusion.small_hbm
  15.6 15.4 %collective-permute-start.2 = (bf16[96,896]{1,0:T(8,128)(2,1)S(1)}, bf16[96,896]{1,0:T(8,128)(2,1)S(1)}, u32[]{:S(2)}, u32[]{:S(2)}) collective-permute-start(bf16[96,896]{1,0:T(8,128)(2,1)S(1)} %get-tuple-element.69), channel_id=1, source_target_pairs={{0,2},{2,0},{1,3},{3,1},{4,6},{6,4},{5,7},{7,5},{8,10},{10,8},{9,1... | collective-permute-start | bytes 516104 | tf_op jit(solution)/shard_map/ppermute | solution.py:20
  31.7 3.1 %collective-permute-done.2 = bf16[96,896]{1,0:T(8,128)(2,1)S(1)} collective-permute-done((bf16[96,896]{1,0:T(8,128)(2,1)S(1)}, bf16[96,896]{1,0:T(8,128)(2,1)S(1)}, u32[]{:S(2)}, u32[]{:S(2)}) %collective-permute-start.2) | collective-permute-done | bytes 172064 | tf_op jit(solution)/shard_map/ppermute | solution.py:20
  34.9 15.4 %all_to_all.15.own_hbm = bf16[4,2,96,896]{3,2,1,0:T(8,128)(2,1)S(1)} all-to-all(bf16[4,2,96,896]{3,2,1,0:T(8,128)(2,1)S(1)} %broadcast_in_dim.33), channel_id=1, replica_groups=mesh['zl'=8,'y'=4,'x'=4,'zh'=2,'core'=2] {'x'}, dimensions={0} | all-to-all | bytes 2752512 | tf_op jit(solution)/shard_map/all_to_all | solution.py:24
  50.3 15.2 %collective-permute-start.3 = (bf16[4,2,96,896]{3,2,1,0:T(8,128)(2,1)S(1)}, bf16[4,2,96,896]{3,2,1,0:T(8,128)(2,1)}, u32[]{:S(2)}, u32[]{:S(2)}) collective-permute-start(bf16[4,2,96,896]{3,2,1,0:T(8,128)(2,1)S(1)} %all_to_all.15.own_hbm), channel_id=1, source_target_pairs={{0,1},{1,0},{2,3},{3,2},{4,5},{5,4},{6,7},{7,6},{8,9},{9,8},{10,11... | collective-permute-start | bytes 4128776 | tf_op jit(solution)/shard_map/ppermute | solution.py:20
  65.6 1.1 copy.35.weight_hbm
  66.6 1.8 %collective-permute-done.3.other_hbm = bf16[4,2,96,896]{3,2,1,0:T(8,128)(2,1)} collective-permute-done((bf16[4,2,96,896]{3,2,1,0:T(8,128)(2,1)S(1)}, bf16[4,2,96,896]{3,2,1,0:T(8,128)(2,1)}, u32[]{:S(2)}, u32[]{:S(2)}) %collective-permute-start.3) | collective-permute-done | bytes 1376288 | tf_op jit(solution)/shard_map/ppermute | solution.py:20
  68.4 10.6 %shard_map.145 = (bf16[8,208,384]{2,1,0:T(8,128)(2,1)}, bf16[8,48,384]{2,1,0:T(8,128)(2,1)S(1)}, bf16[8,48,384]{2,1,0:T(8,128)(2,1)S(1)}, bf16[8,48,384]{2,1,0:T...) custom-call(s32[3]{0:T(128)S(1)} %pad_add_fusion.where_ref, bf16[4,2,96,896]{3,2,1,0:T(8,128)(2,1)} %copy-done, ...), custom_call_target="tpu_custom_call" | custom-call | tf_op jit(solution)/shard_map/pallas_call | solution.py:334
  79.0 3.8 %all-to-all-start.1 = ((bf16[8,208,384]{2,1,0:T(8,128)(2,1)}), bf16[8,208,384]{2,1,0:T(8,128)(2,1)S(1)}, u32[]{:S(2)}, u32[]{:S(2)}) async-start(bf16[8,208,384]{2,1,0:T(8,128)(2,1)} %get-tuple-element.43), calls=%async_computation.1 | async-start | bytes 2555904 | tf_op jit(solution)/shard_map/all_to_all | solution.py:363
  82.9 1.9 %collective-permute-start.4 = (bf16[8,48,384]{2,1,0:T(8,128)(2,1)S(1)}, bf16[8,48,384]{2,1,0:T(8,128)(2,1)S(1)}, u32[]{:S(2)}, u32[]{:S(2)}) collective-permute-start(bf16[8,48,384]{2,1,0:T(8,128)(2,1)S(1)} %get-tuple-element.40), channel_id=1, source_target_pairs={{0,16},{16,32},{32,48},{48,0},{1,17},{17,33},{33,49},{49,1},{2,18}... | collective-permute-start | bytes 884744 | tf_op jit(solution)/shard_map/ppermute | solution.py:366
  84.8 4.6 %collective-permute-start.5 = (bf16[8,48,384]{2,1,0:T(8,128)(2,1)S(1)}, bf16[8,48,384]{2,1,0:T(8,128)(2,1)S(1)}, u32[]{:S(2)}, u32[]{:S(2)}) collective-permute-start(bf16[8,48,384]{2,1,0:T(8,128)(2,1)S(1)} %get-tuple-element.41), channel_id=1, source_target_pairs={{0,48},{16,0},{32,16},{48,32},{1,49},{17,1},{33,17},{49,33},{2,50}... | collective-permute-start | bytes 884744 | tf_op jit(solution)/shard_map/ppermute | solution.py:366
  89.4 1.9 %collective-permute-start.6 = (bf16[8,48,384]{2,1,0:T(8,128)(2,1)S(1)}, bf16[8,48,384]{2,1,0:T(8,128)(2,1)S(1)}, u32[]{:S(2)}, u32[]{:S(2)}) collective-permute-start(bf16[8,48,384]{2,1,0:T(8,128)(2,1)S(1)} %get-tuple-element.42), channel_id=1, source_target_pairs={{0,32},{16,48},{32,0},{48,16},{1,33},{17,49},{33,1},{49,17},{2,34}... | collective-permute-start | bytes 884744 | tf_op jit(solution)/shard_map/ppermute | solution.py:366
  91.5 0.8 slice_reduce_fusion.4
  92.3 2.2 %collective-permute-done.4 = bf16[8,48,384]{2,1,0:T(8,128)(2,1)S(1)} collective-permute-done((bf16[8,48,384]{2,1,0:T(8,128)(2,1)S(1)}, bf16[8,48,384]{2,1,0:T(8,128)(2,1)S(1)}, u32[]{:S(2)}, u32[]{:S(2)}) %collective-permute-start.4) | collective-permute-done | bytes 294944 | tf_op jit(solution)/shard_map/ppermute | solution.py:366
  94.4 7.0 %collective-permute-done.5 = bf16[8,48,384]{2,1,0:T(8,128)(2,1)S(1)} collective-permute-done((bf16[8,48,384]{2,1,0:T(8,128)(2,1)S(1)}, bf16[8,48,384]{2,1,0:T(8,128)(2,1)S(1)}, u32[]{:S(2)}, u32[]{:S(2)}) %collective-permute-start.5) | collective-permute-done | bytes 294944 | tf_op jit(solution)/shard_map/ppermute | solution.py:366
  102.0 12.9 %collective-permute-start.8 = (bf16[112,384]{1,0:T(8,128)(2,1)S(1)}, bf16[112,384]{1,0:T(8,128)(2,1)S(1)}, u32[]{:S(2)}, u32[]{:S(2)}) collective-permute-start(bf16[112,384]{1,0:T(8,128)(2,1)S(1)} %maximum_maximum_fusion), channel_id=1, source_target_pairs={{0,2},{2,0},{1,3},{3,1},{4,6},{6,4},{5,7},{7,5},{8,10},{10,8},{9,1... | collective-permute-start | bytes 258056 | tf_op jit(solution)/shard_map/ppermute | solution.py:20
  114.9 1.1 multiply_reduce_fusion.1
  116.0 9.3 %collective-permute-start.7 = (bf16[4,48,384]{2,1,0:T(8,128)(2,1)S(1)}, bf16[4,48,384]{2,1,0:T(8,128)(2,1)S(1)}, u32[]{:S(2)}, u32[]{:S(2)}) collective-permute-start(bf16[4,48,384]{2,1,0:T(8,128)(2,1)S(1)} %fusion.2), channel_id=1, source_target_pairs={{0,64},{64,0},{128,192},{192,128},{256,320},{320,256},{384,448},{4... | collective-permute-start | bytes 442376 | tf_op jit(solution)/shard_map/ppermute | solution.py:378
  125.9 10.0 %all-to-all-start.2 = ((f32[64,2,96]{2,1,0:T(2,128)}), f32[64,2,96]{2,1,0:T(2,128)S(1)}, u32[]{:S(2)}, u32[]{:S(2)}) async-start(f32[64,2,96]{2,1,0:T(2,128)} %bitcast.24), calls=%async_computation.2 | async-start | bytes 131072 | tf_op jit(solution)/shard_map/all_to_all | solution.py:395
  136.1 3.8 %collective-permute-start.9 = (bf16[2,48,384]{2,1,0:T(8,128)(2,1)S(1)}, bf16[2,48,384]{2,1,0:T(8,128)(2,1)S(1)}, u32[]{:S(2)}, u32[]{:S(2)}) collective-permute-start(bf16[2,48,384]{2,1,0:T(8,128)(2,1)S(1)} %fusion.4), channel_id=1, source_target_pairs={{0,128},{64,192},{128,0},{192,64},{256,384},{320,448},{384,256},{4... | collective-permute-start | bytes 221192 | tf_op jit(solution)/shard_map/ppermute | solution.py:414
  140.0 4.3 %collective-permute-done.9 = bf16[2,48,384]{2,1,0:T(8,128)(2,1)S(1)} collective-permute-done((bf16[2,48,384]{2,1,0:T(8,128)(2,1)S(1)}, bf16[2,48,384]{2,1,0:T(8,128)(2,1)S(1)}, u32[]{:S(2)}, u32[]{:S(2)}) %collective-permute-start.9) | collective-permute-done | bytes 73760 | tf_op jit(solution)/shard_map/ppermute | solution.py:414
  144.3 7.5 %collective-permute-start.10 = (bf16[1,48,384]{2,1,0:T(8,128)(2,1)S(1)}, bf16[1,48,384]{2,1,0:T(8,128)(2,1)S(1)}, u32[]{:S(2)}, u32[]{:S(2)}) collective-permute-start(bf16[1,48,384]{2,1,0:T(8,128)(2,1)S(1)} %dynamic-slice_convert_fusion.1), channel_id=1, source_target_pairs={{0,256},{64,320},{128,384},{192,448},{256,0},{320,64},{384,128},{4... | collective-permute-start | bytes 110600 | tf_op jit(solution)/shard_map/ppermute | solution.py:414
  152.6 1.0 collective-permute-done.10
  (72 shorter events, 6.2 us)
Async XLA Ops:
  0.6 10.9 %copy-start.5 = (f32[1536]{0:T(1024)S(1)}, f32[1536]{0:T(1024)}, u32[]{:S(2)}) copy-start(f32[1536]{0:T(1024)} %param.10) | copy-start | bytes 18436
  0.6 10.9 %copy-start.4 = (f32[1536]{0:T(1024)S(1)}, f32[1536]{0:T(1024)}, u32[]{:S(2)}) copy-start(f32[1536]{0:T(1024)} %param.11) | copy-start | bytes 18436
  2.3 13.3 %collective-permute-start = (bf16[112,128]{1,0:T(8,128)(2,1)S(1)}, bf16[112,128]{1,0:T(8,128)(2,1)S(1)}, u32[]{:S(2)}, u32[]{:S(2)}) collective-permute-start(bf16[112,128]{1,0:T(8,128)(2,1)S(1)} %get-tuple-element.30), channel_id=1, source_target_pairs={{0,16},{16,32},{32,48},{48,64},{64,80},{80,96},{96,112},{112,128},... | collective-permute-start | bytes 86024 | tf_op jit(solution)/shard_map/ppermute | solution.py:297
  6.3 9.2 %collective-permute-start.1 = (bf16[112,128]{1,0:T(8,128)(2,1)S(1)}, bf16[112,128]{1,0:T(8,128)(2,1)S(1)}, u32[]{:S(2)}, u32[]{:S(2)}) collective-permute-start(bf16[112,128]{1,0:T(8,128)(2,1)S(1)} %get-tuple-element.31), channel_id=1, source_target_pairs={{16,0},{32,16},{48,32},{64,48},{80,64},{96,80},{112,96},{128,112},... | collective-permute-start | bytes 86024 | tf_op jit(solution)/shard_map/ppermute | solution.py:297
  12.7 1.8 %copy-start.6 = (f32[31,96]{1,0:T(8,128)S(1)}, f32[31,96]{1,0:T(8,128)}, u32[]{:S(2)}) copy-start(f32[31,96]{1,0:T(8,128)} %param.14) | copy-start | bytes 35716
  12.7 2.8 %copy-start.7 = (s32[384]{0:T(512)S(1)}, s32[384]{0:T(512)}, u32[]{:S(2)}) copy-start(s32[384]{0:T(512)} %param.16) | copy-start | bytes 4612
  12.7 2.9 %copy-start.1 = (bf16[96,384]{1,0:T(8,128)(2,1)S(1)}, bf16[96,384]{1,0:T(8,128)(2,1)}, u32[]{:S(2)}) copy-start(bf16[96,384]{1,0:T(8,128)(2,1)} %inputs_hbm.1) | copy-start | bytes 221188
  12.7 2.9 %copy-start.2 = (bf16[96,384]{1,0:T(8,128)(2,1)S(1)}, bf16[96,384]{1,0:T(8,128)(2,1)}, u32[]{:S(2)}) copy-start(bf16[96,384]{1,0:T(8,128)(2,1)} %upstream_hbm.1) | copy-start | bytes 221188
  15.6 19.1 %collective-permute-start.2 = (bf16[96,896]{1,0:T(8,128)(2,1)S(1)}, bf16[96,896]{1,0:T(8,128)(2,1)S(1)}, u32[]{:S(2)}, u32[]{:S(2)}) collective-permute-start(bf16[96,896]{1,0:T(8,128)(2,1)S(1)} %get-tuple-element.69), channel_id=1, source_target_pairs={{0,2},{2,0},{1,3},{3,1},{4,6},{6,4},{5,7},{7,5},{8,10},{10,8},{9,1... | collective-permute-start | bytes 516104 | tf_op jit(solution)/shard_map/ppermute | solution.py:20
  34.8 15.6 %copy-start.3 = (bf16[96,896]{1,0:T(8,128)(2,1)}, bf16[96,896]{1,0:T(8,128)(2,1)S(1)}, u32[]{:S(2)}) copy-start(bf16[96,896]{1,0:T(8,128)(2,1)S(1)} %collective-permute-done.2) | copy-start | bytes 516100
  50.3 18.1 %copy-start = (bf16[4,2,96,896]{3,2,1,0:T(8,128)(2,1)}, bf16[4,2,96,896]{3,2,1,0:T(8,128)(2,1)S(1)}, u32[]{:S(2)}) copy-start(bf16[4,2,96,896]{3,2,1,0:T(8,128)(2,1)S(1)} %all_to_all.15.own_hbm) | copy-start | bytes 4128772
  50.3 18.1 %collective-permute-start.3 = (bf16[4,2,96,896]{3,2,1,0:T(8,128)(2,1)S(1)}, bf16[4,2,96,896]{3,2,1,0:T(8,128)(2,1)}, u32[]{:S(2)}, u32[]{:S(2)}) collective-permute-start(bf16[4,2,96,896]{3,2,1,0:T(8,128)(2,1)S(1)} %all_to_all.15.own_hbm), channel_id=1, source_target_pairs={{0,1},{1,0},{2,3},{3,2},{4,5},{5,4},{6,7},{7,6},{8,9},{9,8},{10,11... | collective-permute-start | bytes 4128776 | tf_op jit(solution)/shard_map/ppermute | solution.py:20
  79.0 22.6 %all-to-all-start.1 = ((bf16[8,208,384]{2,1,0:T(8,128)(2,1)}), bf16[8,208,384]{2,1,0:T(8,128)(2,1)S(1)}, u32[]{:S(2)}, u32[]{:S(2)}) async-start(bf16[8,208,384]{2,1,0:T(8,128)(2,1)} %get-tuple-element.43), calls=%async_computation.1 | async-start | bytes 2555904 | tf_op jit(solution)/shard_map/all_to_all | solution.py:363
  82.9 11.6 %collective-permute-start.4 = (bf16[8,48,384]{2,1,0:T(8,128)(2,1)S(1)}, bf16[8,48,384]{2,1,0:T(8,128)(2,1)S(1)}, u32[]{:S(2)}, u32[]{:S(2)}) collective-permute-start(bf16[8,48,384]{2,1,0:T(8,128)(2,1)S(1)} %get-tuple-element.40), channel_id=1, source_target_pairs={{0,16},{16,32},{32,48},{48,0},{1,17},{17,33},{33,49},{49,1},{2,18}... | collective-permute-start | bytes 884744 | tf_op jit(solution)/shard_map/ppermute | solution.py:366
  84.8 16.7 %collective-permute-start.5 = (bf16[8,48,384]{2,1,0:T(8,128)(2,1)S(1)}, bf16[8,48,384]{2,1,0:T(8,128)(2,1)S(1)}, u32[]{:S(2)}, u32[]{:S(2)}) collective-permute-start(bf16[8,48,384]{2,1,0:T(8,128)(2,1)S(1)} %get-tuple-element.41), channel_id=1, source_target_pairs={{0,48},{16,0},{32,16},{48,32},{1,49},{17,1},{33,17},{49,33},{2,50}... | collective-permute-start | bytes 884744 | tf_op jit(solution)/shard_map/ppermute | solution.py:366
  89.4 12.1 %collective-permute-start.6 = (bf16[8,48,384]{2,1,0:T(8,128)(2,1)S(1)}, bf16[8,48,384]{2,1,0:T(8,128)(2,1)S(1)}, u32[]{:S(2)}, u32[]{:S(2)}) collective-permute-start(bf16[8,48,384]{2,1,0:T(8,128)(2,1)S(1)} %get-tuple-element.42), channel_id=1, source_target_pairs={{0,32},{16,48},{32,0},{48,16},{1,33},{17,49},{33,1},{49,17},{2,34}... | collective-permute-start | bytes 884744 | tf_op jit(solution)/shard_map/ppermute | solution.py:366
  102.0 34.0 %collective-permute-start.8 = (bf16[112,384]{1,0:T(8,128)(2,1)S(1)}, bf16[112,384]{1,0:T(8,128)(2,1)S(1)}, u32[]{:S(2)}, u32[]{:S(2)}) collective-permute-start(bf16[112,384]{1,0:T(8,128)(2,1)S(1)} %maximum_maximum_fusion), channel_id=1, source_target_pairs={{0,2},{2,0},{1,3},{3,1},{4,6},{6,4},{5,7},{7,5},{8,10},{10,8},{9,1... | collective-permute-start | bytes 258056 | tf_op jit(solution)/shard_map/ppermute | solution.py:20
  116.0 20.0 %collective-permute-start.7 = (bf16[4,48,384]{2,1,0:T(8,128)(2,1)S(1)}, bf16[4,48,384]{2,1,0:T(8,128)(2,1)S(1)}, u32[]{:S(2)}, u32[]{:S(2)}) collective-permute-start(bf16[4,48,384]{2,1,0:T(8,128)(2,1)S(1)} %fusion.2), channel_id=1, source_target_pairs={{0,64},{64,0},{128,192},{192,128},{256,320},{320,256},{384,448},{4... | collective-permute-start | bytes 442376 | tf_op jit(solution)/shard_map/ppermute | solution.py:378
  125.9 27.6 %all-to-all-start.2 = ((f32[64,2,96]{2,1,0:T(2,128)}), f32[64,2,96]{2,1,0:T(2,128)S(1)}, u32[]{:S(2)}, u32[]{:S(2)}) async-start(f32[64,2,96]{2,1,0:T(2,128)} %bitcast.24), calls=%async_computation.2 | async-start | bytes 131072 | tf_op jit(solution)/shard_map/all_to_all | solution.py:395
  136.1 8.2 %collective-permute-start.9 = (bf16[2,48,384]{2,1,0:T(8,128)(2,1)S(1)}, bf16[2,48,384]{2,1,0:T(8,128)(2,1)S(1)}, u32[]{:S(2)}, u32[]{:S(2)}) collective-permute-start(bf16[2,48,384]{2,1,0:T(8,128)(2,1)S(1)} %fusion.4), channel_id=1, source_target_pairs={{0,128},{64,192},{128,0},{192,64},{256,384},{320,448},{384,256},{4... | collective-permute-start | bytes 221192 | tf_op jit(solution)/shard_map/ppermute | solution.py:414
  144.3 9.2 %collective-permute-start.10 = (bf16[1,48,384]{2,1,0:T(8,128)(2,1)S(1)}, bf16[1,48,384]{2,1,0:T(8,128)(2,1)S(1)}, u32[]{:S(2)}, u32[]{:S(2)}) collective-permute-start(bf16[1,48,384]{2,1,0:T(8,128)(2,1)S(1)} %dynamic-slice_convert_fusion.1), channel_id=1, source_target_pairs={{0,256},{64,320},{128,384},{192,448},{256,0},{320,64},{384,128},{4... | collective-permute-start | bytes 110600 | tf_op jit(solution)/shard_map/ppermute | solution.py:414

commit v11 on v10

--- a/solution.py
+++ b/solution.py
@@ -259,6 +259,15 @@
         out[...] = grads_ref[:, lax.rem(where_ref[2] + step, 4)]
     for started in finished:
         started.wait()
+
+
+def unpack(total_ref, part_ref, value_ref, gate_ref, project_ref, kernel_ref):
+    taps, width = kernel_ref.shape
+    total = total_ref[...] + part_ref[...].astype(f32)
+    kernel_ref[...] = total[:taps, :width]
+    turned = jnp.transpose(total)
+    for i, ref in enumerate((value_ref, gate_ref, project_ref)):
+        ref[...] = turned[(i + 1) * width : (i + 2) * width]
 
 
 def on_device(
@@ -390,35 +399,38 @@
     far = jnp.concatenate(
         [mixed[:width].astype(bf16), sent_high, sent_low, jnp.zeros((12, rows), bf16)]
     )
-    came = swap(far, "zh").astype(f32)
-
     tail = lax.all_to_all(
         jnp.broadcast_to(tail[None], (32, 2, 2, width)).reshape(64, 2, width),
         FRAME + ("zh",), 0, 0, tiled=True,
     )
 
+    side = (zl // 2) % 2
+    total = total.reshape(2, 2, piece, 4 * width)
+    sent = lax.dynamic_slice_in_dim(total, 1 - side, 1, 1)[:, 0].astype(bf16)
+    total = lax.dynamic_slice_in_dim(total, side, 1, 1)[:, 0]
+    far, sent = lax.optimization_barrier((far, sent))
+    total = total + lax.ppermute(sent, "zl", [(i, i ^ 2) for i in range(8)]).astype(f32)
+    came = swap(far, "zh").astype(f32)
+
     normed_grad = near + came[:width]
     kept = far[width : width + 4].astype(f32)
     sums = (kept[:2] + kept[2:] + came[width : width + 2] + came[width + 2 : width + 4]) / model
-    total, normed_grad = lax.optimization_barrier((total, normed_grad))
     inputs_grad = (
         upstream.astype(f32)
         + inv_std * (normed_grad * gain_local - sums[0:1] - centred * sums[1:2])
     ).astype(bf16)
 
-    for size in (2, 4):
-        side = (zl // size) % 2
-        total = total.reshape(4 // size, 2, piece, 4 * width)
-        sent = lax.dynamic_slice_in_dim(total, 1 - side, 1, 1)[:, 0].astype(bf16)
-        total = lax.dynamic_slice_in_dim(total, side, 1, 1)[:, 0]
-        total = total + lax.ppermute(sent, "zl", [(i, i ^ size) for i in range(8)]).astype(f32)
-    grads = total[0]
-    tail, grads = lax.optimization_barrier((tail, grads))
+    side = zl // 4
+    sent = lax.dynamic_slice_in_dim(total, 1 - side, 1, 0)[0].astype(bf16)
+    total = lax.dynamic_slice_in_dim(total, side, 1, 0)[0]
+    part = lax.ppermute(sent, "zl", [(i, i ^ 4) for i in range(8)])
+    tail, part = lax.optimization_barrier((tail, part))
+    value_grad, gate_grad, project_grad, kernel_grad = call(
+        unpack,
+        tuple(shape((width, piece), f32) for _ in range(3)) + (shape((taps, width), f32),),
+        specs=[VMEM] * 2,
+    )(total, part)
     tail = jnp.sum(tail, axis=0)
-    kernel_grad = grads[:taps, :width]
-    value_grad = grads[:, width : 2 * width].T
-    gate_grad = grads[:, 2 * width : 3 * width].T
-    project_grad = grads[:, 3 * width :].T
     return (inputs_grad, value_grad, gate_grad, project_grad, kernel_grad, tail[0], tail[1])
 
 

time: 158 us -> 159 us (level)
  waiting for transfers between devices: 19.4 us -> 21.2 us
    all_to_all x1, starting transfers between devices: 10 us -> 15.8 us  [on_device(): lax.all_to_all(jnp.broadcast_to(tail[None], (32, 2, 2, width)).reshape(64...]
    ppermute x2, starting transfers between devices: 11.3 us -> 6.23 us  [the longest x1 3.83 us: on_device(): lax.ppermute(sent, 'zl', [(i, i ^ 2) for i in range(8)]).astype(f32)]
    ppermute x3, starting transfers between devices: 43.6 us -> 40.7 us  [swap(): return lax.ppermute(value, axis, SWAP)]
    unnamed x19 -> x22, local copies, waits for them, and re-layouts: 2.51 us -> 4.57 us
where the time goes in v11:
time: 159 us; the launch traced here: 157 us
  starting transfers between devices  90.3 us (57%)
  waiting for transfers between devices  21.2 us (13%)
  blocking collectives  15.4 us (10%)
  Pallas kernels  12.1 us (8%)
  local copies, waits for them, and re-layouts  10.6 us (7%)
  other arithmetic  6.38 us (4%)
    ppermute x3, starting transfers between devices, swap(): return lax.ppermute(value, axis, SWAP)  40.7 us
    all_to_all x1, starting transfers between devices, on_device(): lax.all_to_all(jnp.broadcast_to(tail[None], (32, 2, 2, width)).reshape(64...  15.8 us
    all_to_all x1, blocking collectives, over_x(): lax.all_to_all(jnp.broadcast_to(pair[None], (4,) + pair.shape), 'x', 0, 0...  15.4 us
    pallas_call x1, Pallas kernels, on_device(): pl.pallas_call(middle, out_shape=(pltpu.HBM((8, 2 * width + 16, rows), bf...  10.6 us
    ppermute x1, starting transfers between devices, on_device(): lax.ppermute(sent, 'zl', [(i, i ^ 1) for i in range(8)]).astype(f32)  10 us
    ppermute x3, waiting for transfers between devices, on_device(): lax.ppermute(sent, 'y', [(i, (i + step) % 4) for i in range(4)])  9.23 us
    ppermute x3, starting transfers between devices, on_device(): lax.ppermute(sent, 'y', [(i, (i + step) % 4) for i in range(4)])  8.4 us
    ppermute x3, waiting for transfers between devices, swap(): return lax.ppermute(value, axis, SWAP)  6.35 us
  transfers between devices with their start and end apart: 13, of which 6 were waited for; matrix products, arithmetic and copies ran while one was open for 8% of the time, Pallas kernels for 0%

profile of v11, /device:TPU:1, one launch (start us, length us, event | category | flops | bytes accessed | tf_op | source)
XLA Modules:
  0.0 157.2 jit_solution(456254233388766286)
XLA Ops:
  1.3 0.9 shard_map.144
  2.3 4.0 %collective-permute-start = (bf16[112,128]{1,0:T(8,128)(2,1)S(1)}, bf16[112,128]{1,0:T(8,128)(2,1)S(1)}, u32[]{:S(2)}, u32[]{:S(2)}) collective-permute-start(bf16[112,128]{1,0:T(8,128)(2,1)S(1)} %get-tuple-element.34), channel_id=1, source_target_pairs={{0,16},{16,32},{32,48},{48,64},{64,80},{80,96},{96,112},{112,128},... | collective-permute-start | bytes 86024 | tf_op jit(solution)/shard_map/ppermute | solution.py:306
  6.3 1.3 collective-permute-start.1
  7.6 0.8 reshape.46
  8.4 0.8 reshape.48
  9.2 1.2 copy.36
  10.4 1.2 copy.37
  11.6 1.1 fusion
  12.7 1.3 fusion.15
  14.7 0.8 select_maximum_fusion.small_hbm
  15.6 15.4 %collective-permute-start.2 = (bf16[96,896]{1,0:T(8,128)(2,1)S(1)}, bf16[96,896]{1,0:T(8,128)(2,1)S(1)}, u32[]{:S(2)}, u32[]{:S(2)}) collective-permute-start(bf16[96,896]{1,0:T(8,128)(2,1)S(1)} %get-tuple-element.98), channel_id=1, source_target_pairs={{0,2},{2,0},{1,3},{3,1},{4,6},{6,4},{5,7},{7,5},{8,10},{10,8},{9,1... | collective-permute-start | bytes 516104 | tf_op jit(solution)/shard_map/ppermute | solution.py:20
  31.7 3.1 %collective-permute-done.2 = bf16[96,896]{1,0:T(8,128)(2,1)S(1)} collective-permute-done((bf16[96,896]{1,0:T(8,128)(2,1)S(1)}, bf16[96,896]{1,0:T(8,128)(2,1)S(1)}, u32[]{:S(2)}, u32[]{:S(2)}) %collective-permute-start.2) | collective-permute-done | bytes 172064 | tf_op jit(solution)/shard_map/ppermute | solution.py:20
  34.9 15.4 %all_to_all.15.own_hbm = bf16[4,2,96,896]{3,2,1,0:T(8,128)(2,1)S(1)} all-to-all(bf16[4,2,96,896]{3,2,1,0:T(8,128)(2,1)S(1)} %broadcast_in_dim.33), channel_id=1, replica_groups=mesh['zl'=8,'y'=4,'x'=4,'zh'=2,'core'=2] {'x'}, dimensions={0} | all-to-all | bytes 2752512 | tf_op jit(solution)/shard_map/all_to_all | solution.py:24
  50.3 15.2 %collective-permute-start.3 = (bf16[4,2,96,896]{3,2,1,0:T(8,128)(2,1)S(1)}, bf16[4,2,96,896]{3,2,1,0:T(8,128)(2,1)}, u32[]{:S(2)}, u32[]{:S(2)}) collective-permute-start(bf16[4,2,96,896]{3,2,1,0:T(8,128)(2,1)S(1)} %all_to_all.15.own_hbm), channel_id=1, source_target_pairs={{0,1},{1,0},{2,3},{3,2},{4,5},{5,4},{6,7},{7,6},{8,9},{9,8},{10,11... | collective-permute-start | bytes 4128776 | tf_op jit(solution)/shard_map/ppermute | solution.py:20
  65.6 1.1 copy.42.weight_hbm
  66.6 1.8 %collective-permute-done.3.other_hbm = bf16[4,2,96,896]{3,2,1,0:T(8,128)(2,1)} collective-permute-done((bf16[4,2,96,896]{3,2,1,0:T(8,128)(2,1)S(1)}, bf16[4,2,96,896]{3,2,1,0:T(8,128)(2,1)}, u32[]{:S(2)}, u32[]{:S(2)}) %collective-permute-start.3) | collective-permute-done | bytes 1376288 | tf_op jit(solution)/shard_map/ppermute | solution.py:20
  68.4 10.6 %shard_map.145 = (bf16[8,208,384]{2,1,0:T(8,128)(2,1)}, bf16[8,48,384]{2,1,0:T(8,128)(2,1)S(1)}, bf16[8,48,384]{2,1,0:T(8,128)(2,1)S(1)}, bf16[8,48,384]{2,1,0:T...) custom-call(s32[3]{0:T(128)S(1)} %pad_add_fusion.where_ref, bf16[4,2,96,896]{3,2,1,0:T(8,128)(2,1)} %copy-done, ...), custom_call_target="tpu_custom_call" | custom-call | tf_op jit(solution)/shard_map/pallas_call | solution.py:343
  79.0 3.8 %all-to-all-start.1 = ((bf16[8,208,384]{2,1,0:T(8,128)(2,1)}), bf16[8,208,384]{2,1,0:T(8,128)(2,1)S(1)}, u32[]{:S(2)}, u32[]{:S(2)}) async-start(bf16[8,208,384]{2,1,0:T(8,128)(2,1)} %get-tuple-element.47), calls=%async_computation.1 | async-start | bytes 2555904 | tf_op jit(solution)/shard_map/all_to_all | solution.py:372
  82.9 1.9 %collective-permute-start.4 = (bf16[8,48,384]{2,1,0:T(8,128)(2,1)S(1)}, bf16[8,48,384]{2,1,0:T(8,128)(2,1)S(1)}, u32[]{:S(2)}, u32[]{:S(2)}) collective-permute-start(bf16[8,48,384]{2,1,0:T(8,128)(2,1)S(1)} %get-tuple-element.44), channel_id=1, source_target_pairs={{0,16},{16,32},{32,48},{48,0},{1,17},{17,33},{33,49},{49,1},{2,18}... | collective-permute-start | bytes 884744 | tf_op jit(solution)/shard_map/ppermute | solution.py:375
  84.8 4.6 %collective-permute-start.5 = (bf16[8,48,384]{2,1,0:T(8,128)(2,1)S(1)}, bf16[8,48,384]{2,1,0:T(8,128)(2,1)S(1)}, u32[]{:S(2)}, u32[]{:S(2)}) collective-permute-start(bf16[8,48,384]{2,1,0:T(8,128)(2,1)S(1)} %get-tuple-element.45), channel_id=1, source_target_pairs={{0,48},{16,0},{32,16},{48,32},{1,49},{17,1},{33,17},{49,33},{2,50}... | collective-permute-start | bytes 884744 | tf_op jit(solution)/shard_map/ppermute | solution.py:375
  89.4 1.9 %collective-permute-start.6 = (bf16[8,48,384]{2,1,0:T(8,128)(2,1)S(1)}, bf16[8,48,384]{2,1,0:T(8,128)(2,1)S(1)}, u32[]{:S(2)}, u32[]{:S(2)}) collective-permute-start(bf16[8,48,384]{2,1,0:T(8,128)(2,1)S(1)} %get-tuple-element.46), channel_id=1, source_target_pairs={{0,32},{16,48},{32,0},{48,16},{1,33},{17,49},{33,1},{49,17},{2,34}... | collective-permute-start | bytes 884744 | tf_op jit(solution)/shard_map/ppermute | solution.py:375
  91.4 0.8 slice_reduce_fusion.4
  92.2 2.2 %collective-permute-done.4 = bf16[8,48,384]{2,1,0:T(8,128)(2,1)S(1)} collective-permute-done((bf16[8,48,384]{2,1,0:T(8,128)(2,1)S(1)}, bf16[8,48,384]{2,1,0:T(8,128)(2,1)S(1)}, u32[]{:S(2)}, u32[]{:S(2)}) %collective-permute-start.4) | collective-permute-done | bytes 294944 | tf_op jit(solution)/shard_map/ppermute | solution.py:375
  94.4 7.0 %collective-permute-done.5 = bf16[8,48,384]{2,1,0:T(8,128)(2,1)S(1)} collective-permute-done((bf16[8,48,384]{2,1,0:T(8,128)(2,1)S(1)}, bf16[8,48,384]{2,1,0:T(8,128)(2,1)S(1)}, u32[]{:S(2)}, u32[]{:S(2)}) %collective-permute-start.5) | collective-permute-done | bytes 294944 | tf_op jit(solution)/shard_map/ppermute | solution.py:375
  101.9 10.0 %collective-permute-start.7 = (bf16[4,48,384]{2,1,0:T(8,128)(2,1)S(1)}, bf16[4,48,384]{2,1,0:T(8,128)(2,1)S(1)}, u32[]{:S(2)}, u32[]{:S(2)}) collective-permute-start(bf16[4,48,384]{2,1,0:T(8,128)(2,1)S(1)} %fusion.2), channel_id=1, source_target_pairs={{0,64},{64,0},{128,192},{192,128},{256,320},{320,256},{384,448},{4... | collective-permute-start | bytes 442376 | tf_op jit(solution)/shard_map/ppermute | solution.py:387
  111.9 1.1 multiply_reduce_fusion.1
  113.7 15.8 %all-to-all-start.2 = ((f32[64,2,96]{2,1,0:T(2,128)}), f32[64,2,96]{2,1,0:T(2,128)S(1)}, u32[]{:S(2)}, u32[]{:S(2)}) async-start(f32[64,2,96]{2,1,0:T(2,128)} %bitcast.28), calls=%async_computation.2 | async-start | bytes 131072 | tf_op jit(solution)/shard_map/all_to_all | solution.py:402
  129.7 3.8 %collective-permute-start.9 = (bf16[2,48,384]{2,1,0:T(8,128)(2,1)S(1)}, bf16[2,48,384]{2,1,0:T(8,128)(2,1)S(1)}, u32[]{:S(2)}, u32[]{:S(2)}) collective-permute-start(bf16[2,48,384]{2,1,0:T(8,128)(2,1)S(1)} %fusion.10), channel_id=1, source_target_pairs={{0,128},{64,192},{128,0},{192,64},{256,384},{320,448},{384,256},{4... | collective-permute-start | bytes 221192 | tf_op jit(solution)/shard_map/ppermute | solution.py:412
  133.5 10.0 %collective-permute-start.8 = (bf16[112,384]{1,0:T(8,128)(2,1)S(1)}, bf16[112,384]{1,0:T(8,128)(2,1)S(1)}, u32[]{:S(2)}, u32[]{:S(2)}) collective-permute-start(bf16[112,384]{1,0:T(8,128)(2,1)S(1)} %maximum_maximum_fusion), channel_id=1, source_target_pairs={{0,2},{2,0},{1,3},{3,1},{4,6},{6,4},{5,7},{7,5},{8,10},{10,8},{9,1... | collective-permute-start | bytes 258056 | tf_op jit(solution)/shard_map/ppermute | solution.py:20
  143.6 2.4 %collective-permute-start.10 = (bf16[48,384]{1,0:T(8,128)(2,1)S(1)}, bf16[48,384]{1,0:T(8,128)(2,1)S(1)}, u32[]{:S(2)}, u32[]{:S(2)}) collective-permute-start(bf16[48,384]{1,0:T(8,128)(2,1)S(1)} %fusion.11), channel_id=1, source_target_pairs={{0,256},{64,320},{128,384},{192,448},{256,0},{320,64},{384,128},{4... | collective-permute-start | bytes 110600 | tf_op jit(solution)/shard_map/ppermute | solution.py:426
  146.0 1.5 collective-permute-done.8
  148.3 5.6 %collective-permute-done.10.part_ref = bf16[48,384]{1,0:T(8,128)(2,1)S(1)} collective-permute-done((bf16[48,384]{1,0:T(8,128)(2,1)S(1)}, bf16[48,384]{1,0:T(8,128)(2,1)S(1)}, u32[]{:S(2)}, u32[]{:S(2)}) %collective-permute-start.10) | collective-permute-done | bytes 36896 | tf_op jit(solution)/shard_map/ppermute | solution.py:426
  (73 shorter events, 7.6 us)
Async XLA Ops:
  0.6 10.9 %copy-start.5 = (f32[1536]{0:T(1024)S(1)}, f32[1536]{0:T(1024)}, u32[]{:S(2)}) copy-start(f32[1536]{0:T(1024)} %param.10) | copy-start | bytes 18436
  0.6 10.9 %copy-start.4 = (f32[1536]{0:T(1024)S(1)}, f32[1536]{0:T(1024)}, u32[]{:S(2)}) copy-start(f32[1536]{0:T(1024)} %param.11) | copy-start | bytes 18436
  2.3 13.3 %collective-permute-start = (bf16[112,128]{1,0:T(8,128)(2,1)S(1)}, bf16[112,128]{1,0:T(8,128)(2,1)S(1)}, u32[]{:S(2)}, u32[]{:S(2)}) collective-permute-start(bf16[112,128]{1,0:T(8,128)(2,1)S(1)} %get-tuple-element.34), channel_id=1, source_target_pairs={{0,16},{16,32},{32,48},{48,64},{64,80},{80,96},{96,112},{112,128},... | collective-permute-start | bytes 86024 | tf_op jit(solution)/shard_map/ppermute | solution.py:306
  6.3 9.2 %collective-permute-start.1 = (bf16[112,128]{1,0:T(8,128)(2,1)S(1)}, bf16[112,128]{1,0:T(8,128)(2,1)S(1)}, u32[]{:S(2)}, u32[]{:S(2)}) collective-permute-start(bf16[112,128]{1,0:T(8,128)(2,1)S(1)} %get-tuple-element.35), channel_id=1, source_target_pairs={{16,0},{32,16},{48,32},{64,48},{80,64},{96,80},{112,96},{128,112},... | collective-permute-start | bytes 86024 | tf_op jit(solution)/shard_map/ppermute | solution.py:306
  12.7 1.8 %copy-start.6 = (f32[31,96]{1,0:T(8,128)S(1)}, f32[31,96]{1,0:T(8,128)}, u32[]{:S(2)}) copy-start(f32[31,96]{1,0:T(8,128)} %param.14) | copy-start | bytes 35716
  12.7 2.8 %copy-start.7 = (s32[384]{0:T(512)S(1)}, s32[384]{0:T(512)}, u32[]{:S(2)}) copy-start(s32[384]{0:T(512)} %param.16) | copy-start | bytes 4612
  12.7 2.9 %copy-start.1 = (bf16[96,384]{1,0:T(8,128)(2,1)S(1)}, bf16[96,384]{1,0:T(8,128)(2,1)}, u32[]{:S(2)}) copy-start(bf16[96,384]{1,0:T(8,128)(2,1)} %inputs_hbm.1) | copy-start | bytes 221188
  12.7 2.9 %copy-start.2 = (bf16[96,384]{1,0:T(8,128)(2,1)S(1)}, bf16[96,384]{1,0:T(8,128)(2,1)}, u32[]{:S(2)}) copy-start(bf16[96,384]{1,0:T(8,128)(2,1)} %upstream_hbm.1) | copy-start | bytes 221188
  15.6 19.1 %collective-permute-start.2 = (bf16[96,896]{1,0:T(8,128)(2,1)S(1)}, bf16[96,896]{1,0:T(8,128)(2,1)S(1)}, u32[]{:S(2)}, u32[]{:S(2)}) collective-permute-start(bf16[96,896]{1,0:T(8,128)(2,1)S(1)} %get-tuple-element.98), channel_id=1, source_target_pairs={{0,2},{2,0},{1,3},{3,1},{4,6},{6,4},{5,7},{7,5},{8,10},{10,8},{9,1... | collective-permute-start | bytes 516104 | tf_op jit(solution)/shard_map/ppermute | solution.py:20
  34.8 15.6 %copy-start.3 = (bf16[96,896]{1,0:T(8,128)(2,1)}, bf16[96,896]{1,0:T(8,128)(2,1)S(1)}, u32[]{:S(2)}) copy-start(bf16[96,896]{1,0:T(8,128)(2,1)S(1)} %collective-permute-done.2) | copy-start | bytes 516100
  50.3 18.1 %copy-start = (bf16[4,2,96,896]{3,2,1,0:T(8,128)(2,1)}, bf16[4,2,96,896]{3,2,1,0:T(8,128)(2,1)S(1)}, u32[]{:S(2)}) copy-start(bf16[4,2,96,896]{3,2,1,0:T(8,128)(2,1)S(1)} %all_to_all.15.own_hbm) | copy-start | bytes 4128772
  50.3 18.1 %collective-permute-start.3 = (bf16[4,2,96,896]{3,2,1,0:T(8,128)(2,1)S(1)}, bf16[4,2,96,896]{3,2,1,0:T(8,128)(2,1)}, u32[]{:S(2)}, u32[]{:S(2)}) collective-permute-start(bf16[4,2,96,896]{3,2,1,0:T(8,128)(2,1)S(1)} %all_to_all.15.own_hbm), channel_id=1, source_target_pairs={{0,1},{1,0},{2,3},{3,2},{4,5},{5,4},{6,7},{7,6},{8,9},{9,8},{10,11... | collective-permute-start | bytes 4128776 | tf_op jit(solution)/shard_map/ppermute | solution.py:20
  79.0 22.6 %all-to-all-start.1 = ((bf16[8,208,384]{2,1,0:T(8,128)(2,1)}), bf16[8,208,384]{2,1,0:T(8,128)(2,1)S(1)}, u32[]{:S(2)}, u32[]{:S(2)}) async-start(bf16[8,208,384]{2,1,0:T(8,128)(2,1)} %get-tuple-element.47), calls=%async_computation.1 | async-start | bytes 2555904 | tf_op jit(solution)/shard_map/all_to_all | solution.py:372
  82.9 11.6 %collective-permute-start.4 = (bf16[8,48,384]{2,1,0:T(8,128)(2,1)S(1)}, bf16[8,48,384]{2,1,0:T(8,128)(2,1)S(1)}, u32[]{:S(2)}, u32[]{:S(2)}) collective-permute-start(bf16[8,48,384]{2,1,0:T(8,128)(2,1)S(1)} %get-tuple-element.44), channel_id=1, source_target_pairs={{0,16},{16,32},{32,48},{48,0},{1,17},{17,33},{33,49},{49,1},{2,18}... | collective-permute-start | bytes 884744 | tf_op jit(solution)/shard_map/ppermute | solution.py:375
  84.8 16.7 %collective-permute-start.5 = (bf16[8,48,384]{2,1,0:T(8,128)(2,1)S(1)}, bf16[8,48,384]{2,1,0:T(8,128)(2,1)S(1)}, u32[]{:S(2)}, u32[]{:S(2)}) collective-permute-start(bf16[8,48,384]{2,1,0:T(8,128)(2,1)S(1)} %get-tuple-element.45), channel_id=1, source_target_pairs={{0,48},{16,0},{32,16},{48,32},{1,49},{17,1},{33,17},{49,33},{2,50}... | collective-permute-start | bytes 884744 | tf_op jit(solution)/shard_map/ppermute | solution.py:375
  89.4 12.1 %collective-permute-start.6 = (bf16[8,48,384]{2,1,0:T(8,128)(2,1)S(1)}, bf16[8,48,384]{2,1,0:T(8,128)(2,1)S(1)}, u32[]{:S(2)}, u32[]{:S(2)}) collective-permute-start(bf16[8,48,384]{2,1,0:T(8,128)(2,1)S(1)} %get-tuple-element.46), channel_id=1, source_target_pairs={{0,32},{16,48},{32,0},{48,16},{1,33},{17,49},{33,1},{49,17},{2,34}... | collective-permute-start | bytes 884744 | tf_op jit(solution)/shard_map/ppermute | solution.py:375
  101.9 27.7 %collective-permute-start.7 = (bf16[4,48,384]{2,1,0:T(8,128)(2,1)S(1)}, bf16[4,48,384]{2,1,0:T(8,128)(2,1)S(1)}, u32[]{:S(2)}, u32[]{:S(2)}) collective-permute-start(bf16[4,48,384]{2,1,0:T(8,128)(2,1)S(1)} %fusion.2), channel_id=1, source_target_pairs={{0,64},{64,0},{128,192},{192,128},{256,320},{320,256},{384,448},{4... | collective-permute-start | bytes 442376 | tf_op jit(solution)/shard_map/ppermute | solution.py:387
  113.7 34.6 %all-to-all-start.2 = ((f32[64,2,96]{2,1,0:T(2,128)}), f32[64,2,96]{2,1,0:T(2,128)S(1)}, u32[]{:S(2)}, u32[]{:S(2)}) async-start(f32[64,2,96]{2,1,0:T(2,128)} %bitcast.28), calls=%async_computation.2 | async-start | bytes 131072 | tf_op jit(solution)/shard_map/all_to_all | solution.py:402
  129.7 13.9 %collective-permute-start.9 = (bf16[2,48,384]{2,1,0:T(8,128)(2,1)S(1)}, bf16[2,48,384]{2,1,0:T(8,128)(2,1)S(1)}, u32[]{:S(2)}, u32[]{:S(2)}) collective-permute-start(bf16[2,48,384]{2,1,0:T(8,128)(2,1)S(1)} %fusion.10), channel_id=1, source_target_pairs={{0,128},{64,192},{128,0},{192,64},{256,384},{320,448},{384,256},{4... | collective-permute-start | bytes 221192 | tf_op jit(solution)/shard_map/ppermute | solution.py:412
  133.5 14.0 %collective-permute-start.8 = (bf16[112,384]{1,0:T(8,128)(2,1)S(1)}, bf16[112,384]{1,0:T(8,128)(2,1)S(1)}, u32[]{:S(2)}, u32[]{:S(2)}) collective-permute-start(bf16[112,384]{1,0:T(8,128)(2,1)S(1)} %maximum_maximum_fusion), channel_id=1, source_target_pairs={{0,2},{2,0},{1,3},{3,1},{4,6},{6,4},{5,7},{7,5},{8,10},{10,8},{9,1... | collective-permute-start | bytes 258056 | tf_op jit(solution)/shard_map/ppermute | solution.py:20
  143.6 10.4 %collective-permute-start.10 = (bf16[48,384]{1,0:T(8,128)(2,1)S(1)}, bf16[48,384]{1,0:T(8,128)(2,1)S(1)}, u32[]{:S(2)}, u32[]{:S(2)}) collective-permute-start(bf16[48,384]{1,0:T(8,128)(2,1)S(1)} %fusion.11), channel_id=1, source_target_pairs={{0,256},{64,320},{128,384},{192,448},{256,0},{320,64},{384,128},{4... | collective-permute-start | bytes 110600 | tf_op jit(solution)/shard_map/ppermute | solution.py:426

commit v12 on v10

--- a/solution.py
+++ b/solution.py
@@ -20,12 +20,6 @@
     return lax.ppermute(value, axis, SWAP)
 
 
-def over_x(pair):
-    return lax.all_to_all(
-        jnp.broadcast_to(pair[None], (4,) + pair.shape), "x", 0, 0, tiled=True
-    )
-
-
 def ordered(own, other, index, axis):
     return jnp.where(
         index == 0, jnp.stack([own, other], axis), jnp.stack([other, own], axis)
@@ -52,13 +46,17 @@
     )
 
 
-def blocks_of(where_ref, own_ref, other_ref):
-    zh, core = where_ref[0], where_ref[1]
-    for x in range(4):
+STEPS = (0, 1, 3, 2)
+
+
+def blocks_of(where_ref, own_refs, other_refs):
+    zh, core, x = where_ref[0], where_ref[1], where_ref[3]
+    for i, step in enumerate(STEPS):
+        first = lax.rem(x + 4 - step, 4) * 4
         for far in range(2):
             side = zh if far == 0 else 1 - zh
-            yield x * 4 + side * 2 + core, own_ref.at[x, far]
-            yield x * 4 + side * 2 + 1 - core, other_ref.at[x, far]
+            yield first + side * 2 + core, own_refs[i].at[far]
+            yield first + side * 2 + 1 - core, other_refs[i].at[far]
 
 
 def edges(inputs_hbm, upstream_hbm, mask_ref, right_ref, left_ref, ends_ref, sems):
@@ -91,14 +89,15 @@
 
 
 def middle(
-    where_ref, own_hbm, other_hbm, small_hbm, weight_hbm, project_hbm, flipped_hbm, mask_hbm,
+    where_ref, own0, own1, own2, own3, other0, other1, other2, other3, small_hbm, weight_hbm, project_hbm, flipped_hbm, mask_hbm,
     mixed_out, part0_out, part1_out, part2_out, part3_out, stats_out,
-    own_ref, other_ref, small_ref, weight_ref, project_ref, flipped_ref, mask_ref,
+    small_ref, weight_ref, project_ref, flipped_ref, mask_ref,
     taps_ref, mixed_ref, grads_ref, stats_ref, normed_ref, full_ref, both_ref, act_ref, kernel_ref,
     proj_ref, grad_ref, moved_ref, back_ref, sems,
 ):
     model = weight_ref.shape[1]
-    width = own_ref.shape[2]
+    own_refs, other_refs = (own0, own1, own2, own3), (other0, other1, other2, other3)
+    width = own0.shape[1]
     lanes = normed_ref.shape[2]
     rows = mixed_ref.shape[2]
     taps = taps_ref.shape[0]
@@ -112,11 +111,6 @@
         return started
 
     small_copy = copy(small_hbm, small_ref)
-    blocks = [
-        copy(source.at[x], target.at[x])
-        for x in range(4)
-        for source, target in ((own_hbm, own_ref), (other_hbm, other_ref))
-    ]
     mask_copy = copy(mask_hbm, mask_ref)
     project_copy = copy(project_hbm, project_ref)
     weight_copy = copy(weight_hbm, weight_ref)
@@ -126,10 +120,7 @@
         taps_ref[k] = jnp.broadcast_to(small_ref[:width, 34 + k : 35 + k], (width, 128))
     total = jnp.zeros((8, lanes), f32)
     square = jnp.zeros((8, lanes), f32)
-    for i, (place, block) in enumerate(blocks_of(where_ref, own_ref, other_ref)):
-        if i % 4 == 0:
-            blocks[i // 2].wait()
-            blocks[i // 2 + 1].wait()
+    for place, block in blocks_of(where_ref, own_refs, other_refs):
         x = block[:, :lanes].astype(f32).reshape(width // 8, 8, lanes)
         total = total + jnp.sum(x, axis=0)
         square = square + jnp.sum(x * x, axis=0)
@@ -144,7 +135,7 @@
         [row_mean, inv_std, jnp.zeros((6, lanes), f32)], axis=0
     )
     finished = [copy(stats_ref, stats_out)]
-    for i, (place, block) in enumerate(blocks_of(where_ref, own_ref, other_ref)):
+    for i, (place, block) in enumerate(blocks_of(where_ref, own_refs, other_refs)):
         centred = (block[:, :lanes].astype(f32) - row_mean) * inv_std
         normed_ref[place] = (
             centred * small_ref[:width, i : i + 1] + small_ref[:width, 16 + i : 17 + i]
@@ -282,7 +273,8 @@
     y = lax.axis_index("y")
     zl = lax.axis_index("zl")
     offset = lax.axis_index(CHAN) * width
-    where = jnp.stack([zh, core, y]).astype(jnp.int32)
+    x = lax.axis_index("x")
+    where = jnp.stack([zh, core, y, x]).astype(jnp.int32)
 
     to_right, to_left = call(
         edges,
@@ -305,6 +297,9 @@
 
     def columns_of(parameter):
         parameter = parameter.reshape(4, 2, 2, width)
+        parameter = jnp.stack(
+            [lax.dynamic_index_in_dim(parameter, (x + 4 - step) % 4, 0, False) for step in STEPS]
+        )
         parameter = jnp.where(zh == 0, parameter, parameter[:, ::-1])
         parameter = jnp.where(core == 0, parameter, parameter[:, :, ::-1])
         return parameter.reshape(16, width).T
@@ -327,10 +322,13 @@
     came, keep, early = lax.optimization_barrier((came, keep, early))
     weights, flipped, small, gain_local, where = early
     far_inputs = came[:, :rows]
-    own = over_x(jnp.stack([held, came]))
-    other = swap(own, "core")
+    pair = jnp.stack([held, came])
+    own = [pair] + [
+        lax.ppermute(pair, "x", [(i, (i + step) % 4) for i in range(4)]) for step in STEPS[1:]
+    ]
+    other = [swap(block, "core") for block in own]
     piece_shape = (8, piece, 4 * width)
-    operands = (own, other, small, weights, project_weight, flipped, keep)
+    operands = (small, weights, project_weight, flipped, keep)
     mixed, *pieces, stats = pl.pallas_call(
         middle,
         out_shape=(
@@ -338,7 +336,7 @@
             *(pltpu.VMEM(piece_shape, bf16) for _ in range(4)),
             pltpu.HBM((8, lanes), f32),
         ),
-        in_specs=[SMEM] + [pl.BlockSpec(memory_space=pltpu.HBM)] * len(operands),
+        in_specs=[SMEM] + [VMEM] * 8 + [pl.BlockSpec(memory_space=pltpu.HBM)] * len(operands),
         out_specs=tuple(pl.BlockSpec(memory_space=pltpu.HBM if i in (0, 5) else pltpu.VMEM) for i in range(6)),
         scratch_shapes=[pltpu.VMEM(operand.shape, operand.dtype) for operand in operands]
         + [
@@ -357,8 +355,8 @@
             pltpu.VMEM((8, 16, lanes), f32),
             pltpu.SemaphoreType.DMA((20,)),
         ],
-        compiler_params=pltpu.CompilerParams(vmem_limit_bytes=40 << 20),
-    )(where, *(pltpu.with_memory_space_constraint(operand, pltpu.HBM) for operand in operands))
+        compiler_params=pltpu.CompilerParams(vmem_limit_bytes=26 << 20),
+    )(where, *own, *other, *(pltpu.with_memory_space_constraint(operand, pltpu.HBM) for operand in operands))
 
     mixed = lax.all_to_all(mixed, ("x", "core"), 0, 0, tiled=True)
 

time: 158 us -> 163 us (1.032)
  starting transfers between devices: 91.7 us -> 110 us
  blocking collectives: 15.4 us -> 0 us
  local copies, waits for them, and re-layouts: 9.87 us -> 13 us
  waiting for transfers between devices: 19.4 us -> 17.1 us
    all_to_all x1 -> x0, blocking collectives: 15.4 us -> none  [over_x(): lax.all_to_all(jnp.broadcast_to(pair[None], (4,) + pair.shape), 'x', 0, 0...]
    ppermute x0 -> x3, starting transfers between devices: none -> 10 us  [on_device(): lax.ppermute(pair, 'x', [(i, (i + step) % 4) for i in range(4)])]
    ppermute x3 -> x6, starting transfers between devices: 43.6 us -> 49.8 us  [swap(): return lax.ppermute(value, axis, SWAP)]
    unnamed x19 -> x25, local copies, waits for them, and re-layouts: 2.51 us -> 4.59 us
    ppermute x3 -> x6, waiting for transfers between devices: 4.85 us -> 3.08 us  [swap(): return lax.ppermute(value, axis, SWAP)]
    ppermute x1, starting transfers between devices: 9.28 us -> 11 us  [on_device(): lax.ppermute(sent, 'zl', [(i, i ^ 1) for i in range(8)]).astype(f32)]
  transfers between devices with their start and end apart: 13 -> 19, of which waited for: 6 -> 5; matrix products, arithmetic and copies ran while one was open for 8% -> 9% of each run, Pallas kernels for 0% -> 0%
where the time goes in v12:
time: 163 us; the launch traced here: 160 us
  starting transfers between devices  110 us (67%)
  waiting for transfers between devices  17.1 us (10%)
  local copies, waits for them, and re-layouts  13 us (8%)
  Pallas kernels  11.4 us (7%)
  other arithmetic  6.66 us (4%)
    ppermute x6, starting transfers between devices, swap(): return lax.ppermute(value, axis, SWAP)  49.8 us
    ppermute x2, starting transfers between devices, on_device(): lax.ppermute(sent, 'zl', [(i, i ^ size) for i in range(8)]).astype(f32)  11.9 us
    ppermute x1, starting transfers between devices, on_device(): lax.ppermute(sent, 'zl', [(i, i ^ 1) for i in range(8)]).astype(f32)  11 us
    pallas_call x1, Pallas kernels, on_device(): pl.pallas_call(middle, out_shape=(pltpu.HBM((8, 2 * width + 16, rows), bf...  10.5 us
    ppermute x3, starting transfers between devices, on_device(): lax.ppermute(pair, 'x', [(i, (i + step) % 4) for i in range(4)])  10 us
    all_to_all x1, starting transfers between devices, on_device(): lax.all_to_all(jnp.broadcast_to(tail[None], (32, 2, 2, width)).reshape(64...  10 us
    ppermute x3, waiting for transfers between devices, on_device(): lax.ppermute(sent, 'y', [(i, (i + step) % 4) for i in range(4)])  9.32 us
    ppermute x3, starting transfers between devices, on_device(): lax.ppermute(sent, 'y', [(i, (i + step) % 4) for i in range(4)])  8.41 us
  transfers between devices with their start and end apart: 19, of which 5 were waited for; matrix products, arithmetic and copies ran while one was open for 9% of the time, Pallas kernels for 0%

profile of v12, /device:TPU:1, one launch (start us, length us, event | category | flops | bytes accessed | tf_op | source)
XLA Modules:
  0.0 159.7 jit_solution(1055412782132563559)
XLA Ops:
  1.3 0.9 shard_map.144
  2.3 4.0 %collective-permute-start = (bf16[112,128]{1,0:T(8,128)(2,1)S(1)}, bf16[112,128]{1,0:T(8,128)(2,1)S(1)}, u32[]{:S(2)}, u32[]{:S(2)}) collective-permute-start(bf16[112,128]{1,0:T(8,128)(2,1)S(1)} %get-tuple-element.30), channel_id=1, source_target_pairs={{0,16},{16,32},{32,48},{48,64},{64,80},{80,96},{96,112},{112,128},... | collective-permute-start | bytes 86024 | tf_op jit(solution)/shard_map/ppermute | solution.py:289
  6.3 1.3 collective-permute-start.1
  9.2 1.2 copy.29
  10.4 1.2 copy.30
  11.6 1.1 fusion
  12.8 1.5 fusion.8
  16.0 15.4 %collective-permute-start.2 = (bf16[96,896]{1,0:T(8,128)(2,1)S(1)}, bf16[96,896]{1,0:T(8,128)(2,1)S(1)}, u32[]{:S(2)}, u32[]{:S(2)}) collective-permute-start(bf16[96,896]{1,0:T(8,128)(2,1)S(1)} %get-tuple-element.69), channel_id=1, source_target_pairs={{0,2},{2,0},{1,3},{3,1},{4,6},{6,4},{5,7},{7,5},{8,10},{10,8},{9,1... | collective-permute-start | bytes 516104 | tf_op jit(solution)/shard_map/ppermute | solution.py:20
  32.0 3.1 %collective-permute-done.2 = bf16[96,896]{1,0:T(8,128)(2,1)S(1)} collective-permute-done((bf16[96,896]{1,0:T(8,128)(2,1)S(1)}, bf16[96,896]{1,0:T(8,128)(2,1)S(1)}, u32[]{:S(2)}, u32[]{:S(2)}) %collective-permute-start.2) | collective-permute-done | bytes 172064 | tf_op jit(solution)/shard_map/ppermute | solution.py:20
  35.8 3.2 %collective-permute-start.3 = (bf16[2,96,896]{2,1,0:T(8,128)(2,1)S(1)}, bf16[2,96,896]{2,1,0:T(8,128)(2,1)S(1)}, u32[]{:S(2)}, u32[]{:S(2)}) collective-permute-start(bf16[2,96,896]{2,1,0:T(8,128)(2,1)S(1)} %pad_maximum_fusion.1.own0), channel_id=1, source_target_pairs={{0,4},{4,8},{8,12},{12,0},{1,5},{5,9},{9,13},{13,1},{2,6},{6,10},{... | collective-permute-start | bytes 1032200 | tf_op jit(solution)/shard_map/ppermute | solution.py:327
  39.0 3.3 %collective-permute-start.4 = (bf16[2,96,896]{2,1,0:T(8,128)(2,1)S(1)}, bf16[2,96,896]{2,1,0:T(8,128)(2,1)S(1)}, u32[]{:S(2)}, u32[]{:S(2)}) collective-permute-start(bf16[2,96,896]{2,1,0:T(8,128)(2,1)S(1)} %pad_maximum_fusion.1.own0), channel_id=1, source_target_pairs={{0,12},{4,0},{8,4},{12,8},{1,13},{5,1},{9,5},{13,9},{2,14},{6,2},{... | collective-permute-start | bytes 1032200 | tf_op jit(solution)/shard_map/ppermute | solution.py:327
  42.3 3.6 %collective-permute-start.5 = (bf16[2,96,896]{2,1,0:T(8,128)(2,1)S(1)}, bf16[2,96,896]{2,1,0:T(8,128)(2,1)S(1)}, u32[]{:S(2)}, u32[]{:S(2)}) collective-permute-start(bf16[2,96,896]{2,1,0:T(8,128)(2,1)S(1)} %pad_maximum_fusion.1.own0), channel_id=1, source_target_pairs={{0,8},{4,12},{8,0},{12,4},{1,9},{5,13},{9,1},{13,5},{2,10},{6,14},... | collective-permute-start | bytes 1032200 | tf_op jit(solution)/shard_map/ppermute | solution.py:327
  45.9 14.6 %collective-permute-start.6 = (bf16[2,96,896]{2,1,0:T(8,128)(2,1)S(1)}, bf16[2,96,896]{2,1,0:T(8,128)(2,1)S(1)}, u32[]{:S(2)}, u32[]{:S(2)}) collective-permute-start(bf16[2,96,896]{2,1,0:T(8,128)(2,1)S(1)} %pad_maximum_fusion.1.own0), channel_id=1, source_target_pairs={{0,1},{1,0},{2,3},{3,2},{4,5},{5,4},{6,7},{7,6},{8,9},{9,8},{10,11... | collective-permute-start | bytes 1032200 | tf_op jit(solution)/shard_map/ppermute | solution.py:20
  60.5 1.9 %collective-permute-start.7 = (bf16[2,96,896]{2,1,0:T(8,128)(2,1)S(1)}, bf16[2,96,896]{2,1,0:T(8,128)(2,1)S(1)}, u32[]{:S(2)}, u32[]{:S(2)}) collective-permute-start(bf16[2,96,896]{2,1,0:T(8,128)(2,1)S(1)} %collective-permute-done.3.own1), channel_id=1, source_target_pairs={{0,1},{1,0},{2,3},{3,2},{4,5},{5,4},{6,7},{7,6},{8,9},{9,8},{10,11... | collective-permute-start | bytes 1032200 | tf_op jit(solution)/shard_map/ppermute | solution.py:20
  62.5 2.4 %collective-permute-start.8 = (bf16[2,96,896]{2,1,0:T(8,128)(2,1)S(1)}, bf16[2,96,896]{2,1,0:T(8,128)(2,1)S(1)}, u32[]{:S(2)}, u32[]{:S(2)}) collective-permute-start(bf16[2,96,896]{2,1,0:T(8,128)(2,1)S(1)} %collective-permute-done.4.own2), channel_id=1, source_target_pairs={{0,1},{1,0},{2,3},{3,2},{4,5},{5,4},{6,7},{7,6},{8,9},{9,8},{10,11... | collective-permute-start | bytes 1032200 | tf_op jit(solution)/shard_map/ppermute | solution.py:20
  64.9 2.5 %collective-permute-start.9 = (bf16[2,96,896]{2,1,0:T(8,128)(2,1)S(1)}, bf16[2,96,896]{2,1,0:T(8,128)(2,1)S(1)}, u32[]{:S(2)}, u32[]{:S(2)}) collective-permute-start(bf16[2,96,896]{2,1,0:T(8,128)(2,1)S(1)} %collective-permute-done.5.own3), channel_id=1, source_target_pairs={{0,1},{1,0},{2,3},{3,2},{4,5},{5,4},{6,7},{7,6},{8,9},{9,8},{10,11... | collective-permute-start | bytes 1032200 | tf_op jit(solution)/shard_map/ppermute | solution.py:20
  67.4 2.2 %copy.35.weight_hbm = bf16[192,1536]{1,0:T(8,128)(2,1)} copy(bf16[192,1536]{0,1:T(8,128)(2,1)} %get-tuple-element.35) | data formatting | bytes 1179648 | tf_op jit(solution)/shard_map/optimization_barrier | solution.py:322
  69.7 10.5 %shard_map.145 = (bf16[8,208,384]{2,1,0:T(8,128)(2,1)}, bf16[8,48,384]{2,1,0:T(8,128)(2,1)S(1)}, bf16[8,48,384]{2,1,0:T(8,128)(2,1)S(1)}, bf16[8,48,384]{2,1,0:T...) custom-call(s32[4]{0:T(128)S(1)} %pad_add_fusion.where_ref, ...), custom_call_target="tpu_custom_call" | custom-call | tf_op jit(solution)/shard_map/pallas_call | solution.py:332
  81.6 3.6 %all-to-all-start = ((bf16[8,208,384]{2,1,0:T(8,128)(2,1)}), bf16[8,208,384]{2,1,0:T(8,128)(2,1)S(1)}, u32[]{:S(2)}, u32[]{:S(2)}) async-start(bf16[8,208,384]{2,1,0:T(8,128)(2,1)} %get-tuple-element.43), calls=%async_computation | async-start | bytes 2555904 | tf_op jit(solution)/shard_map/all_to_all | solution.py:361
  85.3 1.9 %collective-permute-start.10 = (bf16[8,48,384]{2,1,0:T(8,128)(2,1)S(1)}, bf16[8,48,384]{2,1,0:T(8,128)(2,1)S(1)}, u32[]{:S(2)}, u32[]{:S(2)}) collective-permute-start(bf16[8,48,384]{2,1,0:T(8,128)(2,1)S(1)} %copy-done.3), channel_id=1, source_target_pairs={{0,16},{16,32},{32,48},{48,0},{1,17},{17,33},{33,49},{49,1},{2,18}... | collective-permute-start | bytes 884744 | tf_op jit(solution)/shard_map/ppermute | solution.py:364
  87.2 4.6 %collective-permute-start.11 = (bf16[8,48,384]{2,1,0:T(8,128)(2,1)S(1)}, bf16[8,48,384]{2,1,0:T(8,128)(2,1)S(1)}, u32[]{:S(2)}, u32[]{:S(2)}) collective-permute-start(bf16[8,48,384]{2,1,0:T(8,128)(2,1)S(1)} %copy-done.1), channel_id=1, source_target_pairs={{0,48},{16,0},{32,16},{48,32},{1,49},{17,1},{33,17},{49,33},{2,50}... | collective-permute-start | bytes 884744 | tf_op jit(solution)/shard_map/ppermute | solution.py:364
  91.8 1.9 %collective-permute-start.12 = (bf16[8,48,384]{2,1,0:T(8,128)(2,1)S(1)}, bf16[8,48,384]{2,1,0:T(8,128)(2,1)S(1)}, u32[]{:S(2)}, u32[]{:S(2)}) collective-permute-start(bf16[8,48,384]{2,1,0:T(8,128)(2,1)S(1)} %get-tuple-element.42), channel_id=1, source_target_pairs={{0,32},{16,48},{32,0},{48,16},{1,33},{17,49},{33,1},{49,17},{2,34}... | collective-permute-start | bytes 884744 | tf_op jit(solution)/shard_map/ppermute | solution.py:364
  93.9 0.8 slice_reduce_fusion.4
  94.7 2.3 %collective-permute-done.10 = bf16[8,48,384]{2,1,0:T(8,128)(2,1)S(1)} collective-permute-done((bf16[8,48,384]{2,1,0:T(8,128)(2,1)S(1)}, bf16[8,48,384]{2,1,0:T(8,128)(2,1)S(1)}, u32[]{:S(2)}, u32[]{:S(2)}) %collective-permute-start.10) | collective-permute-done | bytes 294944 | tf_op jit(solution)/shard_map/ppermute | solution.py:364
  97.0 7.1 %collective-permute-done.11 = bf16[8,48,384]{2,1,0:T(8,128)(2,1)S(1)} collective-permute-done((bf16[8,48,384]{2,1,0:T(8,128)(2,1)S(1)}, bf16[8,48,384]{2,1,0:T(8,128)(2,1)S(1)}, u32[]{:S(2)}, u32[]{:S(2)}) %collective-permute-start.11) | collective-permute-done | bytes 294944 | tf_op jit(solution)/shard_map/ppermute | solution.py:364
  104.5 12.9 %collective-permute-start.14 = (bf16[112,384]{1,0:T(8,128)(2,1)S(1)}, bf16[112,384]{1,0:T(8,128)(2,1)S(1)}, u32[]{:S(2)}, u32[]{:S(2)}) collective-permute-start(bf16[112,384]{1,0:T(8,128)(2,1)S(1)} %maximum_maximum_fusion), channel_id=1, source_target_pairs={{0,2},{2,0},{1,3},{3,1},{4,6},{6,4},{5,7},{7,5},{8,10},{10,8},{9,1... | collective-permute-start | bytes 258056 | tf_op jit(solution)/shard_map/ppermute | solution.py:20
  117.4 1.1 multiply_reduce_fusion.1
  118.5 11.0 %collective-permute-start.13 = (bf16[4,48,384]{2,1,0:T(8,128)(2,1)S(1)}, bf16[4,48,384]{2,1,0:T(8,128)(2,1)S(1)}, u32[]{:S(2)}, u32[]{:S(2)}) collective-permute-start(bf16[4,48,384]{2,1,0:T(8,128)(2,1)S(1)} %fusion.2), channel_id=1, source_target_pairs={{0,64},{64,0},{128,192},{192,128},{256,320},{320,256},{384,448},{4... | collective-permute-start | bytes 442376 | tf_op jit(solution)/shard_map/ppermute | solution.py:376
  130.2 10.0 %all-to-all-start.1 = ((f32[64,2,96]{2,1,0:T(2,128)}), f32[64,2,96]{2,1,0:T(2,128)S(1)}, u32[]{:S(2)}, u32[]{:S(2)}) async-start(f32[64,2,96]{2,1,0:T(2,128)} %bitcast.25), calls=%async_computation.1 | async-start | bytes 131072 | tf_op jit(solution)/shard_map/all_to_all | solution.py:393
  140.3 3.8 %collective-permute-start.15 = (bf16[2,48,384]{2,1,0:T(8,128)(2,1)S(1)}, bf16[2,48,384]{2,1,0:T(8,128)(2,1)S(1)}, u32[]{:S(2)}, u32[]{:S(2)}) collective-permute-start(bf16[2,48,384]{2,1,0:T(8,128)(2,1)S(1)} %fusion.4), channel_id=1, source_target_pairs={{0,128},{64,192},{128,0},{192,64},{256,384},{320,448},{384,256},{4... | collective-permute-start | bytes 221192 | tf_op jit(solution)/shard_map/ppermute | solution.py:412
  144.2 4.1 %collective-permute-done.15 = bf16[2,48,384]{2,1,0:T(8,128)(2,1)S(1)} collective-permute-done((bf16[2,48,384]{2,1,0:T(8,128)(2,1)S(1)}, bf16[2,48,384]{2,1,0:T(8,128)(2,1)S(1)}, u32[]{:S(2)}, u32[]{:S(2)}) %collective-permute-start.15) | collective-permute-done | bytes 73760 | tf_op jit(solution)/shard_map/ppermute | solution.py:412
  148.3 8.1 %collective-permute-start.16 = (bf16[1,48,384]{2,1,0:T(8,128)(2,1)S(1)}, bf16[1,48,384]{2,1,0:T(8,128)(2,1)S(1)}, u32[]{:S(2)}, u32[]{:S(2)}) collective-permute-start(bf16[1,48,384]{2,1,0:T(8,128)(2,1)S(1)} %dynamic-slice_convert_fusion.1), channel_id=1, source_target_pairs={{0,256},{64,320},{128,384},{192,448},{256,0},{320,64},{384,128},{4... | collective-permute-start | bytes 110600 | tf_op jit(solution)/shard_map/ppermute | solution.py:412
  (92 shorter events, 11.2 us)
Async XLA Ops:
  0.6 11.0 %copy-start.8 = (f32[1536]{0:T(1024)S(1)}, f32[1536]{0:T(1024)}, u32[]{:S(2)}) copy-start(f32[1536]{0:T(1024)} %param.10) | copy-start | bytes 18436
  0.6 11.0 %copy-start.7 = (f32[1536]{0:T(1024)S(1)}, f32[1536]{0:T(1024)}, u32[]{:S(2)}) copy-start(f32[1536]{0:T(1024)} %param.11) | copy-start | bytes 18436
  2.3 13.6 %collective-permute-start = (bf16[112,128]{1,0:T(8,128)(2,1)S(1)}, bf16[112,128]{1,0:T(8,128)(2,1)S(1)}, u32[]{:S(2)}, u32[]{:S(2)}) collective-permute-start(bf16[112,128]{1,0:T(8,128)(2,1)S(1)} %get-tuple-element.30), channel_id=1, source_target_pairs={{0,16},{16,32},{32,48},{48,64},{64,80},{80,96},{96,112},{112,128},... | collective-permute-start | bytes 86024 | tf_op jit(solution)/shard_map/ppermute | solution.py:289
  6.3 9.6 %collective-permute-start.1 = (bf16[112,128]{1,0:T(8,128)(2,1)S(1)}, bf16[112,128]{1,0:T(8,128)(2,1)S(1)}, u32[]{:S(2)}, u32[]{:S(2)}) collective-permute-start(bf16[112,128]{1,0:T(8,128)(2,1)S(1)} %get-tuple-element.31), channel_id=1, source_target_pairs={{16,0},{32,16},{48,32},{64,48},{80,64},{96,80},{112,96},{128,112},... | collective-permute-start | bytes 86024 | tf_op jit(solution)/shard_map/ppermute | solution.py:289
  12.8 2.1 %copy-start.9 = (f32[31,96]{1,0:T(8,128)S(1)}, f32[31,96]{1,0:T(8,128)}, u32[]{:S(2)}) copy-start(f32[31,96]{1,0:T(8,128)} %param.14) | copy-start | bytes 35716
  12.8 3.1 %copy-start.10 = (s32[384]{0:T(512)S(1)}, s32[384]{0:T(512)}, u32[]{:S(2)}) copy-start(s32[384]{0:T(512)} %param.16) | copy-start | bytes 4612
  12.8 3.2 %copy-start.4 = (bf16[96,384]{1,0:T(8,128)(2,1)S(1)}, bf16[96,384]{1,0:T(8,128)(2,1)}, u32[]{:S(2)}) copy-start(bf16[96,384]{1,0:T(8,128)(2,1)} %inputs_hbm.1) | copy-start | bytes 221188
  12.8 3.2 %copy-start.5 = (bf16[96,384]{1,0:T(8,128)(2,1)S(1)}, bf16[96,384]{1,0:T(8,128)(2,1)}, u32[]{:S(2)}) copy-start(bf16[96,384]{1,0:T(8,128)(2,1)} %upstream_hbm.1) | copy-start | bytes 221188
  16.0 19.1 %collective-permute-start.2 = (bf16[96,896]{1,0:T(8,128)(2,1)S(1)}, bf16[96,896]{1,0:T(8,128)(2,1)S(1)}, u32[]{:S(2)}, u32[]{:S(2)}) collective-permute-start(bf16[96,896]{1,0:T(8,128)(2,1)S(1)} %get-tuple-element.69), channel_id=1, source_target_pairs={{0,2},{2,0},{1,3},{3,1},{4,6},{6,4},{5,7},{7,5},{8,10},{10,8},{9,1... | collective-permute-start | bytes 516104 | tf_op jit(solution)/shard_map/ppermute | solution.py:20
  35.1 0.7 copy-start.6
  35.8 24.7 %collective-permute-start.3 = (bf16[2,96,896]{2,1,0:T(8,128)(2,1)S(1)}, bf16[2,96,896]{2,1,0:T(8,128)(2,1)S(1)}, u32[]{:S(2)}, u32[]{:S(2)}) collective-permute-start(bf16[2,96,896]{2,1,0:T(8,128)(2,1)S(1)} %pad_maximum_fusion.1.own0), channel_id=1, source_target_pairs={{0,4},{4,8},{8,12},{12,0},{1,5},{5,9},{9,13},{13,1},{2,6},{6,10},{... | collective-permute-start | bytes 1032200 | tf_op jit(solution)/shard_map/ppermute | solution.py:327
  39.0 23.4 %collective-permute-start.4 = (bf16[2,96,896]{2,1,0:T(8,128)(2,1)S(1)}, bf16[2,96,896]{2,1,0:T(8,128)(2,1)S(1)}, u32[]{:S(2)}, u32[]{:S(2)}) collective-permute-start(bf16[2,96,896]{2,1,0:T(8,128)(2,1)S(1)} %pad_maximum_fusion.1.own0), channel_id=1, source_target_pairs={{0,12},{4,0},{8,4},{12,8},{1,13},{5,1},{9,5},{13,9},{2,14},{6,2},{... | collective-permute-start | bytes 1032200 | tf_op jit(solution)/shard_map/ppermute | solution.py:327
  42.3 22.6 %collective-permute-start.5 = (bf16[2,96,896]{2,1,0:T(8,128)(2,1)S(1)}, bf16[2,96,896]{2,1,0:T(8,128)(2,1)S(1)}, u32[]{:S(2)}, u32[]{:S(2)}) collective-permute-start(bf16[2,96,896]{2,1,0:T(8,128)(2,1)S(1)} %pad_maximum_fusion.1.own0), channel_id=1, source_target_pairs={{0,8},{4,12},{8,0},{12,4},{1,9},{5,13},{9,1},{13,5},{2,10},{6,14},... | collective-permute-start | bytes 1032200 | tf_op jit(solution)/shard_map/ppermute | solution.py:327
  45.9 23.8 %collective-permute-start.6 = (bf16[2,96,896]{2,1,0:T(8,128)(2,1)S(1)}, bf16[2,96,896]{2,1,0:T(8,128)(2,1)S(1)}, u32[]{:S(2)}, u32[]{:S(2)}) collective-permute-start(bf16[2,96,896]{2,1,0:T(8,128)(2,1)S(1)} %pad_maximum_fusion.1.own0), channel_id=1, source_target_pairs={{0,1},{1,0},{2,3},{3,2},{4,5},{5,4},{6,7},{7,6},{8,9},{9,8},{10,11... | collective-permute-start | bytes 1032200 | tf_op jit(solution)/shard_map/ppermute | solution.py:20
  60.5 9.1 %collective-permute-start.7 = (bf16[2,96,896]{2,1,0:T(8,128)(2,1)S(1)}, bf16[2,96,896]{2,1,0:T(8,128)(2,1)S(1)}, u32[]{:S(2)}, u32[]{:S(2)}) collective-permute-start(bf16[2,96,896]{2,1,0:T(8,128)(2,1)S(1)} %collective-permute-done.3.own1), channel_id=1, source_target_pairs={{0,1},{1,0},{2,3},{3,2},{4,5},{5,4},{6,7},{7,6},{8,9},{9,8},{10,11... | collective-permute-start | bytes 1032200 | tf_op jit(solution)/shard_map/ppermute | solution.py:20
  62.5 7.2 %collective-permute-start.8 = (bf16[2,96,896]{2,1,0:T(8,128)(2,1)S(1)}, bf16[2,96,896]{2,1,0:T(8,128)(2,1)S(1)}, u32[]{:S(2)}, u32[]{:S(2)}) collective-permute-start(bf16[2,96,896]{2,1,0:T(8,128)(2,1)S(1)} %collective-permute-done.4.own2), channel_id=1, source_target_pairs={{0,1},{1,0},{2,3},{3,2},{4,5},{5,4},{6,7},{7,6},{8,9},{9,8},{10,11... | collective-permute-start | bytes 1032200 | tf_op jit(solution)/shard_map/ppermute | solution.py:20
  64.9 4.8 %collective-permute-start.9 = (bf16[2,96,896]{2,1,0:T(8,128)(2,1)S(1)}, bf16[2,96,896]{2,1,0:T(8,128)(2,1)S(1)}, u32[]{:S(2)}, u32[]{:S(2)}) collective-permute-start(bf16[2,96,896]{2,1,0:T(8,128)(2,1)S(1)} %collective-permute-done.5.own3), channel_id=1, source_target_pairs={{0,1},{1,0},{2,3},{3,2},{4,5},{5,4},{6,7},{7,6},{8,9},{9,8},{10,11... | collective-permute-start | bytes 1032200 | tf_op jit(solution)/shard_map/ppermute | solution.py:20
  80.2 0.7 copy-start
  80.9 0.7 copy-start.2
  81.6 3.7 %copy-start.3 = (bf16[8,48,384]{2,1,0:T(8,128)(2,1)S(1)}, bf16[8,48,384]{2,1,0:T(8,128)(2,1)}, u32[]{:S(2)}) copy-start(bf16[8,48,384]{2,1,0:T(8,128)(2,1)} %copy-done.2) | copy-start | bytes 884740
  81.6 5.6 %copy-start.1 = (bf16[8,48,384]{2,1,0:T(8,128)(2,1)S(1)}, bf16[8,48,384]{2,1,0:T(8,128)(2,1)}, u32[]{:S(2)}) copy-start(bf16[8,48,384]{2,1,0:T(8,128)(2,1)} %copy-done) | copy-start | bytes 884740
  81.6 22.6 %all-to-all-start = ((bf16[8,208,384]{2,1,0:T(8,128)(2,1)}), bf16[8,208,384]{2,1,0:T(8,128)(2,1)S(1)}, u32[]{:S(2)}, u32[]{:S(2)}) async-start(bf16[8,208,384]{2,1,0:T(8,128)(2,1)} %get-tuple-element.43), calls=%async_computation | async-start | bytes 2555904 | tf_op jit(solution)/shard_map/all_to_all | solution.py:361
  85.3 11.7 %collective-permute-start.10 = (bf16[8,48,384]{2,1,0:T(8,128)(2,1)S(1)}, bf16[8,48,384]{2,1,0:T(8,128)(2,1)S(1)}, u32[]{:S(2)}, u32[]{:S(2)}) collective-permute-start(bf16[8,48,384]{2,1,0:T(8,128)(2,1)S(1)} %copy-done.3), channel_id=1, source_target_pairs={{0,16},{16,32},{32,48},{48,0},{1,17},{17,33},{33,49},{49,1},{2,18}... | collective-permute-start | bytes 884744 | tf_op jit(solution)/shard_map/ppermute | solution.py:364
  87.2 16.8 %collective-permute-start.11 = (bf16[8,48,384]{2,1,0:T(8,128)(2,1)S(1)}, bf16[8,48,384]{2,1,0:T(8,128)(2,1)S(1)}, u32[]{:S(2)}, u32[]{:S(2)}) collective-permute-start(bf16[8,48,384]{2,1,0:T(8,128)(2,1)S(1)} %copy-done.1), channel_id=1, source_target_pairs={{0,48},{16,0},{32,16},{48,32},{1,49},{17,1},{33,17},{49,33},{2,50}... | collective-permute-start | bytes 884744 | tf_op jit(solution)/shard_map/ppermute | solution.py:364
  91.8 12.2 %collective-permute-start.12 = (bf16[8,48,384]{2,1,0:T(8,128)(2,1)S(1)}, bf16[8,48,384]{2,1,0:T(8,128)(2,1)S(1)}, u32[]{:S(2)}, u32[]{:S(2)}) collective-permute-start(bf16[8,48,384]{2,1,0:T(8,128)(2,1)S(1)} %get-tuple-element.42), channel_id=1, source_target_pairs={{0,32},{16,48},{32,0},{48,16},{1,33},{17,49},{33,1},{49,17},{2,34}... | collective-permute-start | bytes 884744 | tf_op jit(solution)/shard_map/ppermute | solution.py:364
  104.5 35.7 %collective-permute-start.14 = (bf16[112,384]{1,0:T(8,128)(2,1)S(1)}, bf16[112,384]{1,0:T(8,128)(2,1)S(1)}, u32[]{:S(2)}, u32[]{:S(2)}) collective-permute-start(bf16[112,384]{1,0:T(8,128)(2,1)S(1)} %maximum_maximum_fusion), channel_id=1, source_target_pairs={{0,2},{2,0},{1,3},{3,1},{4,6},{6,4},{5,7},{7,5},{8,10},{10,8},{9,1... | collective-permute-start | bytes 258056 | tf_op jit(solution)/shard_map/ppermute | solution.py:20
  118.5 21.7 %collective-permute-start.13 = (bf16[4,48,384]{2,1,0:T(8,128)(2,1)S(1)}, bf16[4,48,384]{2,1,0:T(8,128)(2,1)S(1)}, u32[]{:S(2)}, u32[]{:S(2)}) collective-permute-start(bf16[4,48,384]{2,1,0:T(8,128)(2,1)S(1)} %fusion.2), channel_id=1, source_target_pairs={{0,64},{64,0},{128,192},{192,128},{256,320},{320,256},{384,448},{4... | collective-permute-start | bytes 442376 | tf_op jit(solution)/shard_map/ppermute | solution.py:376
  130.2 27.7 %all-to-all-start.1 = ((f32[64,2,96]{2,1,0:T(2,128)}), f32[64,2,96]{2,1,0:T(2,128)S(1)}, u32[]{:S(2)}, u32[]{:S(2)}) async-start(f32[64,2,96]{2,1,0:T(2,128)} %bitcast.25), calls=%async_computation.1 | async-start | bytes 131072 | tf_op jit(solution)/shard_map/all_to_all | solution.py:393
  140.3 7.9 %collective-permute-start.15 = (bf16[2,48,384]{2,1,0:T(8,128)(2,1)S(1)}, bf16[2,48,384]{2,1,0:T(8,128)(2,1)S(1)}, u32[]{:S(2)}, u32[]{:S(2)}) collective-permute-start(bf16[2,48,384]{2,1,0:T(8,128)(2,1)S(1)} %fusion.4), channel_id=1, source_target_pairs={{0,128},{64,192},{128,0},{192,64},{256,384},{320,448},{384,256},{4... | collective-permute-start | bytes 221192 | tf_op jit(solution)/shard_map/ppermute | solution.py:412
  148.3 9.5 %collective-permute-start.16 = (bf16[1,48,384]{2,1,0:T(8,128)(2,1)S(1)}, bf16[1,48,384]{2,1,0:T(8,128)(2,1)S(1)}, u32[]{:S(2)}, u32[]{:S(2)}) collective-permute-start(bf16[1,48,384]{2,1,0:T(8,128)(2,1)S(1)} %dynamic-slice_convert_fusion.1), channel_id=1, source_target_pairs={{0,256},{64,320},{128,384},{192,448},{256,0},{320,64},{384,128},{4... | collective-permute-start | bytes 110600 | tf_op jit(solution)/shard_map/ppermute | solution.py:412

commit v13 on v10

--- a/solution.py
+++ b/solution.py
@@ -158,7 +158,7 @@
         weight_ref[...], normed_ref[...].reshape(model, lanes), preferred_element_type=f32
     )
     mask_copy.wait()
-    group = 16
+    group = 32
     lane = lax.broadcasted_iota(jnp.int32, (group, 128), 1)
     inside = lax.broadcasted_iota(jnp.int32, (group, lanes), 1) < rows
 
@@ -238,23 +238,29 @@
             mixed_ref[x * 2 + core, 2 * width :] = extra
     finished.append(copy(mixed_ref, mixed_out))
 
-    zero = jnp.zeros((width, rows), bf16)
-    grads = lax.dot_general(
-        normed_ref[:, :, :rows].reshape(model, rows),
-        jnp.concatenate([zero, both_ref[...], zero], axis=0),
-        OVER,
-        preferred_element_type=f32,
-    ) + lax.dot_general(
-        full_ref[:, :, :rows].reshape(model, rows),
-        jnp.concatenate([zero, zero, zero, act_ref[...]], axis=0),
-        OVER,
-        preferred_element_type=f32,
-    )
-    grads_ref[...] = grads.astype(bf16).reshape(grads_ref.shape)
-    kernel = jnp.transpose(kernel_ref[...])[: grads_ref.shape[2]].astype(bf16)
-    for zl in range(8):
-        for y in range(4):
-            grads_ref[zl, y, :, :width] = kernel
+    piece = grads_ref.shape[2]
+    kernel = jnp.transpose(kernel_ref[...])[:piece]
+    kernel = jnp.concatenate([kernel, jnp.zeros((piece, 128 - width), f32)], axis=1)
+    lane = lax.broadcasted_iota(jnp.int32, (piece, 128), 1)
+    for source, factor, start, by, first in (
+        (normed_ref, both_ref, 0, 64, 64),
+        (full_ref, act_ref, 256, 32, 96),
+    ):
+        rest = -factor.shape[0] % 128
+        part = lax.dot_general(
+            source[:, :, :rows].reshape(model, rows),
+            jnp.concatenate([factor[...], jnp.zeros((rest, rows), bf16)], axis=0),
+            OVER,
+            preferred_element_type=f32,
+        )
+        size = part.shape[1]
+        part = part.reshape(8, 4, piece, size)
+        taps_here = jnp.where(lane >= first, pltpu.roll(kernel, by, 1), 0.0)
+        if size > 128:
+            grads_ref[:, :, :, start : start + size - 128] = part[..., : size - 128].astype(bf16)
+        grads_ref[:, :, :, start + size - 128 : start + size] = (
+            part[..., size - 128 :] + taps_here
+        ).astype(bf16)
     for step, out in zip((0, 1, 3, 2), (part0_out, part1_out, part2_out, part3_out)):
         out[...] = grads_ref[:, lax.rem(where_ref[2] + step, 4)]
     for started in finished:
@@ -353,8 +359,8 @@
             pltpu.VMEM((width, 128), f32),
             pltpu.VMEM((2 * width, lanes), f32),
             pltpu.VMEM((width, lanes), f32),
-            pltpu.VMEM((8, 16, lanes), f32),
-            pltpu.VMEM((8, 16, lanes), f32),
+            pltpu.VMEM((8, 32, lanes), f32),
+            pltpu.VMEM((8, 32, lanes), f32),
             pltpu.SemaphoreType.DMA((20,)),
         ],
         compiler_params=pltpu.CompilerParams(vmem_limit_bytes=40 << 20),
@@ -415,10 +421,10 @@
     grads = total[0]
     tail, grads = lax.optimization_barrier((tail, grads))
     tail = jnp.sum(tail, axis=0)
-    kernel_grad = grads[:taps, :width]
-    value_grad = grads[:, width : 2 * width].T
-    gate_grad = grads[:, 2 * width : 3 * width].T
-    project_grad = grads[:, 3 * width :].T
+    kernel_grad = jnp.concatenate([grads[:taps, 192:256], grads[:taps, 352:384]], axis=1)
+    value_grad = grads[:, :width].T
+    gate_grad = grads[:, width : 2 * width].T
+    project_grad = grads[:, 256 : 256 + width].T
     return (inputs_grad, value_grad, gate_grad, project_grad, kernel_grad, tail[0], tail[1])
 
 

time: 158 us -> 157 us (level)
  transfers between devices with their start and end apart: 13 -> 13, of which waited for: 6 -> 6; matrix products, arithmetic and copies ran while one was open for 8% -> 9% of each run, Pallas kernels for 0% -> 0%
where the time goes in v13:
time: 157 us; the launch traced here: 155 us
  starting transfers between devices  91.7 us (58%)
  waiting for transfers between devices  19.4 us (12%)
  blocking collectives  15.4 us (10%)
  Pallas kernels  10.3 us (7%)
  local copies, waits for them, and re-layouts  9.4 us (6%)
  other arithmetic  7.09 us (5%)
    ppermute x3, starting transfers between devices, swap(): return lax.ppermute(value, axis, SWAP)  43.5 us
    all_to_all x1, blocking collectives, over_x(): lax.all_to_all(jnp.broadcast_to(pair[None], (4,) + pair.shape), 'x', 0, 0...  15.4 us
    ppermute x2, starting transfers between devices, on_device(): lax.ppermute(sent, 'zl', [(i, i ^ size) for i in range(8)]).astype(f32)  11.3 us
    all_to_all x1, starting transfers between devices, on_device(): lax.all_to_all(jnp.broadcast_to(tail[None], (32, 2, 2, width)).reshape(64...  10 us
    pallas_call x1, Pallas kernels, on_device(): pl.pallas_call(middle, out_shape=(pltpu.HBM((8, 2 * width + 16, rows), bf...  9.39 us
    ppermute x1, starting transfers between devices, on_device(): lax.ppermute(sent, 'zl', [(i, i ^ 1) for i in range(8)]).astype(f32)  9.29 us
    ppermute x3, waiting for transfers between devices, on_device(): lax.ppermute(sent, 'y', [(i, (i + step) % 4) for i in range(4)])  9.21 us
    ppermute x3, starting transfers between devices, on_device(): lax.ppermute(sent, 'y', [(i, (i + step) % 4) for i in range(4)])  8.4 us
  transfers between devices with their start and end apart: 13, of which 6 were waited for; matrix products, arithmetic and copies ran while one was open for 9% of the time, Pallas kernels for 0%

profile of v13, /device:TPU:1, one launch (start us, length us, event | category | flops | bytes accessed | tf_op | source)
XLA Modules:
  0.0 154.5 jit_solution(11659305944584867517)
XLA Ops:
  1.3 0.9 shard_map.144
  2.3 4.0 %collective-permute-start = (bf16[112,128]{1,0:T(8,128)(2,1)S(1)}, bf16[112,128]{1,0:T(8,128)(2,1)S(1)}, u32[]{:S(2)}, u32[]{:S(2)}) collective-permute-start(bf16[112,128]{1,0:T(8,128)(2,1)S(1)} %get-tuple-element.30), channel_id=1, source_target_pairs={{0,16},{16,32},{32,48},{48,64},{64,80},{80,96},{96,112},{112,128},... | collective-permute-start | bytes 86024 | tf_op jit(solution)/shard_map/ppermute | solution.py:303
  6.3 1.3 collective-permute-start.1
  7.6 0.8 reshape.52
  8.4 0.8 reshape.54
  9.2 1.2 copy.29
  10.4 1.2 copy.30
  11.6 1.1 fusion
  12.7 1.3 fusion.8
  14.7 0.8 select_maximum_fusion.small_hbm
  15.6 15.4 %collective-permute-start.2 = (bf16[96,896]{1,0:T(8,128)(2,1)S(1)}, bf16[96,896]{1,0:T(8,128)(2,1)S(1)}, u32[]{:S(2)}, u32[]{:S(2)}) collective-permute-start(bf16[96,896]{1,0:T(8,128)(2,1)S(1)} %get-tuple-element.69), channel_id=1, source_target_pairs={{0,2},{2,0},{1,3},{3,1},{4,6},{6,4},{5,7},{7,5},{8,10},{10,8},{9,1... | collective-permute-start | bytes 516104 | tf_op jit(solution)/shard_map/ppermute | solution.py:20
  31.7 3.1 %collective-permute-done.2 = bf16[96,896]{1,0:T(8,128)(2,1)S(1)} collective-permute-done((bf16[96,896]{1,0:T(8,128)(2,1)S(1)}, bf16[96,896]{1,0:T(8,128)(2,1)S(1)}, u32[]{:S(2)}, u32[]{:S(2)}) %collective-permute-start.2) | collective-permute-done | bytes 172064 | tf_op jit(solution)/shard_map/ppermute | solution.py:20
  34.9 15.4 %all_to_all.15.own_hbm = bf16[4,2,96,896]{3,2,1,0:T(8,128)(2,1)S(1)} all-to-all(bf16[4,2,96,896]{3,2,1,0:T(8,128)(2,1)S(1)} %broadcast_in_dim.33), channel_id=1, replica_groups=mesh['zl'=8,'y'=4,'x'=4,'zh'=2,'core'=2] {'x'}, dimensions={0} | all-to-all | bytes 2752512 | tf_op jit(solution)/shard_map/all_to_all | solution.py:24
  50.3 15.2 %collective-permute-start.3 = (bf16[4,2,96,896]{3,2,1,0:T(8,128)(2,1)S(1)}, bf16[4,2,96,896]{3,2,1,0:T(8,128)(2,1)}, u32[]{:S(2)}, u32[]{:S(2)}) collective-permute-start(bf16[4,2,96,896]{3,2,1,0:T(8,128)(2,1)S(1)} %all_to_all.15.own_hbm), channel_id=1, source_target_pairs={{0,1},{1,0},{2,3},{3,2},{4,5},{5,4},{6,7},{7,6},{8,9},{9,8},{10,11... | collective-permute-start | bytes 4128776 | tf_op jit(solution)/shard_map/ppermute | solution.py:20
  65.6 1.1 copy.35.weight_hbm
  66.6 1.8 %collective-permute-done.3.other_hbm = bf16[4,2,96,896]{3,2,1,0:T(8,128)(2,1)} collective-permute-done((bf16[4,2,96,896]{3,2,1,0:T(8,128)(2,1)S(1)}, bf16[4,2,96,896]{3,2,1,0:T(8,128)(2,1)}, u32[]{:S(2)}, u32[]{:S(2)}) %collective-permute-start.3) | collective-permute-done | bytes 1376288 | tf_op jit(solution)/shard_map/ppermute | solution.py:20
  68.4 9.4 %shard_map.145 = (bf16[8,208,384]{2,1,0:T(8,128)(2,1)}, bf16[8,48,384]{2,1,0:T(8,128)(2,1)S(1)}, bf16[8,48,384]{2,1,0:T(8,128)(2,1)S(1)}, bf16[8,48,384]{2,1,0:T...) custom-call(s32[3]{0:T(128)S(1)} %pad_add_fusion.where_ref, bf16[4,2,96,896]{3,2,1,0:T(8,128)(2,1)} %copy-done, ...), custom_call_target="tpu_custom_call" | custom-call | tf_op jit(solution)/shard_map/pallas_call | solution.py:340
  77.8 3.9 %all-to-all-start.1 = ((bf16[8,208,384]{2,1,0:T(8,128)(2,1)}), bf16[8,208,384]{2,1,0:T(8,128)(2,1)S(1)}, u32[]{:S(2)}, u32[]{:S(2)}) async-start(bf16[8,208,384]{2,1,0:T(8,128)(2,1)} %get-tuple-element.43), calls=%async_computation.1 | async-start | bytes 2555904 | tf_op jit(solution)/shard_map/all_to_all | solution.py:369
  81.7 1.9 %collective-permute-start.4 = (bf16[8,48,384]{2,1,0:T(8,128)(2,1)S(1)}, bf16[8,48,384]{2,1,0:T(8,128)(2,1)S(1)}, u32[]{:S(2)}, u32[]{:S(2)}) collective-permute-start(bf16[8,48,384]{2,1,0:T(8,128)(2,1)S(1)} %get-tuple-element.40), channel_id=1, source_target_pairs={{0,16},{16,32},{32,48},{48,0},{1,17},{17,33},{33,49},{49,1},{2,18}... | collective-permute-start | bytes 884744 | tf_op jit(solution)/shard_map/ppermute | solution.py:372
  83.6 4.6 %collective-permute-start.5 = (bf16[8,48,384]{2,1,0:T(8,128)(2,1)S(1)}, bf16[8,48,384]{2,1,0:T(8,128)(2,1)S(1)}, u32[]{:S(2)}, u32[]{:S(2)}) collective-permute-start(bf16[8,48,384]{2,1,0:T(8,128)(2,1)S(1)} %get-tuple-element.41), channel_id=1, source_target_pairs={{0,48},{16,0},{32,16},{48,32},{1,49},{17,1},{33,17},{49,33},{2,50}... | collective-permute-start | bytes 884744 | tf_op jit(solution)/shard_map/ppermute | solution.py:372
  88.2 1.9 %collective-permute-start.6 = (bf16[8,48,384]{2,1,0:T(8,128)(2,1)S(1)}, bf16[8,48,384]{2,1,0:T(8,128)(2,1)S(1)}, u32[]{:S(2)}, u32[]{:S(2)}) collective-permute-start(bf16[8,48,384]{2,1,0:T(8,128)(2,1)S(1)} %get-tuple-element.42), channel_id=1, source_target_pairs={{0,32},{16,48},{32,0},{48,16},{1,33},{17,49},{33,1},{49,17},{2,34}... | collective-permute-start | bytes 884744 | tf_op jit(solution)/shard_map/ppermute | solution.py:372
  90.3 0.8 slice_reduce_fusion.4
  91.1 2.2 %collective-permute-done.4 = bf16[8,48,384]{2,1,0:T(8,128)(2,1)S(1)} collective-permute-done((bf16[8,48,384]{2,1,0:T(8,128)(2,1)S(1)}, bf16[8,48,384]{2,1,0:T(8,128)(2,1)S(1)}, u32[]{:S(2)}, u32[]{:S(2)}) %collective-permute-start.4) | collective-permute-done | bytes 294944 | tf_op jit(solution)/shard_map/ppermute | solution.py:372
  93.3 7.0 %collective-permute-done.5 = bf16[8,48,384]{2,1,0:T(8,128)(2,1)S(1)} collective-permute-done((bf16[8,48,384]{2,1,0:T(8,128)(2,1)S(1)}, bf16[8,48,384]{2,1,0:T(8,128)(2,1)S(1)}, u32[]{:S(2)}, u32[]{:S(2)}) %collective-permute-start.5) | collective-permute-done | bytes 294944 | tf_op jit(solution)/shard_map/ppermute | solution.py:372
  100.8 12.9 %collective-permute-start.8 = (bf16[112,384]{1,0:T(8,128)(2,1)S(1)}, bf16[112,384]{1,0:T(8,128)(2,1)S(1)}, u32[]{:S(2)}, u32[]{:S(2)}) collective-permute-start(bf16[112,384]{1,0:T(8,128)(2,1)S(1)} %maximum_maximum_fusion), channel_id=1, source_target_pairs={{0,2},{2,0},{1,3},{3,1},{4,6},{6,4},{5,7},{7,5},{8,10},{10,8},{9,1... | collective-permute-start | bytes 258056 | tf_op jit(solution)/shard_map/ppermute | solution.py:20
  113.7 1.1 multiply_reduce_fusion.1
  114.8 9.3 %collective-permute-start.7 = (bf16[4,48,384]{2,1,0:T(8,128)(2,1)S(1)}, bf16[4,48,384]{2,1,0:T(8,128)(2,1)S(1)}, u32[]{:S(2)}, u32[]{:S(2)}) collective-permute-start(bf16[4,48,384]{2,1,0:T(8,128)(2,1)S(1)} %fusion.2), channel_id=1, source_target_pairs={{0,64},{64,0},{128,192},{192,128},{256,320},{320,256},{384,448},{4... | collective-permute-start | bytes 442376 | tf_op jit(solution)/shard_map/ppermute | solution.py:384
  124.8 10.0 %all-to-all-start.2 = ((f32[64,2,96]{2,1,0:T(2,128)}), f32[64,2,96]{2,1,0:T(2,128)S(1)}, u32[]{:S(2)}, u32[]{:S(2)}) async-start(f32[64,2,96]{2,1,0:T(2,128)} %bitcast.24), calls=%async_computation.2 | async-start | bytes 131072 | tf_op jit(solution)/shard_map/all_to_all | solution.py:401
  134.9 3.8 %collective-permute-start.9 = (bf16[2,48,384]{2,1,0:T(8,128)(2,1)S(1)}, bf16[2,48,384]{2,1,0:T(8,128)(2,1)S(1)}, u32[]{:S(2)}, u32[]{:S(2)}) collective-permute-start(bf16[2,48,384]{2,1,0:T(8,128)(2,1)S(1)} %fusion.4), channel_id=1, source_target_pairs={{0,128},{64,192},{128,0},{192,64},{256,384},{320,448},{384,256},{4... | collective-permute-start | bytes 221192 | tf_op jit(solution)/shard_map/ppermute | solution.py:420
  138.8 4.3 %collective-permute-done.9 = bf16[2,48,384]{2,1,0:T(8,128)(2,1)S(1)} collective-permute-done((bf16[2,48,384]{2,1,0:T(8,128)(2,1)S(1)}, bf16[2,48,384]{2,1,0:T(8,128)(2,1)S(1)}, u32[]{:S(2)}, u32[]{:S(2)}) %collective-permute-start.9) | collective-permute-done | bytes 73760 | tf_op jit(solution)/shard_map/ppermute | solution.py:420
  143.1 7.5 %collective-permute-start.10 = (bf16[1,48,384]{2,1,0:T(8,128)(2,1)S(1)}, bf16[1,48,384]{2,1,0:T(8,128)(2,1)S(1)}, u32[]{:S(2)}, u32[]{:S(2)}) collective-permute-start(bf16[1,48,384]{2,1,0:T(8,128)(2,1)S(1)} %dynamic-slice_convert_fusion.1), channel_id=1, source_target_pairs={{0,256},{64,320},{128,384},{192,448},{256,0},{320,64},{384,128},{4... | collective-permute-start | bytes 110600 | tf_op jit(solution)/shard_map/ppermute | solution.py:420
  151.4 1.0 collective-permute-done.10
  (74 shorter events, 6.4 us)
Async XLA Ops:
  0.6 10.9 %copy-start.5 = (f32[1536]{0:T(1024)S(1)}, f32[1536]{0:T(1024)}, u32[]{:S(2)}) copy-start(f32[1536]{0:T(1024)} %param.10) | copy-start | bytes 18436
  0.6 10.9 %copy-start.4 = (f32[1536]{0:T(1024)S(1)}, f32[1536]{0:T(1024)}, u32[]{:S(2)}) copy-start(f32[1536]{0:T(1024)} %param.11) | copy-start | bytes 18436
  2.3 13.3 %collective-permute-start = (bf16[112,128]{1,0:T(8,128)(2,1)S(1)}, bf16[112,128]{1,0:T(8,128)(2,1)S(1)}, u32[]{:S(2)}, u32[]{:S(2)}) collective-permute-start(bf16[112,128]{1,0:T(8,128)(2,1)S(1)} %get-tuple-element.30), channel_id=1, source_target_pairs={{0,16},{16,32},{32,48},{48,64},{64,80},{80,96},{96,112},{112,128},... | collective-permute-start | bytes 86024 | tf_op jit(solution)/shard_map/ppermute | solution.py:303
  6.3 9.2 %collective-permute-start.1 = (bf16[112,128]{1,0:T(8,128)(2,1)S(1)}, bf16[112,128]{1,0:T(8,128)(2,1)S(1)}, u32[]{:S(2)}, u32[]{:S(2)}) collective-permute-start(bf16[112,128]{1,0:T(8,128)(2,1)S(1)} %get-tuple-element.31), channel_id=1, source_target_pairs={{16,0},{32,16},{48,32},{64,48},{80,64},{96,80},{112,96},{128,112},... | collective-permute-start | bytes 86024 | tf_op jit(solution)/shard_map/ppermute | solution.py:303
  12.7 1.8 %copy-start.6 = (f32[31,96]{1,0:T(8,128)S(1)}, f32[31,96]{1,0:T(8,128)}, u32[]{:S(2)}) copy-start(f32[31,96]{1,0:T(8,128)} %param.14) | copy-start | bytes 35716
  12.7 2.8 %copy-start.7 = (s32[384]{0:T(512)S(1)}, s32[384]{0:T(512)}, u32[]{:S(2)}) copy-start(s32[384]{0:T(512)} %param.16) | copy-start | bytes 4612
  12.7 2.9 %copy-start.1 = (bf16[96,384]{1,0:T(8,128)(2,1)S(1)}, bf16[96,384]{1,0:T(8,128)(2,1)}, u32[]{:S(2)}) copy-start(bf16[96,384]{1,0:T(8,128)(2,1)} %inputs_hbm.1) | copy-start | bytes 221188
  12.7 2.9 %copy-start.2 = (bf16[96,384]{1,0:T(8,128)(2,1)S(1)}, bf16[96,384]{1,0:T(8,128)(2,1)}, u32[]{:S(2)}) copy-start(bf16[96,384]{1,0:T(8,128)(2,1)} %upstream_hbm.1) | copy-start | bytes 221188
  15.6 19.1 %collective-permute-start.2 = (bf16[96,896]{1,0:T(8,128)(2,1)S(1)}, bf16[96,896]{1,0:T(8,128)(2,1)S(1)}, u32[]{:S(2)}, u32[]{:S(2)}) collective-permute-start(bf16[96,896]{1,0:T(8,128)(2,1)S(1)} %get-tuple-element.69), channel_id=1, source_target_pairs={{0,2},{2,0},{1,3},{3,1},{4,6},{6,4},{5,7},{7,5},{8,10},{10,8},{9,1... | collective-permute-start | bytes 516104 | tf_op jit(solution)/shard_map/ppermute | solution.py:20
  34.8 15.6 %copy-start.3 = (bf16[96,896]{1,0:T(8,128)(2,1)}, bf16[96,896]{1,0:T(8,128)(2,1)S(1)}, u32[]{:S(2)}) copy-start(bf16[96,896]{1,0:T(8,128)(2,1)S(1)} %collective-permute-done.2) | copy-start | bytes 516100
  50.3 18.1 %copy-start = (bf16[4,2,96,896]{3,2,1,0:T(8,128)(2,1)}, bf16[4,2,96,896]{3,2,1,0:T(8,128)(2,1)S(1)}, u32[]{:S(2)}) copy-start(bf16[4,2,96,896]{3,2,1,0:T(8,128)(2,1)S(1)} %all_to_all.15.own_hbm) | copy-start | bytes 4128772
  50.3 18.1 %collective-permute-start.3 = (bf16[4,2,96,896]{3,2,1,0:T(8,128)(2,1)S(1)}, bf16[4,2,96,896]{3,2,1,0:T(8,128)(2,1)}, u32[]{:S(2)}, u32[]{:S(2)}) collective-permute-start(bf16[4,2,96,896]{3,2,1,0:T(8,128)(2,1)S(1)} %all_to_all.15.own_hbm), channel_id=1, source_target_pairs={{0,1},{1,0},{2,3},{3,2},{4,5},{5,4},{6,7},{7,6},{8,9},{9,8},{10,11... | collective-permute-start | bytes 4128776 | tf_op jit(solution)/shard_map/ppermute | solution.py:20
  77.8 22.7 %all-to-all-start.1 = ((bf16[8,208,384]{2,1,0:T(8,128)(2,1)}), bf16[8,208,384]{2,1,0:T(8,128)(2,1)S(1)}, u32[]{:S(2)}, u32[]{:S(2)}) async-start(bf16[8,208,384]{2,1,0:T(8,128)(2,1)} %get-tuple-element.43), calls=%async_computation.1 | async-start | bytes 2555904 | tf_op jit(solution)/shard_map/all_to_all | solution.py:369
  81.7 11.6 %collective-permute-start.4 = (bf16[8,48,384]{2,1,0:T(8,128)(2,1)S(1)}, bf16[8,48,384]{2,1,0:T(8,128)(2,1)S(1)}, u32[]{:S(2)}, u32[]{:S(2)}) collective-permute-start(bf16[8,48,384]{2,1,0:T(8,128)(2,1)S(1)} %get-tuple-element.40), channel_id=1, source_target_pairs={{0,16},{16,32},{32,48},{48,0},{1,17},{17,33},{33,49},{49,1},{2,18}... | collective-permute-start | bytes 884744 | tf_op jit(solution)/shard_map/ppermute | solution.py:372
  83.6 16.7 %collective-permute-start.5 = (bf16[8,48,384]{2,1,0:T(8,128)(2,1)S(1)}, bf16[8,48,384]{2,1,0:T(8,128)(2,1)S(1)}, u32[]{:S(2)}, u32[]{:S(2)}) collective-permute-start(bf16[8,48,384]{2,1,0:T(8,128)(2,1)S(1)} %get-tuple-element.41), channel_id=1, source_target_pairs={{0,48},{16,0},{32,16},{48,32},{1,49},{17,1},{33,17},{49,33},{2,50}... | collective-permute-start | bytes 884744 | tf_op jit(solution)/shard_map/ppermute | solution.py:372
  88.2 12.1 %collective-permute-start.6 = (bf16[8,48,384]{2,1,0:T(8,128)(2,1)S(1)}, bf16[8,48,384]{2,1,0:T(8,128)(2,1)S(1)}, u32[]{:S(2)}, u32[]{:S(2)}) collective-permute-start(bf16[8,48,384]{2,1,0:T(8,128)(2,1)S(1)} %get-tuple-element.42), channel_id=1, source_target_pairs={{0,32},{16,48},{32,0},{48,16},{1,33},{17,49},{33,1},{49,17},{2,34}... | collective-permute-start | bytes 884744 | tf_op jit(solution)/shard_map/ppermute | solution.py:372
  100.8 34.0 %collective-permute-start.8 = (bf16[112,384]{1,0:T(8,128)(2,1)S(1)}, bf16[112,384]{1,0:T(8,128)(2,1)S(1)}, u32[]{:S(2)}, u32[]{:S(2)}) collective-permute-start(bf16[112,384]{1,0:T(8,128)(2,1)S(1)} %maximum_maximum_fusion), channel_id=1, source_target_pairs={{0,2},{2,0},{1,3},{3,1},{4,6},{6,4},{5,7},{7,5},{8,10},{10,8},{9,1... | collective-permute-start | bytes 258056 | tf_op jit(solution)/shard_map/ppermute | solution.py:20
  114.8 20.0 %collective-permute-start.7 = (bf16[4,48,384]{2,1,0:T(8,128)(2,1)S(1)}, bf16[4,48,384]{2,1,0:T(8,128)(2,1)S(1)}, u32[]{:S(2)}, u32[]{:S(2)}) collective-permute-start(bf16[4,48,384]{2,1,0:T(8,128)(2,1)S(1)} %fusion.2), channel_id=1, source_target_pairs={{0,64},{64,0},{128,192},{192,128},{256,320},{320,256},{384,448},{4... | collective-permute-start | bytes 442376 | tf_op jit(solution)/shard_map/ppermute | solution.py:384
  124.8 27.6 %all-to-all-start.2 = ((f32[64,2,96]{2,1,0:T(2,128)}), f32[64,2,96]{2,1,0:T(2,128)S(1)}, u32[]{:S(2)}, u32[]{:S(2)}) async-start(f32[64,2,96]{2,1,0:T(2,128)} %bitcast.24), calls=%async_computation.2 | async-start | bytes 131072 | tf_op jit(solution)/shard_map/all_to_all | solution.py:401
  134.9 8.2 %collective-permute-start.9 = (bf16[2,48,384]{2,1,0:T(8,128)(2,1)S(1)}, bf16[2,48,384]{2,1,0:T(8,128)(2,1)S(1)}, u32[]{:S(2)}, u32[]{:S(2)}) collective-permute-start(bf16[2,48,384]{2,1,0:T(8,128)(2,1)S(1)} %fusion.4), channel_id=1, source_target_pairs={{0,128},{64,192},{128,0},{192,64},{256,384},{320,448},{384,256},{4... | collective-permute-start | bytes 221192 | tf_op jit(solution)/shard_map/ppermute | solution.py:420
  143.1 9.2 %collective-permute-start.10 = (bf16[1,48,384]{2,1,0:T(8,128)(2,1)S(1)}, bf16[1,48,384]{2,1,0:T(8,128)(2,1)S(1)}, u32[]{:S(2)}, u32[]{:S(2)}) collective-permute-start(bf16[1,48,384]{2,1,0:T(8,128)(2,1)S(1)} %dynamic-slice_convert_fusion.1), channel_id=1, source_target_pairs={{0,256},{64,320},{128,384},{192,448},{256,0},{320,64},{384,128},{4... | collective-permute-start | bytes 110600 | tf_op jit(solution)/shard_map/ppermute | solution.py:420

commit v14 on v13

--- a/solution.py
+++ b/solution.py
@@ -83,7 +83,7 @@
         ref[:width] = jnp.where(
             own(lane), ends_ref[i, 0].astype(f32), jnp.where(moved(lane), up, 0.0)
         ).astype(bf16)
-        mask = mask_ref[:, starts[i] : starts[i] + 128].astype(f32)
+        mask = mask_ref[pl.ds(starts[i], 128)].reshape(1, 128).astype(f32)
         ref[width:] = jnp.where(own(low), jnp.broadcast_to(mask, (16, 128)), 0.0).astype(bf16)
 
     pack(0, lambda i: i >= 98, lambda i: (i >= 49) & (i < 64), right_ref)
@@ -298,7 +298,7 @@
     )(
         pltpu.with_memory_space_constraint(inputs, pltpu.HBM),
         pltpu.with_memory_space_constraint(upstream, pltpu.HBM),
-        frame_mask.reshape(1, rows),
+        frame_mask,
     )
     edge = lax.ppermute(to_right, FRAME, [(i, i + 1) for i in range(31)]) + lax.ppermute(
         to_left, FRAME, [(i + 1, i) for i in range(31)]

time: 157 us -> 157 us (level)
    unnamed x19 -> x21, local copies, waits for them, and re-layouts: 2.51 us -> 3.18 us
where the time goes in v14:
time: 157 us; the launch traced here: 155 us
  starting transfers between devices  91.7 us (58%)
  waiting for transfers between devices  19.4 us (12%)
  blocking collectives  15.4 us (10%)
  Pallas kernels  10.3 us (7%)
  local copies, waits for them, and re-layouts  9.37 us (6%)
  other arithmetic  7.07 us (5%)
    ppermute x3, starting transfers between devices, swap(): return lax.ppermute(value, axis, SWAP)  43.6 us
    all_to_all x1, blocking collectives, over_x(): lax.all_to_all(jnp.broadcast_to(pair[None], (4,) + pair.shape), 'x', 0, 0...  15.4 us
    ppermute x2, starting transfers between devices, on_device(): lax.ppermute(sent, 'zl', [(i, i ^ size) for i in range(8)]).astype(f32)  11.3 us
    all_to_all x1, starting transfers between devices, on_device(): lax.all_to_all(jnp.broadcast_to(tail[None], (32, 2, 2, width)).reshape(64...  9.99 us
    pallas_call x1, Pallas kernels, on_device(): pl.pallas_call(middle, out_shape=(pltpu.HBM((8, 2 * width + 16, rows), bf...  9.4 us
    ppermute x1, starting transfers between devices, on_device(): lax.ppermute(sent, 'zl', [(i, i ^ 1) for i in range(8)]).astype(f32)  9.28 us
    ppermute x3, waiting for transfers between devices, on_device(): lax.ppermute(sent, 'y', [(i, (i + step) % 4) for i in range(4)])  9.21 us
    ppermute x3, starting transfers between devices, on_device(): lax.ppermute(sent, 'y', [(i, (i + step) % 4) for i in range(4)])  8.4 us
  transfers between devices with their start and end apart: 13, of which 6 were waited for; matrix products, arithmetic and copies ran while one was open for 9% of the time, Pallas kernels for 0%

profile of v14, /device:TPU:1, one launch (start us, length us, event | category | flops | bytes accessed | tf_op | source)
XLA Modules:
  0.0 154.5 jit_solution(11788608873777563416)
XLA Ops:
  1.3 0.9 shard_map.144
  2.3 4.0 %collective-permute-start = (bf16[112,128]{1,0:T(8,128)(2,1)S(1)}, bf16[112,128]{1,0:T(8,128)(2,1)S(1)}, u32[]{:S(2)}, u32[]{:S(2)}) collective-permute-start(bf16[112,128]{1,0:T(8,128)(2,1)S(1)} %get-tuple-element.30), channel_id=1, source_target_pairs={{0,16},{16,32},{32,48},{48,64},{64,80},{80,96},{96,112},{112,128},... | collective-permute-start | bytes 86024 | tf_op jit(solution)/shard_map/ppermute | solution.py:303
  6.3 1.3 collective-permute-start.1
  7.6 0.8 reshape.48
  8.4 0.8 reshape.50
  9.2 1.2 copy.29
  10.4 1.2 copy.30
  11.6 1.1 fusion
  12.7 1.3 fusion.8
  14.7 0.8 select_maximum_fusion.small_hbm
  15.6 15.4 %collective-permute-start.2 = (bf16[96,896]{1,0:T(8,128)(2,1)S(1)}, bf16[96,896]{1,0:T(8,128)(2,1)S(1)}, u32[]{:S(2)}, u32[]{:S(2)}) collective-permute-start(bf16[96,896]{1,0:T(8,128)(2,1)S(1)} %get-tuple-element.69), channel_id=1, source_target_pairs={{0,2},{2,0},{1,3},{3,1},{4,6},{6,4},{5,7},{7,5},{8,10},{10,8},{9,1... | collective-permute-start | bytes 516104 | tf_op jit(solution)/shard_map/ppermute | solution.py:20
  31.7 3.1 %collective-permute-done.2 = bf16[96,896]{1,0:T(8,128)(2,1)S(1)} collective-permute-done((bf16[96,896]{1,0:T(8,128)(2,1)S(1)}, bf16[96,896]{1,0:T(8,128)(2,1)S(1)}, u32[]{:S(2)}, u32[]{:S(2)}) %collective-permute-start.2) | collective-permute-done | bytes 172064 | tf_op jit(solution)/shard_map/ppermute | solution.py:20
  34.9 15.4 %all_to_all.15.own_hbm = bf16[4,2,96,896]{3,2,1,0:T(8,128)(2,1)S(1)} all-to-all(bf16[4,2,96,896]{3,2,1,0:T(8,128)(2,1)S(1)} %broadcast_in_dim.33), channel_id=1, replica_groups=mesh['zl'=8,'y'=4,'x'=4,'zh'=2,'core'=2] {'x'}, dimensions={0} | all-to-all | bytes 2752512 | tf_op jit(solution)/shard_map/all_to_all | solution.py:24
  50.3 15.2 %collective-permute-start.3 = (bf16[4,2,96,896]{3,2,1,0:T(8,128)(2,1)S(1)}, bf16[4,2,96,896]{3,2,1,0:T(8,128)(2,1)}, u32[]{:S(2)}, u32[]{:S(2)}) collective-permute-start(bf16[4,2,96,896]{3,2,1,0:T(8,128)(2,1)S(1)} %all_to_all.15.own_hbm), channel_id=1, source_target_pairs={{0,1},{1,0},{2,3},{3,2},{4,5},{5,4},{6,7},{7,6},{8,9},{9,8},{10,11... | collective-permute-start | bytes 4128776 | tf_op jit(solution)/shard_map/ppermute | solution.py:20
  65.5 1.1 copy.35.weight_hbm
  66.6 1.8 %collective-permute-done.3.other_hbm = bf16[4,2,96,896]{3,2,1,0:T(8,128)(2,1)} collective-permute-done((bf16[4,2,96,896]{3,2,1,0:T(8,128)(2,1)S(1)}, bf16[4,2,96,896]{3,2,1,0:T(8,128)(2,1)}, u32[]{:S(2)}, u32[]{:S(2)}) %collective-permute-start.3) | collective-permute-done | bytes 1376288 | tf_op jit(solution)/shard_map/ppermute | solution.py:20
  68.4 9.4 %shard_map.145 = (bf16[8,208,384]{2,1,0:T(8,128)(2,1)}, bf16[8,48,384]{2,1,0:T(8,128)(2,1)S(1)}, bf16[8,48,384]{2,1,0:T(8,128)(2,1)S(1)}, bf16[8,48,384]{2,1,0:T...) custom-call(s32[3]{0:T(128)S(1)} %pad_add_fusion.where_ref, bf16[4,2,96,896]{3,2,1,0:T(8,128)(2,1)} %copy-done.2, ...), custom_call_target="tpu_custom_call" | custom-call | tf_op jit(solution)/shard_map/pallas_call | solution.py:340
  77.8 3.8 %all-to-all-start.1 = ((bf16[8,208,384]{2,1,0:T(8,128)(2,1)}), bf16[8,208,384]{2,1,0:T(8,128)(2,1)S(1)}, u32[]{:S(2)}, u32[]{:S(2)}) async-start(bf16[8,208,384]{2,1,0:T(8,128)(2,1)} %get-tuple-element.43), calls=%async_computation.1 | async-start | bytes 2555904 | tf_op jit(solution)/shard_map/all_to_all | solution.py:369
  81.7 1.9 %collective-permute-start.4 = (bf16[8,48,384]{2,1,0:T(8,128)(2,1)S(1)}, bf16[8,48,384]{2,1,0:T(8,128)(2,1)S(1)}, u32[]{:S(2)}, u32[]{:S(2)}) collective-permute-start(bf16[8,48,384]{2,1,0:T(8,128)(2,1)S(1)} %get-tuple-element.40), channel_id=1, source_target_pairs={{0,16},{16,32},{32,48},{48,0},{1,17},{17,33},{33,49},{49,1},{2,18}... | collective-permute-start | bytes 884744 | tf_op jit(solution)/shard_map/ppermute | solution.py:372
  83.6 4.6 %collective-permute-start.5 = (bf16[8,48,384]{2,1,0:T(8,128)(2,1)S(1)}, bf16[8,48,384]{2,1,0:T(8,128)(2,1)S(1)}, u32[]{:S(2)}, u32[]{:S(2)}) collective-permute-start(bf16[8,48,384]{2,1,0:T(8,128)(2,1)S(1)} %get-tuple-element.41), channel_id=1, source_target_pairs={{0,48},{16,0},{32,16},{48,32},{1,49},{17,1},{33,17},{49,33},{2,50}... | collective-permute-start | bytes 884744 | tf_op jit(solution)/shard_map/ppermute | solution.py:372
  88.2 1.9 %collective-permute-start.6 = (bf16[8,48,384]{2,1,0:T(8,128)(2,1)S(1)}, bf16[8,48,384]{2,1,0:T(8,128)(2,1)S(1)}, u32[]{:S(2)}, u32[]{:S(2)}) collective-permute-start(bf16[8,48,384]{2,1,0:T(8,128)(2,1)S(1)} %get-tuple-element.42), channel_id=1, source_target_pairs={{0,32},{16,48},{32,0},{48,16},{1,33},{17,49},{33,1},{49,17},{2,34}... | collective-permute-start | bytes 884744 | tf_op jit(solution)/shard_map/ppermute | solution.py:372
  90.3 0.8 slice_reduce_fusion.4
  91.1 2.2 %collective-permute-done.4 = bf16[8,48,384]{2,1,0:T(8,128)(2,1)S(1)} collective-permute-done((bf16[8,48,384]{2,1,0:T(8,128)(2,1)S(1)}, bf16[8,48,384]{2,1,0:T(8,128)(2,1)S(1)}, u32[]{:S(2)}, u32[]{:S(2)}) %collective-permute-start.4) | collective-permute-done | bytes 294944 | tf_op jit(solution)/shard_map/ppermute | solution.py:372
  93.2 7.0 %collective-permute-done.5 = bf16[8,48,384]{2,1,0:T(8,128)(2,1)S(1)} collective-permute-done((bf16[8,48,384]{2,1,0:T(8,128)(2,1)S(1)}, bf16[8,48,384]{2,1,0:T(8,128)(2,1)S(1)}, u32[]{:S(2)}, u32[]{:S(2)}) %collective-permute-start.5) | collective-permute-done | bytes 294944 | tf_op jit(solution)/shard_map/ppermute | solution.py:372
  100.8 12.9 %collective-permute-start.8 = (bf16[112,384]{1,0:T(8,128)(2,1)S(1)}, bf16[112,384]{1,0:T(8,128)(2,1)S(1)}, u32[]{:S(2)}, u32[]{:S(2)}) collective-permute-start(bf16[112,384]{1,0:T(8,128)(2,1)S(1)} %maximum_maximum_fusion), channel_id=1, source_target_pairs={{0,2},{2,0},{1,3},{3,1},{4,6},{6,4},{5,7},{7,5},{8,10},{10,8},{9,1... | collective-permute-start | bytes 258056 | tf_op jit(solution)/shard_map/ppermute | solution.py:20
  113.7 1.1 multiply_reduce_fusion.1
  114.8 9.3 %collective-permute-start.7 = (bf16[4,48,384]{2,1,0:T(8,128)(2,1)S(1)}, bf16[4,48,384]{2,1,0:T(8,128)(2,1)S(1)}, u32[]{:S(2)}, u32[]{:S(2)}) collective-permute-start(bf16[4,48,384]{2,1,0:T(8,128)(2,1)S(1)} %fusion.2), channel_id=1, source_target_pairs={{0,64},{64,0},{128,192},{192,128},{256,320},{320,256},{384,448},{4... | collective-permute-start | bytes 442376 | tf_op jit(solution)/shard_map/ppermute | solution.py:384
  124.7 10.0 %all-to-all-start.2 = ((f32[64,2,96]{2,1,0:T(2,128)}), f32[64,2,96]{2,1,0:T(2,128)S(1)}, u32[]{:S(2)}, u32[]{:S(2)}) async-start(f32[64,2,96]{2,1,0:T(2,128)} %bitcast.24), calls=%async_computation.2 | async-start | bytes 131072 | tf_op jit(solution)/shard_map/all_to_all | solution.py:401
  134.9 3.8 %collective-permute-start.9 = (bf16[2,48,384]{2,1,0:T(8,128)(2,1)S(1)}, bf16[2,48,384]{2,1,0:T(8,128)(2,1)S(1)}, u32[]{:S(2)}, u32[]{:S(2)}) collective-permute-start(bf16[2,48,384]{2,1,0:T(8,128)(2,1)S(1)} %fusion.4), channel_id=1, source_target_pairs={{0,128},{64,192},{128,0},{192,64},{256,384},{320,448},{384,256},{4... | collective-permute-start | bytes 221192 | tf_op jit(solution)/shard_map/ppermute | solution.py:420
  138.8 4.3 %collective-permute-done.9 = bf16[2,48,384]{2,1,0:T(8,128)(2,1)S(1)} collective-permute-done((bf16[2,48,384]{2,1,0:T(8,128)(2,1)S(1)}, bf16[2,48,384]{2,1,0:T(8,128)(2,1)S(1)}, u32[]{:S(2)}, u32[]{:S(2)}) %collective-permute-start.9) | collective-permute-done | bytes 73760 | tf_op jit(solution)/shard_map/ppermute | solution.py:420
  143.1 7.5 %collective-permute-start.10 = (bf16[1,48,384]{2,1,0:T(8,128)(2,1)S(1)}, bf16[1,48,384]{2,1,0:T(8,128)(2,1)S(1)}, u32[]{:S(2)}, u32[]{:S(2)}) collective-permute-start(bf16[1,48,384]{2,1,0:T(8,128)(2,1)S(1)} %dynamic-slice_convert_fusion.1), channel_id=1, source_target_pairs={{0,256},{64,320},{128,384},{192,448},{256,0},{320,64},{384,128},{4... | collective-permute-start | bytes 110600 | tf_op jit(solution)/shard_map/ppermute | solution.py:420
  151.4 1.0 collective-permute-done.10
  (75 shorter events, 6.4 us)
Async XLA Ops:
  0.6 0.7 copy-start
  1.3 10.2 %copy-start.6 = (f32[1536]{0:T(1024)S(1)}, f32[1536]{0:T(1024)}, u32[]{:S(2)}) copy-start(f32[1536]{0:T(1024)} %param.11) | copy-start | bytes 18436
  1.3 10.2 %copy-start.7 = (f32[1536]{0:T(1024)S(1)}, f32[1536]{0:T(1024)}, u32[]{:S(2)}) copy-start(f32[1536]{0:T(1024)} %param.10) | copy-start | bytes 18436
  2.3 13.3 %collective-permute-start = (bf16[112,128]{1,0:T(8,128)(2,1)S(1)}, bf16[112,128]{1,0:T(8,128)(2,1)S(1)}, u32[]{:S(2)}, u32[]{:S(2)}) collective-permute-start(bf16[112,128]{1,0:T(8,128)(2,1)S(1)} %get-tuple-element.30), channel_id=1, source_target_pairs={{0,16},{16,32},{32,48},{48,64},{64,80},{80,96},{96,112},{112,128},... | collective-permute-start | bytes 86024 | tf_op jit(solution)/shard_map/ppermute | solution.py:303
  6.3 9.2 %collective-permute-start.1 = (bf16[112,128]{1,0:T(8,128)(2,1)S(1)}, bf16[112,128]{1,0:T(8,128)(2,1)S(1)}, u32[]{:S(2)}, u32[]{:S(2)}) collective-permute-start(bf16[112,128]{1,0:T(8,128)(2,1)S(1)} %get-tuple-element.31), channel_id=1, source_target_pairs={{16,0},{32,16},{48,32},{64,48},{80,64},{96,80},{112,96},{128,112},... | collective-permute-start | bytes 86024 | tf_op jit(solution)/shard_map/ppermute | solution.py:303
  12.7 1.8 %copy-start.8 = (f32[31,96]{1,0:T(8,128)S(1)}, f32[31,96]{1,0:T(8,128)}, u32[]{:S(2)}) copy-start(f32[31,96]{1,0:T(8,128)} %param.14) | copy-start | bytes 35716
  12.7 2.8 %copy-start.1 = (s32[384]{0:T(512)S(1)}, s32[384]{0:T(512)}, u32[]{:S(2)}) copy-start(s32[384]{0:T(512)} %mask_ref.1) | copy-start | bytes 4612
  12.7 2.9 %copy-start.3 = (bf16[96,384]{1,0:T(8,128)(2,1)S(1)}, bf16[96,384]{1,0:T(8,128)(2,1)}, u32[]{:S(2)}) copy-start(bf16[96,384]{1,0:T(8,128)(2,1)} %inputs_hbm.1) | copy-start | bytes 221188
  12.7 2.9 %copy-start.4 = (bf16[96,384]{1,0:T(8,128)(2,1)S(1)}, bf16[96,384]{1,0:T(8,128)(2,1)}, u32[]{:S(2)}) copy-start(bf16[96,384]{1,0:T(8,128)(2,1)} %upstream_hbm.1) | copy-start | bytes 221188
  15.6 19.1 %collective-permute-start.2 = (bf16[96,896]{1,0:T(8,128)(2,1)S(1)}, bf16[96,896]{1,0:T(8,128)(2,1)S(1)}, u32[]{:S(2)}, u32[]{:S(2)}) collective-permute-start(bf16[96,896]{1,0:T(8,128)(2,1)S(1)} %get-tuple-element.69), channel_id=1, source_target_pairs={{0,2},{2,0},{1,3},{3,1},{4,6},{6,4},{5,7},{7,5},{8,10},{10,8},{9,1... | collective-permute-start | bytes 516104 | tf_op jit(solution)/shard_map/ppermute | solution.py:20
  34.7 15.6 %copy-start.5 = (bf16[96,896]{1,0:T(8,128)(2,1)}, bf16[96,896]{1,0:T(8,128)(2,1)S(1)}, u32[]{:S(2)}) copy-start(bf16[96,896]{1,0:T(8,128)(2,1)S(1)} %collective-permute-done.2) | copy-start | bytes 516100
  50.3 18.1 %copy-start.2 = (bf16[4,2,96,896]{3,2,1,0:T(8,128)(2,1)}, bf16[4,2,96,896]{3,2,1,0:T(8,128)(2,1)S(1)}, u32[]{:S(2)}) copy-start(bf16[4,2,96,896]{3,2,1,0:T(8,128)(2,1)S(1)} %all_to_all.15.own_hbm) | copy-start | bytes 4128772
  50.3 18.1 %collective-permute-start.3 = (bf16[4,2,96,896]{3,2,1,0:T(8,128)(2,1)S(1)}, bf16[4,2,96,896]{3,2,1,0:T(8,128)(2,1)}, u32[]{:S(2)}, u32[]{:S(2)}) collective-permute-start(bf16[4,2,96,896]{3,2,1,0:T(8,128)(2,1)S(1)} %all_to_all.15.own_hbm), channel_id=1, source_target_pairs={{0,1},{1,0},{2,3},{3,2},{4,5},{5,4},{6,7},{7,6},{8,9},{9,8},{10,11... | collective-permute-start | bytes 4128776 | tf_op jit(solution)/shard_map/ppermute | solution.py:20
  77.8 22.6 %all-to-all-start.1 = ((bf16[8,208,384]{2,1,0:T(8,128)(2,1)}), bf16[8,208,384]{2,1,0:T(8,128)(2,1)S(1)}, u32[]{:S(2)}, u32[]{:S(2)}) async-start(bf16[8,208,384]{2,1,0:T(8,128)(2,1)} %get-tuple-element.43), calls=%async_computation.1 | async-start | bytes 2555904 | tf_op jit(solution)/shard_map/all_to_all | solution.py:369
  81.7 11.6 %collective-permute-start.4 = (bf16[8,48,384]{2,1,0:T(8,128)(2,1)S(1)}, bf16[8,48,384]{2,1,0:T(8,128)(2,1)S(1)}, u32[]{:S(2)}, u32[]{:S(2)}) collective-permute-start(bf16[8,48,384]{2,1,0:T(8,128)(2,1)S(1)} %get-tuple-element.40), channel_id=1, source_target_pairs={{0,16},{16,32},{32,48},{48,0},{1,17},{17,33},{33,49},{49,1},{2,18}... | collective-permute-start | bytes 884744 | tf_op jit(solution)/shard_map/ppermute | solution.py:372
  83.6 16.7 %collective-permute-start.5 = (bf16[8,48,384]{2,1,0:T(8,128)(2,1)S(1)}, bf16[8,48,384]{2,1,0:T(8,128)(2,1)S(1)}, u32[]{:S(2)}, u32[]{:S(2)}) collective-permute-start(bf16[8,48,384]{2,1,0:T(8,128)(2,1)S(1)} %get-tuple-element.41), channel_id=1, source_target_pairs={{0,48},{16,0},{32,16},{48,32},{1,49},{17,1},{33,17},{49,33},{2,50}... | collective-permute-start | bytes 884744 | tf_op jit(solution)/shard_map/ppermute | solution.py:372
  88.2 12.1 %collective-permute-start.6 = (bf16[8,48,384]{2,1,0:T(8,128)(2,1)S(1)}, bf16[8,48,384]{2,1,0:T(8,128)(2,1)S(1)}, u32[]{:S(2)}, u32[]{:S(2)}) collective-permute-start(bf16[8,48,384]{2,1,0:T(8,128)(2,1)S(1)} %get-tuple-element.42), channel_id=1, source_target_pairs={{0,32},{16,48},{32,0},{48,16},{1,33},{17,49},{33,1},{49,17},{2,34}... | collective-permute-start | bytes 884744 | tf_op jit(solution)/shard_map/ppermute | solution.py:372
  100.8 34.0 %collective-permute-start.8 = (bf16[112,384]{1,0:T(8,128)(2,1)S(1)}, bf16[112,384]{1,0:T(8,128)(2,1)S(1)}, u32[]{:S(2)}, u32[]{:S(2)}) collective-permute-start(bf16[112,384]{1,0:T(8,128)(2,1)S(1)} %maximum_maximum_fusion), channel_id=1, source_target_pairs={{0,2},{2,0},{1,3},{3,1},{4,6},{6,4},{5,7},{7,5},{8,10},{10,8},{9,1... | collective-permute-start | bytes 258056 | tf_op jit(solution)/shard_map/ppermute | solution.py:20
  114.8 20.0 %collective-permute-start.7 = (bf16[4,48,384]{2,1,0:T(8,128)(2,1)S(1)}, bf16[4,48,384]{2,1,0:T(8,128)(2,1)S(1)}, u32[]{:S(2)}, u32[]{:S(2)}) collective-permute-start(bf16[4,48,384]{2,1,0:T(8,128)(2,1)S(1)} %fusion.2), channel_id=1, source_target_pairs={{0,64},{64,0},{128,192},{192,128},{256,320},{320,256},{384,448},{4... | collective-permute-start | bytes 442376 | tf_op jit(solution)/shard_map/ppermute | solution.py:384
  124.7 27.6 %all-to-all-start.2 = ((f32[64,2,96]{2,1,0:T(2,128)}), f32[64,2,96]{2,1,0:T(2,128)S(1)}, u32[]{:S(2)}, u32[]{:S(2)}) async-start(f32[64,2,96]{2,1,0:T(2,128)} %bitcast.24), calls=%async_computation.2 | async-start | bytes 131072 | tf_op jit(solution)/shard_map/all_to_all | solution.py:401
  134.9 8.2 %collective-permute-start.9 = (bf16[2,48,384]{2,1,0:T(8,128)(2,1)S(1)}, bf16[2,48,384]{2,1,0:T(8,128)(2,1)S(1)}, u32[]{:S(2)}, u32[]{:S(2)}) collective-permute-start(bf16[2,48,384]{2,1,0:T(8,128)(2,1)S(1)} %fusion.4), channel_id=1, source_target_pairs={{0,128},{64,192},{128,0},{192,64},{256,384},{320,448},{384,256},{4... | collective-permute-start | bytes 221192 | tf_op jit(solution)/shard_map/ppermute | solution.py:420
  143.1 9.2 %collective-permute-start.10 = (bf16[1,48,384]{2,1,0:T(8,128)(2,1)S(1)}, bf16[1,48,384]{2,1,0:T(8,128)(2,1)S(1)}, u32[]{:S(2)}, u32[]{:S(2)}) collective-permute-start(bf16[1,48,384]{2,1,0:T(8,128)(2,1)S(1)} %dynamic-slice_convert_fusion.1), channel_id=1, source_target_pairs={{0,256},{64,320},{128,384},{192,448},{256,0},{320,64},{384,128},{4... | collective-permute-start | bytes 110600 | tf_op jit(solution)/shard_map/ppermute | solution.py:420
